TPU v7x, 32 devices: a whole 2x2x4 slice. The times are simulated.
32 devices in a mesh: dp: 4 (over z), row: 4 (over y, core), col: 2 (over x).
Axes of the slice: x: 2, y: 2, z: 4, core: 2. Of those that a mesh axis runs over, the one named last changes fastest.
Arguments:
- tokens: bfloat16 [8192, 2048], P(('dp', 'col'), 'row'), may hold values from -6 to 6
- seq_ids: int32 [8192], P('dp'), may hold values from 0 to 7, as said below
- block_ids: int32 [8192], P('dp'), may hold values from 0 to 5, as said below
- positions: int32 [8192], P('dp'), may hold values from 0 to 1535, as said below
- norm1_gain: float32 [2048], P('row'), may hold values from 0.5 to 1.5
- norm2_gain: float32 [2048], P('row'), may hold values from 0.5 to 1.5
- w_query: bfloat16 [2048, 2048], P('row', 'col'), may hold values from -0.1875 to 0.1875
- w_kv: bfloat16 [2048, 256], P('row'), may hold values from -0.1875 to 0.1875
- w_out: bfloat16 [2048, 2048], P('col', 'row'), may hold values from -2 to 2
- w_gate: bfloat16 [2048, 5632], P('row', 'col'), may hold values from -0.125 to 0.125
- w_up: bfloat16 [2048, 5632], P('row', 'col'), may hold values from -0.125 to 0.125
- w_down: bfloat16 [5632, 2048], P('col', 'row'), may hold values from -0.078125 to 0.078125
- grad_output: float32 [8192, 2048], P(('dp', 'col'), 'row'), may hold values from -6 to 6
Outputs:
- output: float32 [8192, 2048], P(('dp', 'col'), 'row')
- input_grad: float32 [8192, 2048], P(('dp', 'col'), 'row')
- grad_query: float32 [4, 512, 2048], P('row', 'dp', 'col')
- grad_kv: float32 [4, 512, 256], P('row', ('dp', 'col'))
- grad_out: float32 [2, 1024, 2048], P('col', 'dp', 'row')
- grad_gate: float32 [4, 512, 5632], P('row', 'dp', 'col')
- grad_up: float32 [4, 512, 5632], P('row', 'dp', 'col')
- grad_down: float32 [2, 2816, 2048], P('col', 'dp', 'row')
- grad_norm1: float32 [4, 512], P('row', ('dp', 'col'))
- grad_norm2: float32 [4, 512], P('row', ('dp', 'col'))
Inputs may be any that keep to these rules, and one draw needn't show every extreme that they name: `seq_ids`: tokens of one sequence lie in one aligned run of 2048 tokens; each run holds two sequences of whole 256-token blocks, each a quarter of the run or more; in the first run the first sequence has exactly 2 blocks. block_ids equal positions // 256. positions count from 0 at each sequence's first token.
All inputs are finite; a program needn't handle non-finite values.
Results may differ from a plain program's by a relative error of at most 0.023.
Values may be sent and summed in bfloat16 or wider, within the bound.
No kernel may reach another device: no remote copies, remote signals or barrier semaphores. Data moves between devices by JAX's collectives and lax.ppermute only.
A program may use at most 256 MiB of HBM per device.

v0:
```python
import jax
import jax.numpy as jnp
from jax import lax
from jax.sharding import PartitionSpec as P

D = 2048


EPS = 1e-05
ROPE_BASE = 500000.0
MASKED = -1e30
CONTRACT_ROWS = (((0,), (0,)), ((), ()))
CONTRACT_LAST = (((1,), (1,)), ((), ()))


def rope_tables(positions, head_width):
    halfway = head_width // 2
    frequency = ROPE_BASE ** (-2.0 * jnp.arange(halfway, dtype=jnp.float32) / head_width)
    angles = positions.astype(jnp.float32)[:, None] * frequency[None, :]
    return (jnp.cos(angles), jnp.sin(angles))


def rotate(operand, cosine, sine_part):
    halfway = operand.shape[-1] // 2
    first_half = operand[..., :halfway]
    second_half = operand[..., halfway:]
    return jnp.concatenate(
        [
            first_half * cosine - second_half * sine_part,
            second_half * cosine + first_half * sine_part,
        ],
        axis=-1,
    )


def rotate_back(operand, cosine, sine_part):
    halfway = operand.shape[-1] // 2
    first_half = operand[..., :halfway]
    second_half = operand[..., halfway:]
    return jnp.concatenate(
        [
            first_half * cosine + second_half * sine_part,
            second_half * cosine - first_half * sine_part,
        ],
        axis=-1,
    )


def row_total(operand):
    return lax.psum(operand, "row")


def gather_columns(operand):
    return lax.all_gather(operand, "col", axis=0, tiled=True)


def spread_columns(operand):
    return lax.psum_scatter(
        operand.astype(jnp.bfloat16), "col", scatter_dimension=0, tiled=True
    ).astype(jnp.float32)


def spread_rows(gathered, matrix, contract_dim):
    return lax.psum_scatter(
        lax.dot_general(
            gathered,
            matrix,
            (((1,), (contract_dim,)), ((), ())),
            preferred_element_type=jnp.float32,
        ),
        "row",
        scatter_dimension=0,
        tiled=True,
    )


def fold_rows(operand, matrix, contract_dim, partner, keeping):
    full_rows = operand.shape[0] * lax.axis_size("row")
    grad_shape = (partner.shape[1], operand.shape[1]) if partner is not None else (1, 1)
    grad_zero = jnp.zeros(grad_shape, jnp.float32)
    kept_zero = jnp.zeros((full_rows, operand.shape[1]) if keeping else (1, 1), operand.dtype)
    shard_rows = lax.all_gather(operand, "row", axis=0, tiled=True)
    grad_acc = grad_zero
    kept_rows = kept_zero
    row_block = lax.dot_general(
        shard_rows, matrix, (((1,), (contract_dim,)), ((), ())), preferred_element_type=jnp.float32
    )
    if partner is not None:
        grad_acc = lax.dot_general(
            partner, shard_rows, CONTRACT_ROWS, preferred_element_type=jnp.float32
        )
    if keeping:
        kept_rows = shard_rows
    return (row_block, grad_acc, kept_rows)


def norm_forward(residual, gain):
    rms_factor = lax.rsqrt(row_total(jnp.sum(residual * residual, axis=1)) / D + EPS)[:, None]
    return (rms_factor, (residual * rms_factor * gain[None, :]).astype(jnp.bfloat16))


def norm_backward(residual, rms_factor, gain, normed_grad):
    weighted = normed_grad * gain[None, :]
    inner_sum = row_total(jnp.sum(weighted * residual, axis=1))[:, None]
    input_part = (
        rms_factor * weighted - residual * (rms_factor * rms_factor * rms_factor) * inner_sum / D
    )
    return (input_part, jnp.sum(normed_grad * residual * rms_factor, axis=0))


def per_device(
    tokens,
    seq_ids,
    block_ids,
    positions,
    norm1_gain,
    norm2_gain,
    w_query,
    w_kv,
    w_out,
    w_gate,
    w_up,
    w_down,
    grad_output,
):
    row_count = lax.axis_size("row")
    full_rows = seq_ids.shape[0]
    slab_rows = full_rows // row_count
    slab_start = lax.axis_index("row") * slab_rows
    half_rows = tokens.shape[0]
    half_start = lax.axis_index("col") * half_rows
    head_width = w_kv.shape[1] // 2
    heads_local = w_query.shape[1] // head_width
    ff_local = w_gate.shape[1]
    score_scale = head_width ** (-0.5)
    w_both = jnp.concatenate([w_gate, w_up], axis=1)
    residual = tokens.astype(jnp.float32)
    factor_one, normed = norm_forward(residual, norm1_gain)
    gathered_in = gather_columns(normed)
    query_pre = spread_rows(gathered_in, w_query, 0)
    kv_pre = lax.psum(jnp.dot(gathered_in, w_kv, preferred_element_type=jnp.float32), "row")
    cosine_all, sine_all = rope_tables(positions, head_width)
    cosine_slab = lax.dynamic_slice_in_dim(cosine_all, slab_start, slab_rows, 0)[:, None, :]
    sine_slab = lax.dynamic_slice_in_dim(sine_all, slab_start, slab_rows, 0)[:, None, :]
    queries = rotate(
        query_pre.reshape(slab_rows, heads_local, head_width), cosine_slab, sine_slab
    ).astype(jnp.bfloat16)
    key_rows = rotate(kv_pre[:, :head_width], cosine_all, sine_all).astype(jnp.bfloat16)
    values = kv_pre[:, head_width:].astype(jnp.bfloat16)
    seq_slab = lax.dynamic_slice_in_dim(seq_ids, slab_start, slab_rows, 0)
    block_slab = lax.dynamic_slice_in_dim(block_ids, slab_start, slab_rows, 0)
    allowed = (seq_slab[:, None] == seq_ids[None, :]) & (block_ids[None, :] <= block_slab[:, None])
    head_queries = queries.transpose(1, 0, 2)

    def head_scores(query_head):
        scores = (
            lax.dot_general(query_head, key_rows, CONTRACT_LAST, preferred_element_type=jnp.float32)
            * score_scale
        )
        return jnp.where(allowed, scores, MASKED)

    def head_forward(query_head):
        scores = head_scores(query_head)
        row_max = jnp.max(scores, axis=1, keepdims=True)
        weights_exp = jnp.exp(scores - row_max)
        denominator = jnp.sum(weights_exp, axis=1, keepdims=True)
        probability = (weights_exp / denominator).astype(jnp.bfloat16)
        head_out = jnp.dot(probability, values, preferred_element_type=jnp.float32)
        return (head_out, (row_max + jnp.log(denominator))[:, 0])

    head_outs, log_totals = lax.map(head_forward, head_queries)
    attended = (
        head_outs.transpose(1, 0, 2)
        .reshape(slab_rows, heads_local * head_width)
        .astype(jnp.bfloat16)
    )
    out_product, _, kept_attended = fold_rows(attended, w_out, 0, None, True)
    hidden = residual + spread_columns(out_product)
    factor_two, normed_two = norm_forward(hidden, norm2_gain)
    gathered_mid = gather_columns(normed_two)
    both_proj = spread_rows(gathered_mid, w_both, 0)
    gate_proj = both_proj[:, :ff_local]
    up_proj = both_proj[:, ff_local:]
    sigmoid_gate = jax.nn.sigmoid(gate_proj)
    silu_gate = gate_proj * sigmoid_gate
    mixed_act = (silu_gate * up_proj).astype(jnp.bfloat16)
    down_product, _, kept_mixed = fold_rows(mixed_act, w_down, 0, None, True)
    output = hidden + spread_columns(down_product)
    down_grad = grad_output.astype(jnp.bfloat16)
    gathered_down = gather_columns(down_grad)
    mixed_grad = spread_rows(gathered_down, w_down, 1)
    grad_down_local = lax.dot_general(
        kept_mixed, gathered_down, CONTRACT_ROWS, preferred_element_type=jnp.float32
    )
    gate_grad = (
        mixed_grad * up_proj * sigmoid_gate * (1.0 + gate_proj * (1.0 - sigmoid_gate))
    ).astype(jnp.bfloat16)
    up_grad = (mixed_grad * silu_gate).astype(jnp.bfloat16)
    both_grad = jnp.concatenate([gate_grad, up_grad], axis=1)
    mid_product, grad_both_local, _ = fold_rows(both_grad, w_both, 1, gathered_mid, False)
    norm_two_part, gain_two_part = norm_backward(
        hidden, factor_two, norm2_gain, spread_columns(mid_product)
    )
    hidden_grad = grad_output + norm_two_part
    branch_grad = hidden_grad.astype(jnp.bfloat16)
    gathered_branch = gather_columns(branch_grad)
    attended_grad = spread_rows(gathered_branch, w_out, 1).astype(jnp.bfloat16)
    grad_out_local = lax.dot_general(
        kept_attended, gathered_branch, CONTRACT_ROWS, preferred_element_type=jnp.float32
    )
    head_grads = attended_grad.reshape(slab_rows, heads_local, head_width).transpose(1, 0, 2)

    def head_backward(running, head_inputs):
        key_acc, value_acc = running
        query_head, grad_head, log_total = head_inputs
        probs_full = jnp.exp(head_scores(query_head) - log_total[:, None])
        probs_low = probs_full.astype(jnp.bfloat16)
        value_acc = value_acc + lax.dot_general(
            probs_low, grad_head, CONTRACT_ROWS, preferred_element_type=jnp.float32
        )
        prob_grad = lax.dot_general(
            grad_head, values, CONTRACT_LAST, preferred_element_type=jnp.float32
        )
        row_dot = jnp.sum(probs_full * prob_grad, axis=1, keepdims=True)
        score_grad = (probs_full * (prob_grad - row_dot)).astype(jnp.bfloat16)
        query_grad = jnp.dot(score_grad, key_rows, preferred_element_type=jnp.float32) * score_scale
        key_acc = (
            key_acc
            + lax.dot_general(
                score_grad, query_head, CONTRACT_ROWS, preferred_element_type=jnp.float32
            )
            * score_scale
        )
        return ((key_acc, value_acc), query_grad)

    zero_rows = jnp.zeros((full_rows, head_width), jnp.float32)
    (key_acc, value_acc), query_grads = lax.scan(
        head_backward, (zero_rows, zero_rows), (head_queries, head_grads, log_totals)
    )
    key_total, value_total = (
        lax.psum(key_acc.astype(jnp.bfloat16), ("row", "col")).astype(jnp.float32),
        lax.psum(value_acc.astype(jnp.bfloat16), ("row", "col")).astype(jnp.float32),
    )
    query_pre_grad = (
        rotate_back(query_grads.transpose(1, 0, 2), cosine_slab, sine_slab)
        .reshape(slab_rows, heads_local * head_width)
        .astype(jnp.bfloat16)
    )
    kv_pre_grad = jnp.concatenate(
        [rotate_back(key_total, cosine_all, sine_all), value_total], axis=1
    ).astype(jnp.bfloat16)
    in_product, grad_query_local, _ = fold_rows(query_pre_grad, w_query, 1, gathered_in, False)
    kv_rows = lax.dynamic_slice_in_dim(kv_pre_grad, half_start, half_rows, 0)
    normed_grad = spread_columns(in_product) + lax.dot_general(
        kv_rows, w_kv, CONTRACT_LAST, preferred_element_type=jnp.float32
    )
    grad_kv_local = lax.dot_general(
        normed, kv_rows, CONTRACT_ROWS, preferred_element_type=jnp.float32
    )
    norm_one_part, gain_one_part = norm_backward(residual, factor_one, norm1_gain, normed_grad)
    input_grad = hidden_grad + norm_one_part
    reduced = (
        lax.psum_scatter(
            grad_query_local.astype(jnp.bfloat16), "dp", scatter_dimension=0, tiled=True
        ).astype(jnp.float32),
        lax.psum_scatter(
            grad_out_local.astype(jnp.bfloat16), "dp", scatter_dimension=0, tiled=True
        ).astype(jnp.float32),
        lax.psum_scatter(
            grad_both_local[:, :ff_local].astype(jnp.bfloat16),
            "dp",
            scatter_dimension=0,
            tiled=True,
        ).astype(jnp.float32),
        lax.psum_scatter(
            grad_both_local[:, ff_local:].astype(jnp.bfloat16),
            "dp",
            scatter_dimension=0,
            tiled=True,
        ).astype(jnp.float32),
        lax.psum_scatter(
            grad_down_local.astype(jnp.bfloat16), "dp", scatter_dimension=0, tiled=True
        ).astype(jnp.float32),
    )
    small_sums = (
        lax.psum_scatter(
            grad_kv_local.astype(jnp.bfloat16), ("dp", "col"), scatter_dimension=0, tiled=True
        ).astype(jnp.float32),
        lax.psum_scatter(
            jnp.stack([gain_one_part, gain_two_part], axis=1).astype(jnp.bfloat16),
            ("dp", "col"),
            scatter_dimension=0,
            tiled=True,
        ).astype(jnp.float32),
    )
    return (
        output,
        input_grad,
        reduced[0][None],
        small_sums[0][None],
        reduced[1][None],
        reduced[2][None],
        reduced[3][None],
        reduced[4][None],
        small_sums[1][:, 0][None, :],
        small_sums[1][:, 1][None, :],
    )


def solution(mesh):
    placed = (
        P(("dp", "col"), "row"),
        P("dp"),
        P("dp"),
        P("dp"),
        P("row"),
        P("row"),
        P("row", "col"),
        P("row", None),
        P("col", "row"),
        P("row", "col"),
        P("row", "col"),
        P("col", "row"),
        P(("dp", "col"), "row"),
    )
    return jax.shard_map(
        per_device,
        mesh=mesh,
        in_specs=placed,
        out_specs=(
            P(("dp", "col"), "row"),
            P(("dp", "col"), "row"),
            P("row", "dp", "col"),
            P("row", ("dp", "col"), None),
            P("col", "dp", "row"),
            P("row", "dp", "col"),
            P("row", "dp", "col"),
            P("col", "dp", "row"),
            P("row", ("dp", "col")),
            P("row", ("dp", "col")),
        ),
        check_vma=False,
    )
```

profile of v0, /device:TPU:0, one launch (start us, length us, event | category | flops | bytes accessed | tf_op | source)
XLA Modules:
  0.0 1890.9 jit_solution(8827306254039716388)
XLA Ops:
  8.9 8.4 psum.49
  21.1 33.5 %all-gather.9.cloned.1.call-done = bf16[2048,512]{1,0:T(8,128)(2,1)} async-done(((bf16[1024,512]{1,0:T(8,128)(2,1)}), bf16[2048,512]{1,0:T(8,128)(2,1)}) %all-gather.9.cloned.1.call-update) | async-done | bytes 2097168 | tf_op jit(solution)/shard_map/all_gather | solution.py:54
  58.3 7.5 fusion.66
  70.2 39.6 %all-reduce.4.cloned.1.call-done = f32[2048,256]{1,0:T(8,128)} async-done(((f32[2048,256]{1,0:T(8,128)}), f32[2048,256]{1,0:T(8,128)}) %all-reduce.4.cloned.1.call-update) | async-done | bytes 2097168 | tf_op jit(solution)/shard_map/psum | solution.py:141
  109.8 7.8 fusion.54
  122.4 62.0 %reduce-scatter.18.cloned.1.call-done = f32[512,1024]{1,0:T(8,128)} async-done(((f32[2048,1024]{1,0:T(8,128)}), f32[512,1024]{1,0:T(8,128)}) %reduce-scatter.18.cloned.1.call-update) | async-done | bytes 2097168 | tf_op jit(solution)/shard_map/reduce_scatter | solution.py:64
  192.5 66.3 %while.30 = (s32[]{:T(128)}, bf16[8,512,128]{1,2,0:T(8,128)(2,1)}, f32[8,512]{1,0:T(8,128)S(1)}, bf16[8,512,128]{2,1,0:T(8,128)(2,1)}, bf16[2048,128]{1,0:T(8,12...) while((s32[]{:T(128)}, bf16[8,512,128]{1,2,0:T(8,128)(2,1)}, ...), condition=%wide.region_7.8_spmd.clone.clone, body=%wide.region_4.7_spmd.clone.sunk.clone | while | flops 548404736 | bytes 30844036 | solution.py:171
  213.5 3.9 fusion.146
  258.9 34.6 %all-gather.11.cloned.1.call-done = bf16[2048,1024]{0,1:T(8,128)(2,1)} async-done(((bf16[512,1024]{0,1:T(8,128)(2,1)}), bf16[2048,1024]{0,1:T(8,128)(2,1)}) %all-gather.11.cloned.1.call-update) | async-done | bytes 4194320 | tf_op jit(solution)/shard_map/all_gather | solution.py:82
  293.5 6.2 convolution_convert_fusion.4
  303.0 28.7 %reduce-scatter.20.cloned.1.call-done = bf16[1024,512]{1,0:T(8,128)(2,1)} async-done(((bf16[2048,512]{1,0:T(8,128)(2,1)}), bf16[1024,512]{1,0:T(8,128)(2,1)}) %reduce-scatter.20.cloned.1.call-update) | async-done | bytes 1048592 | tf_op jit(solution)/shard_map/reduce_scatter | solution.py:58
  333.6 6.9 psum.51
  343.7 23.2 %all-gather.17.cloned.1.call-done = bf16[2048,512]{1,0:T(8,128)(2,1)} async-done(((bf16[1024,512]{1,0:T(8,128)(2,1)}), bf16[2048,512]{1,0:T(8,128)(2,1)}) %all-gather.17.cloned.1.call-update) | async-done | bytes 2097168 | tf_op jit(solution)/shard_map/all_gather | solution.py:54
  366.9 13.4 fusion.69
  385.9 16.3 all-gather.13.cloned.1.call-done
  402.2 34.2 %fusion.68 = f32[2048,5632]{1,0:T(8,128)} fusion(bf16[2048,512]{1,0:T(8,128)(2,1)} %all-gather.13.cloned.1.call-done, bf16[512,5632]{1,0:T(8,128)(2,1)} %constant_dynamic-update-slice_fusion.1), kind=kOutput, calls=%fused_computation.138 | convolution fusion | flops 11811160064 | bytes 54001664 | tf_op jit(solution)/shard_map/dot_general | solution.py:65
  436.5 135.3 %reduce-scatter.26.cloned.1.call-done = f32[512,2816]{1,0:T(8,128)} async-done(((f32[2048,2816]{1,0:T(8,128)}), f32[512,2816]{1,0:T(8,128)}) %reduce-scatter.26.cloned.1.call-update) | async-done | bytes 5767184 | tf_op jit(solution)/shard_map/reduce_scatter | solution.py:64
  571.8 318.6 %reduce-scatter.22.cloned.1.call-done = f32[512,5632]{1,0:T(8,128)} async-done(((f32[2048,5632]{1,0:T(8,128)}), f32[512,5632]{1,0:T(8,128)}) %reduce-scatter.22.cloned.1.call-update) | async-done | bytes 11534352 | tf_op jit(solution)/shard_map/reduce_scatter | solution.py:64
  890.4 8.8 multiply_convert_fusion.2
  902.3 143.2 %all-gather.19.cloned.1.call-done = bf16[2048,5632]{1,0:T(8,128)(2,1)} async-done(((bf16[512,5632]{1,0:T(8,128)(2,1)}), bf16[2048,5632]{1,0:T(8,128)(2,1)}) %all-gather.19.cloned.1.call-update) | async-done | bytes 23068688 | tf_op jit(solution)/shard_map/all_gather | solution.py:82
  1045.4 19.2 %convolution_convert_fusion.2 = bf16[2048,512]{1,0:T(8,128)(2,1)} fusion(bf16[2048,5632]{1,0:T(8,128)(2,1)} %all-gather.19.cloned.1.call-done, bf16[512,5632]{1,0:T(8,128)(2,1)} %constant_dynamic-update-slice_fusion.1), kind=kOutput, calls=%fused_computation.51 | convolution fusion | flops 11812208640 | bytes 30932992 | tf_op jit(solution)/shard_map/dot_general | solution.py:85
  1064.7 31.9 %reduce-scatter.28.cloned.1.call-done = bf16[1024,512]{1,0:T(8,128)(2,1)} async-done(((bf16[2048,512]{1,0:T(8,128)(2,1)}), bf16[1024,512]{1,0:T(8,128)(2,1)}) %reduce-scatter.28.cloned.1.call-update) | async-done | bytes 1048592 | tf_op jit(solution)/shard_map/reduce_scatter | solution.py:58
  1099.4 6.9 psum.52
  1110.1 32.3 %all-gather.21.cloned.1.call-done = bf16[2048,512]{1,0:T(8,128)(2,1)} async-done(((bf16[1024,512]{1,0:T(8,128)(2,1)}), bf16[2048,512]{1,0:T(8,128)(2,1)}) %all-gather.21.cloned.1.call-update) | async-done | bytes 2097168 | tf_op jit(solution)/shard_map/all_gather | solution.py:54
  1142.4 7.5 fusion.70
  1150.6 71.2 %reduce-scatter.30.cloned.1.call-done = f32[512,1024]{1,0:T(8,128)} async-done(((f32[2048,1024]{1,0:T(8,128)}), f32[512,1024]{1,0:T(8,128)}) %reduce-scatter.30.cloned.1.call-update) | async-done | bytes 2097168 | tf_op jit(solution)/shard_map/reduce_scatter | solution.py:64
  1224.6 133.2 %while.31 = (s32[]{:T(128)}, f32[2048,128]{1,0:T(8,128)}, f32[2048,128]{1,0:T(8,128)}, f32[8,512,128]{1,2,0:T(8,128)}, bf16[8,512,128]{2,1,0:T(8,128)(2,1)}, /*i...) while((s32[]{:T(128)}, f32[2048,128]{1,0:T(8,128)}, ...), condition=%wide.region_20.21_spmd.clone.clone, body=%wide.region_18.20_spmd.clone.sunk.clone | while | flops 1356135936 | bytes 87327544 | solution.py:237
  1234.4 4.0 fusion.157
  1364.1 11.0 convolution_convert_fusion.1
  1375.2 17.5 convolution_convert_fusion
  1396.4 6.2 convolution_convert_fusion.6
  1402.9 14.7 all-reduce.6.cloned.1.call-done
  1418.8 4.8 fusion.60
  1425.2 28.0 %all-gather.23.cloned.1.call-done = bf16[2048,1024]{0,1:T(8,128)(2,1)} async-done(((bf16[512,1024]{0,1:T(8,128)(2,1)}), bf16[2048,1024]{0,1:T(8,128)(2,1)}) %all-gather.23.cloned.1.call-update) | async-done | bytes 4194320 | tf_op jit(solution)/shard_map/all_gather | solution.py:82
  1453.3 6.2 convolution_convert_fusion.7
  1459.5 6.7 convolution_convert_fusion.3
  1466.3 9.9 convolution_convert_fusion.5
  1476.2 35.5 %reduce-scatter.44.cloned.1.call-done = bf16[704,512]{1,0:T(8,128)(2,1)} async-done(((bf16[2816,512]{1,0:T(8,128)(2,1)}), bf16[704,512]{1,0:T(8,128)(2,1)}) %reduce-scatter.44.cloned.1.call-update) | async-done | bytes 720912 | tf_op jit(solution)/shard_map/reduce_scatter | solution.py:281
  1514.1 55.9 %reduce-scatter.42.cloned.1.call-done = bf16[128,2816]{1,0:T(8,128)(2,1)} async-done(((bf16[512,2816]{1,0:T(8,128)(2,1)}), bf16[128,2816]{1,0:T(8,128)(2,1)}) %reduce-scatter.42.cloned.1.call-update) | async-done | bytes 720912 | tf_op jit(solution)/shard_map/reduce_scatter | solution.py:275
  1572.4 56.2 %reduce-scatter.40.cloned.1.call-done = bf16[128,2816]{1,0:T(8,128)(2,1)} async-done(((bf16[512,2816]{1,0:T(8,128)(2,1)}), bf16[128,2816]{1,0:T(8,128)(2,1)}) %reduce-scatter.40.cloned.1.call-update) | async-done | bytes 720912 | tf_op jit(solution)/shard_map/reduce_scatter | solution.py:269
  1630.8 27.0 %reduce-scatter.38.cloned.1.call-done = bf16[256,512]{1,0:T(8,128)(2,1)} async-done(((bf16[1024,512]{1,0:T(8,128)(2,1)}), bf16[256,512]{1,0:T(8,128)(2,1)}) %reduce-scatter.38.cloned.1.call-update) | async-done | bytes 262160 | tf_op jit(solution)/shard_map/reduce_scatter | solution.py:266
  1659.6 62.0 %reduce-scatter.36.cloned.1.call-done = bf16[64,256]{1,0:T(8,128)(2,1)} async-done(((bf16[512,256]{1,0:T(8,128)(2,1)}), bf16[64,256]{1,0:T(8,128)(2,1)}) %reduce-scatter.36.cloned.1.call-update) | async-done | bytes 32784 | tf_op jit(solution)/shard_map/reduce_scatter | solution.py:286
  1723.0 27.2 %reduce-scatter.34.cloned.1.call-done = bf16[128,1024]{1,0:T(8,128)(2,1)} async-done(((bf16[512,1024]{1,0:T(8,128)(2,1)}), bf16[128,1024]{1,0:T(8,128)(2,1)}) %reduce-scatter.34.cloned.1.call-update) | async-done | bytes 262160 | tf_op jit(solution)/shard_map/reduce_scatter | solution.py:263
  1751.9 31.6 %reduce-scatter.32.cloned.1.call-done = bf16[1024,512]{1,0:T(8,128)(2,1)} async-done(((bf16[2048,512]{1,0:T(8,128)(2,1)}), bf16[1024,512]{1,0:T(8,128)(2,1)}) %reduce-scatter.32.cloned.1.call-update) | async-done | bytes 1048592 | tf_op jit(solution)/shard_map/reduce_scatter | solution.py:58
  1788.2 6.8 psum.55
  1795.0 23.1 %reduce-scatter.24.cloned.1.call-done = bf16[1024,512]{1,0:T(8,128)(2,1)} async-done(((bf16[2048,512]{1,0:T(8,128)(2,1)}), bf16[1024,512]{1,0:T(8,128)(2,1)}) %reduce-scatter.24.cloned.1.call-update) | async-done | bytes 1048592 | tf_op jit(solution)/shard_map/reduce_scatter | solution.py:58
  1818.1 5.4 fusion.41
  1823.5 59.1 %reduce-scatter.46.cloned.1.call-done = bf16[64,2]{1,0:T(8,128)(2,1)} async-done(((bf16[512,2]{1,0:T(8,128)(2,1)}), bf16[64,2]{1,0:T(8,128)(2,1)}) %reduce-scatter.46.cloned.1.call-update) | async-done | bytes 272
  (373 shorter events, 275.8 us)
Async XLA Ops:
  7.2 359.7 %copy-start = (bf16[2816,512]{1,0:T(8,128)(2,1)S(1)}, bf16[2816,512]{1,0:T(8,128)(2,1)}, u32[]{:S(2)}) copy-start(bf16[2816,512]{1,0:T(8,128)(2,1)} %param.28) | copy-start | bytes 8650756
  7.2 47.4 %copy-start.15 = (bf16[512,256]{1,0:T(8,128)(2,1)S(1)}, bf16[512,256]{1,0:T(8,128)(2,1)}, u32[]{:S(2)}) copy-start(bf16[512,256]{1,0:T(8,128)(2,1)} %param.24) | copy-start | bytes 786436
  7.2 47.4 %all-gather.9.cloned.1.call-start = ((), (), s32[]{:S(2)}) async-start(), calls=%async_computation.15 | async-start | bytes 3145728 | tf_op jit(solution)/shard_map/all_gather | solution.py:54
  21.0 88.7 %all-reduce.4.cloned.1.call-start = ((), (), s32[]{:S(2)}) async-start(), calls=%async_computation.17 | async-start | bytes 4194304 | tf_op jit(solution)/shard_map/psum | solution.py:141
  58.2 126.1 %reduce-scatter.18.cloned.1.call-start = ((), (), s32[]{:S(2)}) async-start(), calls=%async_computation.16 | async-start | bytes 10485760 | tf_op jit(solution)/shard_map/reduce_scatter | solution.py:64
  65.8 227.7 %all-gather.11.cloned.1.call-start = ((), (), s32[]{:S(2)}) async-start(), calls=%async_computation.18 | async-start | bytes 5242880 | tf_op jit(solution)/shard_map/all_gather | solution.py:82
  66.4 51.1 %copy-start.16 = (f32[2048]{0:T(1024)}, f32[2048]{0:T(1024)S(1)}, u32[]{:S(2)}) copy-start(f32[2048]{0:T(1024)S(1)} %convert_element_type.116) | copy-start | bytes 24580
  69.1 48.4 %copy-start.26 = (f32[64]{0:T(128)}, f32[64]{0:T(128)S(1)}, u32[]{:S(2)}) copy-start(f32[64]{0:T(128)S(1)} %multiply_power_fusion) | copy-start | bytes 772
  117.7 69.5 %copy-start.11 = (f32[512,64]{0,1:T(8,128)}, f32[512,64]{0,1:T(8,128)S(1)}, u32[]{:S(2)}) copy-start(f32[512,64]{0,1:T(8,128)S(1)} %copy.36) | copy-start | bytes 393220
  189.1 3.4 copy-start.24
  258.8 72.8 %reduce-scatter.20.cloned.1.call-start = ((), (), s32[]{:S(2)}) async-start(), calls=%async_computation.19 | async-start | bytes 3145728 | tf_op jit(solution)/shard_map/reduce_scatter | solution.py:58
  299.7 67.2 %all-gather.17.cloned.1.call-start = ((), (), s32[]{:S(2)}) async-start(), calls=%async_computation.24 | async-start | bytes 3145728 | tf_op jit(solution)/shard_map/all_gather | solution.py:54
  302.4 38.1 %copy-start.20 = (f32[512]{0:T(512)S(1)}, f32[512]{0:T(512)}, u32[]{:S(2)}) copy-start(f32[512]{0:T(512)} %param.22) | copy-start | bytes 6148
  302.5 99.8 %all-gather.13.cloned.1.call-start = ((), (), s32[]{:S(2)}) async-start(), calls=%async_computation.20 | async-start | bytes 3145728 | tf_op jit(solution)/shard_map/all_gather | solution.py:54
  343.6 228.2 %reduce-scatter.26.cloned.1.call-start = ((), (), s32[]{:S(2)}) async-start(), calls=%async_computation.25 | async-start | bytes 28835840 | tf_op jit(solution)/shard_map/reduce_scatter | solution.py:64
  380.3 510.1 %reduce-scatter.22.cloned.1.call-start = ((), (), s32[]{:S(2)}) async-start(), calls=%async_computation.21 | async-start | bytes 57671680 | tf_op jit(solution)/shard_map/reduce_scatter | solution.py:64
  380.4 3.8 copy-start.10
  436.5 608.9 %all-gather.19.cloned.1.call-start = ((), (), s32[]{:S(2)}) async-start(), calls=%async_computation.26 | async-start | bytes 28835840 | tf_op jit(solution)/shard_map/all_gather | solution.py:82
  902.1 194.5 %reduce-scatter.28.cloned.1.call-start = ((), (), s32[]{:S(2)}) async-start(), calls=%async_computation.27 | async-start | bytes 3145728 | tf_op jit(solution)/shard_map/reduce_scatter | solution.py:58
  1064.6 77.8 %all-gather.21.cloned.1.call-start = ((), (), s32[]{:S(2)}) async-start(), calls=%async_computation.28 | async-start | bytes 3145728 | tf_op jit(solution)/shard_map/all_gather | solution.py:54
  1110.1 111.8 %reduce-scatter.30.cloned.1.call-start = ((), (), s32[]{:S(2)}) async-start(), calls=%async_computation.29 | async-start | bytes 10485760 | tf_op jit(solution)/shard_map/reduce_scatter | solution.py:64
  1150.0 214.1 %all-gather.15.cloned.1.call-start = ((), (), s32[]{:S(2)}) async-start(), calls=%async_computation.22 | async-start | bytes 14417920 | tf_op jit(solution)/shard_map/all_gather | solution.py:82
  1150.6 267.1 %all-reduce.6.cloned.1.call-start = ((), (), s32[]{:S(2)}) async-start(), calls=%async_computation.39 | async-start | bytes 2097152 | tf_op jit(solution)/shard_map/psum | solution.py:241
  1234.4 4.7 copy-start.3
  1251.5 3.9 copy-start.3
  1268.2 3.8 copy-start.3
  1284.7 3.8 copy-start.3
  1301.3 3.8 copy-start.3
  1317.8 3.8 copy-start.3
  1334.4 3.8 copy-start.3
  1350.9 3.8 copy-start.3
  1360.8 92.4 %all-gather.23.cloned.1.call-start = ((), (), s32[]{:S(2)}) async-start(), calls=%async_computation.30 | async-start | bytes 5242880 | tf_op jit(solution)/shard_map/all_gather | solution.py:82
  1364.1 147.7 %reduce-scatter.44.cloned.1.call-start = ((), (), s32[]{:S(2)}) async-start(), calls=%async_computation.37 | async-start | bytes 3604480 | tf_op jit(solution)/shard_map/reduce_scatter | solution.py:281
  1375.2 194.9 %reduce-scatter.42.cloned.1.call-start = ((), (), s32[]{:S(2)}) async-start(), calls=%async_computation.36 | async-start | bytes 3604480 | tf_op jit(solution)/shard_map/reduce_scatter | solution.py:275
  1395.6 232.9 %reduce-scatter.40.cloned.1.call-start = ((), (), s32[]{:S(2)}) async-start(), calls=%async_computation.35 | async-start | bytes 3604480 | tf_op jit(solution)/shard_map/reduce_scatter | solution.py:269
  1396.4 261.5 %reduce-scatter.38.cloned.1.call-start = ((), (), s32[]{:S(2)}) async-start(), calls=%async_computation.34 | async-start | bytes 1310720 | tf_op jit(solution)/shard_map/reduce_scatter | solution.py:266
  1402.6 16.2 copy-start.17
  1402.6 16.2 copy-start.27
  1402.6 319.0 %reduce-scatter.36.cloned.1.call-start = ((), (), s32[]{:S(2)}) async-start(), calls=%async_computation.33 | async-start | bytes 294912 | tf_op jit(solution)/shard_map/reduce_scatter | solution.py:286
  1417.6 6.1 copy-start.14
  1418.8 5.1 copy-start.9
  1425.2 324.9 %reduce-scatter.34.cloned.1.call-start = ((), (), s32[]{:S(2)}) async-start(), calls=%async_computation.32 | async-start | bytes 1310720 | tf_op jit(solution)/shard_map/reduce_scatter | solution.py:263
  1459.5 324.1 %reduce-scatter.32.cloned.1.call-start = ((), (), s32[]{:S(2)}) async-start(), calls=%async_computation.31 | async-start | bytes 3145728 | tf_op jit(solution)/shard_map/reduce_scatter | solution.py:58
  1466.2 351.9 %reduce-scatter.24.cloned.1.call-start = ((), (), s32[]{:S(2)}) async-start(), calls=%async_computation.23 | async-start | bytes 3145728 | tf_op jit(solution)/shard_map/reduce_scatter | solution.py:58
  1476.2 406.4 %reduce-scatter.46.cloned.1.call-start = ((), (), s32[]{:S(2)}) async-start(), calls=%async_computation.38 | async-start | bytes 147456
  1572.4 211.2 %copy-start.19 = (f32[1024]{0:T(1024)S(1)}, f32[1024]{0:T(1024)}, u32[]{:S(2)}) copy-start(f32[1024]{0:T(1024)} %copy-done.18) | copy-start | bytes 12292
  1572.4 211.2 %copy-start.22 = (f32[512]{0:T(512)S(1)}, f32[512]{0:T(512)}, u32[]{:S(2)}) copy-start(f32[512]{0:T(512)} %param.21) | copy-start | bytes 6148
  1751.9 66.2 %copy-start.21 = (f32[1024]{0:T(1024)S(1)}, f32[1024]{0:T(1024)}, u32[]{:S(2)}) copy-start(f32[1024]{0:T(1024)} %get-tuple-element.300) | copy-start | bytes 12292
  (56 other events, 116.3 us)
Sparse Core Ops, SparseCore 0:
  21.1 33.3 all-gather.8
  58.3 51.3 all-reduce.3
  112.5 71.7 reduce-scatter.17
  259.0 34.4 all-gather.10
  299.8 31.8 reduce-scatter.19
  333.7 33.1 all-gather.16
  369.1 33.1 all-gather.12
  405.0 166.7 reduce-scatter.25
  574.4 315.9 reduce-scatter.21
  902.2 143.2 all-gather.18
  1064.8 31.8 reduce-scatter.27
  1110.2 32.2 all-gather.20
  1150.1 71.7 reduce-scatter.29
  1223.4 76.1 all-gather.14
  1360.9 56.6 all-reduce.5
  1419.7 33.5 all-gather.22
  1455.5 56.1 reduce-scatter.43
  1514.0 56.0 reduce-scatter.41
  1572.5 56.0 reduce-scatter.39
  1630.8 26.9 reduce-scatter.37
  1661.7 59.8 reduce-scatter.35
  1723.9 26.2 reduce-scatter.33
  1753.0 30.4 reduce-scatter.31
  1786.2 31.8 reduce-scatter.23
  1821.8 60.7 reduce-scatter.45
where the time goes:
time: 1900 us; the launch traced here: 1890 us
  waiting for transfers between devices  1390 us (73%)
  matrix products  303 us (16%)
  other arithmetic  86.5 us (5%)
  local copies, waits for them, and re-layouts  63 us (3%)
  blocking collectives  28.9 us (2%)
    reduce_scatter x4, waiting for transfers between devices, spread_rows(): lax.psum_scatter(lax.dot_general(gathered, matrix, (((1,), (contract_dim,...  587 us
    all_gather x4, waiting for transfers between devices, fold_rows(): shard_rows = lax.all_gather(operand, 'row', axis=0, tiled=True)  206 us
    reduce_scatter x4, waiting for transfers between devices, spread_columns(): lax.psum_scatter(operand.astype(jnp.bfloat16), 'col', scatter_dimension=0...  115 us
    all_gather x4, waiting for transfers between devices, gather_columns(): return lax.all_gather(operand, 'col', axis=0, tiled=True)  105 us
    dot_general x4, matrix products, spread_rows(): lax.dot_general(gathered, matrix, (((1,), (contract_dim,)), ((), ())), pr...  62.7 us
    reduce_scatter x1, waiting for transfers between devices, per_device(): lax.psum_scatter(grad_kv_local.astype(jnp.bfloat16), ('dp', 'col'), scatt...  62 us
    unnamed x26, waiting for transfers between devices  60.6 us
    reduce_scatter x1, waiting for transfers between devices, per_device(): lax.psum_scatter(grad_both_local[:, :ff_local].astype(jnp.bfloat16), 'dp'...  56.2 us
  transfers between devices with their start and end apart: 25, of which 24 were waited for; matrix products, arithmetic and copies ran while one was open for 15% of the time, Pallas kernels for 0%

commit v1 on v0

v1 whole, which is shorter than its diff:
```python
import functools

import jax
import jax.numpy as jnp
from jax import lax
from jax.experimental import pallas as pl
from jax.experimental.pallas import tpu as pltpu
from jax.sharding import PartitionSpec as P

D = 2048
EPS = 1e-05
ROPE_BASE = 500000.0
BLOCK = 256
LOG2E = 1.4426950408889634
BF = jnp.bfloat16
F32 = jnp.float32
HEADS_PER_STEP = 2


def dot_nn(a, b):
    return lax.dot_general(a, b, (((1,), (0,)), ((), ())), preferred_element_type=F32)


def dot_nt(a, b):
    return lax.dot_general(a, b, (((1,), (1,)), ((), ())), preferred_element_type=F32)


def dot_tn(a, b):
    return lax.dot_general(a, b, (((0,), (0,)), ((), ())), preferred_element_type=F32)


def attend_body(meta, q_ref, cos_ref, sin_ref, k_ref, vt_ref, att_ref, rot_ref, lse_ref, *, factor, width):
    cosine = cos_ref[...]
    sine = sin_ref[...]
    rows = q_ref.shape[0]
    for head in range(HEADS_PER_STEP):
        cols = slice(head * width, (head + 1) * width)
        pre = q_ref[:, cols]
        rot = (pre * cosine + pltpu.roll(pre, width // 2, 1) * sine).astype(BF)
        rot_ref[:, cols] = rot

        def step(t, carry):
            top, total, acc = carry
            chunk = meta[2 + meta[0] + t]
            scores = dot_nt(k_ref[chunk], rot) * factor
            new_top = jnp.maximum(top, jnp.max(scores, axis=0, keepdims=True))
            decay = jnp.exp2(top - new_top)
            weights = jnp.exp2(scores - new_top)
            total = total * decay + jnp.sum(weights, axis=0, keepdims=True)
            acc = acc * decay + dot_nn(vt_ref[chunk], weights.astype(BF))
            return (new_top, total, acc)

        top, total, acc = lax.fori_loop(
            0,
            meta[1],
            step,
            (
                jnp.full((1, rows), -1e30, F32),
                jnp.zeros((1, rows), F32),
                jnp.zeros((width, rows), F32),
            ),
        )
        att_ref[:, cols] = (acc / total).T.astype(BF)
        lse_ref[head] = top + jnp.log2(total)


def attend(meta, q_pre, cosine, sine, keys, values_t, width):
    rows, columns = q_pre.shape
    heads = columns // width
    chunks = keys.shape[0]
    span = HEADS_PER_STEP * width
    whole2 = lambda i, m: (0, 0)
    whole3 = lambda i, m: (0, 0, 0)
    return pl.pallas_call(
        functools.partial(attend_body, factor=width**-0.5 * LOG2E, width=width),
        grid_spec=pltpu.PrefetchScalarGridSpec(
            num_scalar_prefetch=1,
            grid=(heads // HEADS_PER_STEP,),
            in_specs=[
                pl.BlockSpec((rows, span), lambda i, m: (0, i)),
                pl.BlockSpec((rows, width), whole2),
                pl.BlockSpec((rows, width), whole2),
                pl.BlockSpec((chunks, rows, width), whole3),
                pl.BlockSpec((chunks, width, rows), whole3),
            ],
            out_specs=[
                pl.BlockSpec((rows, span), lambda i, m: (0, i)),
                pl.BlockSpec((rows, span), lambda i, m: (0, i)),
                pl.BlockSpec((HEADS_PER_STEP, 1, rows), lambda i, m: (i, 0, 0)),
            ],
        ),
        out_shape=[
            jax.ShapeDtypeStruct((rows, columns), BF),
            jax.ShapeDtypeStruct((rows, columns), BF),
            jax.ShapeDtypeStruct((heads, 1, rows), F32),
        ],
        name="attend",
    )(meta, q_pre, cosine, sine, keys, values_t)


def attend_back_body(
    meta, rot_ref, grad_ref, att_ref, lse_ref, cos_ref, sin_ref, k_ref, kt_ref, v_ref,
    qpg_ref, dk_ref, dv_ref, *, factor, scale, width,
):
    @pl.when(pl.program_id(0) == 0)
    def _():
        dk_ref[...] = jnp.zeros_like(dk_ref)
        dv_ref[...] = jnp.zeros_like(dv_ref)

    cosine = cos_ref[...]
    sine = sin_ref[...]
    rows = rot_ref.shape[0]
    for head in range(HEADS_PER_STEP):
        cols = slice(head * width, (head + 1) * width)
        rot = rot_ref[:, cols]
        grad = grad_ref[:, cols]
        inner = (grad.astype(F32) * att_ref[:, cols].astype(F32)).T
        inner = jnp.sum(inner, axis=0, keepdims=True)
        lse = lse_ref[head]

        def step(t, dq):
            chunk = meta[2 + meta[0] + t]
            probs = jnp.exp2(dot_nt(k_ref[chunk], rot) * factor - lse)
            back = dot_nt(v_ref[chunk], grad)
            score_grad = (probs * (back - inner)).astype(BF)
            dv_ref[chunk] += dot_nn(probs.astype(BF), grad)
            dk_ref[chunk] += dot_nn(score_grad, rot)
            return dq + dot_nn(kt_ref[chunk], score_grad)

        dq = lax.fori_loop(0, meta[1], step, jnp.zeros((width, rows), F32)).T * scale
        qpg_ref[:, cols] = (dq * cosine - pltpu.roll(dq, width // 2, 1) * sine).astype(BF)


def attend_back(meta, rot, grad, att, lse, cosine, sine, keys, keys_t, values, width):
    rows, columns = rot.shape
    heads = columns // width
    chunks = keys.shape[0]
    span = HEADS_PER_STEP * width
    whole2 = lambda i, m: (0, 0)
    whole3 = lambda i, m: (0, 0, 0)
    by_head = lambda i, m: (0, i)
    return pl.pallas_call(
        functools.partial(
            attend_back_body, factor=width**-0.5 * LOG2E, scale=width**-0.5, width=width
        ),
        grid_spec=pltpu.PrefetchScalarGridSpec(
            num_scalar_prefetch=1,
            grid=(heads // HEADS_PER_STEP,),
            in_specs=[
                pl.BlockSpec((rows, span), by_head),
                pl.BlockSpec((rows, span), by_head),
                pl.BlockSpec((rows, span), by_head),
                pl.BlockSpec((HEADS_PER_STEP, 1, rows), lambda i, m: (i, 0, 0)),
                pl.BlockSpec((rows, width), whole2),
                pl.BlockSpec((rows, width), whole2),
                pl.BlockSpec((chunks, rows, width), whole3),
                pl.BlockSpec((chunks, width, rows), whole3),
                pl.BlockSpec((chunks, rows, width), whole3),
            ],
            out_specs=[
                pl.BlockSpec((rows, span), by_head),
                pl.BlockSpec((chunks, rows, width), whole3),
                pl.BlockSpec((chunks, rows, width), whole3),
            ],
        ),
        out_shape=[
            jax.ShapeDtypeStruct((rows, columns), BF),
            jax.ShapeDtypeStruct((chunks, rows, width), F32),
            jax.ShapeDtypeStruct((chunks, rows, width), F32),
        ],
        name="attend_back",
    )(meta, rot, grad, att, lse, cosine, sine, keys, keys_t, values)


def per_device(
    rows_n,
    tokens,
    seq_ids,
    block_ids,
    positions,
    norm1_gain,
    norm2_gain,
    w_query,
    w_kv,
    w_out,
    w_gate,
    w_up,
    w_down,
    grad_output,
):
    R = rows_n
    bits = []
    while (1 << len(bits)) < R:
        bits.append(1 << len(bits))
    nbits = len(bits)

    def reverse(v):
        out = 0
        for b in range(nbits):
            out = out | (((v >> b) & 1) << (nbits - 1 - b))
        return out

    order = [reverse(v) for v in range(R)]
    row = lax.axis_index("row")
    col = lax.axis_index("col")
    half_rows, dslice = tokens.shape
    B = half_rows // R
    full_rows = 2 * half_rows
    width = w_kv.shape[1] // 2
    dp_n = lax.axis_size("dp")

    def swap_row(a, bit):
        return lax.ppermute(a, "row", [(i, i ^ bit) for i in range(R)])

    def swap_col(a):
        return lax.ppermute(a, "col", [(0, 1), (1, 0)])

    def psum_row(a):
        for bit in bits:
            a = a + swap_row(a, bit)
        return a

    def pick(a, index, size):
        return lax.dynamic_slice_in_dim(a, index * size, size, 0)

    def to_order(a):
        return jnp.concatenate([pick(a, row ^ order[p], B) for p in range(R)], axis=0)

    def from_order(a):
        return jnp.concatenate([pick(a, reverse(row ^ b), B) for b in range(R)], axis=0)

    def reduce_row(a):
        a = a.astype(BF)
        for bit in bits:
            half = a.shape[0] // 2
            total = a[:half].astype(F32) + swap_row(a[half:], bit).astype(F32)
            a = total.astype(BF)
        return total

    def gather_row(a):
        for bit in reversed(bits):
            a = jnp.concatenate([a, swap_row(a, bit)], axis=0)
        return a

    def spread(pieces, bit):
        out = dict(pieces)
        for (a, k), value in pieces.items():
            out[(a, k ^ bit)] = swap_row(value, bit)
        return out

    def spread_col(pieces):
        out = dict(pieces)
        for (a, k), value in pieces.items():
            out[(1 - a, k)] = swap_col(value)
        return out

    def gather_plane(mine):
        half = half_rows // 2
        first = spread_col({(0, 0): mine[:half]})
        for bit in reversed(bits[1:]):
            first = spread(first, bit)
        second = {(0, 0): mine[half:]}
        for bit in reversed(bits[1:]):
            second = spread(second, bit)
        second = spread_col(second)
        first = spread(first, 1)
        second = spread(second, 1)
        rows_out = []
        for a in range(2):
            for part in (first, second):
                rows_out.append(jnp.concatenate([part[(a, k)] for k in range(R)], axis=1))
        return jnp.concatenate(rows_out, axis=0)

    def add(a, b):
        return (a.astype(F32) + b.astype(F32)).astype(BF)

    def reduce_plane(blocks):
        keep = {k: add(blocks[k], swap_row(blocks[k ^ 1], 1)) for k in range(0, R, 2)}
        half = half_rows // 2
        outs = []
        for part in range(2):
            cur = {
                (a, k): v[a * half_rows + part * half : a * half_rows + (part + 1) * half]
                for k, v in keep.items()
                for a in range(2)
            }

            def by_col(cur):
                return {
                    (0, k): add(cur[(0, k)], swap_col(cur[(1, k)])) for (a, k) in cur if a == 0
                }

            def by_rows(cur):
                for bit in bits[1:]:
                    cur = {
                        (a, k): add(v, swap_row(cur[(a, k ^ bit)], bit))
                        for (a, k), v in cur.items()
                        if not k & bit
                    }
                return cur

            cur = by_rows(by_col(cur)) if part == 0 else by_col(by_rows(cur))
            outs.append(cur[(0, 0)])
        return jnp.concatenate(outs, axis=0).astype(F32)

    def split_ff(w, axis):
        size = w.shape[axis] // R
        return [
            lax.dynamic_slice_in_dim(w, (row ^ k) * size, size, axis) for k in range(R)
        ]

    def exchange(parts):
        return [parts[0]] + [swap_row(parts[k], k) for k in range(1, R)]

    residual = tokens.astype(F32)
    scale_one = lax.rsqrt(psum_row(jnp.sum(residual * residual, axis=1)) / D + EPS)
    weighted_in = (residual * norm1_gain[None, :]).astype(BF)
    ordered_in = to_order(weighted_in)
    w_query_far = swap_col(w_query)
    own = col * R + row
    own_scale = lax.dynamic_slice_in_dim(scale_one, row * B, B)[:, None]

    kv_pre = reduce_row(dot_nn(ordered_in, w_kv)) * own_scale
    query_near = reduce_row(dot_nn(ordered_in, w_query))
    query_far = reduce_row(dot_nn(ordered_in, w_query_far))
    query_pre = jnp.concatenate([query_near, query_far], axis=1) * own_scale

    half_width = width // 2
    frequency = ROPE_BASE ** (-2.0 * jnp.arange(half_width, dtype=F32) / width)
    own_positions = lax.dynamic_slice_in_dim(positions, own * B, B)
    angles = own_positions.astype(F32)[:, None] * frequency[None, :]
    cosine = jnp.concatenate([jnp.cos(angles)] * 2, axis=1)
    sine_half = jnp.sin(angles)
    sine = jnp.concatenate([-sine_half, sine_half], axis=1)

    key_pre = kv_pre[:, :width]
    key_turned = jnp.concatenate([key_pre[:, half_width:], key_pre[:, :half_width]], axis=1)
    key_own = key_pre * cosine + key_turned * sine
    kv_own = jnp.concatenate([key_own, kv_pre[:, width:]], axis=1).astype(BF)
    kv_pieces = spread_col({(0, 0): kv_own})
    for bit in reversed(bits):
        kv_pieces = spread(kv_pieces, bit)
    kv_all = jnp.stack([kv_pieces[(a, k)] for a in range(2) for k in range(R)])
    keys = kv_all[:, :, :width]
    values = kv_all[:, :, width:]
    keys_t = keys.transpose(0, 2, 1)
    values_t = values.transpose(0, 2, 1)

    chunks = 2 * R
    chunk_seq = seq_ids[::B]
    chunk_block = block_ids[::B]
    numbers = jnp.arange(chunks, dtype=jnp.int32)
    my_seq = lax.dynamic_slice_in_dim(chunk_seq, own, 1)
    my_block = lax.dynamic_slice_in_dim(chunk_block, own, 1)
    visible = (chunk_seq == my_seq) & (chunk_block <= my_block)
    first_chunk = jnp.min(jnp.where(visible, numbers, chunks))
    count = jnp.sum(visible.astype(jnp.int32))
    place = ((numbers // R) ^ col) * R + ((numbers % R) ^ row)
    meta = jnp.concatenate([first_chunk[None], count[None], place]).astype(jnp.int32)

    att_own, rot_own, lse = attend(meta, query_pre, cosine, sine, keys, values_t, width)

    w_out_far = swap_col(w_out)
    w_out_all = jnp.concatenate([w_out, w_out_far], axis=0)
    w_query_all = jnp.concatenate([w_query, w_query_far], axis=1)
    att_all = gather_row(att_own)
    hidden = residual + from_order(dot_nn(att_all, w_out_all))

    down_grad = grad_output.astype(BF)
    grad_full = gather_plane(down_grad)
    gate_parts = exchange(split_ff(w_gate, 1))
    up_parts = exchange(split_ff(w_up, 1))
    down_parts = exchange(split_ff(w_down, 0))
    gate_full = jnp.concatenate(gate_parts, axis=0)
    up_full = jnp.concatenate(up_parts, axis=0)
    down_full = jnp.concatenate(down_parts, axis=1)

    scale_two = lax.rsqrt(psum_row(jnp.sum(hidden * hidden, axis=1)) / D + EPS)[:, None]
    normed_two = (hidden * scale_two * norm2_gain[None, :]).astype(BF)
    normed_full = gather_plane(normed_two)

    mixed_grad = dot_nt(grad_full, down_full)
    gate_proj = dot_nn(normed_full, gate_full)
    up_proj = dot_nn(normed_full, up_full)
    sigmoid_gate = jax.nn.sigmoid(gate_proj)
    silu_gate = gate_proj * sigmoid_gate
    mixed_act = (silu_gate * up_proj).astype(BF)
    gate_grad = (
        mixed_grad * up_proj * sigmoid_gate * (1.0 + gate_proj * (1.0 - sigmoid_gate))
    ).astype(BF)
    up_grad = (mixed_grad * silu_gate).astype(BF)

    normed2_grad = reduce_plane(
        [
            (dot_nt(gate_grad, gate_parts[k]) + dot_nt(up_grad, up_parts[k])).astype(BF)
            for k in range(R)
        ]
    )

    def ff_input_grad(grad):
        local = dot_tn(normed_full, grad).astype(BF)
        quarter = dslice // dp_n
        local = local.reshape(R, dp_n, quarter, grad.shape[1]).transpose(1, 0, 2, 3)
        return lax.psum_scatter(local, "dp", scatter_dimension=0, tiled=True)[0]

    def ff_input_place(piece):
        moved = jnp.stack(exchange([piece[k] for k in range(R)]))
        ordered = jnp.concatenate(
            [lax.dynamic_index_in_dim(moved, row ^ s, 0, keepdims=False) for s in range(R)], axis=1
        )
        return ordered.astype(F32)[None]

    gate_piece = ff_input_grad(gate_grad)
    up_piece = ff_input_grad(up_grad)
    down_local = [
        dot_tn(mixed_act, grad_full[:, k * dslice : (k + 1) * dslice]).astype(BF) for k in range(R)
    ]
    down_moved = jnp.stack(exchange(down_local))
    down_ordered = jnp.concatenate(
        [lax.dynamic_index_in_dim(down_moved, row ^ s, 0, keepdims=False) for s in range(R)], axis=0
    )
    grad_down = lax.psum_scatter(down_ordered, "dp", scatter_dimension=0, tiled=True)

    output = hidden + reduce_plane([dot_nn(mixed_act, down_parts[k]).astype(BF) for k in range(R)])

    weighted = normed2_grad * norm2_gain[None, :]
    inner_two = psum_row(jnp.sum(weighted * hidden, axis=1))[:, None]
    hidden_grad = grad_output + (
        scale_two * weighted - hidden * (scale_two * scale_two * scale_two) * inner_two / D
    )
    gain_two = jnp.sum(normed2_grad * hidden * scale_two, axis=0)
    branch_ordered = to_order(hidden_grad.astype(BF))
    att_grad = jnp.concatenate(
        [
            reduce_row(dot_nt(branch_ordered, w_out)),
            reduce_row(dot_nt(branch_ordered, w_out_far)),
        ],
        axis=1,
    ).astype(BF)
    columns = w_query.shape[1]

    def over_col(far, near):
        return add(near, swap_col(far.astype(BF)))

    grad_out_local = over_col(
        dot_tn(att_all[:, columns:], branch_ordered), dot_tn(att_all[:, :columns], branch_ordered)
    )
    grad_out = lax.psum_scatter(grad_out_local, "dp", scatter_dimension=0, tiled=True)

    qpg_own, dk, dv = attend_back(
        meta, rot_own, att_grad, att_own, lse, cosine, sine, keys, keys_t, values, width
    )
    dkv = jnp.concatenate([dk * width**-0.5, dv], axis=2).astype(BF)
    cur = {(a, k): dkv[a * R + k] for a in range(2) for k in range(R)}
    for bit in bits:
        cur = {
            (a, k): add(v, swap_row(cur[(a, k ^ bit)], bit))
            for (a, k), v in cur.items()
            if not k & bit
        }
    dkv_own = cur[(0, 0)].astype(F32) + swap_col(cur[(1, 0)]).astype(F32)
    dk_own = dkv_own[:, :width]
    dk_turned = jnp.concatenate([dk_own[:, half_width:], dk_own[:, :half_width]], axis=1)
    kvg_own = jnp.concatenate(
        [dk_own * cosine - dk_turned * sine, dkv_own[:, width:]], axis=1
    ).astype(BF)

    qpg_all = gather_row(qpg_own)
    kvg_all = gather_row(kvg_own)
    normed1_grad = from_order(dot_nt(qpg_all, w_query_all) + dot_nt(kvg_all, w_kv))
    weighted_one = normed1_grad * norm1_gain[None, :]
    inner_one = psum_row(jnp.sum(weighted_one * residual, axis=1))[:, None]
    scale_col = scale_one[:, None]
    input_grad = hidden_grad + (
        scale_col * weighted_one - residual * (scale_col * scale_col * scale_col) * inner_one / D
    )
    gain_one = jnp.sum(normed1_grad * residual * scale_col, axis=0)

    normed_ordered = to_order((residual * scale_col * norm1_gain[None, :]).astype(BF))
    grad_query_local = over_col(
        dot_tn(normed_ordered, qpg_all[:, columns:]), dot_tn(normed_ordered, qpg_all[:, :columns])
    )
    grad_query = lax.psum_scatter(grad_query_local, "dp", scatter_dimension=0, tiled=True)
    grad_kv = lax.psum_scatter(
        dot_tn(normed_ordered, kvg_all).astype(BF),
        ("dp", "col"),
        scatter_dimension=0,
        tiled=True,
    )
    gains = lax.psum_scatter(
        jnp.stack([gain_one, gain_two], axis=1).astype(BF),
        ("dp", "col"),
        scatter_dimension=0,
        tiled=True,
    ).astype(F32)
    return (
        output,
        input_grad,
        grad_query.astype(F32)[None],
        grad_kv.astype(F32)[None],
        grad_out.astype(F32)[None],
        ff_input_place(gate_piece),
        ff_input_place(up_piece),
        grad_down.astype(F32)[None],
        gains[:, 0][None, :],
        gains[:, 1][None, :],
    )


def solution(mesh):
    placed = (
        P(("dp", "col"), "row"),
        P("dp"),
        P("dp"),
        P("dp"),
        P("row"),
        P("row"),
        P("row", "col"),
        P("row", None),
        P("col", "row"),
        P("row", "col"),
        P("row", "col"),
        P("col", "row"),
        P(("dp", "col"), "row"),
    )
    return jax.shard_map(
        functools.partial(per_device, mesh.shape["row"]),
        mesh=mesh,
        in_specs=placed,
        out_specs=(
            P(("dp", "col"), "row"),
            P(("dp", "col"), "row"),
            P("row", "dp", "col"),
            P("row", ("dp", "col"), None),
            P("col", "dp", "row"),
            P("row", "dp", "col"),
            P("row", "dp", "col"),
            P("col", "dp", "row"),
            P("row", ("dp", "col")),
            P("row", ("dp", "col")),
        ),
        check_vma=False,
    )
```

time: 1900 us -> 969 us (0.51)
  waiting for transfers between devices: 1390 us -> 422 us
  matrix products: 303 us -> 139 us
  starting transfers between devices: 2.14 us -> 131 us
  other arithmetic: 86.5 us -> 144 us
  blocking collectives: 28.9 us -> 0 us
  Pallas kernels: 0 us -> 28.4 us
    reduce_scatter x14 -> x6, waiting for transfers between devices: 966 us -> 90.3 us  [the longest x1 63 us: per_device(): lax.psum_scatter(dot_tn(normed_ordered, kvg_all).astype(BF), ('dp', 'col'...]
    ppermute x0 -> x104, waiting for transfers between devices: none -> 318 us  [the longest x86 227 us: swap_row(): return lax.ppermute(a, 'row', [(i, i ^ bit) for i in range(R)])]
    all_gather x8 -> x0, waiting for transfers between devices: 311 us -> none  [the longest x4 206 us: fold_rows(): shard_rows = lax.all_gather(operand, 'row', axis=0, tiled=True)]
    dot_general x71 -> x34, matrix products: 303 us -> 139 us  [the longest x13 50.4 us: dot_nt(): lax.dot_general(a, b, (((1,), (1,)), ((), ())), preferred_element_type=F32)]
    ppermute x0 -> x104, starting transfers between devices: none -> 131 us  [the longest x18 71.6 us: swap_col(): return lax.ppermute(a, 'col', [(0, 1), (1, 0)])]
    concatenate x4 -> x10, other arithmetic: 6.78 us -> 91 us  [the longest x2 81.1 us: gather_plane(): return jnp.concatenate(rows_out, axis=0)]
    psum x2 -> x0, waiting for transfers between devices: 54.3 us -> none  [the longest x1 39.6 us: per_device(): lax.psum(jnp.dot(gathered_in, w_kv, preferred_element_type=jnp.float32),...]
    unnamed x26 -> x8, waiting for transfers between devices: 60.6 us -> 13.6 us
  transfers between devices with their start and end apart: 25 -> 111, of which waited for: 24 -> 39; matrix products, arithmetic and copies ran while one was open for 15% -> 34% of each run, Pallas kernels for 0% -> 2%
where the time goes in v1:
time: 969 us; the launch traced here: 961 us
  waiting for transfers between devices  422 us (44%)
  other arithmetic  144 us (15%)
  matrix products  139 us (14%)
  starting transfers between devices  131 us (14%)
  local copies, waits for them, and re-layouts  80.5 us (8%)
  Pallas kernels  28.4 us (3%)
  between operations  16.2 us (2%)
    ppermute x86, waiting for transfers between devices, swap_row(): return lax.ppermute(a, 'row', [(i, i ^ bit) for i in range(R)])  227 us
    ppermute x18, waiting for transfers between devices, swap_col(): return lax.ppermute(a, 'col', [(0, 1), (1, 0)])  90.4 us
    concatenate x2, other arithmetic, gather_plane(): return jnp.concatenate(rows_out, axis=0)  81.1 us
    ppermute x18, starting transfers between devices, swap_col(): return lax.ppermute(a, 'col', [(0, 1), (1, 0)])  71.6 us
    reduce_scatter x1, waiting for transfers between devices, per_device(): lax.psum_scatter(dot_tn(normed_ordered, kvg_all).astype(BF), ('dp', 'col'...  63 us
    ppermute x86, starting transfers between devices, swap_row(): return lax.ppermute(a, 'row', [(i, i ^ bit) for i in range(R)])  59.3 us
    dot_general x13, matrix products, dot_nt(): lax.dot_general(a, b, (((1,), (1,)), ((), ())), preferred_element_type=F32)  50.4 us
    dot_general x10, matrix products, dot_nn(): lax.dot_general(a, b, (((1,), (0,)), ((), ())), preferred_element_type=F32)  46.2 us
  transfers between devices with their start and end apart: 111, of which 39 were waited for; matrix products, arithmetic and copies ran while one was open for 34% of the time, Pallas kernels for 2%

profile of v1, /device:TPU:0, one launch (start us, length us, event | category | flops | bytes accessed | tf_op | source)
XLA Modules:
  0.0 961.4 jit_solution(12550040656514703732)
XLA Ops:
  56.6 9.2 collective-permute-done.1
  67.0 9.1 collective-permute-done.4
  78.8 13.3 %attend.1 = (bf16[256,2048]{1,0:T(8,128)(2,1)}, bf16[256,2048]{1,0:T(8,128)(2,1)}, f32[16,1,256]{2,1,0:T(1,128)}) custom-call(s32[10]{0:T(128)} %pad_add_fusion.meta, f32[256,2048]{1,0:T(8,128)} %maximum_multiply_fusion.q_ref, f32[256,128]{1,0:T(8,128)} %get-tuple-element.126.cos_ref, f32[256,128]{1,0:T(8,128)} %get-tuple-element.37.sin_ref, ...), custom_call_target="tpu_custom_call" | custom-call | tf_op jit(solution)/shard_map/attend/pallas_call | solution.py:74
  92.7 20.4 %collective-permute-done.16 = bf16[256,2048]{1,0:T(8,128)(2,1)S(1)} collective-permute-done((bf16[256,2048]{1,0:T(8,128)(2,1)}, bf16[256,2048]{1,0:T(8,128)(2,1)S(1)}, u32[]{:S(2)}, u32[]{:S(2)}) %collective-permute-start.16) | collective-permute-done | bytes 1048608 | tf_op jit(solution)/shard_map/ppermute | solution.py:213
  115.9 5.1 collective-permute-start.17
  121.0 28.0 %collective-permute-start.18 = (bf16[1024,512]{1,0:T(8,128)(2,1)}, bf16[1024,512]{1,0:T(8,128)(2,1)}, u32[]{:S(2)}, u32[]{:S(2)}) collective-permute-start(bf16[1024,512]{1,0:T(8,128)(2,1)} %param.21), channel_id=1, source_target_pairs={{0,1},{1,0},{2,3},{3,2},{4,5},{5,4},{6,7},{7,6},{8,9},{9,8},{10,11... | collective-permute-start | bytes 3145736 | tf_op jit(solution)/shard_map/ppermute | solution.py:216
  156.2 17.1 %collective-permute-done.18 = bf16[1024,512]{1,0:T(8,128)(2,1)} collective-permute-done((bf16[1024,512]{1,0:T(8,128)(2,1)}, bf16[1024,512]{1,0:T(8,128)(2,1)}, u32[]{:S(2)}, u32[]{:S(2)}) %collective-permute-start.18) | collective-permute-done | bytes 1048608 | tf_op jit(solution)/shard_map/ppermute | solution.py:216
  179.4 5.0 collective-permute-done.58
  187.2 7.8 collective-permute-done.62
  199.2 30.3 %collective-permute-done.20 = f32[1024]{0:T(1024)S(1)} collective-permute-done((f32[1024]{0:T(1024)S(1)}, f32[1024]{0:T(1024)S(1)}, u32[]{:S(2)}, u32[]{:S(2)}) %collective-permute-start.20) | collective-permute-done | bytes 4128 | tf_op jit(solution)/shard_map/ppermute | solution.py:213
  232.4 7.8 collective-permute-done.60
  275.7 30.2 %maximum_maximum_fusion.1 = bf16[2048,2048]{1,0:T(8,128)(2,1)S(1)} fusion(bf16[512,512]{1,0:T(8,128)(2,1)} %collective-permute-done.65, bf16[512,512]{1,0:T(8,128)(2,1)} %collective-permute-done.64, bf16[512,512]{1,0:T(8,128)(2,1)} %copy-done.40, bf16[512,512]{1,0:T(8,128)(2,1)} %copy-done.33, bf16[512,512]{1,0:T(8,128)(2,1)} %copy-done.41, ...), kind=kLoop, calls=%fused_computation.1 | loop fusion | flops 134217728 | bytes 16777216 | tf_op jit(solution)/shard_map/concatenate | solution.py:272
  307.1 10.1 %fusion.17 = f32[2048,704]{0,1:T(8,128)} fusion(bf16[2048,2048]{1,0:T(8,128)(2,1)S(1)} %maximum_maximum_fusion.1, bf16[704,512]{1,0:T(8,128)(2,1)} %copy-done.79, bf16[704,512]{1,0:T(8,128)(2,1)} %copy-done.77, bf16[704,512]{1,0:T(8,128)(2,1)} %copy-done.75, bf16[704,512]{1,0:T(8,128)(2,1)S(1)} %copy-done.28), kind=kOutput, calls=%fused_computation.44 | convolution fusion | flops 5917114368 | bytes 17039360 | tf_op jit(solution)/shard_map/dot_general | solution.py:25
  321.4 50.9 %maximum_maximum_fusion = bf16[2048,2048]{1,0:T(8,128)(2,1)} fusion(bf16[512,512]{1,0:T(8,128)(2,1)} %collective-permute-done.34, bf16[512,512]{1,0:T(8,128)(2,1)} %collective-permute-done.33, bf16[512,512]{1,0:T(8,128)(2,1)} %copy-done.43, bf16[512,512]{1,0:T(8,128)(2,1)} %collective-permute-done.31, bf16[512,512]{1,0:T(8,128)(2,1)} %copy-done.44, ...), kind=kLoop, calls=%fused_computation | loop fusion | flops 134217728 | bytes 16777216 | tf_op jit(solution)/shard_map/concatenate | solution.py:272
  373.4 11.8 %fusion.9 = f32[2048,704]{0,1:T(8,128)} fusion(bf16[2048,2048]{1,0:T(8,128)(2,1)} %maximum_maximum_fusion, bf16[512,704]{0,1:T(8,128)(2,1)} %collective-permute-done.40, bf16[512,704]{0,1:T(8,128)(2,1)} %collective-permute-done.39, bf16[512,704]{0,1:T(8,128)(2,1)} %collective-permute-done.38, bf16[512,704]{0,1:T(8,128)(2,1)} %copy.60), kind=kOutput, calls=%fused_computation.36 | convolution fusion | flops 5917114368 | bytes 17039360 | tf_op jit(solution)/shard_map/dot_general | solution.py:21
  385.3 5.3 collective-permute-done.36
  390.6 16.3 %multiply_convert_fusion.1 = (bf16[2048,704]{0,1:T(8,128)(2,1)}, bf16[2048,704]{0,1:T(8,128)(2,1)}, bf16[2048,704]{0,1:T(8,128)(2,1)}) fusion(f32[2048,704]{0,1:T(8,128)} %fusion.17, f32[2048,704]{0,1:T(8,128)} %fusion.9, bf16[2048,2048]{1,0:T(8,128)(2,1)} %maximum_maximum_fusion, bf16[512,704]{0,1:T(8,128)(2,1)} %collective-permute-done.37, ...), kind=kOutput, calls=%fused_computation.3 | convolution fusion | flops 5938741248 | bytes 31457280 | tf_op jit(solution)/shard_map/dot_general | solution.py:21
  406.9 4.5 fusion.86
  418.5 7.7 convolution_convert_fusion.1
  426.2 6.0 reshape.192
  432.2 4.6 copy.47
  438.7 10.9 %convolution_convert_fusion = bf16[2048,704]{0,1:T(8,128)(2,1)} fusion(bf16[2048,704]{0,1:T(8,128)(2,1)S(1)} %copy-done.88, bf16[2048,2048]{1,0:T(8,128)(2,1)} %maximum_maximum_fusion), kind=kOutput, calls=%fused_computation.22 | convolution fusion | flops 5907021824 | bytes 14155776 | tf_op jit(solution)/shard_map/dot_general | solution.py:29
  449.5 6.0 reshape.193
  455.6 4.8 copy.48
  464.4 4.6 add_convert_fusion.1
  472.3 4.6 add_convert_fusion.4
  510.7 18.3 %collective-permute-done.69 = bf16[512,512]{1,0:T(8,128)(2,1)S(1)} collective-permute-done((bf16[512,512]{1,0:T(8,128)(2,1)S(1)}, bf16[512,512]{1,0:T(8,128)(2,1)S(1)}, u32[]{:S(2)}, u32[]{:S(2)}) %collective-permute-start.69) | collective-permute-done | bytes 524320 | tf_op jit(solution)/shard_map/ppermute | solution.py:216
  532.7 25.4 %collective-permute-done.72 = bf16[512,512]{1,0:T(8,128)(2,1)S(1)} collective-permute-done((bf16[512,512]{1,0:T(8,128)(2,1)S(1)}, bf16[512,512]{1,0:T(8,128)(2,1)S(1)}, u32[]{:S(2)}, u32[]{:S(2)}) %collective-permute-start.72) | collective-permute-done | bytes 524320 | tf_op jit(solution)/shard_map/ppermute | solution.py:213
  559.6 9.8 %collective-permute-done.70 = bf16[512,512]{1,0:T(8,128)(2,1)S(1)} collective-permute-done((bf16[512,512]{1,0:T(8,128)(2,1)S(1)}, bf16[512,512]{1,0:T(8,128)(2,1)S(1)}, u32[]{:S(2)}, u32[]{:S(2)}) %collective-permute-start.70) | collective-permute-done | bytes 524320 | tf_op jit(solution)/shard_map/ppermute | solution.py:213
  574.9 5.7 collective-permute-done.50
  580.6 11.2 %collective-permute-done.48 = bf16[512,512]{1,0:T(8,128)(2,1)S(1)} collective-permute-done((bf16[512,512]{1,0:T(8,128)(2,1)S(1)}, bf16[512,512]{1,0:T(8,128)(2,1)S(1)}, u32[]{:S(2)}, u32[]{:S(2)}) %collective-permute-start.48) | collective-permute-done | bytes 524320 | tf_op jit(solution)/shard_map/ppermute | solution.py:213
  592.5 10.6 %collective-permute-done.71 = bf16[512,512]{1,0:T(8,128)(2,1)S(1)} collective-permute-done((bf16[512,512]{1,0:T(8,128)(2,1)S(1)}, bf16[512,512]{1,0:T(8,128)(2,1)S(1)}, u32[]{:S(2)}, u32[]{:S(2)}) %collective-permute-start.71) | collective-permute-done | bytes 524320 | tf_op jit(solution)/shard_map/ppermute | solution.py:213
  606.8 7.5 collective-permute-done.49
  638.9 7.6 collective-permute-done.77
  647.7 9.3 collective-permute-done.79
  659.4 15.1 %attend_back.1 = (bf16[256,2048]{1,0:T(8,128)(2,1)}, f32[8,256,128]{2,1,0:T(8,128)}, f32[8,256,128]{2,1,0:T(8,128)}) custom-call(s32[10]{0:T(128)} %pad_add_fusion.meta, bf16[256,2048]{1,0:T(8,128)(2,1)} %get-tuple-element.17.rot_ref, bf16[256,2048]{1,0:T(8,128)(2,1)} %pad_maximum_fusion.8.grad_ref, bf16[256,2048]{1,0:T(8,128)(2,1)} %get-tuple-element.16.att_ref, ...), custom_call_target="tpu_custom_call" | custom-call | tf_op jit(solution)/shard_map/attend_back/pallas_call | solution.py:142
  677.5 6.3 collective-permute-start.86
  686.5 25.8 %collective-permute-done.87 = bf16[256,256]{1,0:T(8,128)(2,1)S(1)} collective-permute-done((bf16[256,256]{1,0:T(8,128)(2,1)S(1)}, bf16[256,256]{1,0:T(8,128)(2,1)S(1)}, u32[]{:S(2)}, u32[]{:S(2)}) %collective-permute-start.87) | collective-permute-done | bytes 131104 | tf_op jit(solution)/shard_map/ppermute | solution.py:213
  713.4 28.0 %collective-permute-start.88 = (bf16[256,256]{1,0:T(8,128)(2,1)S(1)}, bf16[256,256]{1,0:T(8,128)(2,1)S(1)}, u32[]{:S(2)}, u32[]{:S(2)}) collective-permute-start(bf16[256,256]{1,0:T(8,128)(2,1)S(1)} %get-tuple-element.87), channel_id=1, source_target_pairs={{0,1},{1,0},{2,3},{3,2},{4,5},{5,4},{6,7},{7,6},{8,9},{9,8},{10,11... | collective-permute-start | bytes 393224 | tf_op jit(solution)/shard_map/ppermute | solution.py:216
  747.6 5.6 collective-permute-done.89
  754.0 12.8 %collective-permute-done.94 = bf16[1024,512]{1,0:T(8,128)(2,1)S(1)} collective-permute-done((bf16[1024,512]{1,0:T(8,128)(2,1)S(1)}, bf16[1024,512]{1,0:T(8,128)(2,1)S(1)}, u32[]{:S(2)}, u32[]{:S(2)}) %collective-permute-start.94) | collective-permute-done | bytes 1048608 | tf_op jit(solution)/shard_map/ppermute | solution.py:216
  772.8 5.4 fusion.67
  794.6 20.4 %collective-permute-done.93 = bf16[512,1024]{1,0:T(8,128)(2,1)} collective-permute-done((bf16[512,1024]{1,0:T(8,128)(2,1)}, bf16[512,1024]{1,0:T(8,128)(2,1)}, u32[]{:S(2)}, u32[]{:S(2)}) %collective-permute-start.93) | collective-permute-done | bytes 1048608 | tf_op jit(solution)/shard_map/ppermute | solution.py:216
  815.1 4.1 add_convert_fusion.9
  830.2 6.0 collective-permute-done.100
  846.1 13.5 %reduce-scatter.22.cloned.1.call-done = bf16[64,2]{1,0:T(8,128)(2,1)} async-done(((bf16[512,2]{1,0:T(8,128)(2,1)}), bf16[64,2]{1,0:T(8,128)(2,1)}) %reduce-scatter.22.cloned.1.call-update) | async-done | bytes 272
  860.9 63.0 %reduce-scatter.12.cloned.1.call-done = bf16[64,256]{1,0:T(8,128)(2,1)} async-done(((bf16[512,256]{1,0:T(8,128)(2,1)}), bf16[64,256]{1,0:T(8,128)(2,1)}) %reduce-scatter.12.cloned.1.call-update) | async-done | bytes 32784 | tf_op jit(solution)/shard_map/reduce_scatter | solution.py:484
  925.3 27.2 %reduce-scatter.10.cloned.1.call-done = bf16[128,1024]{1,0:T(8,128)(2,1)} async-done(((bf16[512,1024]{1,0:T(8,128)(2,1)}), bf16[128,1024]{1,0:T(8,128)(2,1)}) %reduce-scatter.10.cloned.1.call-update) | async-done | bytes 262160 | tf_op jit(solution)/shard_map/reduce_scatter | solution.py:483
  (560 shorter events, 274.9 us)
Async XLA Ops:
  7.2 812.0 %reduce-scatter.16.cloned.1.call-start = ((), (), s32[]{:S(2)}) async-start(), calls=%async_computation.10 | async-start | bytes 3932160 | tf_op jit(solution)/shard_map/reduce_scatter | solution.py:404
  10.1 35.7 %collective-permute-start.2 = (bf16[512,1024]{1,0:T(8,128)(2,1)}, bf16[512,1024]{1,0:T(8,128)(2,1)}, u32[]{:S(2)}, u32[]{:S(2)}) collective-permute-start(bf16[512,1024]{1,0:T(8,128)(2,1)} %param.19), channel_id=1, source_target_pairs={{0,1},{1,0},{2,3},{3,2},{4,5},{5,4},{6,7},{7,6},{8,9},{9,8},{10,11... | collective-permute-start | bytes 3145736 | tf_op jit(solution)/shard_map/ppermute | solution.py:216
  16.7 32.5 %collective-permute-start = (bf16[512,1024]{1,0:T(8,128)(2,1)}, bf16[512,1024]{1,0:T(8,128)(2,1)}, u32[]{:S(2)}, u32[]{:S(2)}) collective-permute-start(bf16[512,1024]{1,0:T(8,128)(2,1)} %slice.332), channel_id=1, source_target_pairs={{0,2},{2,0},{4,6},{6,4},{1,3},{3,1},{5,7},{7,5},{8,10},{10,8},{12,... | collective-permute-start | bytes 3145736 | tf_op jit(solution)/shard_map/ppermute | solution.py:213
  115.9 36.5 %collective-permute-start.17 = (bf16[512,2048]{1,0:T(8,128)(2,1)}, bf16[512,2048]{1,0:T(8,128)(2,1)}, u32[]{:S(2)}, u32[]{:S(2)}) collective-permute-start(bf16[512,2048]{1,0:T(8,128)(2,1)} %pad_maximum_fusion.2), channel_id=1, source_target_pairs={{0,2},{2,0},{4,6},{6,4},{1,3},{3,1},{5,7},{7,5},{8,10},{10,8},{12,... | collective-permute-start | bytes 6291464 | tf_op jit(solution)/shard_map/ppermute | solution.py:213
  121.0 52.2 %collective-permute-start.18 = (bf16[1024,512]{1,0:T(8,128)(2,1)}, bf16[1024,512]{1,0:T(8,128)(2,1)}, u32[]{:S(2)}, u32[]{:S(2)}) collective-permute-start(bf16[1024,512]{1,0:T(8,128)(2,1)} %param.21), channel_id=1, source_target_pairs={{0,1},{1,0},{2,3},{3,2},{4,5},{5,4},{6,7},{7,6},{8,9},{9,8},{10,11... | collective-permute-start | bytes 3145736 | tf_op jit(solution)/shard_map/ppermute | solution.py:216
  150.2 34.2 %collective-permute-start.58 = (bf16[512,512]{1,0:T(8,128)(2,1)}, bf16[512,512]{1,0:T(8,128)(2,1)S(1)}, u32[]{:S(2)}, u32[]{:S(2)}) collective-permute-start(bf16[512,512]{1,0:T(8,128)(2,1)} %get-tuple-element.96), channel_id=1, source_target_pairs={{0,1},{1,0},{2,3},{3,2},{4,5},{5,4},{6,7},{7,6},{8,9},{9,8},{10,11... | collective-permute-start | bytes 1572872 | tf_op jit(solution)/shard_map/ppermute | solution.py:216
  150.2 34.6 %collective-permute-start.53 = (bf16[512,512]{1,0:T(8,128)(2,1)}, bf16[512,512]{1,0:T(8,128)(2,1)S(1)}, u32[]{:S(2)}, u32[]{:S(2)}) collective-permute-start(bf16[512,512]{1,0:T(8,128)(2,1)} %get-tuple-element.96), channel_id=1, source_target_pairs={{0,4},{2,6},{4,0},{6,2},{1,5},{3,7},{5,1},{7,3},{8,12},{10,14},{12... | collective-permute-start | bytes 1572872 | tf_op jit(solution)/shard_map/ppermute | solution.py:213
  152.2 34.5 %collective-permute-start.52 = (bf16[512,512]{1,0:T(8,128)(2,1)}, bf16[512,512]{1,0:T(8,128)(2,1)}, u32[]{:S(2)}, u32[]{:S(2)}) collective-permute-start(bf16[512,512]{1,0:T(8,128)(2,1)} %get-tuple-element.96), channel_id=1, source_target_pairs={{0,2},{2,0},{4,6},{6,4},{1,3},{3,1},{5,7},{7,5},{8,10},{10,8},{12,... | collective-permute-start | bytes 1572872 | tf_op jit(solution)/shard_map/ppermute | solution.py:213
  152.4 42.6 %collective-permute-start.62 = (bf16[512,512]{1,0:T(8,128)(2,1)}, bf16[512,512]{1,0:T(8,128)(2,1)S(1)}, u32[]{:S(2)}, u32[]{:S(2)}) collective-permute-start(bf16[512,512]{1,0:T(8,128)(2,1)} %get-tuple-element.97), channel_id=1, source_target_pairs={{0,1},{1,0},{2,3},{3,2},{4,5},{5,4},{6,7},{7,6},{8,9},{9,8},{10,11... | collective-permute-start | bytes 1572872 | tf_op jit(solution)/shard_map/ppermute | solution.py:216
  186.7 43.4 %collective-permute-start.41 = (bf16[704,512]{1,0:T(8,128)(2,1)S(1)}, bf16[704,512]{1,0:T(8,128)(2,1)S(1)}, u32[]{:S(2)}, u32[]{:S(2)}) collective-permute-start(bf16[704,512]{1,0:T(8,128)(2,1)S(1)} %get-tuple-element.46), channel_id=1, source_target_pairs={{0,2},{2,0},{4,6},{6,4},{1,3},{3,1},{5,7},{7,5},{8,10},{10,8},{12,... | collective-permute-start | bytes 2162696 | tf_op jit(solution)/shard_map/ppermute | solution.py:213
  195.0 36.8 %collective-permute-start.45 = (bf16[704,512]{1,0:T(8,128)(2,1)S(1)}, bf16[704,512]{1,0:T(8,128)(2,1)S(1)}, u32[]{:S(2)}, u32[]{:S(2)}) collective-permute-start(bf16[704,512]{1,0:T(8,128)(2,1)S(1)} %get-tuple-element.47), channel_id=1, source_target_pairs={{0,6},{2,4},{4,2},{6,0},{1,7},{3,5},{5,3},{7,1},{8,14},{10,12},{12... | collective-permute-start | bytes 2162696 | tf_op jit(solution)/shard_map/ppermute | solution.py:213
  196.1 36.0 %collective-permute-start.44 = (bf16[704,512]{1,0:T(8,128)(2,1)S(1)}, bf16[704,512]{1,0:T(8,128)(2,1)S(1)}, u32[]{:S(2)}, u32[]{:S(2)}) collective-permute-start(bf16[704,512]{1,0:T(8,128)(2,1)S(1)} %get-tuple-element.48), channel_id=1, source_target_pairs={{0,4},{2,6},{4,0},{6,2},{1,5},{3,7},{5,1},{7,3},{8,12},{10,14},{12... | collective-permute-start | bytes 2162696 | tf_op jit(solution)/shard_map/ppermute | solution.py:213
  197.1 32.4 %collective-permute-start.20 = (f32[1024]{0:T(1024)S(1)}, f32[1024]{0:T(1024)S(1)}, u32[]{:S(2)}, u32[]{:S(2)}) collective-permute-start(f32[1024]{0:T(1024)S(1)} %add.308), channel_id=1, source_target_pairs={{0,4},{2,6},{4,0},{6,2},{1,5},{3,7},{5,1},{7,3},{8,12},{10,14},{12... | collective-permute-start | bytes 12296 | tf_op jit(solution)/shard_map/ppermute | solution.py:213
  198.2 42.0 %collective-permute-start.60 = (bf16[512,512]{1,0:T(8,128)(2,1)}, bf16[512,512]{1,0:T(8,128)(2,1)S(1)}, u32[]{:S(2)}, u32[]{:S(2)}) collective-permute-start(bf16[512,512]{1,0:T(8,128)(2,1)} %copy-done.30), channel_id=1, source_target_pairs={{0,4},{2,6},{4,0},{6,2},{1,5},{3,7},{5,1},{7,3},{8,12},{10,14},{12... | collective-permute-start | bytes 1572872 | tf_op jit(solution)/shard_map/ppermute | solution.py:213
  244.5 28.1 %collective-permute-start.27 = (bf16[512,512]{1,0:T(8,128)(2,1)}, bf16[512,512]{1,0:T(8,128)(2,1)}, u32[]{:S(2)}, u32[]{:S(2)}) collective-permute-start(bf16[512,512]{1,0:T(8,128)(2,1)} %get-tuple-element.98), channel_id=1, source_target_pairs={{0,1},{1,0},{2,3},{3,2},{4,5},{5,4},{6,7},{7,6},{8,9},{9,8},{10,11... | collective-permute-start | bytes 1572872 | tf_op jit(solution)/shard_map/ppermute | solution.py:216
  272.4 33.6 %collective-permute-start.31 = (bf16[512,512]{1,0:T(8,128)(2,1)}, bf16[512,512]{1,0:T(8,128)(2,1)}, u32[]{:S(2)}, u32[]{:S(2)}) collective-permute-start(bf16[512,512]{1,0:T(8,128)(2,1)} %get-tuple-element.99), channel_id=1, source_target_pairs={{0,1},{1,0},{2,3},{3,2},{4,5},{5,4},{6,7},{7,6},{8,9},{9,8},{10,11... | collective-permute-start | bytes 1572872 | tf_op jit(solution)/shard_map/ppermute | solution.py:216
  272.7 33.4 %collective-permute-start.24 = (bf16[512,512]{1,0:T(8,128)(2,1)}, bf16[512,512]{1,0:T(8,128)(2,1)}, u32[]{:S(2)}, u32[]{:S(2)}) collective-permute-start(bf16[512,512]{1,0:T(8,128)(2,1)} %get-tuple-element.99), channel_id=1, source_target_pairs={{0,2},{2,0},{4,6},{6,4},{1,3},{3,1},{5,7},{7,5},{8,10},{10,8},{12,... | collective-permute-start | bytes 1572872 | tf_op jit(solution)/shard_map/ppermute | solution.py:213
  272.7 33.9 %collective-permute-start.29 = (bf16[512,512]{1,0:T(8,128)(2,1)}, bf16[512,512]{1,0:T(8,128)(2,1)}, u32[]{:S(2)}, u32[]{:S(2)}) collective-permute-start(bf16[512,512]{1,0:T(8,128)(2,1)} %collective-permute-done.27), channel_id=1, source_target_pairs={{0,4},{2,6},{4,0},{6,2},{1,5},{3,7},{5,1},{7,3},{8,12},{10,14},{12... | collective-permute-start | bytes 1572872 | tf_op jit(solution)/shard_map/ppermute | solution.py:213
  273.8 32.8 %collective-permute-start.28 = (bf16[512,512]{1,0:T(8,128)(2,1)}, bf16[512,512]{1,0:T(8,128)(2,1)}, u32[]{:S(2)}, u32[]{:S(2)}) collective-permute-start(bf16[512,512]{1,0:T(8,128)(2,1)} %collective-permute-done.27), channel_id=1, source_target_pairs={{0,2},{2,0},{4,6},{6,4},{1,3},{3,1},{5,7},{7,5},{8,10},{10,8},{12,... | collective-permute-start | bytes 1572872 | tf_op jit(solution)/shard_map/ppermute | solution.py:213
  273.9 33.1 %collective-permute-start.33 = (bf16[512,512]{1,0:T(8,128)(2,1)}, bf16[512,512]{1,0:T(8,128)(2,1)}, u32[]{:S(2)}, u32[]{:S(2)}) collective-permute-start(bf16[512,512]{1,0:T(8,128)(2,1)} %collective-permute-done.25), channel_id=1, source_target_pairs={{0,1},{1,0},{2,3},{3,2},{4,5},{5,4},{6,7},{7,6},{8,9},{9,8},{10,11... | collective-permute-start | bytes 1572872 | tf_op jit(solution)/shard_map/ppermute | solution.py:216
  317.3 68.0 %collective-permute-start.37 = (bf16[512,704]{0,1:T(8,128)(2,1)}, bf16[512,704]{0,1:T(8,128)(2,1)}, u32[]{:S(2)}, u32[]{:S(2)}) collective-permute-start(bf16[512,704]{0,1:T(8,128)(2,1)} %copy.59), channel_id=1, source_target_pairs={{0,6},{2,4},{4,2},{6,0},{1,7},{3,5},{5,3},{7,1},{8,14},{10,12},{12... | collective-permute-start | bytes 2162696 | tf_op jit(solution)/shard_map/ppermute | solution.py:213
  318.3 66.9 %collective-permute-start.35 = (bf16[512,704]{0,1:T(8,128)(2,1)}, bf16[512,704]{0,1:T(8,128)(2,1)}, u32[]{:S(2)}, u32[]{:S(2)}) collective-permute-start(bf16[512,704]{0,1:T(8,128)(2,1)} %copy.57), channel_id=1, source_target_pairs={{0,2},{2,0},{4,6},{6,4},{1,3},{3,1},{5,7},{7,5},{8,10},{10,8},{12,... | collective-permute-start | bytes 2162696 | tf_op jit(solution)/shard_map/ppermute | solution.py:213
  318.4 53.9 %collective-permute-start.40 = (bf16[512,704]{0,1:T(8,128)(2,1)}, bf16[512,704]{0,1:T(8,128)(2,1)}, u32[]{:S(2)}, u32[]{:S(2)}) collective-permute-start(bf16[512,704]{0,1:T(8,128)(2,1)} %copy.63), channel_id=1, source_target_pairs={{0,6},{2,4},{4,2},{6,0},{1,7},{3,5},{5,3},{7,1},{8,14},{10,12},{12... | collective-permute-start | bytes 2162696 | tf_op jit(solution)/shard_map/ppermute | solution.py:213
  320.3 53.1 %collective-permute-start.38 = (bf16[512,704]{0,1:T(8,128)(2,1)}, bf16[512,704]{0,1:T(8,128)(2,1)}, u32[]{:S(2)}, u32[]{:S(2)}) collective-permute-start(bf16[512,704]{0,1:T(8,128)(2,1)} %copy.61), channel_id=1, source_target_pairs={{0,2},{2,0},{4,6},{6,4},{1,3},{3,1},{5,7},{7,5},{8,10},{10,8},{12,... | collective-permute-start | bytes 2162696 | tf_op jit(solution)/shard_map/ppermute | solution.py:213
  320.4 53.0 %collective-permute-start.39 = (bf16[512,704]{0,1:T(8,128)(2,1)}, bf16[512,704]{0,1:T(8,128)(2,1)}, u32[]{:S(2)}, u32[]{:S(2)}) collective-permute-start(bf16[512,704]{0,1:T(8,128)(2,1)} %copy.62), channel_id=1, source_target_pairs={{0,4},{2,6},{4,0},{6,2},{1,5},{3,7},{5,1},{7,3},{8,12},{10,14},{12... | collective-permute-start | bytes 2162696 | tf_op jit(solution)/shard_map/ppermute | solution.py:213
  414.0 115.3 %collective-permute-start.101 = (bf16[704,512]{1,0:T(8,128)(2,1)}, bf16[704,512]{1,0:T(8,128)(2,1)}, u32[]{:S(2)}, u32[]{:S(2)}) collective-permute-start(bf16[704,512]{1,0:T(8,128)(2,1)} %fusion.83), channel_id=1, source_target_pairs={{0,2},{2,0},{4,6},{6,4},{1,3},{3,1},{5,7},{7,5},{8,10},{10,8},{12,... | collective-permute-start | bytes 2162696 | tf_op jit(solution)/shard_map/ppermute | solution.py:213
  414.0 156.7 %collective-permute-start.102 = (bf16[704,512]{1,0:T(8,128)(2,1)}, bf16[704,512]{1,0:T(8,128)(2,1)}, u32[]{:S(2)}, u32[]{:S(2)}) collective-permute-start(bf16[704,512]{1,0:T(8,128)(2,1)} %fusion.86), channel_id=1, source_target_pairs={{0,4},{2,6},{4,0},{6,2},{1,5},{3,7},{5,1},{7,3},{8,12},{10,14},{12... | collective-permute-start | bytes 2162696 | tf_op jit(solution)/shard_map/ppermute | solution.py:213
  418.3 82.7 %collective-permute-start.46 = (bf16[2048,512]{1,0:T(8,128)(2,1)}, bf16[2048,512]{1,0:T(8,128)(2,1)}, u32[]{:S(2)}, u32[]{:S(2)}) collective-permute-start(bf16[2048,512]{1,0:T(8,128)(2,1)} %convolution_convert_fusion.2), channel_id=1, source_target_pairs={{0,2},{2,0},{4,6},{6,4},{1,3},{3,1},{5,7},{7,5},{8,10},{10,8},{12,... | collective-permute-start | bytes 6291464 | tf_op jit(solution)/shard_map/ppermute | solution.py:213
  436.9 385.6 %reduce-scatter.18.cloned.1.call-start = ((), (), s32[]{:S(2)}) async-start(), calls=%async_computation.11 | async-start | bytes 3932160 | tf_op jit(solution)/shard_map/reduce_scatter | solution.py:404
  469.0 34.6 %collective-permute-start.68 = (bf16[2048,512]{1,0:T(8,128)(2,1)}, bf16[2048,512]{1,0:T(8,128)(2,1)}, u32[]{:S(2)}, u32[]{:S(2)}) collective-permute-start(bf16[2048,512]{1,0:T(8,128)(2,1)} %add_convert_fusion.1), channel_id=1, source_target_pairs={{0,2},{2,0},{4,6},{6,4},{1,3},{3,1},{5,7},{7,5},{8,10},{10,8},{12,... | collective-permute-start | bytes 6291464 | tf_op jit(solution)/shard_map/ppermute | solution.py:213
  476.9 29.9 %collective-permute-start.66 = (bf16[2048,512]{1,0:T(8,128)(2,1)}, bf16[2048,512]{1,0:T(8,128)(2,1)}, u32[]{:S(2)}, u32[]{:S(2)}) collective-permute-start(bf16[2048,512]{1,0:T(8,128)(2,1)} %add_convert_fusion.4), channel_id=1, source_target_pairs={{0,2},{2,0},{4,6},{6,4},{1,3},{3,1},{5,7},{7,5},{8,10},{10,8},{12,... | collective-permute-start | bytes 6291464 | tf_op jit(solution)/shard_map/ppermute | solution.py:213
  487.7 354.2 %reduce-scatter.20.cloned.1.call-start = ((), (), s32[]{:S(2)}) async-start(), calls=%async_computation.12 | async-start | bytes 3604480 | tf_op jit(solution)/shard_map/reduce_scatter | solution.py:422
  501.0 29.4 %collective-permute-start.42 = (bf16[2048,512]{1,0:T(8,128)(2,1)S(1)}, bf16[2048,512]{1,0:T(8,128)(2,1)S(1)}, u32[]{:S(2)}, u32[]{:S(2)}) collective-permute-start(bf16[2048,512]{1,0:T(8,128)(2,1)S(1)} %convolution_convert_fusion.4), channel_id=1, source_target_pairs={{0,2},{2,0},{4,6},{6,4},{1,3},{3,1},{5,7},{7,5},{8,10},{10,8},{12,... | collective-permute-start | bytes 6291464 | tf_op jit(solution)/shard_map/ppermute | solution.py:213
  529.0 42.8 %collective-permute-start.103 = (bf16[704,512]{1,0:T(8,128)(2,1)S(1)}, bf16[704,512]{1,0:T(8,128)(2,1)S(1)}, u32[]{:S(2)}, u32[]{:S(2)}) collective-permute-start(bf16[704,512]{1,0:T(8,128)(2,1)S(1)} %copy-done.81), channel_id=1, source_target_pairs={{0,6},{2,4},{4,2},{6,0},{1,7},{3,5},{5,3},{7,1},{8,14},{10,12},{12... | collective-permute-start | bytes 2162696 | tf_op jit(solution)/shard_map/ppermute | solution.py:213
  529.3 28.8 %collective-permute-start.72 = (bf16[512,512]{1,0:T(8,128)(2,1)S(1)}, bf16[512,512]{1,0:T(8,128)(2,1)S(1)}, u32[]{:S(2)}, u32[]{:S(2)}) collective-permute-start(bf16[512,512]{1,0:T(8,128)(2,1)S(1)} %get-tuple-element.65), channel_id=1, source_target_pairs={{0,4},{2,6},{4,0},{6,2},{1,5},{3,7},{5,1},{7,3},{8,12},{10,14},{12... | collective-permute-start | bytes 1572872 | tf_op jit(solution)/shard_map/ppermute | solution.py:213
  530.4 28.0 %collective-permute-start.67 = (bf16[512,512]{1,0:T(8,128)(2,1)S(1)}, bf16[512,512]{1,0:T(8,128)(2,1)S(1)}, u32[]{:S(2)}, u32[]{:S(2)}) collective-permute-start(bf16[512,512]{1,0:T(8,128)(2,1)S(1)} %slice.362), channel_id=1, source_target_pairs={{0,1},{1,0},{2,3},{3,2},{4,5},{5,4},{6,7},{7,6},{8,9},{9,8},{10,11... | collective-permute-start | bytes 1572872 | tf_op jit(solution)/shard_map/ppermute | solution.py:216
  530.6 38.8 %collective-permute-start.70 = (bf16[512,512]{1,0:T(8,128)(2,1)S(1)}, bf16[512,512]{1,0:T(8,128)(2,1)S(1)}, u32[]{:S(2)}, u32[]{:S(2)}) collective-permute-start(bf16[512,512]{1,0:T(8,128)(2,1)S(1)} %add_convert_fusion.20), channel_id=1, source_target_pairs={{0,4},{2,6},{4,0},{6,2},{1,5},{3,7},{5,1},{7,3},{8,12},{10,14},{12... | collective-permute-start | bytes 1572872 | tf_op jit(solution)/shard_map/ppermute | solution.py:213
  570.7 32.4 %collective-permute-start.71 = (bf16[512,512]{1,0:T(8,128)(2,1)S(1)}, bf16[512,512]{1,0:T(8,128)(2,1)S(1)}, u32[]{:S(2)}, u32[]{:S(2)}) collective-permute-start(bf16[512,512]{1,0:T(8,128)(2,1)S(1)} %get-tuple-element.66), channel_id=1, source_target_pairs={{0,4},{2,6},{4,0},{6,2},{1,5},{3,7},{5,1},{7,3},{8,12},{10,14},{12... | collective-permute-start | bytes 1572872 | tf_op jit(solution)/shard_map/ppermute | solution.py:213
  571.9 31.2 %collective-permute-start.73 = (bf16[512,512]{1,0:T(8,128)(2,1)S(1)}, bf16[512,512]{1,0:T(8,128)(2,1)S(1)}, u32[]{:S(2)}, u32[]{:S(2)}) collective-permute-start(bf16[512,512]{1,0:T(8,128)(2,1)S(1)} %get-tuple-element.63), channel_id=1, source_target_pairs={{0,1},{1,0},{2,3},{3,2},{4,5},{5,4},{6,7},{7,6},{8,9},{9,8},{10,11... | collective-permute-start | bytes 1572872 | tf_op jit(solution)/shard_map/ppermute | solution.py:216
  573.6 40.7 %collective-permute-start.49 = (bf16[512,512]{1,0:T(8,128)(2,1)S(1)}, bf16[512,512]{1,0:T(8,128)(2,1)S(1)}, u32[]{:S(2)}, u32[]{:S(2)}) collective-permute-start(bf16[512,512]{1,0:T(8,128)(2,1)S(1)} %get-tuple-element.71), channel_id=1, source_target_pairs={{0,4},{2,6},{4,0},{6,2},{1,5},{3,7},{5,1},{7,3},{8,12},{10,14},{12... | collective-permute-start | bytes 1572872 | tf_op jit(solution)/shard_map/ppermute | solution.py:213
  627.9 216.4 %reduce-scatter.14.cloned.1.call-start = ((), (), s32[]{:S(2)}) async-start(), calls=%async_computation.9 | async-start | bytes 1310720 | tf_op jit(solution)/shard_map/reduce_scatter | solution.py:448
  684.3 61.0 %collective-permute-start.80 = (bf16[256,2048]{1,0:T(8,128)(2,1)S(1)}, bf16[256,2048]{1,0:T(8,128)(2,1)S(1)}, u32[]{:S(2)}, u32[]{:S(2)}) collective-permute-start(bf16[256,2048]{1,0:T(8,128)(2,1)S(1)} %copy-done.10), channel_id=1, source_target_pairs={{0,4},{2,6},{4,0},{6,2},{1,5},{3,7},{5,1},{7,3},{8,12},{10,14},{12... | collective-permute-start | bytes 3145736 | tf_op jit(solution)/shard_map/ppermute | solution.py:213
  686.4 56.3 %collective-permute-start.82 = (bf16[256,256]{1,0:T(8,128)(2,1)S(1)}, bf16[256,256]{1,0:T(8,128)(2,1)S(1)}, u32[]{:S(2)}, u32[]{:S(2)}) collective-permute-start(bf16[256,256]{1,0:T(8,128)(2,1)S(1)} %get-tuple-element.82), channel_id=1, source_target_pairs={{0,2},{2,0},{4,6},{6,4},{1,3},{3,1},{5,7},{7,5},{8,10},{10,8},{12,... | collective-permute-start | bytes 393224 | tf_op jit(solution)/shard_map/ppermute | solution.py:213
  712.3 30.4 %collective-permute-start.84 = (bf16[256,256]{1,0:T(8,128)(2,1)S(1)}, bf16[256,256]{1,0:T(8,128)(2,1)S(1)}, u32[]{:S(2)}, u32[]{:S(2)}) collective-permute-start(bf16[256,256]{1,0:T(8,128)(2,1)S(1)} %get-tuple-element.86), channel_id=1, source_target_pairs={{0,4},{2,6},{4,0},{6,2},{1,5},{3,7},{5,1},{7,3},{8,12},{10,14},{12... | collective-permute-start | bytes 393224 | tf_op jit(solution)/shard_map/ppermute | solution.py:213
  713.4 31.8 %collective-permute-start.88 = (bf16[256,256]{1,0:T(8,128)(2,1)S(1)}, bf16[256,256]{1,0:T(8,128)(2,1)S(1)}, u32[]{:S(2)}, u32[]{:S(2)}) collective-permute-start(bf16[256,256]{1,0:T(8,128)(2,1)S(1)} %get-tuple-element.87), channel_id=1, source_target_pairs={{0,1},{1,0},{2,3},{3,2},{4,5},{5,4},{6,7},{7,6},{8,9},{9,8},{10,11... | collective-permute-start | bytes 393224 | tf_op jit(solution)/shard_map/ppermute | solution.py:216
  769.0 90.5 %reduce-scatter.22.cloned.1.call-start = ((), (), s32[]{:S(2)}) async-start(), calls=%async_computation.13 | async-start | bytes 147456
  792.4 131.5 %reduce-scatter.12.cloned.1.call-start = ((), (), s32[]{:S(2)}) async-start(), calls=%async_computation.8 | async-start | bytes 294912 | tf_op jit(solution)/shard_map/reduce_scatter | solution.py:484
  794.6 157.9 %reduce-scatter.10.cloned.1.call-start = ((), (), s32[]{:S(2)}) async-start(), calls=%async_computation.7 | async-start | bytes 1310720 | tf_op jit(solution)/shard_map/reduce_scatter | solution.py:483
  (161 other events, 2429.6 us)
Sparse Core Ops, SparseCore 0:
  437.0 59.7 reduce-scatter.15
  499.1 60.2 reduce-scatter.17
  628.0 55.6 reduce-scatter.19
  769.2 27.2 reduce-scatter.13
  800.0 59.4 reduce-scatter.21
  863.7 60.1 reduce-scatter.11
  926.3 26.1 reduce-scatter.9

commit v2 on v1

v2 whole, which is shorter than its diff:
```python
import functools

import jax
import jax.numpy as jnp
from jax import lax
from jax.experimental import pallas as pl
from jax.experimental.pallas import tpu as pltpu
from jax.sharding import PartitionSpec as P

D = 2048
EPS = 1e-05
ROPE_BASE = 500000.0
BLOCK = 256
LOG2E = 1.4426950408889634
BF = jnp.bfloat16
F32 = jnp.float32
HEADS_PER_STEP = 4


def dot_nn(a, b):
    return lax.dot_general(a, b, (((1,), (0,)), ((), ())), preferred_element_type=F32)


def dot_nt(a, b):
    return lax.dot_general(a, b, (((1,), (1,)), ((), ())), preferred_element_type=F32)


def dot_tn(a, b):
    return lax.dot_general(a, b, (((0,), (0,)), ((), ())), preferred_element_type=F32)


def list_visible(where, seq_ref, block_ref, list_ref, *, rows_n, rows):
    row, col = where[0], where[1]
    chunks = 2 * rows_n
    own = (col * rows_n + row) * rows
    count = jnp.int32(0)
    for j in range(chunks):
        seen = (seq_ref[j * rows] == seq_ref[own]) & (block_ref[j * rows] <= block_ref[own])

        @pl.when(seen)
        def _(j=j, count=count):
            list_ref[count] = ((j // rows_n) ^ col) * rows_n + ((j % rows_n) ^ row)

        count = count + seen.astype(jnp.int32)
    list_ref[chunks] = count


def attend_body(
    where, seq_ref, block_ref, q_ref, cos_ref, sin_ref, k_ref, vt_ref,
    att_ref, rot_ref, lse_ref, list_ref, *, factor, width, rows_n,
):
    @pl.when(pl.program_id(0) == 0)
    def _():
        list_visible(where, seq_ref, block_ref, list_ref, rows_n=rows_n, rows=q_ref.shape[0])

    cosine = cos_ref[...]
    sine = sin_ref[...]
    rows = q_ref.shape[0]
    heads = [slice(h * width, (h + 1) * width) for h in range(HEADS_PER_STEP)]
    for cols in heads:
        pre = q_ref[:, cols]
        rot_ref[:, cols] = (pre * cosine + pltpu.roll(pre, width // 2, 1) * sine).astype(BF)

    def step(t, carry):
        chunk = list_ref[t]
        key = k_ref[chunk]
        value_t = vt_ref[chunk]
        all_scores = [dot_nt(key, rot_ref[:, cols]) * factor for cols in heads]
        out = []
        for (top, total, acc), scores in zip(carry, all_scores):
            new_top = jnp.maximum(top, jnp.max(scores, axis=0, keepdims=True))
            decay = jnp.exp2(top - new_top)
            weights = jnp.exp2(scores - new_top)
            total = total * decay + jnp.sum(weights, axis=0, keepdims=True)
            acc = acc * decay + dot_nn(value_t, weights.astype(BF))
            out.append((new_top, total, acc))
        return out

    start = (
        jnp.full((1, rows), -1e30, F32),
        jnp.zeros((1, rows), F32),
        jnp.zeros((width, rows), F32),
    )
    done = lax.fori_loop(0, list_ref[2 * rows_n], step, [start] * HEADS_PER_STEP)
    for head, (top, total, acc) in enumerate(done):
        att_ref[:, heads[head]] = (acc / total).T.astype(BF)
        lse_ref[head] = top + jnp.log2(total)


def attend(meta, q_pre, cosine, sine, keys, values_t, width, rows_n):
    where, seq_ids, block_ids = meta
    rows, columns = q_pre.shape
    heads = columns // width
    chunks = keys.shape[0]
    span = HEADS_PER_STEP * width
    whole2 = lambda i, m: (0, 0)
    whole3 = lambda i, m: (0, 0, 0)
    return pl.pallas_call(
        functools.partial(attend_body, factor=width**-0.5 * LOG2E, width=width, rows_n=rows_n),
        grid_spec=pltpu.PrefetchScalarGridSpec(
            num_scalar_prefetch=1,
            grid=(heads // HEADS_PER_STEP,),
            in_specs=[
                pl.BlockSpec(memory_space=pltpu.SMEM),
                pl.BlockSpec(memory_space=pltpu.SMEM),
                pl.BlockSpec((rows, span), lambda i, m: (0, i)),
                pl.BlockSpec((rows, width), whole2),
                pl.BlockSpec((rows, width), whole2),
                pl.BlockSpec((chunks, rows, width), whole3),
                pl.BlockSpec((chunks, width, rows), whole3),
            ],
            out_specs=[
                pl.BlockSpec((rows, span), lambda i, m: (0, i)),
                pl.BlockSpec((rows, span), lambda i, m: (0, i)),
                pl.BlockSpec((HEADS_PER_STEP, 1, rows), lambda i, m: (i, 0, 0)),
            ],
            scratch_shapes=[pltpu.SMEM((chunks + 1,), jnp.int32)],
        ),
        out_shape=[
            jax.ShapeDtypeStruct((rows, columns), BF),
            jax.ShapeDtypeStruct((rows, columns), BF),
            jax.ShapeDtypeStruct((heads, 1, rows), F32),
        ],
        cost_estimate=pl.CostEstimate(
            flops=4 * rows * columns * chunks * rows // 2,
            transcendentals=heads * rows * chunks * rows // 2,
            bytes_accessed=8 * rows * columns + 4 * chunks * rows * width,
        ),
        name="attend",
    )(where, seq_ids, block_ids, q_pre, cosine, sine, keys, values_t)


def attend_back_body(
    where, seq_ref, block_ref, rot_ref, grad_ref, att_ref, lse_ref, cos_ref, sin_ref, k_ref, kt_ref, v_ref,
    *outs, factor, scale, width, rows_n,
):
    qpg_ref, dk_ref, dv_ref, list_ref = outs[-4:]

    @pl.when(pl.program_id(0) == 0)
    def _():
        list_visible(where, seq_ref, block_ref, list_ref, rows_n=rows_n, rows=rot_ref.shape[0])
        dk_ref[...] = jnp.zeros_like(dk_ref) if len(outs) == 4 else outs[0][...]
        dv_ref[...] = jnp.zeros_like(dv_ref) if len(outs) == 4 else outs[1][...]

    cosine = cos_ref[...]
    sine = sin_ref[...]
    rows = rot_ref.shape[0]
    heads = [slice(h * width, (h + 1) * width) for h in range(HEADS_PER_STEP)]
    inners = []
    for cols in heads:
        inner = (grad_ref[:, cols].astype(F32) * att_ref[:, cols].astype(F32)).T
        inners.append(jnp.sum(inner, axis=0, keepdims=True))

    def step(t, dqs):
        chunk = list_ref[t]
        key = k_ref[chunk]
        key_t = kt_ref[chunk]
        value = v_ref[chunk]
        all_scores = [dot_nt(key, rot_ref[:, cols]) for cols in heads]
        backs = [dot_nt(value, grad_ref[:, cols]) for cols in heads]
        dv = dv_ref[chunk]
        dk = dk_ref[chunk]
        out = []
        for h, cols in enumerate(heads):
            probs = jnp.exp2(all_scores[h] * factor - lse_ref[h])
            score_grad = (probs * (backs[h] - inners[h])).astype(BF)
            dv = dv + dot_nn(probs.astype(BF), grad_ref[:, cols])
            dk = dk + dot_nn(score_grad, rot_ref[:, cols])
            out.append(dqs[h] + dot_nn(key_t, score_grad))
        dv_ref[chunk] = dv
        dk_ref[chunk] = dk
        return out

    dqs = lax.fori_loop(0, list_ref[2 * rows_n], step, [jnp.zeros((width, rows), F32)] * HEADS_PER_STEP)
    for h, cols in enumerate(heads):
        dq = dqs[h].T * scale
        qpg_ref[:, cols] = (dq * cosine - pltpu.roll(dq, width // 2, 1) * sine).astype(BF)


def attend_back(meta, rot, grad, att, lse, cosine, sine, keys, keys_t, values, width, rows_n, running=()):
    where, seq_ids, block_ids = meta
    rows, columns = rot.shape
    heads = columns // width
    chunks = keys.shape[0]
    span = HEADS_PER_STEP * width
    whole2 = lambda i, m: (0, 0)
    whole3 = lambda i, m: (0, 0, 0)
    by_head = lambda i, m: (0, i)
    return pl.pallas_call(
        functools.partial(
            attend_back_body,
            factor=width**-0.5 * LOG2E,
            scale=width**-0.5,
            width=width,
            rows_n=rows_n,
        ),
        grid_spec=pltpu.PrefetchScalarGridSpec(
            num_scalar_prefetch=1,
            grid=(heads // HEADS_PER_STEP,),
            in_specs=[
                pl.BlockSpec(memory_space=pltpu.SMEM),
                pl.BlockSpec(memory_space=pltpu.SMEM),
                pl.BlockSpec((rows, span), by_head),
                pl.BlockSpec((rows, span), by_head),
                pl.BlockSpec((rows, span), by_head),
                pl.BlockSpec((HEADS_PER_STEP, 1, rows), lambda i, m: (i, 0, 0)),
                pl.BlockSpec((rows, width), whole2),
                pl.BlockSpec((rows, width), whole2),
                pl.BlockSpec((chunks, rows, width), whole3),
                pl.BlockSpec((chunks, width, rows), whole3),
                pl.BlockSpec((chunks, rows, width), whole3),
            ]
            + [pl.BlockSpec((chunks, rows, width), whole3)] * len(running),
            out_specs=[
                pl.BlockSpec((rows, span), by_head),
                pl.BlockSpec((chunks, rows, width), whole3),
                pl.BlockSpec((chunks, rows, width), whole3),
            ],
            scratch_shapes=[pltpu.SMEM((chunks + 1,), jnp.int32)],
        ),
        out_shape=[
            jax.ShapeDtypeStruct((rows, columns), BF),
            jax.ShapeDtypeStruct((chunks, rows, width), F32),
            jax.ShapeDtypeStruct((chunks, rows, width), F32),
        ],
        cost_estimate=pl.CostEstimate(
            flops=10 * rows * columns * chunks * rows // 2,
            transcendentals=heads * rows * chunks * rows // 2,
            bytes_accessed=8 * rows * columns + 12 * chunks * rows * width,
        ),
        name="attend_back",
    )(where, seq_ids, block_ids, rot, grad, att, lse, cosine, sine, keys, keys_t, values, *running)


def feed_body(*refs, rows_n, parts, near, shared):
    R = rows_n
    refs = list(refs)
    take = lambda n: [refs.pop(0) for _ in range(n)]
    normed = take(parts * R)
    grads = take(R)
    close_in, close_down = take(near), take(near)
    far_in = take(1 if shared[0] else R - near)
    far_down = take(1 if shared[1] else R - near)
    act_ref, gate_grad_ref, up_grad_ref = take(3)
    back_refs = take(R)
    normed_out, grads_out = take(2)
    x_ref, g_ref, wg_ref, wu_ref, wd_ref, x_sem, g_sem, w_sem, o_sem = refs
    step = pl.program_id(0)
    tile, span = normed[0].shape

    def x_copy(p, k):
        return pltpu.make_async_copy(
            normed[p * R + k], x_ref.at[p, :, pl.ds(k * span, span)], x_sem.at[p, k]
        )

    def g_copy(p, k):
        return pltpu.make_async_copy(
            grads[k].at[pl.ds(p * tile, tile)], g_ref.at[p, :, pl.ds(k * span, span)], g_sem.at[p, k]
        )

    def w_copies(j, k):
        target = (wg_ref, wu_ref, wd_ref)[j].at[k]
        if k < near or not shared[j // 2]:
            whole = (close_in + far_in, close_down + far_down)[j // 2][k]
            whole = whole if j == 2 else whole.at[j]
            return [pltpu.make_async_copy(whole, target, w_sem.at[j, k, 0])]
        source = far_down[0] if j == 2 else far_in[0]
        copies = []
        for z in range(source.shape[0]):
            if j == 2:
                size = source.shape[-2]
                share, place = source.at[z, k - near], target.at[pl.ds(z * size, size)]
            else:
                size = source.shape[-1]
                share, place = source.at[z, k - near, j], target.at[:, pl.ds(z * size, size)]
            copies.append(pltpu.make_async_copy(share, place, w_sem.at[j, k, z]))
        return copies

    def x_out(p):
        return pltpu.make_async_copy(
            x_ref.at[p], normed_out.at[pl.ds(p * tile, tile)], o_sem.at[0, p]
        )

    def g_out(p):
        return pltpu.make_async_copy(
            g_ref.at[p], grads_out.at[pl.ds(p * tile, tile)], o_sem.at[1, p]
        )

    @pl.when(step == 0)
    def _():
        weights = [w_copies(j, k) for j in range(3) for k in range(R)]
        for k in range(R):
            x_copy(0, k).start()
            g_copy(0, k).start()
        for group in weights:
            for copy in group:
                copy.start()
        for p in range(1, parts):
            for k in range(R):
                x_copy(p, k).start()
                g_copy(p, k).start()
        for k in range(R):
            x_copy(0, k).wait()
            g_copy(0, k).wait()
        for group in weights:
            for copy in group:
                copy.wait()
        x_out(0).start()
        g_out(0).start()

    for p in range(1, parts):

        @pl.when(step == p)
        def _(p=p):
            for k in range(R):
                x_copy(p, k).wait()
                g_copy(p, k).wait()
            x_out(p).start()
            g_out(p).start()

    def over_parts(left, right, dot):
        total = None
        for k in range(R):
            value = dot(left[step, :, pl.ds(k * span, span)], right[k])
            total = value if total is None else total + value
        return total

    gate = over_parts(x_ref, wg_ref, dot_nt)
    up = over_parts(x_ref, wu_ref, dot_nt)
    mixed_grad = over_parts(g_ref, wd_ref, dot_nt)
    sig = 1.0 / (1.0 + jnp.exp(-gate))
    silu = gate * sig
    act_ref[...] = (silu * up).astype(BF)
    gate_grad = (mixed_grad * up * sig * (1.0 + gate * (1.0 - sig))).astype(BF)
    up_grad = (mixed_grad * silu).astype(BF)
    gate_grad_ref[...] = gate_grad
    up_grad_ref[...] = up_grad
    for k in range(R):
        back_refs[k][...] = (dot_nn(gate_grad, wg_ref[k]) + dot_nn(up_grad, wu_ref[k])).astype(BF)

    @pl.when(step == parts - 1)
    def _():
        for p in range(parts):
            x_out(p).wait()
            g_out(p).wait()


def feed(normed, grads, close_in, close_down, far_in, far_down, shared, slots):
    parts = len(normed)
    R = len(grads)
    near = len(close_in)
    tile, span = normed[0][0].shape
    hidden_n = close_in[0].shape[1]
    total = parts * tile
    operands = [a for p in normed for a in p] + list(grads)
    operands += [*close_in, *close_down, *far_in, *far_down]
    by_tile = pl.BlockSpec((tile, hidden_n), lambda i: (i, 0))
    anywhere = pl.BlockSpec(memory_space=pl.ANY)
    return pl.pallas_call(
        functools.partial(feed_body, rows_n=R, parts=parts, near=near, shared=shared),
        grid=(parts,),
        in_specs=[anywhere] * len(operands),
        out_specs=[by_tile] * 3
        + [pl.BlockSpec((tile, span), lambda i: (i, 0))] * R
        + [anywhere] * 2,
        out_shape=[jax.ShapeDtypeStruct((total, hidden_n), BF)] * 3
        + [jax.ShapeDtypeStruct((total, span), BF)] * R
        + [jax.ShapeDtypeStruct((total, R * span), BF)] * 2,
        scratch_shapes=[
            pltpu.VMEM((parts, tile, R * span), BF),
            pltpu.VMEM((parts, tile, R * span), BF),
            pltpu.VMEM((R, hidden_n, span), BF),
            pltpu.VMEM((R, hidden_n, span), BF),
            pltpu.VMEM((R, hidden_n, span), BF),
            pltpu.SemaphoreType.DMA((parts, R)),
            pltpu.SemaphoreType.DMA((parts, R)),
            pltpu.SemaphoreType.DMA((3, R, slots)),
            pltpu.SemaphoreType.DMA((2, parts)),
        ],
        compiler_params=pltpu.CompilerParams(vmem_limit_bytes=56 << 20),
        cost_estimate=pl.CostEstimate(
            flops=10 * total * R * span * hidden_n,
            transcendentals=total * hidden_n,
            bytes_accessed=10 * total * R * span + 6 * R * span * hidden_n,
        ),
        name="feed",
    )(*operands)


def feed_weight_body(x0, x1, g0, g1, out_ref):
    total = (dot_tn(g0[...], x0[...]) + dot_tn(g1[...], x1[...])).astype(BF)
    share = out_ref.shape[3]
    for q in range(out_ref.shape[0]):
        out_ref[q, 0] = total[:, q * share : (q + 1) * share]


def feed_weight_grad(x, grads, rows_n, dp_n):
    tokens, features = x[0].shape
    span = features // rows_n
    hidden_n = grads[0].shape[1]
    return pl.pallas_call(
        feed_weight_body,
        grid=(rows_n,),
        in_specs=[pl.BlockSpec((tokens, span), lambda k: (0, k))] * 2
        + [pl.BlockSpec((tokens, hidden_n), lambda k: (0, 0))] * 2,
        out_specs=pl.BlockSpec((dp_n, 1, hidden_n, span // dp_n), lambda k: (0, k, 0, 0)),
        out_shape=jax.ShapeDtypeStruct((dp_n, rows_n, hidden_n, span // dp_n), BF),
        compiler_params=pltpu.CompilerParams(vmem_limit_bytes=48 << 20),
        cost_estimate=pl.CostEstimate(
            flops=4 * tokens * features * hidden_n,
            transcendentals=0,
            bytes_accessed=4 * tokens * (features + hidden_n) + 2 * features * hidden_n,
        ),
        name="feed_weights",
    )(*x, *grads)


def down_weight_body(a0, a1, g0, g1, *outs):
    total = (dot_tn(a0[...], g0[...]) + dot_tn(a1[...], g1[...])).astype(BF)
    for k, out in enumerate(outs):

        @pl.when(pl.program_id(0) == k)
        def _(out=out):
            out[...] = total


def down_weight_grad(acts, grads, rows_n):
    tokens, features = grads[0].shape
    span = features // rows_n
    hidden_n = acts[0].shape[1]
    return pl.pallas_call(
        down_weight_body,
        grid=(rows_n,),
        in_specs=[pl.BlockSpec((tokens, hidden_n), lambda k: (0, 0))] * 2
        + [pl.BlockSpec((tokens, span), lambda k: (0, k))] * 2,
        out_specs=[pl.BlockSpec((hidden_n, span), lambda k: (0, 0))] * rows_n,
        out_shape=[jax.ShapeDtypeStruct((hidden_n, span), BF)] * rows_n,
        compiler_params=pltpu.CompilerParams(vmem_limit_bytes=48 << 20),
        cost_estimate=pl.CostEstimate(
            flops=4 * tokens * features * hidden_n,
            transcendentals=0,
            bytes_accessed=4 * tokens * (features + hidden_n) + 2 * features * hidden_n,
        ),
        name="down_weights",
    )(*acts, *grads)


def cut_body(where, *refs, ks, rows_n):
    gate, up = refs[:2]
    down_in = refs[2 : 2 + len(ks)]
    outs = refs[2 + len(ks) :]
    hidden_n = gate.shape[1] // rows_n
    for n, k in enumerate(ks):
        slot = where[0] ^ k
        for i in range(rows_n):

            @pl.when(slot == i)
            def _(n=n, i=i):
                here = slice(i * hidden_n, (i + 1) * hidden_n)
                outs[2 * n][0] = gate[:, here].T
                outs[2 * n][1] = up[:, here].T

        outs[2 * n + 1][...] = down_in[n][...]


def cut_weights(where, w_gate, w_up, w_down, ks, rows_n, rows_in, rows_down):
    hidden_n = w_gate.shape[1] // rows_n
    span = w_down.shape[1]
    per = hidden_n // rows_down
    ins = [pl.BlockSpec((rows_in, w_gate.shape[1]), lambda i, w: (w[1], 0))] * 2
    for k in ks:
        ins.append(pl.BlockSpec((rows_down, span), lambda i, w, k=k: ((w[0] ^ k) * per + w[2], 0)))
    out_specs, out_shape = [], []
    for _ in ks:
        out_specs += [
            pl.BlockSpec((2, hidden_n, rows_in), lambda i, w: (0, 0, 0)),
            pl.BlockSpec((rows_down, span), lambda i, w: (0, 0)),
        ]
        out_shape += [
            jax.ShapeDtypeStruct((2, hidden_n, rows_in), BF),
            jax.ShapeDtypeStruct((rows_down, span), BF),
        ]
    out = pl.pallas_call(
        functools.partial(cut_body, ks=ks, rows_n=rows_n),
        grid_spec=pltpu.PrefetchScalarGridSpec(
            num_scalar_prefetch=1, grid=(1,), in_specs=ins, out_specs=out_specs
        ),
        out_shape=out_shape,
        compiler_params=pltpu.CompilerParams(vmem_limit_bytes=40 << 20),
        name="cut_weights",
    )(where, w_gate, w_up, *([w_down] * len(ks)))
    return out[0::2], out[1::2]


def tie(value, *others):
    return lax.optimization_barrier((value, others))[0]


def per_device(
    rows_n,
    tokens,
    seq_ids,
    block_ids,
    positions,
    norm1_gain,
    norm2_gain,
    w_query,
    w_kv,
    w_out,
    w_gate,
    w_up,
    w_down,
    grad_output,
):
    R = rows_n
    bits = []
    while (1 << len(bits)) < R:
        bits.append(1 << len(bits))
    nbits = len(bits)

    def reverse(v):
        out = 0
        for b in range(nbits):
            out = out | (((v >> b) & 1) << (nbits - 1 - b))
        return out

    order = [reverse(v) for v in range(R)]
    row = lax.axis_index("row")
    col = lax.axis_index("col")
    half_rows, dslice = tokens.shape
    B = half_rows // R
    full_rows = 2 * half_rows
    width = w_kv.shape[1] // 2
    dp_n = lax.axis_size("dp")

    def swap_row(a, bit):
        return lax.ppermute(a, "row", [(i, i ^ bit) for i in range(R)])

    def swap_col(a):
        return lax.ppermute(a, "col", [(0, 1), (1, 0)])

    def psum_row(a):
        for bit in bits:
            a = a + swap_row(a, bit)
        return a

    def pick(a, index, size):
        return lax.dynamic_slice_in_dim(a, index * size, size, 0)

    def to_order(a):
        return jnp.concatenate([pick(a, row ^ order[p], B) for p in range(R)], axis=0)

    def from_order(a):
        return jnp.concatenate([pick(a, reverse(row ^ b), B) for b in range(R)], axis=0)

    def reduce_row(a, send_after=(), use_after=()):
        a = a.astype(BF)
        for bit in bits:
            half = a.shape[0] // 2
            keep, send = a[:half], a[half:]
            if bit == bits[-1]:
                send = tie(send, send_after)
            came = swap_row(send, bit)
            if bit == bits[-1]:
                came = tie(came, use_after)
            total = keep.astype(F32) + came.astype(F32)
            a = total.astype(BF)
        return total

    def gather_row(a):
        for bit in reversed(bits):
            a = jnp.concatenate([a, swap_row(a, bit)], axis=0)
        return a

    def spread(pieces, bit):
        out = dict(pieces)
        for (a, k), value in pieces.items():
            out[(a, k ^ bit)] = swap_row(value, bit)
        return out

    def spread_col(pieces):
        out = dict(pieces)
        for (a, k), value in pieces.items():
            out[(1 - a, k)] = swap_col(value)
        return out

    half = half_rows // 2

    def gather_plane(mine):
        first = came = spread_col({(0, 0): mine[:half]})
        for bit in reversed(bits[1:]):
            first = spread(first, bit)
        second = {(0, 0): mine[half:]}
        for bit in reversed(bits[1:]):
            second = spread(second, bit)
        second = spread_col(second)
        return (spread(first, 1), spread(second, 1)), came

    def add(a, b, wide=False):
        total = a.astype(F32) + b.astype(F32)
        return total if wide else total.astype(BF)

    def reduce_plane(blocks, after=()):
        moved = {(a, k): swap_row(blocks[(a, k ^ 1)], 1) for a in (1, 0) for k in range(0, R, 2)}
        outs = []
        for part in range(2):
            here = slice(part * half, (part + 1) * half)
            cur = {key: add(blocks[key][here], value[here]) for key, value in moved.items()}
            cur = tie(cur, after)

            def by_col(cur, last):
                return {
                    (0, k): add(cur[(0, k)], swap_col(cur[(1, k)]), last)
                    for (a, k) in cur
                    if a == 0
                }

            def by_rows(cur, last):
                for bit in bits[1:]:
                    cur = {
                        (a, k): add(v, swap_row(cur[(a, k ^ bit)], bit), last and bit == bits[-1])
                        for (a, k), v in cur.items()
                        if not k & bit
                    }
                return cur

            if part == 0:
                cur = by_rows(by_col(cur, False), True)
            else:
                cur = by_col(by_rows(cur, False), True)
            outs.append(cur[(0, 0)])
        return jnp.concatenate(outs, axis=0)

    residual = tokens.astype(F32)
    scale_one = lax.rsqrt(psum_row(jnp.sum(residual * residual, axis=1)) / D + EPS)
    weighted_in = (residual * norm1_gain[None, :]).astype(BF)
    ordered_in = to_order(weighted_in)
    w_query_far = swap_col(w_query)
    own = col * R + row
    own_scale = lax.dynamic_slice_in_dim(scale_one, row * B, B)[:, None]

    kv_pre = reduce_row(dot_nn(ordered_in, w_kv)) * own_scale
    query_near = reduce_row(dot_nn(ordered_in, w_query)) * own_scale

    z = lax.axis_index("dp")
    near = min(2, R)
    hidden_n = w_gate.shape[1] // R
    shared = (dslice % (128 * dp_n) == 0, hidden_n % (16 * dp_n) == 0)
    rows_in = dslice // dp_n if shared[0] else dslice
    rows_down = hidden_n // dp_n if shared[1] else hidden_n

    shares = jnp.stack([row, z if shared[0] else 0 * z, z if shared[1] else 0 * z])
    shares = tie(shares, kv_pre)
    far_ks = tuple(range(near, R))
    cut_in, cut_down = cut_weights(shares, w_gate, w_up, w_down, far_ks, R, rows_in, rows_down)
    far_in = [swap_row(a, k) for a, k in zip(cut_in, far_ks)]
    cut_down = tie(cut_down, query_near)
    far_down = [swap_row(a, k) for a, k in zip(cut_down, far_ks)]
    if shared[0]:
        far_in = [jnp.stack(far_in)]
    w_out_far = swap_col(tie(w_out, w_query_far))
    query_near = tie(query_near, far_in, w_out_far)
    if shared[0]:
        far_in = [lax.all_gather(far_in[0], "dp", axis=0)]

    half_width = width // 2
    frequency = ROPE_BASE ** (-2.0 * jnp.arange(half_width, dtype=F32) / width)
    own_positions = lax.dynamic_slice_in_dim(positions, own * B, B)
    angles = own_positions.astype(F32)[:, None] * frequency[None, :]
    cosine = jnp.concatenate([jnp.cos(angles)] * 2, axis=1)
    sine_half = jnp.sin(angles)
    sine = jnp.concatenate([-sine_half, sine_half], axis=1)

    key_pre = kv_pre[:, :width]
    key_turned = jnp.concatenate([key_pre[:, half_width:], key_pre[:, :half_width]], axis=1)
    key_own = key_pre * cosine + key_turned * sine
    kv_own = jnp.concatenate([key_own, kv_pre[:, width:]], axis=1).astype(BF)
    kv_pieces = spread_col({(0, 0): kv_own})
    for bit in reversed(bits):
        kv_pieces = spread(kv_pieces, bit)
    kv_all = jnp.stack([kv_pieces[(a, k)] for a in range(2) for k in range(R)])
    keys = kv_all[:, :, :width]
    values = kv_all[:, :, width:]
    keys_t = keys.transpose(0, 2, 1)
    values_t = values.transpose(0, 2, 1)

    meta = (jnp.stack([row, col]), seq_ids, block_ids)
    cut_in, cut_down = cut_weights(
        shares * jnp.array([1, 0, 0], jnp.int32), w_gate, w_up, w_down, tuple(range(near)), R, dslice, hidden_n
    )
    close_in = [swap_row(a, k) if k else a for k, a in enumerate(cut_in)]
    close_down = [swap_row(a, k) if k else a for k, a in enumerate(cut_down)]
    att_near, rot_near, lse_near = attend(meta, query_near, cosine, sine, keys, values_t, width, R)
    down_grad = grad_output.astype(BF)
    grad_pieces = {(0, 0): tie(down_grad, query_near)}
    for bit in reversed(bits[1:]):
        grad_pieces = spread(grad_pieces, bit)
    grad_rows = dict(grad_pieces)
    grad_pieces[(1, 0)] = swap_col(tie(down_grad, w_query_far))
    query_far = reduce_row(
        dot_nn(ordered_in, w_query_far), send_after=query_near, use_after=(att_near, close_in)
    )
    query_far = tie(query_far, dict(grad_pieces)) * own_scale
    for (a, k), value in grad_rows.items():
        if k:
            grad_pieces[(1, k)] = swap_col(value)
    att_far, rot_far, lse_far = attend(meta, query_far, cosine, sine, keys, values_t, width, R)

    far_down = tie(far_down, att_near)
    if shared[1]:
        far_down = [lax.all_gather(jnp.stack(far_down), "dp", axis=0)]
    all_near = gather_row(att_near)
    all_far = tie(gather_row(att_far), grad_pieces)
    hidden = residual + from_order(dot_nn(all_near, w_out) + dot_nn(all_far, w_out_far))

    def exchange(parts):
        return [parts[0]] + [swap_row(parts[k], k) for k in range(1, len(parts))]

    scale_two = lax.rsqrt(psum_row(jnp.sum(hidden * hidden, axis=1)) / D + EPS)[:, None]
    normed_two = (hidden * scale_two * norm2_gain[None, :]).astype(BF)
    normed_pieces, came = gather_plane(normed_two)
    grad_pieces = spread(tie(grad_pieces, came), 1)

    fed = {}
    backs = {}
    for a in (0, 1):
        fed[a] = feed(
            [[part[(a, k)] for k in range(R)] for part in normed_pieces],
            [grad_pieces[(a, k)] for k in range(R)],
            close_in,
            close_down,
            far_in,
            far_down,
            shared,
            dp_n,
        )
        for k in range(R):
            backs[(a, k)] = fed[a][3 + k]
    acts, gate_grads, up_grads = ([fed[a][j] for a in range(2)] for j in range(3))
    normed_halves, grad_halves = ([fed[a][3 + R + j] for a in range(2)] for j in range(2))
    normed2_grad = reduce_plane(backs)

    def rows_of_down(k):
        if k < near:
            return close_down[k]
        if shared[1]:
            return far_down[0][:, k - near].reshape(hidden_n, dslice)
        return far_down[k - near]

    def ff_input_place(piece):
        moved = jnp.stack(exchange([piece[k] for k in range(R)]))
        ordered = jnp.concatenate(
            [lax.dynamic_index_in_dim(moved, row ^ s, 0, keepdims=False) for s in range(R)], axis=0
        )
        return ordered.astype(F32).T[None]

    def over_dp(local):
        return lax.psum_scatter(local, "dp", scatter_dimension=0, tiled=True)

    gate_local = feed_weight_grad(normed_halves, gate_grads, R, dp_n)
    up_local = feed_weight_grad(normed_halves, up_grads, R, dp_n)
    gate_piece = over_dp(gate_local)
    up_piece = over_dp(up_local)
    down_local = down_weight_grad(acts, grad_halves, R)
    normed2_grad = tie(normed2_grad, gate_local, up_local, down_local)

    weighted = normed2_grad * norm2_gain[None, :]
    inner_two = psum_row(jnp.sum(weighted * hidden, axis=1))[:, None]
    hidden_grad = grad_output + (
        scale_two * weighted - hidden * (scale_two * scale_two * scale_two) * inner_two / D
    )
    gain_two = jnp.sum(normed2_grad * hidden * scale_two, axis=0)
    branch_ordered = to_order(hidden_grad.astype(BF))
    late_acts = tie(acts, hidden_grad)
    products = {
        (a, k): dot_nn(late_acts[a], rows_of_down(k)).astype(BF) for a in range(2) for k in range(R)
    }
    att_grad_far = reduce_row(dot_nt(branch_ordered, w_out_far), use_after=products).astype(BF)
    grad_out_far = dot_tn(all_far, branch_ordered).astype(BF)
    grad_out_came = swap_col(grad_out_far)
    att_grad_far = tie(att_grad_far, grad_out_far)

    qpg_far, dk, dv = attend_back(
        meta, rot_far, att_grad_far, att_far, lse_far, cosine, sine, keys, keys_t, values, width, R
    )
    att_grad_near = reduce_row(
        dot_nt(branch_ordered, w_out), send_after=att_grad_far, use_after=(qpg_far, grad_out_came)
    ).astype(BF)
    qpg_near, dk, dv = attend_back(
        meta, rot_near, att_grad_near, att_near, lse_near, cosine, sine, keys, keys_t, values, width, R,
        (dk, dv),
    )
    grad_out_local = add(dot_tn(all_near, branch_ordered), grad_out_came)
    grad_out = over_dp(tie(grad_out_local, gate_piece, up_piece))

    dkv = jnp.concatenate([dk * width**-0.5, dv], axis=2).astype(BF)
    cur = {(a, k): dkv[a * R + k] for a in range(2) for k in range(R)}
    for bit in bits:
        cur = {
            (a, k): add(v, swap_row(cur[(a, k ^ bit)], bit))
            for (a, k), v in cur.items()
            if not k & bit
        }
    dkv_own = cur[(0, 0)].astype(F32) + swap_col(cur[(1, 0)]).astype(F32)
    dk_own = dkv_own[:, :width]
    dk_turned = jnp.concatenate([dk_own[:, half_width:], dk_own[:, :half_width]], axis=1)
    kvg_own = jnp.concatenate(
        [dk_own * cosine - dk_turned * sine, dkv_own[:, width:]], axis=1
    ).astype(BF)

    down_sent = [down_local[0]]
    for k in range(1, R):
        down_sent.append(swap_row(tie(down_local[k], normed2_grad if k < 3 else att_grad_far), k))
    down_moved = jnp.stack(down_sent)
    down_ordered = jnp.concatenate(
        [lax.dynamic_index_in_dim(down_moved, row ^ s, 0, keepdims=False) for s in range(R)], axis=0
    )
    grad_down = over_dp(tie(down_ordered, grad_out))
    output = hidden + reduce_plane(products, after=qpg_near)

    scale_col = scale_one[:, None]
    normed_ordered = to_order((residual * scale_col * norm1_gain[None, :]).astype(BF))
    qpg_far_all = gather_row(qpg_far)
    grad_query_far = dot_tn(normed_ordered, qpg_far_all).astype(BF)
    grad_query_came = swap_col(grad_query_far)
    qpg_near_all = tie(gather_row(qpg_near), grad_query_far)
    kvg_all = gather_row(kvg_own)
    normed1_grad = from_order(
        dot_nt(qpg_far_all, w_query_far) + dot_nt(qpg_near_all, w_query) + dot_nt(kvg_all, w_kv)
    )
    weighted_one = normed1_grad * norm1_gain[None, :]
    inner_one = psum_row(jnp.sum(weighted_one * residual, axis=1))[:, None]
    input_grad = hidden_grad + (
        scale_col * weighted_one - residual * (scale_col * scale_col * scale_col) * inner_one / D
    )
    gain_one = jnp.sum(normed1_grad * residual * scale_col, axis=0)

    grad_query_local = add(dot_tn(normed_ordered, qpg_near_all), grad_query_came)
    grad_query = over_dp(tie(grad_query_local, grad_down, output))

    def small_over_dp_col(local):
        rest = local.shape[0] // (dp_n * 2)
        local = local.reshape(dp_n, 2, rest, local.shape[1])
        mine = lax.dynamic_index_in_dim(local, col, 1, keepdims=False)
        other = lax.dynamic_index_in_dim(local, 1 - col, 1, keepdims=False).astype(BF)
        both = mine + swap_col(other).astype(F32)
        total = lax.dynamic_index_in_dim(both, z, 0, keepdims=False)
        for j in range(1, dp_n):
            share = lax.dynamic_index_in_dim(both, z ^ j, 0, keepdims=False).astype(BF)
            share = lax.ppermute(share, "dp", [(i, i ^ j) for i in range(dp_n)])
            total = total + share.astype(F32)
        return total

    grad_kv = small_over_dp_col(dot_tn(normed_ordered, kvg_all))
    gains = small_over_dp_col(jnp.stack([gain_one, gain_two], axis=1))

    return (
        output,
        input_grad,
        grad_query.astype(F32)[None],
        grad_kv[None],
        grad_out.astype(F32)[None],
        ff_input_place(gate_piece[0]),
        ff_input_place(up_piece[0]),
        grad_down.astype(F32)[None],
        gains[:, 0][None, :],
        gains[:, 1][None, :],
    )


def solution(mesh):
    placed = (
        P(("dp", "col"), "row"),
        P("dp"),
        P("dp"),
        P("dp"),
        P("row"),
        P("row"),
        P("row", "col"),
        P("row", None),
        P("col", "row"),
        P("row", "col"),
        P("row", "col"),
        P("col", "row"),
        P(("dp", "col"), "row"),
    )
    return jax.shard_map(
        functools.partial(per_device, mesh.shape["row"]),
        mesh=mesh,
        in_specs=placed,
        out_specs=(
            P(("dp", "col"), "row"),
            P(("dp", "col"), "row"),
            P("row", "dp", "col"),
            P("row", ("dp", "col"), None),
            P("col", "dp", "row"),
            P("row", "dp", "col"),
            P("row", "dp", "col"),
            P("col", "dp", "row"),
            P("row", ("dp", "col")),
            P("row", ("dp", "col")),
        ),
        check_vma=False,
    )
```

time: 969 us -> 608 us (0.63)
  waiting for transfers between devices: 422 us -> 215 us
  matrix products: 139 us -> 41.3 us
  Pallas kernels: 28.4 us -> 107 us
  other arithmetic: 144 us -> 80.7 us
  local copies, waits for them, and re-layouts: 80.5 us -> 40.7 us
  starting transfers between devices: 131 us -> 97.2 us
    ppermute x86 -> x85, waiting for transfers between devices: 227 us -> 109 us  [swap_row(): return lax.ppermute(a, 'row', [(i, i ^ bit) for i in range(R)])]
    concatenate x4 -> x1, other arithmetic: 84.1 us -> 0.17 us  [reduce_plane(): return jnp.concatenate(outs, axis=0)]
    pallas_call x0 -> x7, Pallas kernels: none -> 82.3 us  [the longest x2 51.5 us: feed(): pl.pallas_call(functools.partial(feed_body, rows_n=R, parts=parts, near=n...]
    reduce_scatter x6 -> x5, waiting for transfers between devices: 90.3 us -> 13.2 us  [over_dp(): return lax.psum_scatter(local, 'dp', scatter_dimension=0, tiled=True)]
    dot_general x13 -> x5, matrix products: 50.4 us -> 10.3 us  [dot_nt(): lax.dot_general(a, b, (((1,), (1,)), ((), ())), preferred_element_type=F32)]
    ppermute x18 -> x19, starting transfers between devices: 71.6 us -> 33.6 us  [swap_col(): return lax.ppermute(a, 'col', [(0, 1), (1, 0)])]
    dot_general x11 -> x5, matrix products: 42.4 us -> 12.1 us  [dot_tn(): lax.dot_general(a, b, (((0,), (0,)), ((), ())), preferred_element_type=F32)]
    dot_general x10 -> x13, matrix products: 46.2 us -> 18.8 us  [dot_nn(): lax.dot_general(a, b, (((1,), (0,)), ((), ())), preferred_element_type=F32)]
  transfers between devices with their start and end apart: 111 -> 117, of which waited for: 39 -> 42; matrix products, arithmetic and copies ran while one was open for 34% -> 24% of each run, Pallas kernels for 2% -> 12%
where the time goes in v2:
time: 608 us; the launch traced here: 598 us
  waiting for transfers between devices  215 us (35%)
  Pallas kernels  107 us (18%)
  starting transfers between devices  97.2 us (16%)
  other arithmetic  80.7 us (13%)
  matrix products  41.3 us (7%)
  local copies, waits for them, and re-layouts  40.7 us (7%)
  between operations  16.5 us (3%)
    ppermute x85, waiting for transfers between devices, swap_row(): return lax.ppermute(a, 'row', [(i, i ^ bit) for i in range(R)])  109 us
    ppermute x19, waiting for transfers between devices, swap_col(): return lax.ppermute(a, 'col', [(0, 1), (1, 0)])  87.2 us
    ppermute x85, starting transfers between devices, swap_row(): return lax.ppermute(a, 'row', [(i, i ^ bit) for i in range(R)])  55.7 us
    pallas_call x2, Pallas kernels, feed(): pl.pallas_call(functools.partial(feed_body, rows_n=R, parts=parts, near=n...  51.5 us
    ppermute x19, starting transfers between devices, swap_col(): return lax.ppermute(a, 'col', [(0, 1), (1, 0)])  33.6 us
    unnamed x223, local copies, waits for them, and re-layouts  20.4 us
    pallas_call x2, Pallas kernels, feed_weight_grad(): pl.pallas_call(feed_weight_body, grid=(rows_n,), in_specs=[pl.BlockSpec((...  18.9 us
    dot_general x13, matrix products, dot_nn(): lax.dot_general(a, b, (((1,), (0,)), ((), ())), preferred_element_type=F32)  18.8 us
  transfers between devices with their start and end apart: 117, of which 42 were waited for; matrix products, arithmetic and copies ran while one was open for 24% of the time, Pallas kernels for 12%

profile of v2, /device:TPU:0, one launch (start us, length us, event | category | flops | bytes accessed | tf_op | source)
XLA Modules:
  0.0 598.2 jit_solution(3269162558702113168)
XLA Ops:
  9.3 2.6 collective-permute-start.8
  16.9 2.6 fusion.3
  34.7 3.9 collective-permute-done.13
  42.2 9.4 %collective-permute-done.15 = bf16[256,256]{1,0:T(8,128)(2,1)S(1)} collective-permute-done((bf16[256,256]{1,0:T(8,128)(2,1)S(1)}, bf16[256,256]{1,0:T(8,128)(2,1)S(1)}, u32[]{:S(2)}, u32[]{:S(2)}) %collective-permute-start.15) | collective-permute-done | bytes 131104 | tf_op jit(solution)/shard_map/ppermute | solution.py:537
  54.9 2.5 convolution_convert_fusion.2
  66.8 6.8 %collective-permute-done.1 = bf16[256,1024]{1,0:T(8,128)(2,1)} collective-permute-done((bf16[256,1024]{1,0:T(8,128)(2,1)S(1)}, bf16[256,1024]{1,0:T(8,128)(2,1)}, u32[]{:S(2)}, u32[]{:S(2)}) %collective-permute-start.1) | collective-permute-done | bytes 524320 | tf_op jit(solution)/shard_map/ppermute | solution.py:537
  76.6 3.2 collective-permute-done.9
  86.8 5.2 attend.2
  93.3 25.9 %collective-permute-done.20 = bf16[256,1024]{1,0:T(8,128)(2,1)} collective-permute-done((bf16[256,1024]{1,0:T(8,128)(2,1)}, bf16[256,1024]{1,0:T(8,128)(2,1)}, u32[]{:S(2)}, u32[]{:S(2)}) %collective-permute-start.20) | collective-permute-done | bytes 524320 | tf_op jit(solution)/shard_map/ppermute | solution.py:537
  121.8 5.3 attend.3
  132.3 8.9 %collective-permute-done.24 = bf16[256,1024]{1,0:T(8,128)(2,1)S(1)} collective-permute-done((bf16[256,1024]{1,0:T(8,128)(2,1)}, bf16[256,1024]{1,0:T(8,128)(2,1)S(1)}, u32[]{:S(2)}, u32[]{:S(2)}) %collective-permute-start.24) | collective-permute-done | bytes 524320 | tf_op jit(solution)/shard_map/ppermute | solution.py:537
  143.1 6.6 %collective-permute-start.26 = (bf16[1024,512]{1,0:T(8,128)(2,1)}, bf16[1024,512]{1,0:T(8,128)(2,1)}, u32[]{:S(2)}, u32[]{:S(2)}) collective-permute-start(bf16[1024,512]{1,0:T(8,128)(2,1)} %collective-permute-done.22.refs_10_), channel_id=1, source_target_pairs={{0,1},{1,0},{2,3},{3,2},{4,5},{5,4},{6,7},{7,6},{8,9},{9,8},{10,11... | collective-permute-start | bytes 3145736 | tf_op jit(solution)/shard_map/ppermute | solution.py:540
  153.4 20.0 %collective-permute-done.26.refs_10_ = bf16[1024,512]{1,0:T(8,128)(2,1)} collective-permute-done((bf16[1024,512]{1,0:T(8,128)(2,1)}, bf16[1024,512]{1,0:T(8,128)(2,1)}, u32[]{:S(2)}, u32[]{:S(2)}) %collective-permute-start.26) | collective-permute-done | bytes 1048608 | tf_op jit(solution)/shard_map/ppermute | solution.py:540
  175.9 2.5 convolution_add_fusion
  189.7 10.8 %collective-permute-done.44.refs_4_ = bf16[512,512]{1,0:T(8,128)(2,1)S(1)} collective-permute-done((bf16[512,512]{1,0:T(8,128)(2,1)S(1)}, bf16[512,512]{1,0:T(8,128)(2,1)S(1)}, u32[]{:S(2)}, u32[]{:S(2)}) %collective-permute-start.44) | collective-permute-done | bytes 524320 | tf_op jit(solution)/shard_map/ppermute | solution.py:540
  202.5 7.9 %collective-permute-done.35.refs_0_ = bf16[512,512]{1,0:T(8,128)(2,1)S(1)} collective-permute-done((bf16[512,512]{1,0:T(8,128)(2,1)S(1)}, bf16[512,512]{1,0:T(8,128)(2,1)S(1)}, u32[]{:S(2)}, u32[]{:S(2)}) %collective-permute-start.35) | collective-permute-done | bytes 524320 | tf_op jit(solution)/shard_map/ppermute | solution.py:540
  214.5 8.9 %collective-permute-done.46.refs_6_ = bf16[512,512]{1,0:T(8,128)(2,1)S(1)} collective-permute-done((bf16[512,512]{1,0:T(8,128)(2,1)}, bf16[512,512]{1,0:T(8,128)(2,1)S(1)}, u32[]{:S(2)}, u32[]{:S(2)}) %collective-permute-start.46) | collective-permute-done | bytes 524320 | tf_op jit(solution)/shard_map/ppermute | solution.py:540
  227.5 25.6 %feed.3 = (bf16[1024,704]{1,0:T(8,128)(2,1)}, bf16[1024,704]{1,0:T(8,128)(2,1)}, bf16[1024,704]{1,0:T(8,128)(2,1)}, bf16[1024,512]{1,0:T(8,128)(2,1)}, bf16[1024...) custom-call(bf16[512,512]{1,0:T(8,128)(2,1)} %copy-done.95, ...), custom_call_target="tpu_custom_call" | custom-call | flops 14763950080 | bytes 29622272 | tf_op jit(solution)/shard_map/feed/pallas_call | solution.py:359
  253.2 25.8 %feed.2 = (bf16[1024,704]{1,0:T(8,128)(2,1)}, bf16[1024,704]{1,0:T(8,128)(2,1)}, bf16[1024,704]{1,0:T(8,128)(2,1)}, bf16[1024,512]{1,0:T(8,128)(2,1)}, bf16[1024...) custom-call(bf16[512,512]{1,0:T(8,128)(2,1)} %copy-done.72, ...), custom_call_target="tpu_custom_call" | custom-call | flops 14763950080 | bytes 29622272 | tf_op jit(solution)/shard_map/feed/pallas_call | solution.py:359
  280.5 9.3 %feed_weights.3 = bf16[4,4,704,128]{3,2,1,0:T(8,128)(2,1)} custom-call(bf16[1024,2048]{1,0:T(8,128)(2,1)} %get-tuple-element.144.x0, bf16[1024,2048]{1,0:T(8,128)(2,1)} %get-tuple-element.145.x1, bf16[1024,704]{1,0:T(8,128)(2,1)S(1)} %copy-done.14, bf16[1024,704]{1,0:T(8,128)(2,1)S(1)} %copy-done.13), custom_call_target="tpu_custom_call" | custom-call | flops 5905580032 | bytes 14155776 | tf_op jit(solution)/shard_map/feed_weights/pallas_call | solution.py:401
  296.9 2.5 add_convert_fusion.31
  305.3 9.6 %feed_weights.2 = bf16[4,4,704,128]{3,2,1,0:T(8,128)(2,1)} custom-call(bf16[1024,2048]{1,0:T(8,128)(2,1)} %get-tuple-element.144.x0, bf16[1024,2048]{1,0:T(8,128)(2,1)} %get-tuple-element.145.x1, bf16[1024,704]{1,0:T(8,128)(2,1)S(1)} %copy-done.12, bf16[1024,704]{1,0:T(8,128)(2,1)S(1)} %copy-done.11), custom_call_target="tpu_custom_call" | custom-call | flops 5905580032 | bytes 14155776 | tf_op jit(solution)/shard_map/feed_weights/pallas_call | solution.py:401
  323.3 8.7 %down_weights.1 = (bf16[704,512]{1,0:T(8,128)(2,1)S(1)}, bf16[704,512]{1,0:T(8,128)(2,1)S(1)}, bf16[704,512]{1,0:T(8,128)(2,1)S(1)}, bf16[704,512]{1,0:T(8,128)(2,1)S(1)}) custom-call(bf16[1024,704]{1,0:T(8,128)(2,1)S(1)} %copy-done.9, bf16[1024,704]{1,0:T(8,128)(2,1)S(1)} %copy-done.7, bf16[1024,2048]{1,0:T(8,128)(2,1)} %get-tuple-element.150.g0, ...), custom_call_target="tpu_custom_call" | custom-call | flops 5905580032 | bytes 14155776 | tf_op jit(solution)/shard_map/down_weights/pallas_call | solution.py:431
  332.0 8.2 %collective-permute-done.59 = bf16[512,512]{1,0:T(8,128)(2,1)S(1)} collective-permute-done((bf16[512,512]{1,0:T(8,128)(2,1)S(1)}, bf16[512,512]{1,0:T(8,128)(2,1)S(1)}, u32[]{:S(2)}, u32[]{:S(2)}) %collective-permute-start.59) | collective-permute-done | bytes 524320 | tf_op jit(solution)/shard_map/ppermute | solution.py:540
  348.8 2.5 fusion.48
  351.5 4.5 fusion.47
  365.0 2.5 convolution_convert_fusion.1
  367.5 2.5 convolution_convert_fusion
  386.3 16.6 %collective-permute-done.70 = bf16[1024,512]{1,0:T(8,128)(2,1)S(1)} collective-permute-done((bf16[1024,512]{1,0:T(8,128)(2,1)S(1)}, bf16[1024,512]{1,0:T(8,128)(2,1)S(1)}, u32[]{:S(2)}, u32[]{:S(2)}) %collective-permute-start.70) | collective-permute-done | bytes 1048608 | tf_op jit(solution)/shard_map/ppermute | solution.py:540
  405.2 3.7 collective-permute-done.68
  412.4 2.5 add_convert_fusion.18
  414.9 6.9 %attend_back.2 = (bf16[256,1024]{1,0:T(8,128)(2,1)}, f32[8,256,128]{2,1,0:T(8,128)}, f32[8,256,128]{2,1,0:T(8,128)}) custom-call(s32[2]{0:T(128)} %pad_add_fusion.where, s32[2048]{0:T(1024)} %seq_ref.7, s32[2048]{0:T(1024)} %block_ref.7, bf16[256,1024]{1,0:T(8,128)(2,1)} %get-tuple-element.163.rot_ref, bf16[256,1024]{1,0:T(8,128)(2,1)} %add_convert_fusion.15.grad_ref, ...), custom_call_target="tpu_custom_call" | custom-call | flops 2684354560 | bytes 5242880 | tf_op jit(solution)/shard_map/attend_back/pallas_call | solution.py:189
  428.4 7.3 %attend_back.3 = (bf16[256,1024]{1,0:T(8,128)(2,1)}, f32[8,256,128]{2,1,0:T(8,128)}, f32[8,256,128]{2,1,0:T(8,128)}) custom-call(s32[2]{0:T(128)} %pad_add_fusion.where, s32[2048]{0:T(1024)} %seq_ref.7, s32[2048]{0:T(1024)} %block_ref.7, bf16[256,1024]{1,0:T(8,128)(2,1)} %get-tuple-element.159.rot_ref, bf16[256,1024]{1,0:T(8,128)(2,1)} %add_convert_fusion.14.grad_ref, ...), custom_call_target="tpu_custom_call" | custom-call | flops 2684354560 | bytes 5242880 | tf_op jit(solution)/shard_map/attend_back/pallas_call | solution.py:189
  438.2 2.7 collective-permute-start.85
  441.0 10.0 %collective-permute-done.77 = bf16[256,1024]{1,0:T(8,128)(2,1)} collective-permute-done((bf16[256,1024]{1,0:T(8,128)(2,1)}, bf16[256,1024]{1,0:T(8,128)(2,1)}, u32[]{:S(2)}, u32[]{:S(2)}) %collective-permute-start.77) | collective-permute-done | bytes 524320 | tf_op jit(solution)/shard_map/ppermute | solution.py:537
  461.5 4.7 collective-permute-done.86
  468.8 3.9 collective-permute-start.87
  474.3 3.2 collective-permute-done.87
  482.6 7.1 %collective-permute-done.88 = bf16[256,256]{1,0:T(8,128)(2,1)} collective-permute-done((bf16[256,256]{1,0:T(8,128)(2,1)S(1)}, bf16[256,256]{1,0:T(8,128)(2,1)}, u32[]{:S(2)}, u32[]{:S(2)}) %collective-permute-start.88) | collective-permute-done | bytes 131104 | tf_op jit(solution)/shard_map/ppermute | solution.py:537
  498.9 2.5 collective-permute-done.96
  502.7 3.4 collective-permute-start.98
  516.7 2.6 fusion.54
  519.8 11.5 %collective-permute-done.73 = bf16[512,512]{1,0:T(8,128)(2,1)S(1)} collective-permute-done((bf16[512,512]{1,0:T(8,128)(2,1)S(1)}, bf16[512,512]{1,0:T(8,128)(2,1)S(1)}, u32[]{:S(2)}, u32[]{:S(2)}) %collective-permute-start.73) | collective-permute-done | bytes 524320 | tf_op jit(solution)/shard_map/ppermute | solution.py:537
  547.4 3.4 collective-permute-start.109
  550.8 2.9 collective-permute-done.108
  557.3 4.6 add_convert_fusion.1
  564.3 3.7 fusion.7
  576.0 13.1 %reduce-scatter.14.cloned.1.call-done = bf16[128,1024]{1,0:T(8,128)(2,1)} async-done(((bf16[512,1024]{1,0:T(8,128)(2,1)}), bf16[128,1024]{1,0:T(8,128)(2,1)}) %reduce-scatter.14.cloned.1.call-update) | async-done | bytes 262160 | tf_op jit(solution)/shard_map/reduce_scatter | solution.py:758
  (578 shorter events, 230.8 us)
Async XLA Ops:
  7.2 220.3 %all-gather.7.cloned.1.call-start = ((), (), s32[]{:S(2)}) async-start(), calls=%async_computation.11 | async-start | bytes 1802240 | tf_op jit(solution)/shard_map/all_gather | solution.py:711
  9.3 44.0 %collective-permute-start.8 = (bf16[512,1024]{1,0:T(8,128)(2,1)}, bf16[512,1024]{1,0:T(8,128)(2,1)}, u32[]{:S(2)}, u32[]{:S(2)}) collective-permute-start(bf16[512,1024]{1,0:T(8,128)(2,1)} %param.20), channel_id=1, source_target_pairs={{0,1},{1,0},{2,3},{3,2},{4,5},{5,4},{6,7},{7,6},{8,9},{9,8},{10,11... | collective-permute-start | bytes 3145736 | tf_op jit(solution)/shard_map/ppermute | solution.py:540
  26.1 32.5 %collective-permute-start = (bf16[512,1024]{1,0:T(8,128)(2,1)S(1)}, bf16[512,1024]{1,0:T(8,128)(2,1)S(1)}, u32[]{:S(2)}, u32[]{:S(2)}) collective-permute-start(bf16[512,1024]{1,0:T(8,128)(2,1)S(1)} %slice.358), channel_id=1, source_target_pairs={{0,2},{2,0},{4,6},{6,4},{1,3},{3,1},{5,7},{7,5},{8,10},{10,8},{12,... | collective-permute-start | bytes 3145736 | tf_op jit(solution)/shard_map/ppermute | solution.py:537
  38.6 20.5 %collective-permute-start.6 = (bf16[2,704,128]{2,1,0:T(8,128)(2,1)S(1)}, bf16[2,704,128]{2,1,0:T(8,128)(2,1)S(1)}, u32[]{:S(2)}, u32[]{:S(2)}) collective-permute-start(bf16[2,704,128]{2,1,0:T(8,128)(2,1)S(1)} %get-tuple-element.100), channel_id=1, source_target_pairs={{0,4},{2,6},{4,0},{6,2},{1,5},{3,7},{5,1},{7,3},{8,12},{10,14},{12... | collective-permute-start | bytes 1081352 | tf_op jit(solution)/shard_map/ppermute | solution.py:537
  53.3 26.4 %collective-permute-start.9 = (bf16[1024,512]{1,0:T(8,128)(2,1)}, bf16[1024,512]{1,0:T(8,128)(2,1)}, u32[]{:S(2)}, u32[]{:S(2)}) collective-permute-start(bf16[1024,512]{1,0:T(8,128)(2,1)} %param.22), channel_id=1, source_target_pairs={{0,1},{1,0},{2,3},{3,2},{4,5},{5,4},{6,7},{7,6},{8,9},{9,8},{10,11... | collective-permute-start | bytes 3145736 | tf_op jit(solution)/shard_map/ppermute | solution.py:540
  58.6 21.2 %collective-permute-start.19 = (bf16[512,1024]{1,0:T(8,128)(2,1)}, bf16[512,1024]{1,0:T(8,128)(2,1)}, u32[]{:S(2)}, u32[]{:S(2)}) collective-permute-start(bf16[512,1024]{1,0:T(8,128)(2,1)} %slice.372), channel_id=1, source_target_pairs={{0,2},{2,0},{4,6},{6,4},{1,3},{3,1},{5,7},{7,5},{8,10},{10,8},{12,... | collective-permute-start | bytes 3145736 | tf_op jit(solution)/shard_map/ppermute | solution.py:537
  62.2 31.2 %collective-permute-start.21 = (bf16[2,704,512]{2,1,0:T(8,128)(2,1)S(1)}, bf16[2,704,512]{2,1,0:T(8,128)(2,1)}, u32[]{:S(2)}, u32[]{:S(2)}) collective-permute-start(bf16[2,704,512]{2,1,0:T(8,128)(2,1)S(1)} %get-tuple-element.107), channel_id=1, source_target_pairs={{0,2},{2,0},{4,6},{6,4},{1,3},{3,1},{5,7},{7,5},{8,10},{10,8},{12,... | collective-permute-start | bytes 4325384 | tf_op jit(solution)/shard_map/ppermute | solution.py:537
  65.2 55.4 %collective-permute-start.23 = (bf16[1024,512]{1,0:T(8,128)(2,1)}, bf16[1024,512]{1,0:T(8,128)(2,1)}, u32[]{:S(2)}, u32[]{:S(2)}) collective-permute-start(bf16[1024,512]{1,0:T(8,128)(2,1)} %convert_element_type.579.refs_8_), channel_id=1, source_target_pairs={{0,1},{1,0},{2,3},{3,2},{4,5},{5,4},{6,7},{7,6},{8,9},{9,8},{10,11... | collective-permute-start | bytes 3145736 | tf_op jit(solution)/shard_map/ppermute | solution.py:540
  79.8 40.9 %collective-permute-start.22 = (bf16[1024,512]{1,0:T(8,128)(2,1)}, bf16[1024,512]{1,0:T(8,128)(2,1)}, u32[]{:S(2)}, u32[]{:S(2)}) collective-permute-start(bf16[1024,512]{1,0:T(8,128)(2,1)} %convert_element_type.579.refs_8_), channel_id=1, source_target_pairs={{0,4},{2,6},{4,0},{6,2},{1,5},{3,7},{5,1},{7,3},{8,12},{10,14},{12... | collective-permute-start | bytes 3145736 | tf_op jit(solution)/shard_map/ppermute | solution.py:537
  82.8 36.5 %collective-permute-start.20 = (bf16[256,1024]{1,0:T(8,128)(2,1)}, bf16[256,1024]{1,0:T(8,128)(2,1)}, u32[]{:S(2)}, u32[]{:S(2)}) collective-permute-start(bf16[256,1024]{1,0:T(8,128)(2,1)} %slice.374), channel_id=1, source_target_pairs={{0,4},{2,6},{4,0},{6,2},{1,5},{3,7},{5,1},{7,3},{8,12},{10,14},{12... | collective-permute-start | bytes 1572872 | tf_op jit(solution)/shard_map/ppermute | solution.py:537
  92.8 134.7 %all-gather.5.cloned.1.call-start = ((), (), s32[]{:S(2)}) async-start(), calls=%async_computation.10 | async-start | bytes 3604480 | tf_op jit(solution)/shard_map/all_gather | solution.py:664
  92.8 37.6 %collective-permute-start.17 = (bf16[256,1024]{1,0:T(8,128)(2,1)}, bf16[256,1024]{1,0:T(8,128)(2,1)S(1)}, u32[]{:S(2)}, u32[]{:S(2)}) collective-permute-start(bf16[256,1024]{1,0:T(8,128)(2,1)} %get-tuple-element.104.att_ref), channel_id=1, source_target_pairs={{0,4},{2,6},{4,0},{6,2},{1,5},{3,7},{5,1},{7,3},{8,12},{10,14},{12... | collective-permute-start | bytes 1572872 | tf_op jit(solution)/shard_map/ppermute | solution.py:537
  131.4 18.5 %collective-permute-start.18 = (bf16[512,1024]{1,0:T(8,128)(2,1)}, bf16[512,1024]{1,0:T(8,128)(2,1)}, u32[]{:S(2)}, u32[]{:S(2)}) collective-permute-start(bf16[512,1024]{1,0:T(8,128)(2,1)} %pad_maximum_fusion.7), channel_id=1, source_target_pairs={{0,2},{2,0},{4,6},{6,4},{1,3},{3,1},{5,7},{7,5},{8,10},{10,8},{12,... | collective-permute-start | bytes 3145736 | tf_op jit(solution)/shard_map/ppermute | solution.py:537
  143.1 30.3 %collective-permute-start.26 = (bf16[1024,512]{1,0:T(8,128)(2,1)}, bf16[1024,512]{1,0:T(8,128)(2,1)}, u32[]{:S(2)}, u32[]{:S(2)}) collective-permute-start(bf16[1024,512]{1,0:T(8,128)(2,1)} %collective-permute-done.22.refs_10_), channel_id=1, source_target_pairs={{0,1},{1,0},{2,3},{3,2},{4,5},{5,4},{6,7},{7,6},{8,9},{9,8},{10,11... | collective-permute-start | bytes 3145736 | tf_op jit(solution)/shard_map/ppermute | solution.py:540
  149.8 324.0 %reduce-scatter.8.cloned.1.call-start = ((), (), s32[]{:S(2)}) async-start(), calls=%async_computation.6 | async-start | bytes 3604480 | tf_op jit(solution)/shard_map/reduce_scatter | solution.py:758
  187.4 24.8 %collective-permute-start.38 = (bf16[704,512]{1,0:T(8,128)(2,1)S(1)}, bf16[704,512]{1,0:T(8,128)(2,1)S(1)}, u32[]{:S(2)}, u32[]{:S(2)}) collective-permute-start(bf16[704,512]{1,0:T(8,128)(2,1)S(1)} %get-tuple-element.117), channel_id=1, source_target_pairs={{0,2},{2,0},{4,6},{6,4},{1,3},{3,1},{5,7},{7,5},{8,10},{10,8},{12,... | collective-permute-start | bytes 2162696 | tf_op jit(solution)/shard_map/ppermute | solution.py:537
  189.4 21.0 %collective-permute-start.35 = (bf16[512,512]{1,0:T(8,128)(2,1)S(1)}, bf16[512,512]{1,0:T(8,128)(2,1)S(1)}, u32[]{:S(2)}, u32[]{:S(2)}) collective-permute-start(bf16[512,512]{1,0:T(8,128)(2,1)S(1)} %get-tuple-element.283.refs_0_), channel_id=1, source_target_pairs={{0,1},{1,0},{2,3},{3,2},{4,5},{5,4},{6,7},{7,6},{8,9},{9,8},{10,11... | collective-permute-start | bytes 1572872 | tf_op jit(solution)/shard_map/ppermute | solution.py:540
  189.7 24.2 %collective-permute-start.32 = (bf16[512,512]{1,0:T(8,128)(2,1)S(1)}, bf16[512,512]{1,0:T(8,128)(2,1)S(1)}, u32[]{:S(2)}, u32[]{:S(2)}) collective-permute-start(bf16[512,512]{1,0:T(8,128)(2,1)S(1)} %get-tuple-element.282.refs_4_), channel_id=1, source_target_pairs={{0,2},{2,0},{4,6},{6,4},{1,3},{3,1},{5,7},{7,5},{8,10},{10,8},{12,... | collective-permute-start | bytes 1572872 | tf_op jit(solution)/shard_map/ppermute | solution.py:537
  224.6 28.5 %collective-permute-start.29 = (bf16[512,512]{1,0:T(8,128)(2,1)S(1)}, bf16[512,512]{1,0:T(8,128)(2,1)}, u32[]{:S(2)}, u32[]{:S(2)}) collective-permute-start(bf16[512,512]{1,0:T(8,128)(2,1)S(1)} %get-tuple-element.283.refs_0_), channel_id=1, source_target_pairs={{0,2},{2,0},{4,6},{6,4},{1,3},{3,1},{5,7},{7,5},{8,10},{10,8},{12,... | collective-permute-start | bytes 1572872 | tf_op jit(solution)/shard_map/ppermute | solution.py:537
  225.3 27.9 %collective-permute-start.36 = (bf16[1024,512]{1,0:T(8,128)(2,1)S(1)}, bf16[1024,512]{1,0:T(8,128)(2,1)}, u32[]{:S(2)}, u32[]{:S(2)}) collective-permute-start(bf16[1024,512]{1,0:T(8,128)(2,1)S(1)} %copy-done.55), channel_id=1, source_target_pairs={{0,2},{2,0},{4,6},{6,4},{1,3},{3,1},{5,7},{7,5},{8,10},{10,8},{12,... | collective-permute-start | bytes 3145736 | tf_op jit(solution)/shard_map/ppermute | solution.py:537
  226.5 26.7 %collective-permute-start.37 = (bf16[1024,512]{1,0:T(8,128)(2,1)}, bf16[1024,512]{1,0:T(8,128)(2,1)}, u32[]{:S(2)}, u32[]{:S(2)}) collective-permute-start(bf16[1024,512]{1,0:T(8,128)(2,1)} %collective-permute-done.22.refs_10_), channel_id=1, source_target_pairs={{0,2},{2,0},{4,6},{6,4},{1,3},{3,1},{5,7},{7,5},{8,10},{10,8},{12,... | collective-permute-start | bytes 3145736 | tf_op jit(solution)/shard_map/ppermute | solution.py:537
  226.7 26.5 %collective-permute-start.34 = (bf16[512,512]{1,0:T(8,128)(2,1)}, bf16[512,512]{1,0:T(8,128)(2,1)}, u32[]{:S(2)}, u32[]{:S(2)}) collective-permute-start(bf16[512,512]{1,0:T(8,128)(2,1)} %collective-permute-done.33.refs_6_), channel_id=1, source_target_pairs={{0,2},{2,0},{4,6},{6,4},{1,3},{3,1},{5,7},{7,5},{8,10},{10,8},{12,... | collective-permute-start | bytes 1572872 | tf_op jit(solution)/shard_map/ppermute | solution.py:537
  227.4 25.9 %collective-permute-start.31 = (bf16[512,512]{1,0:T(8,128)(2,1)}, bf16[512,512]{1,0:T(8,128)(2,1)}, u32[]{:S(2)}, u32[]{:S(2)}) collective-permute-start(bf16[512,512]{1,0:T(8,128)(2,1)} %collective-permute-done.30.refs_2_), channel_id=1, source_target_pairs={{0,2},{2,0},{4,6},{6,4},{1,3},{3,1},{5,7},{7,5},{8,10},{10,8},{12,... | collective-permute-start | bytes 1572872 | tf_op jit(solution)/shard_map/ppermute | solution.py:537
  289.9 183.9 %reduce-scatter.6.cloned.1.call-start = ((), (), s32[]{:S(2)}) async-start(), calls=%async_computation.5 | async-start | bytes 3604480 | tf_op jit(solution)/shard_map/reduce_scatter | solution.py:758
  315.4 25.0 %collective-permute-start.54 = (bf16[512,512]{1,0:T(8,128)(2,1)}, bf16[512,512]{1,0:T(8,128)(2,1)S(1)}, u32[]{:S(2)}, u32[]{:S(2)}) collective-permute-start(bf16[512,512]{1,0:T(8,128)(2,1)} %get-tuple-element.137), channel_id=1, source_target_pairs={{0,1},{1,0},{2,3},{3,2},{4,5},{5,4},{6,7},{7,6},{8,9},{9,8},{10,11... | collective-permute-start | bytes 1572872 | tf_op jit(solution)/shard_map/ppermute | solution.py:540
  316.2 24.0 %collective-permute-start.59 = (bf16[512,512]{1,0:T(8,128)(2,1)S(1)}, bf16[512,512]{1,0:T(8,128)(2,1)S(1)}, u32[]{:S(2)}, u32[]{:S(2)}) collective-permute-start(bf16[512,512]{1,0:T(8,128)(2,1)S(1)} %add_convert_fusion.20), channel_id=1, source_target_pairs={{0,1},{1,0},{2,3},{3,2},{4,5},{5,4},{6,7},{7,6},{8,9},{9,8},{10,11... | collective-permute-start | bytes 1572872 | tf_op jit(solution)/shard_map/ppermute | solution.py:540
  318.6 21.8 %collective-permute-start.56 = (bf16[512,512]{1,0:T(8,128)(2,1)S(1)}, bf16[512,512]{1,0:T(8,128)(2,1)S(1)}, u32[]{:S(2)}, u32[]{:S(2)}) collective-permute-start(bf16[512,512]{1,0:T(8,128)(2,1)S(1)} %add_convert_fusion.26), channel_id=1, source_target_pairs={{0,4},{2,6},{4,0},{6,2},{1,5},{3,7},{5,1},{7,3},{8,12},{10,14},{12... | collective-permute-start | bytes 1572872 | tf_op jit(solution)/shard_map/ppermute | solution.py:537
  351.3 147.2 %reduce-scatter.10.cloned.1.call-start = ((), (), s32[]{:S(2)}) async-start(), calls=%async_computation.7 | async-start | bytes 1310720 | tf_op jit(solution)/shard_map/reduce_scatter | solution.py:758
  351.5 105.2 %collective-permute-start.93 = (bf16[704,512]{1,0:T(8,128)(2,1)S(1)}, bf16[704,512]{1,0:T(8,128)(2,1)}, u32[]{:S(2)}, u32[]{:S(2)}) collective-permute-start(bf16[704,512]{1,0:T(8,128)(2,1)S(1)} %get-tuple-element.182), channel_id=1, source_target_pairs={{0,2},{2,0},{4,6},{6,4},{1,3},{3,1},{5,7},{7,5},{8,10},{10,8},{12,... | collective-permute-start | bytes 2162696 | tf_op jit(solution)/shard_map/ppermute | solution.py:537
  377.3 25.6 %collective-permute-start.70 = (bf16[1024,512]{1,0:T(8,128)(2,1)S(1)}, bf16[1024,512]{1,0:T(8,128)(2,1)S(1)}, u32[]{:S(2)}, u32[]{:S(2)}) collective-permute-start(bf16[1024,512]{1,0:T(8,128)(2,1)S(1)} %convolution_convert_fusion.5), channel_id=1, source_target_pairs={{0,1},{1,0},{2,3},{3,2},{4,5},{5,4},{6,7},{7,6},{8,9},{9,8},{10,11... | collective-permute-start | bytes 3145736 | tf_op jit(solution)/shard_map/ppermute | solution.py:540
  379.5 77.7 %collective-permute-start.94 = (bf16[704,512]{1,0:T(8,128)(2,1)S(1)}, bf16[704,512]{1,0:T(8,128)(2,1)}, u32[]{:S(2)}, u32[]{:S(2)}) collective-permute-start(bf16[704,512]{1,0:T(8,128)(2,1)S(1)} %get-tuple-element.183), channel_id=1, source_target_pairs={{0,4},{2,6},{4,0},{6,2},{1,5},{3,7},{5,1},{7,3},{8,12},{10,14},{12... | collective-permute-start | bytes 2162696 | tf_op jit(solution)/shard_map/ppermute | solution.py:537
  381.1 31.4 %collective-permute-start.63 = (bf16[1024,512]{1,0:T(8,128)(2,1)}, bf16[1024,512]{1,0:T(8,128)(2,1)}, u32[]{:S(2)}, u32[]{:S(2)}) collective-permute-start(bf16[1024,512]{1,0:T(8,128)(2,1)} %convolution_convert_fusion.10), channel_id=1, source_target_pairs={{0,2},{2,0},{4,6},{6,4},{1,3},{3,1},{5,7},{7,5},{8,10},{10,8},{12,... | collective-permute-start | bytes 3145736 | tf_op jit(solution)/shard_map/ppermute | solution.py:537
  383.3 25.5 %collective-permute-start.68 = (bf16[256,1024]{1,0:T(8,128)(2,1)}, bf16[256,1024]{1,0:T(8,128)(2,1)}, u32[]{:S(2)}, u32[]{:S(2)}) collective-permute-start(bf16[256,1024]{1,0:T(8,128)(2,1)} %slice.402), channel_id=1, source_target_pairs={{0,4},{2,6},{4,0},{6,2},{1,5},{3,7},{5,1},{7,3},{8,12},{10,14},{12... | collective-permute-start | bytes 1572872 | tf_op jit(solution)/shard_map/ppermute | solution.py:537
  414.9 42.4 %collective-permute-start.95 = (bf16[704,512]{1,0:T(8,128)(2,1)S(1)}, bf16[704,512]{1,0:T(8,128)(2,1)}, u32[]{:S(2)}, u32[]{:S(2)}) collective-permute-start(bf16[704,512]{1,0:T(8,128)(2,1)S(1)} %get-tuple-element.184), channel_id=1, source_target_pairs={{0,6},{2,4},{4,2},{6,0},{1,7},{3,5},{5,3},{7,1},{8,14},{10,12},{12... | collective-permute-start | bytes 2162696 | tf_op jit(solution)/shard_map/ppermute | solution.py:537
  421.8 29.1 %collective-permute-start.77 = (bf16[256,1024]{1,0:T(8,128)(2,1)}, bf16[256,1024]{1,0:T(8,128)(2,1)}, u32[]{:S(2)}, u32[]{:S(2)}) collective-permute-start(bf16[256,1024]{1,0:T(8,128)(2,1)} %get-tuple-element.165), channel_id=1, source_target_pairs={{0,4},{2,6},{4,0},{6,2},{1,5},{3,7},{5,1},{7,3},{8,12},{10,14},{12... | collective-permute-start | bytes 1572872 | tf_op jit(solution)/shard_map/ppermute | solution.py:537
  438.2 18.4 %collective-permute-start.85 = (bf16[256,256]{1,0:T(8,128)(2,1)S(1)}, bf16[256,256]{1,0:T(8,128)(2,1)S(1)}, u32[]{:S(2)}, u32[]{:S(2)}) collective-permute-start(bf16[256,256]{1,0:T(8,128)(2,1)S(1)} %get-tuple-element.267), channel_id=1, source_target_pairs={{0,2},{2,0},{4,6},{6,4},{1,3},{3,1},{5,7},{7,5},{8,10},{10,8},{12,... | collective-permute-start | bytes 393224 | tf_op jit(solution)/shard_map/ppermute | solution.py:537
  450.9 51.7 %collective-permute-start.79 = (bf16[256,1024]{1,0:T(8,128)(2,1)}, bf16[256,1024]{1,0:T(8,128)(2,1)}, u32[]{:S(2)}, u32[]{:S(2)}) collective-permute-start(bf16[256,1024]{1,0:T(8,128)(2,1)} %get-tuple-element.170), channel_id=1, source_target_pairs={{0,4},{2,6},{4,0},{6,2},{1,5},{3,7},{5,1},{7,3},{8,12},{10,14},{12... | collective-permute-start | bytes 1572872 | tf_op jit(solution)/shard_map/ppermute | solution.py:537
  459.4 59.9 %collective-permute-start.71 = (bf16[512,512]{1,0:T(8,128)(2,1)}, bf16[512,512]{1,0:T(8,128)(2,1)}, u32[]{:S(2)}, u32[]{:S(2)}) collective-permute-start(bf16[512,512]{1,0:T(8,128)(2,1)} %get-tuple-element.172), channel_id=1, source_target_pairs={{0,1},{1,0},{2,3},{3,2},{4,5},{5,4},{6,7},{7,6},{8,9},{9,8},{10,11... | collective-permute-start | bytes 1572872 | tf_op jit(solution)/shard_map/ppermute | solution.py:540
  473.8 88.2 %reduce-scatter.12.cloned.1.call-start = ((), (), s32[]{:S(2)}) async-start(), calls=%async_computation.8 | async-start | bytes 3604480 | tf_op jit(solution)/shard_map/reduce_scatter | solution.py:758
  473.9 23.4 %collective-permute-start.75 = (bf16[512,512]{1,0:T(8,128)(2,1)}, bf16[512,512]{1,0:T(8,128)(2,1)}, u32[]{:S(2)}, u32[]{:S(2)}) collective-permute-start(bf16[512,512]{1,0:T(8,128)(2,1)} %get-tuple-element.178), channel_id=1, source_target_pairs={{0,4},{2,6},{4,0},{6,2},{1,5},{3,7},{5,1},{7,3},{8,12},{10,14},{12... | collective-permute-start | bytes 1572872 | tf_op jit(solution)/shard_map/ppermute | solution.py:537
  489.7 24.6 %collective-permute-start.78 = (bf16[512,1024]{1,0:T(8,128)(2,1)}, bf16[512,1024]{1,0:T(8,128)(2,1)S(1)}, u32[]{:S(2)}, u32[]{:S(2)}) collective-permute-start(bf16[512,1024]{1,0:T(8,128)(2,1)} %pad_maximum_fusion.10), channel_id=1, source_target_pairs={{0,2},{2,0},{4,6},{6,4},{1,3},{3,1},{5,7},{7,5},{8,10},{10,8},{12,... | collective-permute-start | bytes 3145736 | tf_op jit(solution)/shard_map/ppermute | solution.py:537
  498.6 90.5 %reduce-scatter.14.cloned.1.call-start = ((), (), s32[]{:S(2)}) async-start(), calls=%async_computation.9 | async-start | bytes 1310720 | tf_op jit(solution)/shard_map/reduce_scatter | solution.py:758
  507.8 24.8 %collective-permute-start.74 = (bf16[512,512]{1,0:T(8,128)(2,1)S(1)}, bf16[512,512]{1,0:T(8,128)(2,1)S(1)}, u32[]{:S(2)}, u32[]{:S(2)}) collective-permute-start(bf16[512,512]{1,0:T(8,128)(2,1)S(1)} %copy-done.70), channel_id=1, source_target_pairs={{0,4},{2,6},{4,0},{6,2},{1,5},{3,7},{5,1},{7,3},{8,12},{10,14},{12... | collective-permute-start | bytes 1572872 | tf_op jit(solution)/shard_map/ppermute | solution.py:537
  509.2 22.1 %collective-permute-start.73 = (bf16[512,512]{1,0:T(8,128)(2,1)S(1)}, bf16[512,512]{1,0:T(8,128)(2,1)S(1)}, u32[]{:S(2)}, u32[]{:S(2)}) collective-permute-start(bf16[512,512]{1,0:T(8,128)(2,1)S(1)} %add_convert_fusion.12), channel_id=1, source_target_pairs={{0,4},{2,6},{4,0},{6,2},{1,5},{3,7},{5,1},{7,3},{8,12},{10,14},{12... | collective-permute-start | bytes 1572872 | tf_op jit(solution)/shard_map/ppermute | solution.py:537
  512.0 20.5 %collective-permute-start.76 = (bf16[512,512]{1,0:T(8,128)(2,1)S(1)}, bf16[512,512]{1,0:T(8,128)(2,1)S(1)}, u32[]{:S(2)}, u32[]{:S(2)}) collective-permute-start(bf16[512,512]{1,0:T(8,128)(2,1)S(1)} %add_convert_fusion.6), channel_id=1, source_target_pairs={{0,1},{1,0},{2,3},{3,2},{4,5},{5,4},{6,7},{7,6},{8,9},{9,8},{10,11... | collective-permute-start | bytes 1572872 | tf_op jit(solution)/shard_map/ppermute | solution.py:540
  514.3 22.1 %collective-permute-start.80 = (bf16[512,1024]{1,0:T(8,128)(2,1)S(1)}, bf16[512,1024]{1,0:T(8,128)(2,1)S(1)}, u32[]{:S(2)}, u32[]{:S(2)}) collective-permute-start(bf16[512,1024]{1,0:T(8,128)(2,1)S(1)} %pad_maximum_fusion.11), channel_id=1, source_target_pairs={{0,2},{2,0},{4,6},{6,4},{1,3},{3,1},{5,7},{7,5},{8,10},{10,8},{12,... | collective-permute-start | bytes 3145736 | tf_op jit(solution)/shard_map/ppermute | solution.py:537
  519.3 37.7 %collective-permute-start.92 = (bf16[512,1024]{1,0:T(8,128)(2,1)}, bf16[512,1024]{1,0:T(8,128)(2,1)}, u32[]{:S(2)}, u32[]{:S(2)}) collective-permute-start(bf16[512,1024]{1,0:T(8,128)(2,1)} %convolution_convert_fusion.4), channel_id=1, source_target_pairs={{0,1},{1,0},{2,3},{3,2},{4,5},{5,4},{6,7},{7,6},{8,9},{9,8},{10,11... | collective-permute-start | bytes 3145736 | tf_op jit(solution)/shard_map/ppermute | solution.py:540
  535.5 28.7 %collective-permute-start.102 = (bf16[704,128]{1,0:T(8,128)(2,1)}, bf16[704,128]{1,0:T(8,128)(2,1)}, u32[]{:S(2)}, u32[]{:S(2)}) collective-permute-start(bf16[704,128]{1,0:T(8,128)(2,1)} %get-tuple-element.301), channel_id=1, source_target_pairs={{0,6},{2,4},{4,2},{6,0},{1,7},{3,5},{5,3},{7,1},{8,14},{10,12},{12... | collective-permute-start | bytes 540680 | tf_op jit(solution)/shard_map/ppermute | solution.py:537
  (172 other events, 1509.1 us)
Sparse Core Ops, SparseCore 0:
  92.9 40.0 all-gather.6
  149.9 57.3 all-gather.4
  290.0 55.1 reduce-scatter.7
  351.5 53.8 reduce-scatter.5
  473.9 23.1 reduce-scatter.9
  499.4 55.9 reduce-scatter.11
  562.1 27.0 reduce-scatter.13

commit v3 on v2

--- a/solution.py
+++ b/solution.py
@@ -15,6 +15,7 @@
 BF = jnp.bfloat16
 F32 = jnp.float32
 HEADS_PER_STEP = 4
+FL = {'f11': 0, 'f13': 1, 'f0': 1, 'f1': 1, 'f5': 2, 'f9': 1, 'f12': 2, 'f2': 1, 'f3': 1, 'f4': 0, 'f8': 0, 'f10': 3, 'f6': 1, 'f7': 1, 'f14': 1, 'f15': 0, 'f16': 0, 'f17': 0, 'b0': 1, 'b1': 1, 'b2': 1, 'b3': 0, 'b4': 0, 'b5': 3, 'b6': 0, 'b7': 1, 'b8': 1, 'b29': 1, 'b28': 0, 'b18': 2, 'b19': 1, 'b24': 2, 'b9': 3, 'b13': 5, 'b14': 3, 'b15': 0, 'b16': 0, 'b17': 2, 'b20': 0, 'b22': 0, 'b23': 0, 'b25': 1, 'b26': 0, 'b27': 0, 'b30': 0, 'b31': 0, 'b32': 1, 'b33': 0, 'b34': 0, 'b36': 0}
 
 
 def dot_nn(a, b):
@@ -46,12 +47,17 @@
 
 
 def attend_body(
-    where, seq_ref, block_ref, q_ref, cos_ref, sin_ref, k_ref, vt_ref,
-    att_ref, rot_ref, lse_ref, list_ref, *, factor, width, rows_n,
+    where, seq_ref, block_ref, q_ref, cos_ref, sin_ref, *refs, factor, width, rows_n,
 ):
+    pieces = refs[:-6]
+    att_ref, rot_ref, lse_ref, list_ref, k_ref, vt_ref = refs[-6:]
+
     @pl.when(pl.program_id(0) == 0)
     def _():
         list_visible(where, seq_ref, block_ref, list_ref, rows_n=rows_n, rows=q_ref.shape[0])
+        for j, piece in enumerate(pieces):
+            k_ref[j] = piece[:, :width]
+            vt_ref[j] = piece[:, width:].T
 
     cosine = cos_ref[...]
     sine = sin_ref[...]
@@ -87,14 +93,13 @@
         lse_ref[head] = top + jnp.log2(total)
 
 
-def attend(meta, q_pre, cosine, sine, keys, values_t, width, rows_n):
+def attend(meta, q_pre, cosine, sine, kv, width, rows_n):
     where, seq_ids, block_ids = meta
     rows, columns = q_pre.shape
     heads = columns // width
-    chunks = keys.shape[0]
+    chunks = len(kv)
     span = HEADS_PER_STEP * width
     whole2 = lambda i, m: (0, 0)
-    whole3 = lambda i, m: (0, 0, 0)
     return pl.pallas_call(
         functools.partial(attend_body, factor=width**-0.5 * LOG2E, width=width, rows_n=rows_n),
         grid_spec=pltpu.PrefetchScalarGridSpec(
@@ -106,15 +111,18 @@
                 pl.BlockSpec((rows, span), lambda i, m: (0, i)),
                 pl.BlockSpec((rows, width), whole2),
                 pl.BlockSpec((rows, width), whole2),
-                pl.BlockSpec((chunks, rows, width), whole3),
-                pl.BlockSpec((chunks, width, rows), whole3),
-            ],
+            ]
+            + [pl.BlockSpec((rows, 2 * width), whole2)] * chunks,
             out_specs=[
                 pl.BlockSpec((rows, span), lambda i, m: (0, i)),
                 pl.BlockSpec((rows, span), lambda i, m: (0, i)),
                 pl.BlockSpec((HEADS_PER_STEP, 1, rows), lambda i, m: (i, 0, 0)),
             ],
-            scratch_shapes=[pltpu.SMEM((chunks + 1,), jnp.int32)],
+            scratch_shapes=[
+                pltpu.SMEM((chunks + 1,), jnp.int32),
+                pltpu.VMEM((chunks, rows, width), BF),
+                pltpu.VMEM((chunks, width, rows), BF),
+            ],
         ),
         out_shape=[
             jax.ShapeDtypeStruct((rows, columns), BF),
@@ -127,20 +135,25 @@
             bytes_accessed=8 * rows * columns + 4 * chunks * rows * width,
         ),
         name="attend",
-    )(where, seq_ids, block_ids, q_pre, cosine, sine, keys, values_t)
+    )(where, seq_ids, block_ids, q_pre, cosine, sine, *kv)
 
 
 def attend_back_body(
-    where, seq_ref, block_ref, rot_ref, grad_ref, att_ref, lse_ref, cos_ref, sin_ref, k_ref, kt_ref, v_ref,
+    where, seq_ref, block_ref, rot_ref, grad_ref, att_ref, lse_ref, cos_ref, sin_ref,
     *outs, factor, scale, width, rows_n,
 ):
-    qpg_ref, dk_ref, dv_ref, list_ref = outs[-4:]
+    pieces, outs = outs[: 2 * rows_n], outs[2 * rows_n :]
+    qpg_ref, dk_ref, dv_ref, list_ref, k_ref, kt_ref, v_ref = outs[-7:]
 
     @pl.when(pl.program_id(0) == 0)
     def _():
         list_visible(where, seq_ref, block_ref, list_ref, rows_n=rows_n, rows=rot_ref.shape[0])
-        dk_ref[...] = jnp.zeros_like(dk_ref) if len(outs) == 4 else outs[0][...]
-        dv_ref[...] = jnp.zeros_like(dv_ref) if len(outs) == 4 else outs[1][...]
+        dk_ref[...] = jnp.zeros_like(dk_ref) if len(outs) == 7 else outs[0][...]
+        dv_ref[...] = jnp.zeros_like(dv_ref) if len(outs) == 7 else outs[1][...]
+        for j, piece in enumerate(pieces):
+            k_ref[j] = piece[:, :width]
+            kt_ref[j] = piece[:, :width].T
+            v_ref[j] = piece[:, width:]
 
     cosine = cos_ref[...]
     sine = sin_ref[...]
@@ -177,11 +190,11 @@
         qpg_ref[:, cols] = (dq * cosine - pltpu.roll(dq, width // 2, 1) * sine).astype(BF)
 
 
-def attend_back(meta, rot, grad, att, lse, cosine, sine, keys, keys_t, values, width, rows_n, running=()):
+def attend_back(meta, rot, grad, att, lse, cosine, sine, kv, width, rows_n, running=()):
     where, seq_ids, block_ids = meta
     rows, columns = rot.shape
     heads = columns // width
-    chunks = keys.shape[0]
+    chunks = len(kv)
     span = HEADS_PER_STEP * width
     whole2 = lambda i, m: (0, 0)
     whole3 = lambda i, m: (0, 0, 0)
@@ -206,17 +219,20 @@
                 pl.BlockSpec((HEADS_PER_STEP, 1, rows), lambda i, m: (i, 0, 0)),
                 pl.BlockSpec((rows, width), whole2),
                 pl.BlockSpec((rows, width), whole2),
-                pl.BlockSpec((chunks, rows, width), whole3),
-                pl.BlockSpec((chunks, width, rows), whole3),
-                pl.BlockSpec((chunks, rows, width), whole3),
             ]
+            + [pl.BlockSpec((rows, 2 * width), whole2)] * chunks
             + [pl.BlockSpec((chunks, rows, width), whole3)] * len(running),
             out_specs=[
                 pl.BlockSpec((rows, span), by_head),
                 pl.BlockSpec((chunks, rows, width), whole3),
                 pl.BlockSpec((chunks, rows, width), whole3),
             ],
-            scratch_shapes=[pltpu.SMEM((chunks + 1,), jnp.int32)],
+            scratch_shapes=[
+                pltpu.SMEM((chunks + 1,), jnp.int32),
+                pltpu.VMEM((chunks, rows, width), BF),
+                pltpu.VMEM((chunks, width, rows), BF),
+                pltpu.VMEM((chunks, rows, width), BF),
+            ],
         ),
         out_shape=[
             jax.ShapeDtypeStruct((rows, columns), BF),
@@ -229,7 +245,7 @@
             bytes_accessed=8 * rows * columns + 12 * chunks * rows * width,
         ),
         name="attend_back",
-    )(where, seq_ids, block_ids, rot, grad, att, lse, cosine, sine, keys, keys_t, values, *running)
+    )(where, seq_ids, block_ids, rot, grad, att, lse, cosine, sine, *kv, *running)
 
 
 def feed_body(*refs, rows_n, parts, near, shared):
@@ -259,20 +275,23 @@
         )
 
     def w_copies(j, k):
-        target = (wg_ref, wu_ref, wd_ref)[j].at[k]
+        target = (wg_ref, wu_ref, wd_ref)[j]
         if k < near or not shared[j // 2]:
             whole = (close_in + far_in, close_down + far_down)[j // 2][k]
             whole = whole if j == 2 else whole.at[j]
-            return [pltpu.make_async_copy(whole, target, w_sem.at[j, k, 0])]
+            place = target.at[:, pl.ds(k * span, span)]
+            return [pltpu.make_async_copy(whole, place, w_sem.at[j, k, 0])]
         source = far_down[0] if j == 2 else far_in[0]
         copies = []
         for z in range(source.shape[0]):
             if j == 2:
                 size = source.shape[-2]
-                share, place = source.at[z, k - near], target.at[pl.ds(z * size, size)]
+                share = source.at[z, k - near]
+                place = target.at[pl.ds(z * size, size), pl.ds(k * span, span)]
             else:
                 size = source.shape[-1]
-                share, place = source.at[z, k - near, j], target.at[:, pl.ds(z * size, size)]
+                share = source.at[z, k - near, j]
+                place = target.at[:, pl.ds(k * span + z * size, size)]
             copies.append(pltpu.make_async_copy(share, place, w_sem.at[j, k, z]))
         return copies
 
@@ -318,16 +337,9 @@
             x_out(p).start()
             g_out(p).start()
 
-    def over_parts(left, right, dot):
-        total = None
-        for k in range(R):
-            value = dot(left[step, :, pl.ds(k * span, span)], right[k])
-            total = value if total is None else total + value
-        return total
-
-    gate = over_parts(x_ref, wg_ref, dot_nt)
-    up = over_parts(x_ref, wu_ref, dot_nt)
-    mixed_grad = over_parts(g_ref, wd_ref, dot_nt)
+    gate = dot_nt(x_ref[step], wg_ref[...])
+    up = dot_nt(x_ref[step], wu_ref[...])
+    mixed_grad = dot_nt(g_ref[step], wd_ref[...])
     sig = 1.0 / (1.0 + jnp.exp(-gate))
     silu = gate * sig
     act_ref[...] = (silu * up).astype(BF)
@@ -336,7 +348,9 @@
     gate_grad_ref[...] = gate_grad
     up_grad_ref[...] = up_grad
     for k in range(R):
-        back_refs[k][...] = (dot_nn(gate_grad, wg_ref[k]) + dot_nn(up_grad, wu_ref[k])).astype(BF)
+        here = slice(k * span, (k + 1) * span)
+        back = dot_nn(gate_grad, wg_ref[:, here]) + dot_nn(up_grad, wu_ref[:, here])
+        back_refs[k][...] = back.astype(BF)
 
     @pl.when(step == parts - 1)
     def _():
@@ -369,9 +383,9 @@
         scratch_shapes=[
             pltpu.VMEM((parts, tile, R * span), BF),
             pltpu.VMEM((parts, tile, R * span), BF),
-            pltpu.VMEM((R, hidden_n, span), BF),
-            pltpu.VMEM((R, hidden_n, span), BF),
-            pltpu.VMEM((R, hidden_n, span), BF),
+            pltpu.VMEM((hidden_n, R * span), BF),
+            pltpu.VMEM((hidden_n, R * span), BF),
+            pltpu.VMEM((hidden_n, R * span), BF),
             pltpu.SemaphoreType.DMA((parts, R)),
             pltpu.SemaphoreType.DMA((parts, R)),
             pltpu.SemaphoreType.DMA((3, R, slots)),
@@ -415,26 +429,25 @@
     )(*x, *grads)
 
 
-def down_weight_body(a0, a1, g0, g1, *outs):
+def down_weight_body(a0, a1, g0, g1, out_ref):
     total = (dot_tn(a0[...], g0[...]) + dot_tn(a1[...], g1[...])).astype(BF)
-    for k, out in enumerate(outs):
-
-        @pl.when(pl.program_id(0) == k)
-        def _(out=out):
-            out[...] = total
-
-
-def down_weight_grad(acts, grads, rows_n):
+    part = out_ref.shape[2]
+    for q in range(out_ref.shape[0]):
+        out_ref[q, 0] = total[q * part : (q + 1) * part]
+
+
+def down_weight_grad(acts, grads, rows_n, dp_n):
     tokens, features = grads[0].shape
     span = features // rows_n
     hidden_n = acts[0].shape[1]
+    part = hidden_n // dp_n
     return pl.pallas_call(
         down_weight_body,
         grid=(rows_n,),
         in_specs=[pl.BlockSpec((tokens, hidden_n), lambda k: (0, 0))] * 2
         + [pl.BlockSpec((tokens, span), lambda k: (0, k))] * 2,
-        out_specs=[pl.BlockSpec((hidden_n, span), lambda k: (0, 0))] * rows_n,
-        out_shape=[jax.ShapeDtypeStruct((hidden_n, span), BF)] * rows_n,
+        out_specs=pl.BlockSpec((dp_n, 1, part, span), lambda k: (0, k, 0, 0)),
+        out_shape=jax.ShapeDtypeStruct((dp_n, rows_n, part, span), BF),
         compiler_params=pltpu.CompilerParams(vmem_limit_bytes=48 << 20),
         cost_estimate=pl.CostEstimate(
             flops=4 * tokens * features * hidden_n,
@@ -445,31 +458,164 @@
     )(*acts, *grads)
 
 
-def cut_body(where, *refs, ks, rows_n):
+def late_weight_body(x0, x1, u0, u1, g0, g1, a0, a1, out_ref, *, rows_n):
+    planes, _, _, rows, share = out_ref.shape
+
+    @pl.when(pl.program_id(0) < rows_n)
+    def _():
+        total = (dot_tn(u0[...], x0[...]) + dot_tn(u1[...], x1[...])).astype(BF)
+        for q in range(planes):
+            out_ref[q, 0, 0] = total[:, q * share : (q + 1) * share]
+
+    @pl.when(pl.program_id(0) >= rows_n)
+    def _():
+        total = (dot_tn(a0[...], g0[...]) + dot_tn(a1[...], g1[...])).astype(BF)
+        part = rows // planes
+        for q in range(planes):
+            for j in range(planes):
+                out_ref[q, 0, 0, j * part : (j + 1) * part] = total[
+                    q * part : (q + 1) * part, j * share : (j + 1) * share
+                ]
+
+
+def late_weight_grads(x, ups, grads, acts, rows_n, dp_n):
+    tokens, features = x[0].shape
+    span = features // rows_n
+    hidden_n = ups[0].shape[1]
+    share = span // dp_n
+    whole = pl.BlockSpec((tokens, hidden_n), lambda i: (0, 0))
+    first = pl.BlockSpec((tokens, span), lambda i: (0, jnp.minimum(i, rows_n - 1)))
+    second = pl.BlockSpec((tokens, span), lambda i: (0, jnp.maximum(i - rows_n, 0)))
+    return pl.pallas_call(
+        functools.partial(late_weight_body, rows_n=rows_n),
+        grid=(2 * rows_n,),
+        in_specs=[first] * 2 + [whole] * 2 + [second] * 2 + [whole] * 2,
+        out_specs=pl.BlockSpec(
+            (dp_n, 1, 1, hidden_n, share), lambda i: (0, i // rows_n, i % rows_n, 0, 0)
+        ),
+        out_shape=jax.ShapeDtypeStruct((dp_n, 2, rows_n, hidden_n, share), BF),
+        compiler_params=pltpu.CompilerParams(vmem_limit_bytes=56 << 20),
+        cost_estimate=pl.CostEstimate(
+            flops=8 * tokens * features * hidden_n,
+            transcendentals=0,
+            bytes_accessed=8 * tokens * (features + hidden_n) + 4 * features * hidden_n,
+        ),
+        name="late_weights",
+    )(*x, *ups, *grads, *acts)
+
+
+def product_body(a0, a1, *refs, near):
+    half = len(refs) // 3
+    outs = refs[half:]
+    for k in range(half):
+
+        @pl.when(pl.program_id(0) == k)
+        def _(k=k):
+            weight = refs[k][...].reshape(a0.shape[1], outs[0].shape[1])
+            outs[2 * k][...] = dot_nn(a0[...], weight).astype(BF)
+            outs[2 * k + 1][...] = dot_nn(a1[...], weight).astype(BF)
+
+
+def down_products(acts, close_down, far_down, rows_n):
+    tokens, hidden_n = acts[0].shape
+    span = close_down[0].shape[1]
+    near = len(close_down)
+    act = pl.BlockSpec((tokens, hidden_n), lambda i: (0, 0))
+    ins, operands = [act] * 2, list(acts)
+    for k in range(rows_n):
+        if k < near or len(far_down) > 1:
+            ins.append(pl.BlockSpec((hidden_n, span), lambda i: (0, 0)))
+            operands.append(close_down[k] if k < near else far_down[k - near])
+        else:
+            planes, _, rows, _ = far_down[0].shape
+            ins.append(
+                pl.BlockSpec((planes, 1, rows, span), lambda i, k=k: (0, k - near, 0, 0))
+            )
+            operands.append(far_down[0])
+    out = pl.pallas_call(
+        functools.partial(product_body, near=near),
+        grid=(rows_n,),
+        in_specs=ins,
+        out_specs=[pl.BlockSpec((tokens, span), lambda i: (0, 0))] * (2 * rows_n),
+        out_shape=[jax.ShapeDtypeStruct((tokens, span), BF)] * (2 * rows_n),
+        compiler_params=pltpu.CompilerParams(vmem_limit_bytes=56 << 20),
+        name="down_products",
+    )(*operands)
+    return {(a, k): out[2 * k + a] for k in range(rows_n) for a in range(2)}
+
+
+def finish_body(where, *refs, rows_n, dp_n):
+    pieces = refs[:rows_n]
+    gate_ref, up_ref, down_ref = refs[rows_n:]
+    part = pieces[0].shape[1] // dp_n
+    share = pieces[0].shape[2]
+    for k in range(rows_n):
+        sender = where[0] ^ k
+        for i in range(rows_n):
+
+            @pl.when(sender == i)
+            def _(k=k, i=i):
+                for q in range(dp_n):
+                    rows = slice(q * part, (q + 1) * part)
+                    here = slice((q * rows_n + i) * part, (q * rows_n + i + 1) * part)
+                    gate_ref[:, here] = pieces[k][0, rows].astype(F32).T
+                    up_ref[:, here] = pieces[k][1, rows].astype(F32).T
+                    down_ref[i * part : (i + 1) * part, q * share : (q + 1) * share] = pieces[k][
+                        2, rows
+                    ].astype(F32)
+
+
+def finish_weight_grads(where, pieces, rows_n, dp_n):
+    _, hidden_n, share = pieces[0].shape
+    spec = pl.BlockSpec((3, hidden_n, share), lambda i, w: (0, 0, 0))
+    shapes = [(share, rows_n * hidden_n)] * 2 + [(hidden_n, dp_n * share)]
+    return pl.pallas_call(
+        functools.partial(finish_body, rows_n=rows_n, dp_n=dp_n),
+        grid_spec=pltpu.PrefetchScalarGridSpec(
+            num_scalar_prefetch=1,
+            grid=(1,),
+            in_specs=[spec] * rows_n,
+            out_specs=[pl.BlockSpec(shape, lambda i, w: (0, 0)) for shape in shapes],
+        ),
+        out_shape=[jax.ShapeDtypeStruct(shape, F32) for shape in shapes],
+        compiler_params=pltpu.CompilerParams(vmem_limit_bytes=40 << 20),
+        name="finish_weights",
+    )(where, *pieces)
+
+
+def cut_body(where, *refs, ks, rows_n, dp_n):
     gate, up = refs[:2]
-    down_in = refs[2 : 2 + len(ks)]
-    outs = refs[2 + len(ks) :]
-    hidden_n = gate.shape[1] // rows_n
+    outs = refs[len(refs) - 2 * len(ks) :]
+    down_in = refs[2 : len(refs) - 2 * len(ks)]
+    part = gate.shape[1] // (dp_n * rows_n)
     for n, k in enumerate(ks):
         slot = where[0] ^ k
         for i in range(rows_n):
 
             @pl.when(slot == i)
             def _(n=n, i=i):
-                here = slice(i * hidden_n, (i + 1) * hidden_n)
-                outs[2 * n][0] = gate[:, here].T
-                outs[2 * n][1] = up[:, here].T
-
-        outs[2 * n + 1][...] = down_in[n][...]
-
-
-def cut_weights(where, w_gate, w_up, w_down, ks, rows_n, rows_in, rows_down):
+                for q in range(dp_n):
+                    here = slice((q * rows_n + i) * part, (q * rows_n + i + 1) * part)
+                    there = slice(q * part, (q + 1) * part)
+                    outs[2 * n][0, there] = gate[:, here].T
+                    outs[2 * n][1, there] = up[:, here].T
+                    if len(down_in) < len(ks):
+                        outs[2 * n + 1][there] = down_in[0][here]
+
+        if len(down_in) == len(ks):
+            outs[2 * n + 1][...] = down_in[n][...]
+
+
+def cut_weights(where, w_gate, w_up, w_down, ks, rows_n, dp_n, rows_in, rows_down):
     hidden_n = w_gate.shape[1] // rows_n
+    part = hidden_n // dp_n
     span = w_down.shape[1]
-    per = hidden_n // rows_down
     ins = [pl.BlockSpec((rows_in, w_gate.shape[1]), lambda i, w: (w[1], 0))] * 2
-    for k in ks:
-        ins.append(pl.BlockSpec((rows_down, span), lambda i, w, k=k: ((w[0] ^ k) * per + w[2], 0)))
+    if rows_down == part:
+        for k in ks:
+            ins.append(pl.BlockSpec((part, span), lambda i, w, k=k: (w[2] * rows_n + (w[0] ^ k), 0)))
+    else:
+        ins.append(pl.BlockSpec(w_down.shape, lambda i, w: (0, 0)))
     out_specs, out_shape = [], []
     for _ in ks:
         out_specs += [
@@ -481,15 +627,30 @@
             jax.ShapeDtypeStruct((rows_down, span), BF),
         ]
     out = pl.pallas_call(
-        functools.partial(cut_body, ks=ks, rows_n=rows_n),
+        functools.partial(cut_body, ks=ks, rows_n=rows_n, dp_n=dp_n),
         grid_spec=pltpu.PrefetchScalarGridSpec(
             num_scalar_prefetch=1, grid=(1,), in_specs=ins, out_specs=out_specs
         ),
         out_shape=out_shape,
         compiler_params=pltpu.CompilerParams(vmem_limit_bytes=40 << 20),
         name="cut_weights",
-    )(where, w_gate, w_up, *([w_down] * len(ks)))
+    )(where, w_gate, w_up, *([w_down] * (len(ins) - 2)))
     return out[0::2], out[1::2]
+
+
+def cut_plain(row, w_gate, w_up, w_down, ks, rows_n, dp_n):
+    part = w_gate.shape[1] // (dp_n * rows_n)
+    cut_in, cut_down = [], []
+    for k in ks:
+        starts = [(q * rows_n + (row ^ k)) * part for q in range(dp_n)]
+        both = []
+        for w in (w_gate.T, w_up.T):
+            both.append(jnp.concatenate([lax.dynamic_slice_in_dim(w, at, part, 0) for at in starts]))
+        cut_in.append(jnp.stack(both))
+        cut_down.append(
+            jnp.concatenate([lax.dynamic_slice_in_dim(w_down, at, part, 0) for at in starts])
+        )
+    return cut_in, cut_down
 
 
 def tie(value, *others):
@@ -533,6 +694,13 @@
     width = w_kv.shape[1] // 2
     dp_n = lax.axis_size("dp")
 
+    def tf(flag, value, *others):
+        return tie(value, *others) if FL.get(flag, 0) else value
+
+    def tc(flag, value, *options):
+        k = FL.get(flag, 0)
+        return tie(value, options[k - 1]) if k else value
+
     def swap_row(a, bit):
         return lax.ppermute(a, "row", [(i, i ^ bit) for i in range(R)])
 
@@ -567,10 +735,16 @@
             a = total.astype(BF)
         return total
 
-    def gather_row(a):
-        for bit in reversed(bits):
+    def gather_outer(a):
+        for bit in reversed(bits[1:]):
             a = jnp.concatenate([a, swap_row(a, bit)], axis=0)
         return a
+
+    def gather_core(a):
+        return jnp.concatenate([a, swap_row(a, 1)], axis=0)
+
+    def gather_row(a):
+        return gather_core(gather_outer(a))
 
     def spread(pieces, bit):
         out = dict(pieces)
@@ -600,13 +774,14 @@
         total = a.astype(F32) + b.astype(F32)
         return total if wide else total.astype(BF)
 
-    def reduce_plane(blocks, after=()):
+    def reduce_plane(blocks, after=((), ()), then=()):
         moved = {(a, k): swap_row(blocks[(a, k ^ 1)], 1) for a in (1, 0) for k in range(0, R, 2)}
-        outs = []
+        outs, firsts, seconds = [], [], []
         for part in range(2):
             here = slice(part * half, (part + 1) * half)
             cur = {key: add(blocks[key][here], value[here]) for key, value in moved.items()}
-            cur = tie(cur, after)
+            firsts.append(list(cur.values()))
+            cur = tie(cur, after[part])
 
             def by_col(cur, last):
                 return {
@@ -625,11 +800,15 @@
                 return cur
 
             if part == 0:
-                cur = by_rows(by_col(cur, False), True)
+                cur = by_col(cur, False)
+                seconds.append(list(cur.values()))
+                cur = by_rows(tie(cur, then), True)
             else:
-                cur = by_col(by_rows(cur, False), True)
+                cur = by_rows(cur, False)
+                seconds.append(list(cur.values()))
+                cur = by_col(tie(cur, then), True)
             outs.append(cur[(0, 0)])
-        return jnp.concatenate(outs, axis=0)
+        return jnp.concatenate(outs, axis=0), firsts, seconds
 
     residual = tokens.astype(F32)
     scale_one = lax.rsqrt(psum_row(jnp.sum(residual * residual, axis=1)) / D + EPS)
@@ -646,23 +825,18 @@
     near = min(2, R)
     hidden_n = w_gate.shape[1] // R
     shared = (dslice % (128 * dp_n) == 0, hidden_n % (16 * dp_n) == 0)
+    shared = (all(shared), all(shared))
     rows_in = dslice // dp_n if shared[0] else dslice
     rows_down = hidden_n // dp_n if shared[1] else hidden_n
 
     shares = jnp.stack([row, z if shared[0] else 0 * z, z if shared[1] else 0 * z])
     shares = tie(shares, kv_pre)
     far_ks = tuple(range(near, R))
-    cut_in, cut_down = cut_weights(shares, w_gate, w_up, w_down, far_ks, R, rows_in, rows_down)
-    far_in = [swap_row(a, k) for a, k in zip(cut_in, far_ks)]
-    cut_down = tie(cut_down, query_near)
-    far_down = [swap_row(a, k) for a, k in zip(cut_down, far_ks)]
-    if shared[0]:
-        far_in = [jnp.stack(far_in)]
-    w_out_far = swap_col(tie(w_out, w_query_far))
-    query_near = tie(query_near, far_in, w_out_far)
-    if shared[0]:
-        far_in = [lax.all_gather(far_in[0], "dp", axis=0)]
-
+    part = hidden_n // dp_n
+    if part % 16 == 0:
+        cut_in, cut_down = cut_weights(shares, w_gate, w_up, w_down, far_ks, R, dp_n, rows_in, rows_down)
+    else:
+        cut_in, cut_down = cut_plain(row, w_gate, w_up, w_down, far_ks, R, dp_n)
     half_width = width // 2
     frequency = ROPE_BASE ** (-2.0 * jnp.arange(half_width, dtype=F32) / width)
     own_positions = lax.dynamic_slice_in_dim(positions, own * B, B)
@@ -678,39 +852,66 @@
     kv_pieces = spread_col({(0, 0): kv_own})
     for bit in reversed(bits):
         kv_pieces = spread(kv_pieces, bit)
-    kv_all = jnp.stack([kv_pieces[(a, k)] for a in range(2) for k in range(R)])
-    keys = kv_all[:, :, :width]
-    values = kv_all[:, :, width:]
-    keys_t = keys.transpose(0, 2, 1)
-    values_t = values.transpose(0, 2, 1)
-
+    kv_all = [kv_pieces[(a, k)] for a in range(2) for k in range(R)]
     meta = (jnp.stack([row, col]), seq_ids, block_ids)
-    cut_in, cut_down = cut_weights(
-        shares * jnp.array([1, 0, 0], jnp.int32), w_gate, w_up, w_down, tuple(range(near)), R, dslice, hidden_n
-    )
+    far_in = [swap_row(a, k) for a, k in zip(tf("f11", cut_in, kv_all), far_ks)]
+    far_cut_down = cut_down
+    if shared[0]:
+        far_in = [jnp.stack(far_in)]
+    w_out_far = swap_col(tc("f13", w_out, w_query_far, query_near, kv_pre))
+    query_near = tf("f0", query_near, w_out_far)
+    query_near = tf("f1", query_near, far_in)
+    close_ks = tuple(range(near))
+    if part % 16 == 0:
+        shares = shares * jnp.array([1, 0, 0], jnp.int32)
+        cut_in, cut_down = cut_weights(shares, w_gate, w_up, w_down, close_ks, R, dp_n, dslice, hidden_n)
+    else:
+        cut_in, cut_down = cut_plain(row, w_gate, w_up, w_down, close_ks, R, dp_n)
     close_in = [swap_row(a, k) if k else a for k, a in enumerate(cut_in)]
     close_down = [swap_row(a, k) if k else a for k, a in enumerate(cut_down)]
-    att_near, rot_near, lse_near = attend(meta, query_near, cosine, sine, keys, values_t, width, R)
+    query_near_raw = query_near
     down_grad = grad_output.astype(BF)
-    grad_pieces = {(0, 0): tie(down_grad, query_near)}
-    for bit in reversed(bits[1:]):
-        grad_pieces = spread(grad_pieces, bit)
+    part_qfar = dot_nn(ordered_in, w_query_far).astype(BF)
+    if FL.get("f5", 0) < 3:
+        grad_pieces = {(0, 0): tc("f5", down_grad, kv_pre, query_near)}
+        for bit in reversed(bits[1:]):
+            grad_pieces = spread(grad_pieces, bit)
+        query_near = tf("f15", query_near, grad_pieces[(0, bits[-1])])
+    att_near, rot_near, lse_near = attend(meta, query_near, cosine, sine, kv_all, width, R)
+    if FL.get("f5", 0) >= 3:
+        grad_pieces = {(0, 0): tie(down_grad, att_near)}
+        for bit in reversed(bits[1:]):
+            grad_pieces = spread(grad_pieces, bit)
     grad_rows = dict(grad_pieces)
-    grad_pieces[(1, 0)] = swap_col(tie(down_grad, w_query_far))
-    query_far = reduce_row(
-        dot_nn(ordered_in, w_query_far), send_after=query_near, use_after=(att_near, close_in)
-    )
-    query_far = tie(query_far, dict(grad_pieces)) * own_scale
     for (a, k), value in grad_rows.items():
         if k:
             grad_pieces[(1, k)] = swap_col(value)
-    att_far, rot_far, lse_far = attend(meta, query_far, cosine, sine, keys, values_t, width, R)
-
-    far_down = tie(far_down, att_near)
+        else:
+            grad_pieces[(1, k)] = swap_col(tc("f12", down_grad, w_query_far, query_near_raw, w_out_far, att_near))
+    query_far = reduce_row(
+        part_qfar,
+        send_after=query_near_raw if FL.get("f9", 0) else (),
+        use_after=(att_near, close_in),
+    )
+    query_far = tf("f2", query_far, grad_pieces[(1, 0)])
+    query_far = tf("f3", query_far, far_in)
+    query_far = tf("f4", query_far, w_out_far)
+    query_far = tf("f8", query_far, grad_rows) * own_scale
+    if shared[0]:
+        far_in = [lax.all_gather(far_in[0], "dp", axis=0)]
+    near_outer = gather_outer(att_near)
+    query_far = tf("f16", query_far, near_outer)
+    att_far, rot_far, lse_far = attend(meta, query_far, cosine, sine, kv_all, width, R)
+    far_cut_down = tc("f10", far_cut_down, query_near_raw, att_near, att_far, near_outer)
+    far_down = [swap_row(a, k) for a, k in zip(far_cut_down, far_ks)]
     if shared[1]:
         far_down = [lax.all_gather(jnp.stack(far_down), "dp", axis=0)]
-    all_near = gather_row(att_near)
-    all_far = tie(gather_row(att_far), grad_pieces)
+
+    all_near = gather_core(near_outer)
+    far_outer = gather_outer(att_far)
+    far_outer = tf("f6", far_outer, grad_rows)
+    far_outer = tf("f17", far_outer, grad_pieces)
+    all_far = gather_core(far_outer)
     hidden = residual + from_order(dot_nn(all_near, w_out) + dot_nn(all_far, w_out_far))
 
     def exchange(parts):
@@ -718,8 +919,8 @@
 
     scale_two = lax.rsqrt(psum_row(jnp.sum(hidden * hidden, axis=1)) / D + EPS)[:, None]
     normed_two = (hidden * scale_two * norm2_gain[None, :]).astype(BF)
-    normed_pieces, came = gather_plane(normed_two)
-    grad_pieces = spread(tie(grad_pieces, came), 1)
+    normed_pieces, came = gather_plane(tf("f7", normed_two, grad_pieces))
+    grad_pieces = spread(tf("f14", grad_pieces, came), 1)
 
     fed = {}
     backs = {}
@@ -738,31 +939,33 @@
             backs[(a, k)] = fed[a][3 + k]
     acts, gate_grads, up_grads = ([fed[a][j] for a in range(2)] for j in range(3))
     normed_halves, grad_halves = ([fed[a][3 + R + j] for a in range(2)] for j in range(2))
-    normed2_grad = reduce_plane(backs)
-
-    def rows_of_down(k):
-        if k < near:
-            return close_down[k]
-        if shared[1]:
-            return far_down[0][:, k - near].reshape(hidden_n, dslice)
-        return far_down[k - near]
-
-    def ff_input_place(piece):
-        moved = jnp.stack(exchange([piece[k] for k in range(R)]))
-        ordered = jnp.concatenate(
-            [lax.dynamic_index_in_dim(moved, row ^ s, 0, keepdims=False) for s in range(R)], axis=0
-        )
-        return ordered.astype(F32).T[None]
+    normed2_grad, firsts, seconds = reduce_plane(backs)
+
+    def place(pieces):
+        moved = jnp.stack(exchange([jnp.stack([p[k] for p in pieces]) for k in range(R)]))
+        ordered = [lax.dynamic_index_in_dim(moved, row ^ s, 0, keepdims=False) for s in range(R)]
+        return [jnp.stack([o[n] for o in ordered]) for n in range(len(pieces))]
+
+    def ff_input_place(rows):
+        rows = rows.reshape(R, dp_n, part, -1).transpose(1, 0, 2, 3)
+        return rows.reshape(R * hidden_n, -1).astype(F32).T
 
     def over_dp(local):
         return lax.psum_scatter(local, "dp", scatter_dimension=0, tiled=True)
 
     gate_local = feed_weight_grad(normed_halves, gate_grads, R, dp_n)
-    up_local = feed_weight_grad(normed_halves, up_grads, R, dp_n)
     gate_piece = over_dp(gate_local)
-    up_piece = over_dp(up_local)
-    down_local = down_weight_grad(acts, grad_halves, R)
-    normed2_grad = tie(normed2_grad, gate_local, up_local, down_local)
+    if shared[1]:
+        late = late_weight_grads(
+            normed_halves, tf("b1", tf("b0", tie(up_grads, gate_local), firsts), seconds), grad_halves, acts, R, dp_n
+        )
+        late_piece = over_dp(tie(late, gate_local))
+        up_piece, down_piece = late_piece[0, 0], late_piece[0, 1]
+        normed2_grad = tie(normed2_grad, gate_local, late)
+    else:
+        late_piece = gate_piece
+        up_piece = over_dp(feed_weight_grad(normed_halves, up_grads, R, dp_n))[0]
+        down_piece = over_dp(down_weight_grad(acts, grad_halves, R, dp_n))[0]
 
     weighted = normed2_grad * norm2_gain[None, :]
     inner_two = psum_row(jnp.sum(weighted * hidden, axis=1))[:, None]
@@ -771,27 +974,78 @@
     )
     gain_two = jnp.sum(normed2_grad * hidden * scale_two, axis=0)
     branch_ordered = to_order(hidden_grad.astype(BF))
-    late_acts = tie(acts, hidden_grad)
-    products = {
-        (a, k): dot_nn(late_acts[a], rows_of_down(k)).astype(BF) for a in range(2) for k in range(R)
-    }
-    att_grad_far = reduce_row(dot_nt(branch_ordered, w_out_far), use_after=products).astype(BF)
-    grad_out_far = dot_tn(all_far, branch_ordered).astype(BF)
-    grad_out_came = swap_col(grad_out_far)
-    att_grad_far = tie(att_grad_far, grad_out_far)
+    part_far = dot_nt(branch_ordered, w_out_far).astype(BF)
+    part_near = dot_nt(branch_ordered, w_out).astype(BF)
+    prod_dep = FL.get("b5", 0)
+    branch_late, late_acts = branch_ordered, acts
+
+    def make_products():
+        return down_products(late_acts, close_down, far_down, R)
+
+    if prod_dep < 2:
+        late_acts = tie(acts, hidden_grad) if prod_dep == 0 else tie(acts, part_far, part_near)
+        products = make_products()
+    b6 = FL.get("b6", 0) if prod_dep < 2 else 0
+    att_grad_far = reduce_row(part_far, use_after=products if b6 == 1 else ()).astype(BF)
+    att_grad_near = reduce_row(
+        part_near, send_after=att_grad_far if FL.get("b25", 0) else (), use_after=products if b6 == 2 else ()
+    ).astype(BF)
+    gout_early = FL.get("b26", 0)
+    if gout_early:
+        grad_out_far = dot_tn(all_far, branch_late).astype(BF)
+        grad_out_came = swap_col(grad_out_far)
+        grad_out_near = dot_tn(all_near, branch_late)
+        att_grad_far = tf("b27", att_grad_far, grad_out_far, grad_out_near)
+        att_grad_far = tf("b4", att_grad_far, grad_out_came)
+    att_grad_far = tf("b2", att_grad_far, gate_piece)
+    att_grad_far = tf("b3", att_grad_far, att_grad_near)
 
     qpg_far, dk, dv = attend_back(
-        meta, rot_far, att_grad_far, att_far, lse_far, cosine, sine, keys, keys_t, values, width, R
+        meta, rot_far, att_grad_far, att_far, lse_far, cosine, sine, kv_all, width, R
     )
-    att_grad_near = reduce_row(
-        dot_nt(branch_ordered, w_out), send_after=att_grad_far, use_after=(qpg_far, grad_out_came)
-    ).astype(BF)
+    if not gout_early:
+        branch_late = tie(branch_ordered, qpg_far)
+        grad_out_far = dot_tn(all_far, branch_late).astype(BF)
+        grad_out_came = swap_col(grad_out_far)
+        grad_out_near = dot_tn(all_near, branch_late)
+    if prod_dep == 2:
+        late_acts = tie(acts, qpg_far)
+        products = make_products()
+    scale_col = scale_one[:, None]
+    normed_ordered = to_order((residual * scale_col * norm1_gain[None, :]).astype(BF))
+    qpg_far_outer = gather_outer(tf("b28", qpg_far, grad_out_far))
+    qpg_far_all = gather_core(qpg_far_outer)
+    qpg_far_used = tf("b8", qpg_far_all, grad_out_near)
+    if prod_dep < 3:
+        qpg_far_used = tf("b29", qpg_far_used, products)
+    grad_query_far = dot_tn(normed_ordered, qpg_far_used).astype(BF)
+    grad_query_came = swap_col(grad_query_far)
+    att_grad_near = tf("b30", att_grad_near, qpg_far_outer)
+    att_grad_near = tf("b7", att_grad_near, grad_query_far)
+    att_grad_near = tf("b31", att_grad_near, grad_out_came)
     qpg_near, dk, dv = attend_back(
-        meta, rot_near, att_grad_near, att_near, lse_near, cosine, sine, keys, keys_t, values, width, R,
+        meta, rot_near, att_grad_near, att_near, lse_near, cosine, sine, kv_all, width, R,
         (dk, dv),
     )
-    grad_out_local = add(dot_tn(all_near, branch_ordered), grad_out_came)
-    grad_out = over_dp(tie(grad_out_local, gate_piece, up_piece))
+    if prod_dep == 3:
+        late_acts = tie(acts, qpg_near)
+        products = make_products()
+    grad_out_local = add(grad_out_near, tc("b24", grad_out_came, qpg_far, qpg_near))
+    grad_out = over_dp(tc("b18", grad_out_local, gate_piece, late_piece))
+    qpg_near_outer = gather_outer(tf("b32", qpg_near, grad_out_local))
+    qpg_near_all = gather_core(qpg_near_outer)
+    qpg_near_used = tf("b19", tie(qpg_near_all, grad_query_came), late_piece)
+    grad_query_near = dot_tn(normed_ordered, qpg_near_used)
+    grad_query_local = add(grad_query_near, grad_query_came)
+    opts = (qpg_far, qpg_near, qpg_near_outer, grad_query_came, grad_query_local)
+    pick_opt = lambda k: () if not k else opts[k - 1]
+    down_sum, _, seconds_out = reduce_plane(
+        products,
+        after=(pick_opt(FL.get("b13", 0)), pick_opt(FL.get("b14", 0))),
+        then=pick_opt(FL.get("b15", 0)),
+    )
+    output = hidden + down_sum
+    dk, dv = tc("b9", (dk, dv), qpg_near_outer, grad_out_local, grad_query_came, grad_query_local)
 
     dkv = jnp.concatenate([dk * width**-0.5, dv], axis=2).astype(BF)
     cur = {(a, k): dkv[a * R + k] for a in range(2) for k in range(R)}
@@ -808,26 +1062,19 @@
         [dk_own * cosine - dk_turned * sine, dkv_own[:, width:]], axis=1
     ).astype(BF)
 
-    down_sent = [down_local[0]]
-    for k in range(1, R):
-        down_sent.append(swap_row(tie(down_local[k], normed2_grad if k < 3 else att_grad_far), k))
-    down_moved = jnp.stack(down_sent)
-    down_ordered = jnp.concatenate(
-        [lax.dynamic_index_in_dim(down_moved, row ^ s, 0, keepdims=False) for s in range(R)], axis=0
-    )
-    grad_down = over_dp(tie(down_ordered, grad_out))
-    output = hidden + reduce_plane(products, after=qpg_near)
-
-    scale_col = scale_one[:, None]
-    normed_ordered = to_order((residual * scale_col * norm1_gain[None, :]).astype(BF))
-    qpg_far_all = gather_row(qpg_far)
-    grad_query_far = dot_tn(normed_ordered, qpg_far_all).astype(BF)
-    grad_query_came = swap_col(grad_query_far)
-    qpg_near_all = tie(gather_row(qpg_near), grad_query_far)
+
+    pieces = tc("b17", (gate_piece[0], up_piece, down_piece), qpg_near, grad_query_local, qpg_near_outer)
+    moved = exchange([jnp.stack([p[k] for p in pieces]) for k in range(R)]) if shared[1] else ()
+    kvg_own = tf("b36", kvg_own, moved)
+    kvg_own = tc("b16", kvg_own, qpg_near_outer, grad_query_came, grad_query_local)
     kvg_all = gather_row(kvg_own)
     normed1_grad = from_order(
         dot_nt(qpg_far_all, w_query_far) + dot_nt(qpg_near_all, w_query) + dot_nt(kvg_all, w_kv)
     )
+    normed1_grad = tf("b22", normed1_grad, grad_out)
+    normed1_grad = tf("b33", normed1_grad, moved)
+    normed1_grad = tf("b34", normed1_grad, grad_query_local)
+    normed1_grad = tf("b23", normed1_grad, output)
     weighted_one = normed1_grad * norm1_gain[None, :]
     inner_one = psum_row(jnp.sum(weighted_one * residual, axis=1))[:, None]
     input_grad = hidden_grad + (
@@ -835,36 +1082,42 @@
     )
     gain_one = jnp.sum(normed1_grad * residual * scale_col, axis=0)
 
-    grad_query_local = add(dot_tn(normed_ordered, qpg_near_all), grad_query_came)
-    grad_query = over_dp(tie(grad_query_local, grad_down, output))
-
-    def small_over_dp_col(local):
-        rest = local.shape[0] // (dp_n * 2)
-        local = local.reshape(dp_n, 2, rest, local.shape[1])
-        mine = lax.dynamic_index_in_dim(local, col, 1, keepdims=False)
-        other = lax.dynamic_index_in_dim(local, 1 - col, 1, keepdims=False).astype(BF)
-        both = mine + swap_col(other).astype(F32)
-        total = lax.dynamic_index_in_dim(both, z, 0, keepdims=False)
-        for j in range(1, dp_n):
-            share = lax.dynamic_index_in_dim(both, z ^ j, 0, keepdims=False).astype(BF)
-            share = lax.ppermute(share, "dp", [(i, i ^ j) for i in range(dp_n)])
-            total = total + share.astype(F32)
-        return total
-
-    grad_kv = small_over_dp_col(dot_tn(normed_ordered, kvg_all))
-    gains = small_over_dp_col(jnp.stack([gain_one, gain_two], axis=1))
+    grad_query = over_dp(tf("b20", grad_query_local, grad_out))
+    if shared[1]:
+        grad_gate, grad_up, grad_down = finish_weight_grads(meta[0], moved, R, dp_n)
+    else:
+        gate_rows, up_rows = place(pieces[:2])
+        grad_gate, grad_up = ff_input_place(gate_rows), ff_input_place(up_rows)
+        grad_down = place(pieces[2:])[0].reshape(hidden_n, dslice).astype(F32)
+
+    rest = dslice // (2 * dp_n)
+    gains = jnp.concatenate(
+        [g.reshape(dp_n, 2, 1, rest) for g in (gain_one, gain_two)]
+        + [jnp.zeros((dp_n, 2, 1, 2 * width - 2 * rest), F32)],
+        axis=3,
+    )
+    local = dot_tn(normed_ordered, kvg_all).reshape(dp_n, 2, rest, 2 * width)
+    local = jnp.concatenate([local, gains], axis=2)
+    mine = lax.dynamic_index_in_dim(local, col, 1, keepdims=False)
+    other = lax.dynamic_index_in_dim(local, 1 - col, 1, keepdims=False).astype(BF)
+    both = mine + swap_col(other).astype(F32)
+    small = lax.dynamic_index_in_dim(both, z, 0, keepdims=False)
+    for j in range(1, dp_n):
+        share = lax.dynamic_index_in_dim(both, z ^ j, 0, keepdims=False).astype(BF)
+        share = lax.ppermute(share, "dp", [(i, i ^ j) for i in range(dp_n)])
+        small = small + share.astype(F32)
 
     return (
         output,
         input_grad,
         grad_query.astype(F32)[None],
-        grad_kv[None],
+        small[None, :rest],
         grad_out.astype(F32)[None],
-        ff_input_place(gate_piece[0]),
-        ff_input_place(up_piece[0]),
-        grad_down.astype(F32)[None],
-        gains[:, 0][None, :],
-        gains[:, 1][None, :],
+        grad_gate[None],
+        grad_up[None],
+        grad_down[None],
+        small[rest:, :rest],
+        small[rest:, rest : 2 * rest],
     )
 
 

time: 608 us -> 580 us (0.954)
  starting transfers between devices: 97.2 us -> 71.1 us
  Pallas kernels: 107 us -> 129 us
  other arithmetic: 80.7 us -> 69 us
  matrix products: 41.3 us -> 32.2 us
    ppermute x85 -> x79, waiting for transfers between devices: 109 us -> 142 us  [swap_row(): return lax.ppermute(a, 'row', [(i, i ^ bit) for i in range(R)])]
    pallas_call x3 -> x5, Pallas kernels: 12 us -> 43 us  [the longest x1 19.5 us: late_weight_grads(): pl.pallas_call(functools.partial(late_weight_body, rows_n=rows_n), grid=(...]
    ppermute x19 -> x18, waiting for transfers between devices: 87.2 us -> 68.8 us  [swap_col(): return lax.ppermute(a, 'col', [(0, 1), (1, 0)])]
    ppermute x85 -> x79, starting transfers between devices: 55.7 us -> 40.1 us  [swap_row(): return lax.ppermute(a, 'row', [(i, i ^ bit) for i in range(R)])]
    reduce_scatter x5 -> x4, waiting for transfers between devices: 13.2 us -> 0.01 us  [over_dp(): return lax.psum_scatter(local, 'dp', scatter_dimension=0, tiled=True)]
    concatenate x9 -> x7, other arithmetic: 12 us -> 1.53 us  [the longest x4 1.2 us: gather_outer(): a = jnp.concatenate([a, swap_row(a, bit)], axis=0)]
    dot_general x13 -> x5, matrix products: 18.8 us -> 9.25 us  [dot_nn(): lax.dot_general(a, b, (((1,), (0,)), ((), ())), preferred_element_type=F32)]
    pallas_call x2 -> x1, Pallas kernels: 18.9 us -> 9.32 us  [feed_weight_grad(): pl.pallas_call(feed_weight_body, grid=(rows_n,), in_specs=[pl.BlockSpec((...]
  transfers between devices with their start and end apart: 117 -> 106, of which waited for: 42 -> 39; matrix products, arithmetic and copies ran while one was open for 24% -> 20% of each run, Pallas kernels for 12% -> 23%
where the time goes in v3:
time: 580 us; the launch traced here: 570 us
  waiting for transfers between devices  215 us (37%)
  Pallas kernels  129 us (22%)
  starting transfers between devices  71.1 us (12%)
  other arithmetic  69 us (12%)
  local copies, waits for them, and re-layouts  37.4 us (6%)
  matrix products  32.2 us (6%)
  between operations  16.2 us (3%)
    ppermute x79, waiting for transfers between devices, swap_row(): return lax.ppermute(a, 'row', [(i, i ^ bit) for i in range(R)])  142 us
    ppermute x18, waiting for transfers between devices, swap_col(): return lax.ppermute(a, 'col', [(0, 1), (1, 0)])  68.8 us
    pallas_call x2, Pallas kernels, feed(): pl.pallas_call(functools.partial(feed_body, rows_n=R, parts=parts, near=n...  51.5 us
    ppermute x79, starting transfers between devices, swap_row(): return lax.ppermute(a, 'row', [(i, i ^ bit) for i in range(R)])  40.1 us
    ppermute x18, starting transfers between devices, swap_col(): return lax.ppermute(a, 'col', [(0, 1), (1, 0)])  24.8 us
    unnamed x233, local copies, waits for them, and re-layouts  20.5 us
    pallas_call x1, Pallas kernels, late_weight_grads(): pl.pallas_call(functools.partial(late_weight_body, rows_n=rows_n), grid=(...  19.5 us
    convert_element_type x19, other arithmetic, add(): return total if wide else total.astype(BF)  16.3 us
  transfers between devices with their start and end apart: 106, of which 39 were waited for; matrix products, arithmetic and copies ran while one was open for 20% of the time, Pallas kernels for 23%

profile of v3, /device:TPU:0, one launch (start us, length us, event | category | flops | bytes accessed | tf_op | source)
XLA Modules:
  0.0 570.0 jit_solution(6595560992129218612)
XLA Ops:
  9.3 2.6 collective-permute-start.4
  16.9 2.6 fusion.3
  27.0 2.8 convert_element_type.509.refs_8_
  38.2 2.6 convolution_convert_fusion.2
  47.3 4.2 cut_weights.3
  58.1 7.5 %collective-permute-done.1 = bf16[256,1024]{1,0:T(8,128)(2,1)} collective-permute-done((bf16[256,1024]{1,0:T(8,128)(2,1)}, bf16[256,1024]{1,0:T(8,128)(2,1)}, u32[]{:S(2)}, u32[]{:S(2)}) %collective-permute-start.1) | collective-permute-done | bytes 524320 | tf_op jit(solution)/shard_map/ppermute | solution.py:705
  72.5 12.8 %collective-permute-done.11.refs_2_.outs_2_ = bf16[256,256]{1,0:T(8,128)(2,1)S(1)} collective-permute-done((bf16[256,256]{1,0:T(8,128)(2,1)S(1)}, bf16[256,256]{1,0:T(8,128)(2,1)S(1)}, u32[]{:S(2)}, u32[]{:S(2)}) %collective-permute-start.11) | collective-permute-done | bytes 131104 | tf_op jit(solution)/shard_map/ppermute | solution.py:705
  85.6 4.7 collective-permute-done.15.refs_6_.outs_6_
  92.6 5.4 attend.2
  103.0 5.5 attend.3
  108.9 20.2 %collective-permute-done.17 = bf16[256,1024]{1,0:T(8,128)(2,1)S(1)} collective-permute-done((bf16[256,1024]{1,0:T(8,128)(2,1)}, bf16[256,1024]{1,0:T(8,128)(2,1)S(1)}, u32[]{:S(2)}, u32[]{:S(2)}) %collective-permute-start.17) | collective-permute-done | bytes 524320 | tf_op jit(solution)/shard_map/ppermute | solution.py:705
  130.2 9.4 %collective-permute-done.23 = bf16[256,1024]{1,0:T(8,128)(2,1)S(1)} collective-permute-done((bf16[256,1024]{1,0:T(8,128)(2,1)}, bf16[256,1024]{1,0:T(8,128)(2,1)S(1)}, u32[]{:S(2)}, u32[]{:S(2)}) %collective-permute-start.23) | collective-permute-done | bytes 524320 | tf_op jit(solution)/shard_map/ppermute | solution.py:705
  159.7 7.8 %collective-permute-done.28.refs_10_ = bf16[1024,512]{1,0:T(8,128)(2,1)} collective-permute-done((bf16[1024,512]{1,0:T(8,128)(2,1)}, bf16[1024,512]{1,0:T(8,128)(2,1)}, u32[]{:S(2)}, u32[]{:S(2)}) %collective-permute-start.28) | collective-permute-done | bytes 1048608 | tf_op jit(solution)/shard_map/ppermute | solution.py:708
  170.7 12.5 %collective-permute-done.44.refs_4_ = bf16[512,512]{1,0:T(8,128)(2,1)S(1)} collective-permute-done((bf16[512,512]{1,0:T(8,128)(2,1)S(1)}, bf16[512,512]{1,0:T(8,128)(2,1)S(1)}, u32[]{:S(2)}, u32[]{:S(2)}) %collective-permute-start.44) | collective-permute-done | bytes 524320 | tf_op jit(solution)/shard_map/ppermute | solution.py:708
  184.7 8.3 %collective-permute-done.35.refs_0_ = bf16[512,512]{1,0:T(8,128)(2,1)S(1)} collective-permute-done((bf16[512,512]{1,0:T(8,128)(2,1)}, bf16[512,512]{1,0:T(8,128)(2,1)S(1)}, u32[]{:S(2)}, u32[]{:S(2)}) %collective-permute-start.35) | collective-permute-done | bytes 524320 | tf_op jit(solution)/shard_map/ppermute | solution.py:708
  196.2 9.6 %collective-permute-done.46.refs_6_ = bf16[512,512]{1,0:T(8,128)(2,1)S(1)} collective-permute-done((bf16[512,512]{1,0:T(8,128)(2,1)}, bf16[512,512]{1,0:T(8,128)(2,1)S(1)}, u32[]{:S(2)}, u32[]{:S(2)}) %collective-permute-start.46) | collective-permute-done | bytes 524320 | tf_op jit(solution)/shard_map/ppermute | solution.py:708
  210.0 25.6 %feed.3 = (bf16[1024,704]{1,0:T(8,128)(2,1)}, bf16[1024,704]{1,0:T(8,128)(2,1)}, bf16[1024,704]{1,0:T(8,128)(2,1)}, bf16[1024,512]{1,0:T(8,128)(2,1)}, bf16[1024...) custom-call(bf16[512,512]{1,0:T(8,128)(2,1)} %copy-done.98, ...), custom_call_target="tpu_custom_call" | custom-call | flops 14763950080 | bytes 29622272 | tf_op jit(solution)/shard_map/feed/pallas_call | solution.py:373
  235.9 25.9 %feed.2 = (bf16[1024,704]{1,0:T(8,128)(2,1)}, bf16[1024,704]{1,0:T(8,128)(2,1)}, bf16[1024,704]{1,0:T(8,128)(2,1)}, bf16[1024,512]{1,0:T(8,128)(2,1)}, bf16[1024...) custom-call(bf16[512,512]{1,0:T(8,128)(2,1)} %get-tuple-element.297., ...), custom_call_target="tpu_custom_call" | custom-call | flops 14763950080 | bytes 29622272 | tf_op jit(solution)/shard_map/feed/pallas_call | solution.py:373
  263.2 9.3 %feed_weights.1 = bf16[4,4,704,128]{3,2,1,0:T(8,128)(2,1)} custom-call(bf16[1024,2048]{1,0:T(8,128)(2,1)} %get-tuple-element.175.x0, bf16[1024,2048]{1,0:T(8,128)(2,1)} %get-tuple-element.176.x1, bf16[1024,704]{1,0:T(8,128)(2,1)S(1)} %copy-done.12, bf16[1024,704]{1,0:T(8,128)(2,1)S(1)} %copy-done.11), custom_call_target="tpu_custom_call" | custom-call | flops 5905580032 | bytes 14155776 | tf_op jit(solution)/shard_map/feed_weights/pallas_call | solution.py:415
  283.0 10.7 %collective-permute-done.57 = bf16[512,512]{1,0:T(8,128)(2,1)S(1)} collective-permute-done((bf16[512,512]{1,0:T(8,128)(2,1)S(1)}, bf16[512,512]{1,0:T(8,128)(2,1)S(1)}, u32[]{:S(2)}, u32[]{:S(2)}) %collective-permute-start.57) | collective-permute-done | bytes 524320 | tf_op jit(solution)/shard_map/ppermute | solution.py:705
  293.8 10.5 %collective-permute-done.58 = bf16[512,512]{1,0:T(8,128)(2,1)S(1)} collective-permute-done((bf16[512,512]{1,0:T(8,128)(2,1)S(1)}, bf16[512,512]{1,0:T(8,128)(2,1)S(1)}, u32[]{:S(2)}, u32[]{:S(2)}) %collective-permute-start.58) | collective-permute-done | bytes 524320 | tf_op jit(solution)/shard_map/ppermute | solution.py:705
  308.6 19.5 %late_weights.1 = bf16[4,2,4,704,128]{4,3,2,1,0:T(8,128)(2,1)} custom-call(bf16[1024,2048]{1,0:T(8,128)(2,1)} %get-tuple-element.175.x0, bf16[1024,2048]{1,0:T(8,128)(2,1)} %get-tuple-element.176.x1, bf16[1024,704]{1,0:T(8,128)(2,1)} %get-tuple-element.185.u0, bf16[1024,704]{1,0:T(8,128)(2,1)} %get-tuple-element.186.u1, ...), custom_call_target="tpu_custom_call" | custom-call | flops 11811160064 | bytes 28311552 | tf_op jit(solution)/shard_map/late_weights/pallas_call | solution.py:489
  337.6 4.1 fusion.42
  341.7 2.9 convolution_convert_fusion
  344.9 2.5 convolution_convert_fusion.1
  351.6 10.9 %collective-permute-done.64 = bf16[256,1024]{1,0:T(8,128)(2,1)S(1)} collective-permute-done((bf16[256,1024]{1,0:T(8,128)(2,1)S(1)}, bf16[256,1024]{1,0:T(8,128)(2,1)S(1)}, u32[]{:S(2)}, u32[]{:S(2)}) %collective-permute-start.64) | collective-permute-done | bytes 524320 | tf_op jit(solution)/shard_map/ppermute | solution.py:705
  365.2 6.8 %attend_back.2 = (bf16[256,1024]{1,0:T(8,128)(2,1)}, f32[8,256,128]{2,1,0:T(8,128)}, f32[8,256,128]{2,1,0:T(8,128)}) custom-call(s32[2]{0:T(128)} %pad_add_fusion.where, s32[2048]{0:T(1024)} %seq_ref.7, s32[2048]{0:T(1024)} %block_ref.7, bf16[256,1024]{1,0:T(8,128)(2,1)} %get-tuple-element.191.rot_ref, bf16[256,1024]{1,0:T(8,128)(2,1)} %add_convert_fusion.19.grad_ref, ...), custom_call_target="tpu_custom_call" | custom-call | flops 2684354560 | bytes 5242880 | tf_op jit(solution)/shard_map/attend_back/pallas_call | solution.py:202
  373.8 4.3 collective-permute-done.65
  378.1 9.9 %collective-permute-done.66 = bf16[256,1024]{1,0:T(8,128)(2,1)S(1)} collective-permute-done((bf16[256,1024]{1,0:T(8,128)(2,1)}, bf16[256,1024]{1,0:T(8,128)(2,1)S(1)}, u32[]{:S(2)}, u32[]{:S(2)}) %collective-permute-start.66) | collective-permute-done | bytes 524320 | tf_op jit(solution)/shard_map/ppermute | solution.py:705
  392.5 4.6 collective-permute-start.72
  397.1 2.6 fusion.51
  402.2 7.7 %attend_back.3 = (bf16[256,1024]{1,0:T(8,128)(2,1)}, f32[8,256,128]{2,1,0:T(8,128)}, f32[8,256,128]{2,1,0:T(8,128)}) custom-call(s32[2]{0:T(128)} %pad_add_fusion.where, s32[2048]{0:T(1024)} %seq_ref.7, s32[2048]{0:T(1024)} %block_ref.7, bf16[256,1024]{1,0:T(8,128)(2,1)} %get-tuple-element.154.rot_ref, bf16[256,1024]{1,0:T(8,128)(2,1)} %add_convert_fusion.18.grad_ref, ...), custom_call_target="tpu_custom_call" | custom-call | flops 2684354560 | bytes 5242880 | tf_op jit(solution)/shard_map/attend_back/pallas_call | solution.py:202
  409.9 11.3 %collective-permute-done.72 = bf16[1024,512]{1,0:T(8,128)(2,1)S(1)} collective-permute-done((bf16[1024,512]{1,0:T(8,128)(2,1)}, bf16[1024,512]{1,0:T(8,128)(2,1)S(1)}, u32[]{:S(2)}, u32[]{:S(2)}) %collective-permute-start.72) | collective-permute-done | bytes 1048608 | tf_op jit(solution)/shard_map/ppermute | solution.py:708
  421.2 3.0 add_convert_fusion.1
  425.9 13.3 %down_products.1 = (bf16[1024,512]{1,0:T(8,128)(2,1)}, bf16[1024,512]{1,0:T(8,128)(2,1)}, bf16[1024,512]{1,0:T(8,128)(2,1)}, bf16[1024,512]{1,0:T(8,128)(2,1)}, ...) custom-call(bf16[1024,704]{1,0:T(8,128)(2,1)} %get-tuple-element.202, ...), custom_call_target="tpu_custom_call" | custom-call | tf_op jit(solution)/shard_map/down_products/pallas_call | solution.py:535
  440.5 3.3 fusion.52
  450.9 3.7 collective-permute-done.87
  468.4 10.0 %collective-permute-done.79 = bf16[512,512]{1,0:T(8,128)(2,1)S(1)} collective-permute-done((bf16[512,512]{1,0:T(8,128)(2,1)S(1)}, bf16[512,512]{1,0:T(8,128)(2,1)S(1)}, u32[]{:S(2)}, u32[]{:S(2)}) %collective-permute-start.79) | collective-permute-done | bytes 524320 | tf_op jit(solution)/shard_map/ppermute | solution.py:705
  482.6 2.7 fusion.10
  497.8 4.7 collective-permute-start.96
  503.1 4.0 fusion.7
  507.1 3.7 collective-permute-done.95
  512.4 3.5 add_convert_fusion
  520.8 10.3 %collective-permute-done.76 = bf16[512,512]{1,0:T(8,128)(2,1)S(1)} collective-permute-done((bf16[512,512]{1,0:T(8,128)(2,1)}, bf16[512,512]{1,0:T(8,128)(2,1)S(1)}, u32[]{:S(2)}, u32[]{:S(2)}) %collective-permute-start.76) | collective-permute-done | bytes 524320 | tf_op jit(solution)/shard_map/ppermute | solution.py:708
  531.2 8.6 %collective-permute-done.77 = bf16[512,512]{1,0:T(8,128)(2,1)S(1)} collective-permute-done((bf16[512,512]{1,0:T(8,128)(2,1)}, bf16[512,512]{1,0:T(8,128)(2,1)S(1)}, u32[]{:S(2)}, u32[]{:S(2)}) %collective-permute-start.77) | collective-permute-done | bytes 524320 | tf_op jit(solution)/shard_map/ppermute | solution.py:708
  542.9 2.8 collective-permute-done.99.refs_3_
  545.8 4.1 finish_weights.1
  549.9 7.5 %collective-permute-done.78 = bf16[512,512]{1,0:T(8,128)(2,1)S(1)} collective-permute-done((bf16[512,512]{1,0:T(8,128)(2,1)S(1)}, bf16[512,512]{1,0:T(8,128)(2,1)S(1)}, u32[]{:S(2)}, u32[]{:S(2)}) %collective-permute-start.78) | collective-permute-done | bytes 524320 | tf_op jit(solution)/shard_map/ppermute | solution.py:705
  (551 shorter events, 181.0 us)
Async XLA Ops:
  7.2 202.8 %all-gather.5.cloned.1.call-start = ((), (), s32[]{:S(2)}) async-start(), calls=%async_computation.8 | async-start | bytes 3604480 | tf_op jit(solution)/shard_map/all_gather | solution.py:901
  9.3 28.4 %collective-permute-start.4 = (bf16[512,1024]{1,0:T(8,128)(2,1)}, bf16[512,1024]{1,0:T(8,128)(2,1)}, u32[]{:S(2)}, u32[]{:S(2)}) collective-permute-start(bf16[512,1024]{1,0:T(8,128)(2,1)} %param.20), channel_id=1, source_target_pairs={{0,1},{1,0},{2,3},{3,2},{4,5},{5,4},{6,7},{7,6},{8,9},{9,8},{10,11... | collective-permute-start | bytes 3145736 | tf_op jit(solution)/shard_map/ppermute | solution.py:708
  23.5 19.1 %collective-permute-start = (bf16[512,1024]{1,0:T(8,128)(2,1)}, bf16[512,1024]{1,0:T(8,128)(2,1)}, u32[]{:S(2)}, u32[]{:S(2)}) collective-permute-start(bf16[512,1024]{1,0:T(8,128)(2,1)} %slice.355), channel_id=1, source_target_pairs={{0,2},{2,0},{4,6},{6,4},{1,3},{3,1},{5,7},{7,5},{8,10},{10,8},{12,... | collective-permute-start | bytes 3145736 | tf_op jit(solution)/shard_map/ppermute | solution.py:705
  36.4 17.9 %collective-permute-start.8 = (bf16[2,704,128]{2,1,0:T(8,128)(2,1)S(1)}, bf16[2,704,128]{2,1,0:T(8,128)(2,1)S(1)}, u32[]{:S(2)}, u32[]{:S(2)}) collective-permute-start(bf16[2,704,128]{2,1,0:T(8,128)(2,1)S(1)} %get-tuple-element.128), channel_id=1, source_target_pairs={{0,4},{2,6},{4,0},{6,2},{1,5},{3,7},{5,1},{7,3},{8,12},{10,14},{12... | collective-permute-start | bytes 1081352 | tf_op jit(solution)/shard_map/ppermute | solution.py:705
  37.7 18.0 %collective-permute-start.9 = (bf16[2,704,128]{2,1,0:T(8,128)(2,1)S(1)}, bf16[2,704,128]{2,1,0:T(8,128)(2,1)S(1)}, u32[]{:S(2)}, u32[]{:S(2)}) collective-permute-start(bf16[2,704,128]{2,1,0:T(8,128)(2,1)S(1)} %get-tuple-element.129), channel_id=1, source_target_pairs={{0,6},{2,4},{4,2},{6,0},{1,7},{3,5},{5,3},{7,1},{8,14},{10,12},{12... | collective-permute-start | bytes 1081352 | tf_op jit(solution)/shard_map/ppermute | solution.py:705
  37.7 30.2 %collective-permute-start.5 = (bf16[1024,512]{1,0:T(8,128)(2,1)}, bf16[1024,512]{1,0:T(8,128)(2,1)}, u32[]{:S(2)}, u32[]{:S(2)}) collective-permute-start(bf16[1024,512]{1,0:T(8,128)(2,1)} %param.22), channel_id=1, source_target_pairs={{0,1},{1,0},{2,3},{3,2},{4,5},{5,4},{6,7},{7,6},{8,9},{9,8},{10,11... | collective-permute-start | bytes 3145736 | tf_op jit(solution)/shard_map/ppermute | solution.py:708
  41.9 26.4 %collective-permute-start.19 = (bf16[512,1024]{1,0:T(8,128)(2,1)}, bf16[512,1024]{1,0:T(8,128)(2,1)}, u32[]{:S(2)}, u32[]{:S(2)}) collective-permute-start(bf16[512,1024]{1,0:T(8,128)(2,1)} %slice.367), channel_id=1, source_target_pairs={{0,2},{2,0},{4,6},{6,4},{1,3},{3,1},{5,7},{7,5},{8,10},{10,8},{12,... | collective-permute-start | bytes 3145736 | tf_op jit(solution)/shard_map/ppermute | solution.py:705
  46.0 19.7 %collective-permute-start.1 = (bf16[256,1024]{1,0:T(8,128)(2,1)}, bf16[256,1024]{1,0:T(8,128)(2,1)}, u32[]{:S(2)}, u32[]{:S(2)}) collective-permute-start(bf16[256,1024]{1,0:T(8,128)(2,1)} %slice.357), channel_id=1, source_target_pairs={{0,4},{2,6},{4,0},{6,2},{1,5},{3,7},{5,1},{7,3},{8,12},{10,14},{12... | collective-permute-start | bytes 1572872 | tf_op jit(solution)/shard_map/ppermute | solution.py:705
  54.4 45.5 %collective-permute-start.21 = (bf16[2,704,512]{2,1,0:T(8,128)(2,1)}, bf16[2,704,512]{2,1,0:T(8,128)(2,1)}, u32[]{:S(2)}, u32[]{:S(2)}) collective-permute-start(bf16[2,704,512]{2,1,0:T(8,128)(2,1)} %get-tuple-element.134), channel_id=1, source_target_pairs={{0,2},{2,0},{4,6},{6,4},{1,3},{3,1},{5,7},{7,5},{8,10},{10,8},{12,... | collective-permute-start | bytes 4325384 | tf_op jit(solution)/shard_map/ppermute | solution.py:705
  55.6 16.5 %collective-permute-start.13 = (bf16[256,256]{1,0:T(8,128)(2,1)S(1)}, bf16[256,256]{1,0:T(8,128)(2,1)S(1)}, u32[]{:S(2)}, u32[]{:S(2)}) collective-permute-start(bf16[256,256]{1,0:T(8,128)(2,1)S(1)} %pad_maximum_fusion.19.refs_0_.outs_0_), channel_id=1, source_target_pairs={{0,1},{1,0},{2,3},{3,2},{4,5},{5,4},{6,7},{7,6},{8,9},{9,8},{10,11... | collective-permute-start | bytes 393224 | tf_op jit(solution)/shard_map/ppermute | solution.py:708
  67.8 34.1 %collective-permute-start.22 = (bf16[1024,512]{1,0:T(8,128)(2,1)}, bf16[1024,512]{1,0:T(8,128)(2,1)}, u32[]{:S(2)}, u32[]{:S(2)}) collective-permute-start(bf16[1024,512]{1,0:T(8,128)(2,1)} %convert_element_type.509.refs_8_), channel_id=1, source_target_pairs={{0,1},{1,0},{2,3},{3,2},{4,5},{5,4},{6,7},{7,6},{8,9},{9,8},{10,11... | collective-permute-start | bytes 3145736 | tf_op jit(solution)/shard_map/ppermute | solution.py:708
  70.0 29.8 %collective-permute-start.20 = (bf16[256,1024]{1,0:T(8,128)(2,1)S(1)}, bf16[256,1024]{1,0:T(8,128)(2,1)S(1)}, u32[]{:S(2)}, u32[]{:S(2)}) collective-permute-start(bf16[256,1024]{1,0:T(8,128)(2,1)S(1)} %slice.369), channel_id=1, source_target_pairs={{0,4},{2,6},{4,0},{6,2},{1,5},{3,7},{5,1},{7,3},{8,12},{10,14},{12... | collective-permute-start | bytes 1572872 | tf_op jit(solution)/shard_map/ppermute | solution.py:705
  72.2 137.8 %all-gather.7.cloned.1.call-start = ((), (), s32[]{:S(2)}) async-start(), calls=%async_computation.9 | async-start | bytes 1802240 | tf_op jit(solution)/shard_map/all_gather | solution.py:908
  91.7 48.0 %collective-permute-start.24 = (bf16[1024,512]{1,0:T(8,128)(2,1)}, bf16[1024,512]{1,0:T(8,128)(2,1)}, u32[]{:S(2)}, u32[]{:S(2)}) collective-permute-start(bf16[1024,512]{1,0:T(8,128)(2,1)} %convert_element_type.509.refs_8_), channel_id=1, source_target_pairs={{0,4},{2,6},{4,0},{6,2},{1,5},{3,7},{5,1},{7,3},{8,12},{10,14},{12... | collective-permute-start | bytes 3145736 | tf_op jit(solution)/shard_map/ppermute | solution.py:705
  98.1 31.0 %collective-permute-start.17 = (bf16[256,1024]{1,0:T(8,128)(2,1)}, bf16[256,1024]{1,0:T(8,128)(2,1)S(1)}, u32[]{:S(2)}, u32[]{:S(2)}) collective-permute-start(bf16[256,1024]{1,0:T(8,128)(2,1)} %get-tuple-element.131.att_ref), channel_id=1, source_target_pairs={{0,4},{2,6},{4,0},{6,2},{1,5},{3,7},{5,1},{7,3},{8,12},{10,14},{12... | collective-permute-start | bytes 1572872 | tf_op jit(solution)/shard_map/ppermute | solution.py:705
  108.5 31.0 %collective-permute-start.23 = (bf16[256,1024]{1,0:T(8,128)(2,1)}, bf16[256,1024]{1,0:T(8,128)(2,1)S(1)}, u32[]{:S(2)}, u32[]{:S(2)}) collective-permute-start(bf16[256,1024]{1,0:T(8,128)(2,1)} %get-tuple-element.139.att_ref), channel_id=1, source_target_pairs={{0,4},{2,6},{4,0},{6,2},{1,5},{3,7},{5,1},{7,3},{8,12},{10,14},{12... | collective-permute-start | bytes 1572872 | tf_op jit(solution)/shard_map/ppermute | solution.py:705
  139.9 16.3 %collective-permute-start.39 = (bf16[176,512]{1,0:T(8,128)(2,1)S(1)}, bf16[176,512]{1,0:T(8,128)(2,1)S(1)}, u32[]{:S(2)}, u32[]{:S(2)}) collective-permute-start(bf16[176,512]{1,0:T(8,128)(2,1)S(1)} %get-tuple-element.148), channel_id=1, source_target_pairs={{0,4},{2,6},{4,0},{6,2},{1,5},{3,7},{5,1},{7,3},{8,12},{10,14},{12... | collective-permute-start | bytes 540680 | tf_op jit(solution)/shard_map/ppermute | solution.py:705
  141.7 25.7 %collective-permute-start.28 = (bf16[1024,512]{1,0:T(8,128)(2,1)}, bf16[1024,512]{1,0:T(8,128)(2,1)}, u32[]{:S(2)}, u32[]{:S(2)}) collective-permute-start(bf16[1024,512]{1,0:T(8,128)(2,1)} %collective-permute-done.24.refs_10_), channel_id=1, source_target_pairs={{0,1},{1,0},{2,3},{3,2},{4,5},{5,4},{6,7},{7,6},{8,9},{9,8},{10,11... | collective-permute-start | bytes 3145736 | tf_op jit(solution)/shard_map/ppermute | solution.py:708
  157.0 208.2 %reduce-scatter.5.cloned.1.call-start = ((), (), s32[]{:S(2)}) async-start(), calls=%async_computation.4 | async-start | bytes 3604480 | tf_op jit(solution)/shard_map/reduce_scatter | solution.py:954
  169.8 24.6 %collective-permute-start.38 = (bf16[704,512]{1,0:T(8,128)(2,1)S(1)}, bf16[704,512]{1,0:T(8,128)(2,1)S(1)}, u32[]{:S(2)}, u32[]{:S(2)}) collective-permute-start(bf16[704,512]{1,0:T(8,128)(2,1)S(1)} %copy-done.10), channel_id=1, source_target_pairs={{0,2},{2,0},{4,6},{6,4},{1,3},{3,1},{5,7},{7,5},{8,10},{10,8},{12,... | collective-permute-start | bytes 2162696 | tf_op jit(solution)/shard_map/ppermute | solution.py:705
  170.1 22.8 %collective-permute-start.35 = (bf16[512,512]{1,0:T(8,128)(2,1)}, bf16[512,512]{1,0:T(8,128)(2,1)S(1)}, u32[]{:S(2)}, u32[]{:S(2)}) collective-permute-start(bf16[512,512]{1,0:T(8,128)(2,1)} %get-tuple-element.297.refs_0_), channel_id=1, source_target_pairs={{0,1},{1,0},{2,3},{3,2},{4,5},{5,4},{6,7},{7,6},{8,9},{9,8},{10,11... | collective-permute-start | bytes 1572872 | tf_op jit(solution)/shard_map/ppermute | solution.py:708
  170.7 24.1 %collective-permute-start.32 = (bf16[512,512]{1,0:T(8,128)(2,1)S(1)}, bf16[512,512]{1,0:T(8,128)(2,1)S(1)}, u32[]{:S(2)}, u32[]{:S(2)}) collective-permute-start(bf16[512,512]{1,0:T(8,128)(2,1)S(1)} %get-tuple-element.296.refs_4_), channel_id=1, source_target_pairs={{0,2},{2,0},{4,6},{6,4},{1,3},{3,1},{5,7},{7,5},{8,10},{10,8},{12,... | collective-permute-start | bytes 1572872 | tf_op jit(solution)/shard_map/ppermute | solution.py:705
  206.8 28.8 %collective-permute-start.29 = (bf16[512,512]{1,0:T(8,128)(2,1)}, bf16[512,512]{1,0:T(8,128)(2,1)}, u32[]{:S(2)}, u32[]{:S(2)}) collective-permute-start(bf16[512,512]{1,0:T(8,128)(2,1)} %get-tuple-element.297.refs_0_), channel_id=1, source_target_pairs={{0,2},{2,0},{4,6},{6,4},{1,3},{3,1},{5,7},{7,5},{8,10},{10,8},{12,... | collective-permute-start | bytes 1572872 | tf_op jit(solution)/shard_map/ppermute | solution.py:705
  207.6 28.2 %collective-permute-start.36 = (bf16[1024,512]{1,0:T(8,128)(2,1)}, bf16[1024,512]{1,0:T(8,128)(2,1)}, u32[]{:S(2)}, u32[]{:S(2)}) collective-permute-start(bf16[1024,512]{1,0:T(8,128)(2,1)} %convert_element_type.509.refs_8_), channel_id=1, source_target_pairs={{0,2},{2,0},{4,6},{6,4},{1,3},{3,1},{5,7},{7,5},{8,10},{10,8},{12,... | collective-permute-start | bytes 3145736 | tf_op jit(solution)/shard_map/ppermute | solution.py:705
  208.7 27.2 %collective-permute-start.37 = (bf16[1024,512]{1,0:T(8,128)(2,1)}, bf16[1024,512]{1,0:T(8,128)(2,1)}, u32[]{:S(2)}, u32[]{:S(2)}) collective-permute-start(bf16[1024,512]{1,0:T(8,128)(2,1)} %collective-permute-done.24.refs_10_), channel_id=1, source_target_pairs={{0,2},{2,0},{4,6},{6,4},{1,3},{3,1},{5,7},{7,5},{8,10},{10,8},{12,... | collective-permute-start | bytes 3145736 | tf_op jit(solution)/shard_map/ppermute | solution.py:705
  209.5 26.3 %collective-permute-start.34 = (bf16[512,512]{1,0:T(8,128)(2,1)}, bf16[512,512]{1,0:T(8,128)(2,1)}, u32[]{:S(2)}, u32[]{:S(2)}) collective-permute-start(bf16[512,512]{1,0:T(8,128)(2,1)} %collective-permute-done.33.refs_6_), channel_id=1, source_target_pairs={{0,2},{2,0},{4,6},{6,4},{1,3},{3,1},{5,7},{7,5},{8,10},{10,8},{12,... | collective-permute-start | bytes 1572872 | tf_op jit(solution)/shard_map/ppermute | solution.py:705
  209.7 26.2 %collective-permute-start.31 = (bf16[512,512]{1,0:T(8,128)(2,1)}, bf16[512,512]{1,0:T(8,128)(2,1)}, u32[]{:S(2)}, u32[]{:S(2)}) collective-permute-start(bf16[512,512]{1,0:T(8,128)(2,1)} %collective-permute-done.30.refs_2_), channel_id=1, source_target_pairs={{0,2},{2,0},{4,6},{6,4},{1,3},{3,1},{5,7},{7,5},{8,10},{10,8},{12,... | collective-permute-start | bytes 1572872 | tf_op jit(solution)/shard_map/ppermute | solution.py:705
  235.6 37.9 %collective-permute-start.52 = (bf16[1024,512]{1,0:T(8,128)(2,1)}, bf16[1024,512]{1,0:T(8,128)(2,1)}, u32[]{:S(2)}, u32[]{:S(2)}) collective-permute-start(bf16[1024,512]{1,0:T(8,128)(2,1)} %get-tuple-element.160), channel_id=1, source_target_pairs={{0,2},{2,0},{4,6},{6,4},{1,3},{3,1},{5,7},{7,5},{8,10},{10,8},{12,... | collective-permute-start | bytes 3145736 | tf_op jit(solution)/shard_map/ppermute | solution.py:705
  272.6 220.9 %reduce-scatter.7.cloned.1.call-start = ((), (), s32[]{:S(2)}) async-start(), calls=%async_computation.5 | async-start | bytes 7208960 | tf_op jit(solution)/shard_map/reduce_scatter | solution.py:954
  279.2 25.1 %collective-permute-start.58 = (bf16[512,512]{1,0:T(8,128)(2,1)S(1)}, bf16[512,512]{1,0:T(8,128)(2,1)S(1)}, u32[]{:S(2)}, u32[]{:S(2)}) collective-permute-start(bf16[512,512]{1,0:T(8,128)(2,1)S(1)} %get-tuple-element.172), channel_id=1, source_target_pairs={{0,4},{2,6},{4,0},{6,2},{1,5},{3,7},{5,1},{7,3},{8,12},{10,14},{12... | collective-permute-start | bytes 1572872 | tf_op jit(solution)/shard_map/ppermute | solution.py:705
  281.0 26.2 %collective-permute-start.54 = (bf16[512,512]{1,0:T(8,128)(2,1)S(1)}, bf16[512,512]{1,0:T(8,128)(2,1)S(1)}, u32[]{:S(2)}, u32[]{:S(2)}) collective-permute-start(bf16[512,512]{1,0:T(8,128)(2,1)S(1)} %get-tuple-element.164), channel_id=1, source_target_pairs={{0,1},{1,0},{2,3},{3,2},{4,5},{5,4},{6,7},{7,6},{8,9},{9,8},{10,11... | collective-permute-start | bytes 1572872 | tf_op jit(solution)/shard_map/ppermute | solution.py:708
  282.9 24.5 %collective-permute-start.55 = (bf16[512,512]{1,0:T(8,128)(2,1)S(1)}, bf16[512,512]{1,0:T(8,128)(2,1)S(1)}, u32[]{:S(2)}, u32[]{:S(2)}) collective-permute-start(bf16[512,512]{1,0:T(8,128)(2,1)S(1)} %get-tuple-element.166), channel_id=1, source_target_pairs={{0,1},{1,0},{2,3},{3,2},{4,5},{5,4},{6,7},{7,6},{8,9},{9,8},{10,11... | collective-permute-start | bytes 1572872 | tf_op jit(solution)/shard_map/ppermute | solution.py:708
  305.3 22.8 %collective-permute-start.59 = (bf16[512,512]{1,0:T(8,128)(2,1)}, bf16[512,512]{1,0:T(8,128)(2,1)}, u32[]{:S(2)}, u32[]{:S(2)}) collective-permute-start(bf16[512,512]{1,0:T(8,128)(2,1)} %add_convert_fusion.20), channel_id=1, source_target_pairs={{0,1},{1,0},{2,3},{3,2},{4,5},{5,4},{6,7},{7,6},{8,9},{9,8},{10,11... | collective-permute-start | bytes 1572872 | tf_op jit(solution)/shard_map/ppermute | solution.py:708
  308.3 21.0 %collective-permute-start.56 = (bf16[512,512]{1,0:T(8,128)(2,1)}, bf16[512,512]{1,0:T(8,128)(2,1)}, u32[]{:S(2)}, u32[]{:S(2)}) collective-permute-start(bf16[512,512]{1,0:T(8,128)(2,1)} %add_convert_fusion.26), channel_id=1, source_target_pairs={{0,4},{2,6},{4,0},{6,2},{1,5},{3,7},{5,1},{7,3},{8,12},{10,14},{12... | collective-permute-start | bytes 1572872 | tf_op jit(solution)/shard_map/ppermute | solution.py:705
  335.7 223.6 %reduce-scatter.11.cloned.1.call-start = ((), (), s32[]{:S(2)}) async-start(), calls=%async_computation.7 | async-start | bytes 1310720 | tf_op jit(solution)/shard_map/reduce_scatter | solution.py:954
  372.0 16.1 %collective-permute-start.66 = (bf16[256,1024]{1,0:T(8,128)(2,1)}, bf16[256,1024]{1,0:T(8,128)(2,1)S(1)}, u32[]{:S(2)}, u32[]{:S(2)}) collective-permute-start(bf16[256,1024]{1,0:T(8,128)(2,1)} %get-tuple-element.194), channel_id=1, source_target_pairs={{0,4},{2,6},{4,0},{6,2},{1,5},{3,7},{5,1},{7,3},{8,12},{10,14},{12... | collective-permute-start | bytes 1572872 | tf_op jit(solution)/shard_map/ppermute | solution.py:705
  392.5 28.7 %collective-permute-start.72 = (bf16[1024,512]{1,0:T(8,128)(2,1)}, bf16[1024,512]{1,0:T(8,128)(2,1)S(1)}, u32[]{:S(2)}, u32[]{:S(2)}) collective-permute-start(bf16[1024,512]{1,0:T(8,128)(2,1)} %convolution_convert_fusion.4), channel_id=1, source_target_pairs={{0,1},{1,0},{2,3},{3,2},{4,5},{5,4},{6,7},{7,6},{8,9},{9,8},{10,11... | collective-permute-start | bytes 3145736 | tf_op jit(solution)/shard_map/ppermute | solution.py:708
  402.2 43.6 %collective-permute-start.75 = (bf16[512,1024]{1,0:T(8,128)(2,1)}, bf16[512,1024]{1,0:T(8,128)(2,1)}, u32[]{:S(2)}, u32[]{:S(2)}) collective-permute-start(bf16[512,1024]{1,0:T(8,128)(2,1)} %convolution_convert_fusion.5), channel_id=1, source_target_pairs={{0,1},{1,0},{2,3},{3,2},{4,5},{5,4},{6,7},{7,6},{8,9},{9,8},{10,11... | collective-permute-start | bytes 3145736 | tf_op jit(solution)/shard_map/ppermute | solution.py:708
  424.2 19.9 %collective-permute-start.73 = (bf16[256,1024]{1,0:T(8,128)(2,1)}, bf16[256,1024]{1,0:T(8,128)(2,1)}, u32[]{:S(2)}, u32[]{:S(2)}) collective-permute-start(bf16[256,1024]{1,0:T(8,128)(2,1)} %get-tuple-element.213), channel_id=1, source_target_pairs={{0,4},{2,6},{4,0},{6,2},{1,5},{3,7},{5,1},{7,3},{8,12},{10,14},{12... | collective-permute-start | bytes 1572872 | tf_op jit(solution)/shard_map/ppermute | solution.py:705
  444.1 18.1 %collective-permute-start.71 = (bf16[1024,512]{1,0:T(8,128)(2,1)S(1)}, bf16[1024,512]{1,0:T(8,128)(2,1)S(1)}, u32[]{:S(2)}, u32[]{:S(2)}) collective-permute-start(bf16[1024,512]{1,0:T(8,128)(2,1)S(1)} %copy-done.94), channel_id=1, source_target_pairs={{0,2},{2,0},{4,6},{6,4},{1,3},{3,1},{5,7},{7,5},{8,10},{10,8},{12,... | collective-permute-start | bytes 3145736 | tf_op jit(solution)/shard_map/ppermute | solution.py:705
  450.4 16.6 %collective-permute-start.74 = (bf16[512,1024]{1,0:T(8,128)(2,1)S(1)}, bf16[512,1024]{1,0:T(8,128)(2,1)S(1)}, u32[]{:S(2)}, u32[]{:S(2)}) collective-permute-start(bf16[512,1024]{1,0:T(8,128)(2,1)S(1)} %get-tuple-element.315), channel_id=1, source_target_pairs={{0,2},{2,0},{4,6},{6,4},{1,3},{3,1},{5,7},{7,5},{8,10},{10,8},{12,... | collective-permute-start | bytes 3145736 | tf_op jit(solution)/shard_map/ppermute | solution.py:705
  463.9 29.7 %collective-permute-start.80 = (bf16[512,512]{1,0:T(8,128)(2,1)}, bf16[512,512]{1,0:T(8,128)(2,1)}, u32[]{:S(2)}, u32[]{:S(2)}) collective-permute-start(bf16[512,512]{1,0:T(8,128)(2,1)} %get-tuple-element.226), channel_id=1, source_target_pairs={{0,4},{2,6},{4,0},{6,2},{1,5},{3,7},{5,1},{7,3},{8,12},{10,14},{12... | collective-permute-start | bytes 1572872 | tf_op jit(solution)/shard_map/ppermute | solution.py:705
  493.5 67.7 %reduce-scatter.9.cloned.1.call-start = ((), (), s32[]{:S(2)}) async-start(), calls=%async_computation.6 | async-start | bytes 1310720 | tf_op jit(solution)/shard_map/reduce_scatter | solution.py:954
  495.9 45.8 %collective-permute-start.81 = (bf16[512,512]{1,0:T(8,128)(2,1)}, bf16[512,512]{1,0:T(8,128)(2,1)}, u32[]{:S(2)}, u32[]{:S(2)}) collective-permute-start(bf16[512,512]{1,0:T(8,128)(2,1)} %add_convert_fusion.6), channel_id=1, source_target_pairs={{0,1},{1,0},{2,3},{3,2},{4,5},{5,4},{6,7},{7,6},{8,9},{9,8},{10,11... | collective-permute-start | bytes 1572872 | tf_op jit(solution)/shard_map/ppermute | solution.py:708
  517.2 22.6 %collective-permute-start.77 = (bf16[512,512]{1,0:T(8,128)(2,1)}, bf16[512,512]{1,0:T(8,128)(2,1)S(1)}, u32[]{:S(2)}, u32[]{:S(2)}) collective-permute-start(bf16[512,512]{1,0:T(8,128)(2,1)} %get-tuple-element.220), channel_id=1, source_target_pairs={{0,1},{1,0},{2,3},{3,2},{4,5},{5,4},{6,7},{7,6},{8,9},{9,8},{10,11... | collective-permute-start | bytes 1572872 | tf_op jit(solution)/shard_map/ppermute | solution.py:708
  519.7 23.2 %collective-permute-start.97 = (bf16[3,704,128]{2,1,0:T(8,128)(2,1)S(1)}, bf16[3,704,128]{2,1,0:T(8,128)(2,1)S(1)}, u32[]{:S(2)}, u32[]{:S(2)}) collective-permute-start(bf16[3,704,128]{2,1,0:T(8,128)(2,1)S(1)} %pad_maximum_fusion.10), channel_id=1, source_target_pairs={{0,2},{2,0},{4,6},{6,4},{1,3},{3,1},{5,7},{7,5},{8,10},{10,8},{12,... | collective-permute-start | bytes 1622024 | tf_op jit(solution)/shard_map/ppermute | solution.py:705
  519.9 23.1 %collective-permute-start.98 = (bf16[3,704,128]{2,1,0:T(8,128)(2,1)S(1)}, bf16[3,704,128]{2,1,0:T(8,128)(2,1)S(1)}, u32[]{:S(2)}, u32[]{:S(2)}) collective-permute-start(bf16[3,704,128]{2,1,0:T(8,128)(2,1)S(1)} %pad_maximum_fusion.11), channel_id=1, source_target_pairs={{0,4},{2,6},{4,0},{6,2},{1,5},{3,7},{5,1},{7,3},{8,12},{10,14},{12... | collective-permute-start | bytes 1622024 | tf_op jit(solution)/shard_map/ppermute | solution.py:705
  540.0 17.4 %collective-permute-start.78 = (bf16[512,512]{1,0:T(8,128)(2,1)S(1)}, bf16[512,512]{1,0:T(8,128)(2,1)S(1)}, u32[]{:S(2)}, u32[]{:S(2)}) collective-permute-start(bf16[512,512]{1,0:T(8,128)(2,1)S(1)} %add_convert_fusion.12), channel_id=1, source_target_pairs={{0,4},{2,6},{4,0},{6,2},{1,5},{3,7},{5,1},{7,3},{8,12},{10,14},{12... | collective-permute-start | bytes 1572872 | tf_op jit(solution)/shard_map/ppermute | solution.py:705
  (171 other events, 1666.0 us)
Sparse Core Ops, SparseCore 0:
  72.4 59.6 all-gather.4
  157.1 35.4 all-gather.6
  272.7 56.9 reduce-scatter.4
  335.8 101.5 reduce-scatter.6
  493.6 29.1 reduce-scatter.10
  525.0 26.5 reduce-scatter.8

commit v4 on v3

--- a/solution.py
+++ b/solution.py
@@ -15,7 +15,7 @@
 BF = jnp.bfloat16
 F32 = jnp.float32
 HEADS_PER_STEP = 4
-FL = {'f11': 0, 'f13': 1, 'f0': 1, 'f1': 1, 'f5': 2, 'f9': 1, 'f12': 2, 'f2': 1, 'f3': 1, 'f4': 0, 'f8': 0, 'f10': 3, 'f6': 1, 'f7': 1, 'f14': 1, 'f15': 0, 'f16': 0, 'f17': 0, 'b0': 1, 'b1': 1, 'b2': 1, 'b3': 0, 'b4': 0, 'b5': 3, 'b6': 0, 'b7': 1, 'b8': 1, 'b29': 1, 'b28': 0, 'b18': 2, 'b19': 1, 'b24': 2, 'b9': 3, 'b13': 5, 'b14': 3, 'b15': 0, 'b16': 0, 'b17': 2, 'b20': 0, 'b22': 0, 'b23': 0, 'b25': 1, 'b26': 0, 'b27': 0, 'b30': 0, 'b31': 0, 'b32': 1, 'b33': 0, 'b34': 0, 'b36': 0}
+FL = {'f11': 0, 'f13': 1, 'f0': 1, 'f1': 1, 'f5': 2, 'f9': 1, 'f12': 2, 'f2': 1, 'f3': 1, 'f4': 0, 'f8': 1, 'f10': 3, 'f6': 1, 'f7': 1, 'f14': 1, 'f15': 0, 'f16': 0, 'f17': 0, 'b0': 1, 'b1': 0, 'b2': 1, 'b3': 0, 'b4': 0, 'b5': 2, 'b6': 0, 'b7': 1, 'b8': 1, 'b29': 0, 'b28': 0, 'b18': 2, 'b19': 1, 'b24': 2, 'b9': 3, 'b13': 5, 'b14': 1, 'b15': 0, 'b16': 0, 'b17': 2, 'b20': 0, 'b22': 0, 'b23': 0, 'b25': 1, 'b26': 1, 'b27': 0, 'b30': 0, 'b31': 0, 'b32': 0, 'b33': 0, 'b34': 0, 'b36': 0, 'b37': 1}
 
 
 def dot_nn(a, b):
@@ -774,41 +774,34 @@
         total = a.astype(F32) + b.astype(F32)
         return total if wide else total.astype(BF)
 
-    def reduce_plane(blocks, after=((), ()), then=()):
+    def plane_core(blocks):
         moved = {(a, k): swap_row(blocks[(a, k ^ 1)], 1) for a in (1, 0) for k in range(0, R, 2)}
-        outs, firsts, seconds = [], [], []
-        for part in range(2):
-            here = slice(part * half, (part + 1) * half)
-            cur = {key: add(blocks[key][here], value[here]) for key, value in moved.items()}
-            firsts.append(list(cur.values()))
-            cur = tie(cur, after[part])
-
-            def by_col(cur, last):
-                return {
-                    (0, k): add(cur[(0, k)], swap_col(cur[(1, k)]), last)
-                    for (a, k) in cur
-                    if a == 0
+        halves = (slice(0, half), slice(half, 2 * half))
+        return [{key: add(blocks[key][h], value[h]) for key, value in moved.items()} for h in halves]
+
+    def plane_rest(parts, after=((), ()), then=(), use_after=()):
+        def by_col(cur, last, use_after=()):
+            return {
+                (0, k): add(v, tie(swap_col(cur[(1, k)]), use_after), last)
+                for (a, k), v in cur.items()
+                if a == 0
+            }
+
+        def by_rows(cur, last, use_after=()):
+            for bit in bits[1:]:
+                cur = {
+                    (a, k): add(
+                        v, tie(swap_row(cur[(a, k ^ bit)], bit), use_after), last and bit == bits[-1]
+                    )
+                    for (a, k), v in cur.items()
+                    if not k & bit
                 }
-
-            def by_rows(cur, last):
-                for bit in bits[1:]:
-                    cur = {
-                        (a, k): add(v, swap_row(cur[(a, k ^ bit)], bit), last and bit == bits[-1])
-                        for (a, k), v in cur.items()
-                        if not k & bit
-                    }
-                return cur
-
-            if part == 0:
-                cur = by_col(cur, False)
-                seconds.append(list(cur.values()))
-                cur = by_rows(tie(cur, then), True)
-            else:
-                cur = by_rows(cur, False)
-                seconds.append(list(cur.values()))
-                cur = by_col(tie(cur, then), True)
-            outs.append(cur[(0, 0)])
-        return jnp.concatenate(outs, axis=0), firsts, seconds
+            return cur
+
+        first = by_col(tie(parts[0], after[0]), False, use_after)
+        second = by_rows(tie(parts[1], after[1]), False, use_after)
+        outs = [by_rows(tie(first, then), True), by_col(tie(second, then), True)]
+        return jnp.concatenate([o[(0, 0)] for o in outs], axis=0)
 
     residual = tokens.astype(F32)
     scale_one = lax.rsqrt(psum_row(jnp.sum(residual * residual, axis=1)) / D + EPS)
@@ -939,7 +932,8 @@
             backs[(a, k)] = fed[a][3 + k]
     acts, gate_grads, up_grads = ([fed[a][j] for a in range(2)] for j in range(3))
     normed_halves, grad_halves = ([fed[a][3 + R + j] for a in range(2)] for j in range(2))
-    normed2_grad, firsts, seconds = reduce_plane(backs)
+    core_sums = plane_core(backs)
+    normed2_grad = None if FL.get("b37", 0) else plane_rest(core_sums)
 
     def place(pieces):
         moved = jnp.stack(exchange([jnp.stack([p[k] for p in pieces]) for k in range(R)]))
@@ -957,13 +951,16 @@
     gate_piece = over_dp(gate_local)
     if shared[1]:
         late = late_weight_grads(
-            normed_halves, tf("b1", tf("b0", tie(up_grads, gate_local), firsts), seconds), grad_halves, acts, R, dp_n
+            normed_halves, tf("b0", tie(up_grads, gate_local), core_sums), grad_halves, acts, R, dp_n
         )
         late_piece = over_dp(tie(late, gate_local))
+        if FL.get("b37", 0):
+            normed2_grad = plane_rest(core_sums, use_after=late)
         up_piece, down_piece = late_piece[0, 0], late_piece[0, 1]
         normed2_grad = tie(normed2_grad, gate_local, late)
     else:
         late_piece = gate_piece
+        normed2_grad = plane_rest(core_sums)
         up_piece = over_dp(feed_weight_grad(normed_halves, up_grads, R, dp_n))[0]
         down_piece = over_dp(down_weight_grad(acts, grad_halves, R, dp_n))[0]
 
@@ -1039,8 +1036,8 @@
     grad_query_local = add(grad_query_near, grad_query_came)
     opts = (qpg_far, qpg_near, qpg_near_outer, grad_query_came, grad_query_local)
     pick_opt = lambda k: () if not k else opts[k - 1]
-    down_sum, _, seconds_out = reduce_plane(
-        products,
+    down_sum = plane_rest(
+        plane_core(products),
         after=(pick_opt(FL.get("b13", 0)), pick_opt(FL.get("b14", 0))),
         then=pick_opt(FL.get("b15", 0)),
     )

time: 580 us -> 569 us (0.981)
  waiting for transfers between devices: 215 us -> 174 us
  starting transfers between devices: 71.1 us -> 90.8 us
  other arithmetic: 69 us -> 75 us
    ppermute x79, waiting for transfers between devices: 142 us -> 102 us  [swap_row(): return lax.ppermute(a, 'row', [(i, i ^ bit) for i in range(R)])]
    ppermute x18, starting transfers between devices: 24.8 us -> 41 us  [swap_col(): return lax.ppermute(a, 'col', [(0, 1), (1, 0)])]
    convert_element_type x19, other arithmetic: 16.3 us -> 23.3 us  [add(): return total if wide else total.astype(BF)]
    unnamed x233 -> x255, local copies, waits for them, and re-layouts: 20.5 us -> 21.1 us
  transfers between devices with their start and end apart: 106 -> 106, of which waited for: 39 -> 40; matrix products, arithmetic and copies ran while one was open for 20% -> 22% of each run, Pallas kernels for 23% -> 23%
where the time goes in v4:
time: 569 us; the launch traced here: 559 us
  waiting for transfers between devices  174 us (31%)
  Pallas kernels  130 us (23%)
  starting transfers between devices  90.8 us (16%)
  other arithmetic  75 us (13%)
  local copies, waits for them, and re-layouts  40.3 us (7%)
  matrix products  32.2 us (6%)
  between operations  16.2 us (3%)
    ppermute x79, waiting for transfers between devices, swap_row(): return lax.ppermute(a, 'row', [(i, i ^ bit) for i in range(R)])  102 us
    ppermute x18, waiting for transfers between devices, swap_col(): return lax.ppermute(a, 'col', [(0, 1), (1, 0)])  66.8 us
    pallas_call x2, Pallas kernels, feed(): pl.pallas_call(functools.partial(feed_body, rows_n=R, parts=parts, near=n...  51.6 us
    ppermute x79, starting transfers between devices, swap_row(): return lax.ppermute(a, 'row', [(i, i ^ bit) for i in range(R)])  45.6 us
    ppermute x18, starting transfers between devices, swap_col(): return lax.ppermute(a, 'col', [(0, 1), (1, 0)])  41 us
    convert_element_type x19, other arithmetic, add(): return total if wide else total.astype(BF)  23.3 us
    unnamed x255, local copies, waits for them, and re-layouts  21.1 us
    pallas_call x1, Pallas kernels, late_weight_grads(): pl.pallas_call(functools.partial(late_weight_body, rows_n=rows_n), grid=(...  19.5 us
  transfers between devices with their start and end apart: 106, of which 40 were waited for; matrix products, arithmetic and copies ran while one was open for 22% of the time, Pallas kernels for 23%

profile of v4, /device:TPU:0, one launch (start us, length us, event | category | flops | bytes accessed | tf_op | source)
XLA Modules:
  0.0 559.1 jit_solution(13592259319386841776)
XLA Ops:
  9.3 2.6 collective-permute-start.4
  16.9 2.6 fusion.3
  27.0 2.7 convert_element_type.509.refs_8_
  38.2 2.6 convolution_convert_fusion.2
  47.3 4.2 cut_weights.3
  58.1 7.4 %collective-permute-done.1 = bf16[256,1024]{1,0:T(8,128)(2,1)} collective-permute-done((bf16[256,1024]{1,0:T(8,128)(2,1)}, bf16[256,1024]{1,0:T(8,128)(2,1)}, u32[]{:S(2)}, u32[]{:S(2)}) %collective-permute-start.1) | collective-permute-done | bytes 524320 | tf_op jit(solution)/shard_map/ppermute | solution.py:705
  79.7 5.4 attend.2
  86.4 22.1 %collective-permute-done.20 = bf16[256,1024]{1,0:T(8,128)(2,1)S(1)} collective-permute-done((bf16[256,1024]{1,0:T(8,128)(2,1)S(1)}, bf16[256,1024]{1,0:T(8,128)(2,1)S(1)}, u32[]{:S(2)}, u32[]{:S(2)}) %collective-permute-start.20) | collective-permute-done | bytes 524320 | tf_op jit(solution)/shard_map/ppermute | solution.py:705
  111.6 5.5 attend.3
  120.3 11.7 %collective-permute-done.24 = bf16[256,1024]{1,0:T(8,128)(2,1)S(1)} collective-permute-done((bf16[256,1024]{1,0:T(8,128)(2,1)}, bf16[256,1024]{1,0:T(8,128)(2,1)S(1)}, u32[]{:S(2)}, u32[]{:S(2)}) %collective-permute-start.24) | collective-permute-done | bytes 524320 | tf_op jit(solution)/shard_map/ppermute | solution.py:705
  134.1 5.8 %collective-permute-start.28 = (bf16[1024,512]{1,0:T(8,128)(2,1)}, bf16[1024,512]{1,0:T(8,128)(2,1)}, u32[]{:S(2)}, u32[]{:S(2)}) collective-permute-start(bf16[1024,512]{1,0:T(8,128)(2,1)} %collective-permute-done.23.refs_10_), channel_id=1, source_target_pairs={{0,1},{1,0},{2,3},{3,2},{4,5},{5,4},{6,7},{7,6},{8,9},{9,8},{10,11... | collective-permute-start | bytes 3145736 | tf_op jit(solution)/shard_map/ppermute | solution.py:708
  156.4 7.5 %collective-permute-done.28.refs_10_ = bf16[1024,512]{1,0:T(8,128)(2,1)} collective-permute-done((bf16[1024,512]{1,0:T(8,128)(2,1)}, bf16[1024,512]{1,0:T(8,128)(2,1)}, u32[]{:S(2)}, u32[]{:S(2)}) %collective-permute-start.28) | collective-permute-done | bytes 1048608 | tf_op jit(solution)/shard_map/ppermute | solution.py:708
  168.5 11.1 %collective-permute-done.44.refs_4_ = bf16[512,512]{1,0:T(8,128)(2,1)S(1)} collective-permute-done((bf16[512,512]{1,0:T(8,128)(2,1)S(1)}, bf16[512,512]{1,0:T(8,128)(2,1)S(1)}, u32[]{:S(2)}, u32[]{:S(2)}) %collective-permute-start.44) | collective-permute-done | bytes 524320 | tf_op jit(solution)/shard_map/ppermute | solution.py:708
  181.4 8.3 %collective-permute-done.35.refs_0_ = bf16[512,512]{1,0:T(8,128)(2,1)S(1)} collective-permute-done((bf16[512,512]{1,0:T(8,128)(2,1)}, bf16[512,512]{1,0:T(8,128)(2,1)S(1)}, u32[]{:S(2)}, u32[]{:S(2)}) %collective-permute-start.35) | collective-permute-done | bytes 524320 | tf_op jit(solution)/shard_map/ppermute | solution.py:708
  194.3 8.3 %collective-permute-done.46.refs_6_ = bf16[512,512]{1,0:T(8,128)(2,1)S(1)} collective-permute-done((bf16[512,512]{1,0:T(8,128)(2,1)}, bf16[512,512]{1,0:T(8,128)(2,1)S(1)}, u32[]{:S(2)}, u32[]{:S(2)}) %collective-permute-start.46) | collective-permute-done | bytes 524320 | tf_op jit(solution)/shard_map/ppermute | solution.py:708
  206.8 25.7 %feed.3 = (bf16[1024,704]{1,0:T(8,128)(2,1)}, bf16[1024,704]{1,0:T(8,128)(2,1)}, bf16[1024,704]{1,0:T(8,128)(2,1)}, bf16[1024,512]{1,0:T(8,128)(2,1)}, bf16[1024...) custom-call(bf16[512,512]{1,0:T(8,128)(2,1)} %copy-done.109, ...), custom_call_target="tpu_custom_call" | custom-call | flops 14763950080 | bytes 29622272 | tf_op jit(solution)/shard_map/feed/pallas_call | solution.py:373
  232.8 25.8 %feed.2 = (bf16[1024,704]{1,0:T(8,128)(2,1)}, bf16[1024,704]{1,0:T(8,128)(2,1)}, bf16[1024,704]{1,0:T(8,128)(2,1)}, bf16[1024,512]{1,0:T(8,128)(2,1)}, bf16[1024...) custom-call(bf16[512,512]{1,0:T(8,128)(2,1)} %get-tuple-element.299., ...), custom_call_target="tpu_custom_call" | custom-call | flops 14763950080 | bytes 29622272 | tf_op jit(solution)/shard_map/feed/pallas_call | solution.py:373
  260.0 9.3 %feed_weights.1 = bf16[4,4,704,128]{3,2,1,0:T(8,128)(2,1)} custom-call(bf16[1024,2048]{1,0:T(8,128)(2,1)} %get-tuple-element.167.x0, bf16[1024,2048]{1,0:T(8,128)(2,1)} %get-tuple-element.168.x1, bf16[1024,704]{1,0:T(8,128)(2,1)S(1)} %copy-done.12, bf16[1024,704]{1,0:T(8,128)(2,1)S(1)} %copy-done.11), custom_call_target="tpu_custom_call" | custom-call | flops 5905580032 | bytes 14155776 | tf_op jit(solution)/shard_map/feed_weights/pallas_call | solution.py:415
  271.3 2.6 add_convert_fusion.29
  282.2 19.5 %late_weights.1 = bf16[4,2,4,704,128]{4,3,2,1,0:T(8,128)(2,1)} custom-call(bf16[1024,2048]{1,0:T(8,128)(2,1)} %get-tuple-element.167.x0, bf16[1024,2048]{1,0:T(8,128)(2,1)} %get-tuple-element.168.x1, bf16[1024,704]{1,0:T(8,128)(2,1)} %get-tuple-element.175.u0, bf16[1024,704]{1,0:T(8,128)(2,1)} %get-tuple-element.176.u1, ...), custom_call_target="tpu_custom_call" | custom-call | flops 11811160064 | bytes 28311552 | tf_op jit(solution)/shard_map/late_weights/pallas_call | solution.py:489
  312.2 9.5 %collective-permute-done.56 = bf16[512,512]{1,0:T(8,128)(2,1)S(1)} collective-permute-done((bf16[512,512]{1,0:T(8,128)(2,1)S(1)}, bf16[512,512]{1,0:T(8,128)(2,1)S(1)}, u32[]{:S(2)}, u32[]{:S(2)}) %collective-permute-start.56) | collective-permute-done | bytes 524320 | tf_op jit(solution)/shard_map/ppermute | solution.py:705
  327.6 3.1 collective-permute-done.61
  330.7 3.9 fusion.43
  334.7 2.9 convolution_convert_fusion.1
  337.9 2.5 convolution_convert_fusion
  349.4 9.0 %collective-permute-done.63 = bf16[256,1024]{1,0:T(8,128)(2,1)} collective-permute-done((bf16[256,1024]{1,0:T(8,128)(2,1)}, bf16[256,1024]{1,0:T(8,128)(2,1)}, u32[]{:S(2)}, u32[]{:S(2)}) %collective-permute-start.63) | collective-permute-done | bytes 524320 | tf_op jit(solution)/shard_map/ppermute | solution.py:705
  361.0 6.7 %attend_back.2 = (bf16[256,1024]{1,0:T(8,128)(2,1)}, f32[8,256,128]{2,1,0:T(8,128)}, f32[8,256,128]{2,1,0:T(8,128)}) custom-call(s32[2]{0:T(128)} %pad_add_fusion.where, s32[2048]{0:T(1024)} %seq_ref.7, s32[2048]{0:T(1024)} %block_ref.7, bf16[256,1024]{1,0:T(8,128)(2,1)} %get-tuple-element.156.rot_ref, bf16[256,1024]{1,0:T(8,128)(2,1)} %add_convert_fusion.19.grad_ref, ...), custom_call_target="tpu_custom_call" | custom-call | flops 2684354560 | bytes 5242880 | tf_op jit(solution)/shard_map/attend_back/pallas_call | solution.py:202
  367.8 13.9 %down_products.1 = (bf16[1024,512]{1,0:T(8,128)(2,1)}, bf16[1024,512]{1,0:T(8,128)(2,1)}, bf16[1024,512]{1,0:T(8,128)(2,1)}, bf16[1024,512]{1,0:T(8,128)(2,1)}, ...) custom-call(bf16[1024,704]{1,0:T(8,128)(2,1)} %get-tuple-element.197, ...), custom_call_target="tpu_custom_call" | custom-call | tf_op jit(solution)/shard_map/down_products/pallas_call | solution.py:535
  386.7 2.7 fusion.42
  389.4 8.3 %collective-permute-start.96 = (bf16[1024,512]{1,0:T(8,128)(2,1)}, bf16[1024,512]{1,0:T(8,128)(2,1)}, u32[]{:S(2)}, u32[]{:S(2)}) collective-permute-start(bf16[1024,512]{1,0:T(8,128)(2,1)} %convolution_convert_fusion.4), channel_id=1, source_target_pairs={{0,1},{1,0},{2,3},{3,2},{4,5},{5,4},{6,7},{7,6},{8,9},{9,8},{10,11... | collective-permute-start | bytes 3145736 | tf_op jit(solution)/shard_map/ppermute | solution.py:708
  409.0 8.1 %collective-permute-start.74 = (bf16[512,1024]{1,0:T(8,128)(2,1)}, bf16[512,1024]{1,0:T(8,128)(2,1)}, u32[]{:S(2)}, u32[]{:S(2)}) collective-permute-start(bf16[512,1024]{1,0:T(8,128)(2,1)} %convolution_convert_fusion.5), channel_id=1, source_target_pairs={{0,1},{1,0},{2,3},{3,2},{4,5},{5,4},{6,7},{7,6},{8,9},{9,8},{10,11... | collective-permute-start | bytes 3145736 | tf_op jit(solution)/shard_map/ppermute | solution.py:708
  419.1 7.7 %attend_back.3 = (bf16[256,1024]{1,0:T(8,128)(2,1)}, f32[8,256,128]{2,1,0:T(8,128)}, f32[8,256,128]{2,1,0:T(8,128)}) custom-call(s32[2]{0:T(128)} %pad_add_fusion.where, s32[2048]{0:T(1024)} %seq_ref.7, s32[2048]{0:T(1024)} %block_ref.7, bf16[256,1024]{1,0:T(8,128)(2,1)} %get-tuple-element.207.rot_ref, bf16[256,1024]{1,0:T(8,128)(2,1)} %add_convert_fusion.14.grad_ref, ...), custom_call_target="tpu_custom_call" | custom-call | flops 2684354560 | bytes 5242880 | tf_op jit(solution)/shard_map/attend_back/pallas_call | solution.py:202
  432.0 3.2 add_convert_fusion
  435.2 8.7 %collective-permute-done.74 = bf16[512,1024]{1,0:T(8,128)(2,1)} collective-permute-done((bf16[512,1024]{1,0:T(8,128)(2,1)}, bf16[512,1024]{1,0:T(8,128)(2,1)}, u32[]{:S(2)}, u32[]{:S(2)}) %collective-permute-start.74) | collective-permute-done | bytes 1048608 | tf_op jit(solution)/shard_map/ppermute | solution.py:708
  449.4 2.5 fusion.52
  452.1 2.7 collective-permute-done.86
  455.8 4.1 collective-permute-done.83
  460.0 4.0 collective-permute-done.87
  464.6 4.8 collective-permute-done.88
  478.0 2.6 fusion.31
  491.9 2.6 fusion.7
  496.4 4.1 collective-permute-done.94
  501.4 3.5 add_convert_fusion.1
  510.9 9.2 %collective-permute-done.75 = bf16[512,512]{1,0:T(8,128)(2,1)S(1)} collective-permute-done((bf16[512,512]{1,0:T(8,128)(2,1)}, bf16[512,512]{1,0:T(8,128)(2,1)S(1)}, u32[]{:S(2)}, u32[]{:S(2)}) %collective-permute-start.75) | collective-permute-done | bytes 524320 | tf_op jit(solution)/shard_map/ppermute | solution.py:708
  520.1 8.0 %collective-permute-done.76 = bf16[512,512]{1,0:T(8,128)(2,1)S(1)} collective-permute-done((bf16[512,512]{1,0:T(8,128)(2,1)}, bf16[512,512]{1,0:T(8,128)(2,1)S(1)}, u32[]{:S(2)}, u32[]{:S(2)}) %collective-permute-start.76) | collective-permute-done | bytes 524320 | tf_op jit(solution)/shard_map/ppermute | solution.py:708
  531.9 2.9 collective-permute-done.99.refs_3_
  534.8 4.3 finish_weights.1
  539.1 7.3 %collective-permute-done.77 = bf16[512,512]{1,0:T(8,128)(2,1)S(1)} collective-permute-done((bf16[512,512]{1,0:T(8,128)(2,1)S(1)}, bf16[512,512]{1,0:T(8,128)(2,1)S(1)}, u32[]{:S(2)}, u32[]{:S(2)}) %collective-permute-start.77) | collective-permute-done | bytes 524320 | tf_op jit(solution)/shard_map/ppermute | solution.py:705
  (573 shorter events, 199.0 us)
Async XLA Ops:
  7.2 199.6 %all-gather.5.cloned.1.call-start = ((), (), s32[]{:S(2)}) async-start(), calls=%async_computation.8 | async-start | bytes 3604480 | tf_op jit(solution)/shard_map/all_gather | solution.py:894
  9.3 28.3 %collective-permute-start.4 = (bf16[512,1024]{1,0:T(8,128)(2,1)}, bf16[512,1024]{1,0:T(8,128)(2,1)}, u32[]{:S(2)}, u32[]{:S(2)}) collective-permute-start(bf16[512,1024]{1,0:T(8,128)(2,1)} %param.20), channel_id=1, source_target_pairs={{0,1},{1,0},{2,3},{3,2},{4,5},{5,4},{6,7},{7,6},{8,9},{9,8},{10,11... | collective-permute-start | bytes 3145736 | tf_op jit(solution)/shard_map/ppermute | solution.py:708
  23.5 19.0 %collective-permute-start = (bf16[512,1024]{1,0:T(8,128)(2,1)}, bf16[512,1024]{1,0:T(8,128)(2,1)}, u32[]{:S(2)}, u32[]{:S(2)}) collective-permute-start(bf16[512,1024]{1,0:T(8,128)(2,1)} %slice.355), channel_id=1, source_target_pairs={{0,2},{2,0},{4,6},{6,4},{1,3},{3,1},{5,7},{7,5},{8,10},{10,8},{12,... | collective-permute-start | bytes 3145736 | tf_op jit(solution)/shard_map/ppermute | solution.py:705
  36.4 18.0 %collective-permute-start.8 = (bf16[2,704,128]{2,1,0:T(8,128)(2,1)S(1)}, bf16[2,704,128]{2,1,0:T(8,128)(2,1)S(1)}, u32[]{:S(2)}, u32[]{:S(2)}) collective-permute-start(bf16[2,704,128]{2,1,0:T(8,128)(2,1)S(1)} %get-tuple-element.129), channel_id=1, source_target_pairs={{0,4},{2,6},{4,0},{6,2},{1,5},{3,7},{5,1},{7,3},{8,12},{10,14},{12... | collective-permute-start | bytes 1081352 | tf_op jit(solution)/shard_map/ppermute | solution.py:705
  37.6 18.0 %collective-permute-start.9 = (bf16[2,704,128]{2,1,0:T(8,128)(2,1)S(1)}, bf16[2,704,128]{2,1,0:T(8,128)(2,1)S(1)}, u32[]{:S(2)}, u32[]{:S(2)}) collective-permute-start(bf16[2,704,128]{2,1,0:T(8,128)(2,1)S(1)} %get-tuple-element.130), channel_id=1, source_target_pairs={{0,6},{2,4},{4,2},{6,0},{1,7},{3,5},{5,3},{7,1},{8,14},{10,12},{12... | collective-permute-start | bytes 1081352 | tf_op jit(solution)/shard_map/ppermute | solution.py:705
  37.6 30.8 %collective-permute-start.5 = (bf16[1024,512]{1,0:T(8,128)(2,1)}, bf16[1024,512]{1,0:T(8,128)(2,1)}, u32[]{:S(2)}, u32[]{:S(2)}) collective-permute-start(bf16[1024,512]{1,0:T(8,128)(2,1)} %param.22), channel_id=1, source_target_pairs={{0,1},{1,0},{2,3},{3,2},{4,5},{5,4},{6,7},{7,6},{8,9},{9,8},{10,11... | collective-permute-start | bytes 3145736 | tf_op jit(solution)/shard_map/ppermute | solution.py:708
  41.9 29.3 %collective-permute-start.19 = (bf16[512,1024]{1,0:T(8,128)(2,1)}, bf16[512,1024]{1,0:T(8,128)(2,1)}, u32[]{:S(2)}, u32[]{:S(2)}) collective-permute-start(bf16[512,1024]{1,0:T(8,128)(2,1)} %slice.367), channel_id=1, source_target_pairs={{0,2},{2,0},{4,6},{6,4},{1,3},{3,1},{5,7},{7,5},{8,10},{10,8},{12,... | collective-permute-start | bytes 3145736 | tf_op jit(solution)/shard_map/ppermute | solution.py:705
  45.9 19.7 %collective-permute-start.1 = (bf16[256,1024]{1,0:T(8,128)(2,1)}, bf16[256,1024]{1,0:T(8,128)(2,1)}, u32[]{:S(2)}, u32[]{:S(2)}) collective-permute-start(bf16[256,1024]{1,0:T(8,128)(2,1)} %slice.357), channel_id=1, source_target_pairs={{0,4},{2,6},{4,0},{6,2},{1,5},{3,7},{5,1},{7,3},{8,12},{10,14},{12... | collective-permute-start | bytes 1572872 | tf_op jit(solution)/shard_map/ppermute | solution.py:705
  54.4 32.0 %collective-permute-start.21 = (bf16[2,704,512]{2,1,0:T(8,128)(2,1)}, bf16[2,704,512]{2,1,0:T(8,128)(2,1)}, u32[]{:S(2)}, u32[]{:S(2)}) collective-permute-start(bf16[2,704,512]{2,1,0:T(8,128)(2,1)} %get-tuple-element.135), channel_id=1, source_target_pairs={{0,2},{2,0},{4,6},{6,4},{1,3},{3,1},{5,7},{7,5},{8,10},{10,8},{12,... | collective-permute-start | bytes 4325384 | tf_op jit(solution)/shard_map/ppermute | solution.py:705
  70.6 39.9 %collective-permute-start.23 = (bf16[1024,512]{1,0:T(8,128)(2,1)}, bf16[1024,512]{1,0:T(8,128)(2,1)}, u32[]{:S(2)}, u32[]{:S(2)}) collective-permute-start(bf16[1024,512]{1,0:T(8,128)(2,1)} %convert_element_type.509.refs_8_), channel_id=1, source_target_pairs={{0,4},{2,6},{4,0},{6,2},{1,5},{3,7},{5,1},{7,3},{8,12},{10,14},{12... | collective-permute-start | bytes 3145736 | tf_op jit(solution)/shard_map/ppermute | solution.py:705
  71.2 39.3 %collective-permute-start.22 = (bf16[1024,512]{1,0:T(8,128)(2,1)}, bf16[1024,512]{1,0:T(8,128)(2,1)}, u32[]{:S(2)}, u32[]{:S(2)}) collective-permute-start(bf16[1024,512]{1,0:T(8,128)(2,1)} %convert_element_type.509.refs_8_), channel_id=1, source_target_pairs={{0,1},{1,0},{2,3},{3,2},{4,5},{5,4},{6,7},{7,6},{8,9},{9,8},{10,11... | collective-permute-start | bytes 3145736 | tf_op jit(solution)/shard_map/ppermute | solution.py:708
  73.4 35.1 %collective-permute-start.20 = (bf16[256,1024]{1,0:T(8,128)(2,1)S(1)}, bf16[256,1024]{1,0:T(8,128)(2,1)S(1)}, u32[]{:S(2)}, u32[]{:S(2)}) collective-permute-start(bf16[256,1024]{1,0:T(8,128)(2,1)S(1)} %slice.369), channel_id=1, source_target_pairs={{0,4},{2,6},{4,0},{6,2},{1,5},{3,7},{5,1},{7,3},{8,12},{10,14},{12... | collective-permute-start | bytes 1572872 | tf_op jit(solution)/shard_map/ppermute | solution.py:705
  75.0 131.8 %all-gather.7.cloned.1.call-start = ((), (), s32[]{:S(2)}) async-start(), calls=%async_computation.9 | async-start | bytes 1802240 | tf_op jit(solution)/shard_map/all_gather | solution.py:901
  85.1 34.2 %collective-permute-start.17 = (bf16[256,1024]{1,0:T(8,128)(2,1)}, bf16[256,1024]{1,0:T(8,128)(2,1)S(1)}, u32[]{:S(2)}, u32[]{:S(2)}) collective-permute-start(bf16[256,1024]{1,0:T(8,128)(2,1)} %get-tuple-element.132.att_ref), channel_id=1, source_target_pairs={{0,4},{2,6},{4,0},{6,2},{1,5},{3,7},{5,1},{7,3},{8,12},{10,14},{12... | collective-permute-start | bytes 1572872 | tf_op jit(solution)/shard_map/ppermute | solution.py:705
  120.3 19.7 %collective-permute-start.18 = (bf16[512,1024]{1,0:T(8,128)(2,1)}, bf16[512,1024]{1,0:T(8,128)(2,1)}, u32[]{:S(2)}, u32[]{:S(2)}) collective-permute-start(bf16[512,1024]{1,0:T(8,128)(2,1)} %pad_maximum_fusion.3), channel_id=1, source_target_pairs={{0,2},{2,0},{4,6},{6,4},{1,3},{3,1},{5,7},{7,5},{8,10},{10,8},{12,... | collective-permute-start | bytes 3145736 | tf_op jit(solution)/shard_map/ppermute | solution.py:705
  132.3 21.9 %collective-permute-start.39 = (bf16[176,512]{1,0:T(8,128)(2,1)S(1)}, bf16[176,512]{1,0:T(8,128)(2,1)S(1)}, u32[]{:S(2)}, u32[]{:S(2)}) collective-permute-start(bf16[176,512]{1,0:T(8,128)(2,1)S(1)} %get-tuple-element.150), channel_id=1, source_target_pairs={{0,4},{2,6},{4,0},{6,2},{1,5},{3,7},{5,1},{7,3},{8,12},{10,14},{12... | collective-permute-start | bytes 540680 | tf_op jit(solution)/shard_map/ppermute | solution.py:705
  133.7 20.5 %collective-permute-start.40 = (bf16[176,512]{1,0:T(8,128)(2,1)S(1)}, bf16[176,512]{1,0:T(8,128)(2,1)S(1)}, u32[]{:S(2)}, u32[]{:S(2)}) collective-permute-start(bf16[176,512]{1,0:T(8,128)(2,1)S(1)} %get-tuple-element.151), channel_id=1, source_target_pairs={{0,6},{2,4},{4,2},{6,0},{1,7},{3,5},{5,3},{7,1},{8,14},{10,12},{12... | collective-permute-start | bytes 540680 | tf_op jit(solution)/shard_map/ppermute | solution.py:705
  134.1 29.8 %collective-permute-start.28 = (bf16[1024,512]{1,0:T(8,128)(2,1)}, bf16[1024,512]{1,0:T(8,128)(2,1)}, u32[]{:S(2)}, u32[]{:S(2)}) collective-permute-start(bf16[1024,512]{1,0:T(8,128)(2,1)} %collective-permute-done.23.refs_10_), channel_id=1, source_target_pairs={{0,1},{1,0},{2,3},{3,2},{4,5},{5,4},{6,7},{7,6},{8,9},{9,8},{10,11... | collective-permute-start | bytes 3145736 | tf_op jit(solution)/shard_map/ppermute | solution.py:708
  155.0 206.0 %reduce-scatter.5.cloned.1.call-start = ((), (), s32[]{:S(2)}) async-start(), calls=%async_computation.4 | async-start | bytes 3604480 | tf_op jit(solution)/shard_map/reduce_scatter | solution.py:948
  166.5 24.6 %collective-permute-start.38 = (bf16[704,512]{1,0:T(8,128)(2,1)S(1)}, bf16[704,512]{1,0:T(8,128)(2,1)S(1)}, u32[]{:S(2)}, u32[]{:S(2)}) collective-permute-start(bf16[704,512]{1,0:T(8,128)(2,1)S(1)} %copy-done.10), channel_id=1, source_target_pairs={{0,2},{2,0},{4,6},{6,4},{1,3},{3,1},{5,7},{7,5},{8,10},{10,8},{12,... | collective-permute-start | bytes 2162696 | tf_op jit(solution)/shard_map/ppermute | solution.py:705
  168.2 21.4 %collective-permute-start.35 = (bf16[512,512]{1,0:T(8,128)(2,1)}, bf16[512,512]{1,0:T(8,128)(2,1)S(1)}, u32[]{:S(2)}, u32[]{:S(2)}) collective-permute-start(bf16[512,512]{1,0:T(8,128)(2,1)} %get-tuple-element.299.refs_0_), channel_id=1, source_target_pairs={{0,1},{1,0},{2,3},{3,2},{4,5},{5,4},{6,7},{7,6},{8,9},{9,8},{10,11... | collective-permute-start | bytes 1572872 | tf_op jit(solution)/shard_map/ppermute | solution.py:708
  168.5 24.4 %collective-permute-start.32 = (bf16[512,512]{1,0:T(8,128)(2,1)S(1)}, bf16[512,512]{1,0:T(8,128)(2,1)S(1)}, u32[]{:S(2)}, u32[]{:S(2)}) collective-permute-start(bf16[512,512]{1,0:T(8,128)(2,1)S(1)} %get-tuple-element.298.refs_4_), channel_id=1, source_target_pairs={{0,2},{2,0},{4,6},{6,4},{1,3},{3,1},{5,7},{7,5},{8,10},{10,8},{12,... | collective-permute-start | bytes 1572872 | tf_op jit(solution)/shard_map/ppermute | solution.py:705
  203.5 29.0 %collective-permute-start.29 = (bf16[512,512]{1,0:T(8,128)(2,1)}, bf16[512,512]{1,0:T(8,128)(2,1)}, u32[]{:S(2)}, u32[]{:S(2)}) collective-permute-start(bf16[512,512]{1,0:T(8,128)(2,1)} %get-tuple-element.299.refs_0_), channel_id=1, source_target_pairs={{0,2},{2,0},{4,6},{6,4},{1,3},{3,1},{5,7},{7,5},{8,10},{10,8},{12,... | collective-permute-start | bytes 1572872 | tf_op jit(solution)/shard_map/ppermute | solution.py:705
  204.6 28.2 %collective-permute-start.36 = (bf16[1024,512]{1,0:T(8,128)(2,1)}, bf16[1024,512]{1,0:T(8,128)(2,1)}, u32[]{:S(2)}, u32[]{:S(2)}) collective-permute-start(bf16[1024,512]{1,0:T(8,128)(2,1)} %convert_element_type.509.refs_8_), channel_id=1, source_target_pairs={{0,2},{2,0},{4,6},{6,4},{1,3},{3,1},{5,7},{7,5},{8,10},{10,8},{12,... | collective-permute-start | bytes 3145736 | tf_op jit(solution)/shard_map/ppermute | solution.py:705
  205.4 27.3 %collective-permute-start.37 = (bf16[1024,512]{1,0:T(8,128)(2,1)}, bf16[1024,512]{1,0:T(8,128)(2,1)}, u32[]{:S(2)}, u32[]{:S(2)}) collective-permute-start(bf16[1024,512]{1,0:T(8,128)(2,1)} %collective-permute-done.23.refs_10_), channel_id=1, source_target_pairs={{0,2},{2,0},{4,6},{6,4},{1,3},{3,1},{5,7},{7,5},{8,10},{10,8},{12,... | collective-permute-start | bytes 3145736 | tf_op jit(solution)/shard_map/ppermute | solution.py:705
  206.2 26.5 %collective-permute-start.34 = (bf16[512,512]{1,0:T(8,128)(2,1)}, bf16[512,512]{1,0:T(8,128)(2,1)}, u32[]{:S(2)}, u32[]{:S(2)}) collective-permute-start(bf16[512,512]{1,0:T(8,128)(2,1)} %collective-permute-done.33.refs_6_), channel_id=1, source_target_pairs={{0,2},{2,0},{4,6},{6,4},{1,3},{3,1},{5,7},{7,5},{8,10},{10,8},{12,... | collective-permute-start | bytes 1572872 | tf_op jit(solution)/shard_map/ppermute | solution.py:705
  206.4 26.4 %collective-permute-start.31 = (bf16[512,512]{1,0:T(8,128)(2,1)}, bf16[512,512]{1,0:T(8,128)(2,1)}, u32[]{:S(2)}, u32[]{:S(2)}) collective-permute-start(bf16[512,512]{1,0:T(8,128)(2,1)} %collective-permute-done.30.refs_2_), channel_id=1, source_target_pairs={{0,2},{2,0},{4,6},{6,4},{1,3},{3,1},{5,7},{7,5},{8,10},{10,8},{12,... | collective-permute-start | bytes 1572872 | tf_op jit(solution)/shard_map/ppermute | solution.py:705
  232.5 37.8 %collective-permute-start.52 = (bf16[1024,512]{1,0:T(8,128)(2,1)}, bf16[1024,512]{1,0:T(8,128)(2,1)S(1)}, u32[]{:S(2)}, u32[]{:S(2)}) collective-permute-start(bf16[1024,512]{1,0:T(8,128)(2,1)} %get-tuple-element.162), channel_id=1, source_target_pairs={{0,2},{2,0},{4,6},{6,4},{1,3},{3,1},{5,7},{7,5},{8,10},{10,8},{12,... | collective-permute-start | bytes 3145736 | tf_op jit(solution)/shard_map/ppermute | solution.py:705
  269.4 211.2 %reduce-scatter.7.cloned.1.call-start = ((), (), s32[]{:S(2)}) async-start(), calls=%async_computation.5 | async-start | bytes 7208960 | tf_op jit(solution)/shard_map/reduce_scatter | solution.py:948
  278.2 25.5 %collective-permute-start.57 = (bf16[512,512]{1,0:T(8,128)(2,1)}, bf16[512,512]{1,0:T(8,128)(2,1)}, u32[]{:S(2)}, u32[]{:S(2)}) collective-permute-start(bf16[512,512]{1,0:T(8,128)(2,1)} %get-tuple-element.186), channel_id=1, source_target_pairs={{0,4},{2,6},{4,0},{6,2},{1,5},{3,7},{5,1},{7,3},{8,12},{10,14},{12... | collective-permute-start | bytes 1572872 | tf_op jit(solution)/shard_map/ppermute | solution.py:705
  279.8 23.9 %collective-permute-start.58 = (bf16[512,512]{1,0:T(8,128)(2,1)}, bf16[512,512]{1,0:T(8,128)(2,1)}, u32[]{:S(2)}, u32[]{:S(2)}) collective-permute-start(bf16[512,512]{1,0:T(8,128)(2,1)} %get-tuple-element.189), channel_id=1, source_target_pairs={{0,4},{2,6},{4,0},{6,2},{1,5},{3,7},{5,1},{7,3},{8,12},{10,14},{12... | collective-permute-start | bytes 1572872 | tf_op jit(solution)/shard_map/ppermute | solution.py:705
  280.2 26.0 %collective-permute-start.54 = (bf16[512,512]{1,0:T(8,128)(2,1)}, bf16[512,512]{1,0:T(8,128)(2,1)}, u32[]{:S(2)}, u32[]{:S(2)}) collective-permute-start(bf16[512,512]{1,0:T(8,128)(2,1)} %get-tuple-element.166), channel_id=1, source_target_pairs={{0,1},{1,0},{2,3},{3,2},{4,5},{5,4},{6,7},{7,6},{8,9},{9,8},{10,11... | collective-permute-start | bytes 1572872 | tf_op jit(solution)/shard_map/ppermute | solution.py:708
  282.1 24.1 %collective-permute-start.55 = (bf16[512,512]{1,0:T(8,128)(2,1)}, bf16[512,512]{1,0:T(8,128)(2,1)}, u32[]{:S(2)}, u32[]{:S(2)}) collective-permute-start(bf16[512,512]{1,0:T(8,128)(2,1)} %get-tuple-element.181), channel_id=1, source_target_pairs={{0,1},{1,0},{2,3},{3,2},{4,5},{5,4},{6,7},{7,6},{8,9},{9,8},{10,11... | collective-permute-start | bytes 1572872 | tf_op jit(solution)/shard_map/ppermute | solution.py:708
  327.5 220.8 %reduce-scatter.11.cloned.1.call-start = ((), (), s32[]{:S(2)}) async-start(), calls=%async_computation.7 | async-start | bytes 1310720 | tf_op jit(solution)/shard_map/reduce_scatter | solution.py:948
  360.4 29.0 %collective-permute-start.69 = (bf16[256,1024]{1,0:T(8,128)(2,1)}, bf16[256,1024]{1,0:T(8,128)(2,1)}, u32[]{:S(2)}, u32[]{:S(2)}) collective-permute-start(bf16[256,1024]{1,0:T(8,128)(2,1)} %slice.389), channel_id=1, source_target_pairs={{0,4},{2,6},{4,0},{6,2},{1,5},{3,7},{5,1},{7,3},{8,12},{10,14},{12... | collective-permute-start | bytes 1572872 | tf_op jit(solution)/shard_map/ppermute | solution.py:705
  381.8 16.9 %collective-permute-start.64 = (bf16[1024,512]{1,0:T(8,128)(2,1)}, bf16[1024,512]{1,0:T(8,128)(2,1)S(1)}, u32[]{:S(2)}, u32[]{:S(2)}) collective-permute-start(bf16[1024,512]{1,0:T(8,128)(2,1)} %get-tuple-element.200), channel_id=1, source_target_pairs={{0,2},{2,0},{4,6},{6,4},{1,3},{3,1},{5,7},{7,5},{8,10},{10,8},{12,... | collective-permute-start | bytes 3145736 | tf_op jit(solution)/shard_map/ppermute | solution.py:705
  389.4 39.3 %collective-permute-start.96 = (bf16[1024,512]{1,0:T(8,128)(2,1)}, bf16[1024,512]{1,0:T(8,128)(2,1)}, u32[]{:S(2)}, u32[]{:S(2)}) collective-permute-start(bf16[1024,512]{1,0:T(8,128)(2,1)} %convolution_convert_fusion.4), channel_id=1, source_target_pairs={{0,1},{1,0},{2,3},{3,2},{4,5},{5,4},{6,7},{7,6},{8,9},{9,8},{10,11... | collective-permute-start | bytes 3145736 | tf_op jit(solution)/shard_map/ppermute | solution.py:708
  404.6 24.1 %collective-permute-start.78 = (bf16[512,512]{1,0:T(8,128)(2,1)}, bf16[512,512]{1,0:T(8,128)(2,1)}, u32[]{:S(2)}, u32[]{:S(2)}) collective-permute-start(bf16[512,512]{1,0:T(8,128)(2,1)} %get-tuple-element.225), channel_id=1, source_target_pairs={{0,4},{2,6},{4,0},{6,2},{1,5},{3,7},{5,1},{7,3},{8,12},{10,14},{12... | collective-permute-start | bytes 1572872 | tf_op jit(solution)/shard_map/ppermute | solution.py:705
  406.1 23.9 %collective-permute-start.79 = (bf16[512,512]{1,0:T(8,128)(2,1)}, bf16[512,512]{1,0:T(8,128)(2,1)}, u32[]{:S(2)}, u32[]{:S(2)}) collective-permute-start(bf16[512,512]{1,0:T(8,128)(2,1)} %get-tuple-element.227), channel_id=1, source_target_pairs={{0,4},{2,6},{4,0},{6,2},{1,5},{3,7},{5,1},{7,3},{8,12},{10,14},{12... | collective-permute-start | bytes 1572872 | tf_op jit(solution)/shard_map/ppermute | solution.py:705
  409.0 34.9 %collective-permute-start.74 = (bf16[512,1024]{1,0:T(8,128)(2,1)}, bf16[512,1024]{1,0:T(8,128)(2,1)}, u32[]{:S(2)}, u32[]{:S(2)}) collective-permute-start(bf16[512,1024]{1,0:T(8,128)(2,1)} %convolution_convert_fusion.5), channel_id=1, source_target_pairs={{0,1},{1,0},{2,3},{3,2},{4,5},{5,4},{6,7},{7,6},{8,9},{9,8},{10,11... | collective-permute-start | bytes 3145736 | tf_op jit(solution)/shard_map/ppermute | solution.py:708
  426.8 28.8 %collective-permute-start.72 = (bf16[256,1024]{1,0:T(8,128)(2,1)}, bf16[256,1024]{1,0:T(8,128)(2,1)S(1)}, u32[]{:S(2)}, u32[]{:S(2)}) collective-permute-start(bf16[256,1024]{1,0:T(8,128)(2,1)} %get-tuple-element.214), channel_id=1, source_target_pairs={{0,4},{2,6},{4,0},{6,2},{1,5},{3,7},{5,1},{7,3},{8,12},{10,14},{12... | collective-permute-start | bytes 1572872 | tf_op jit(solution)/shard_map/ppermute | solution.py:705
  446.9 17.7 %collective-permute-start.80 = (bf16[512,512]{1,0:T(8,128)(2,1)S(1)}, bf16[512,512]{1,0:T(8,128)(2,1)S(1)}, u32[]{:S(2)}, u32[]{:S(2)}) collective-permute-start(bf16[512,512]{1,0:T(8,128)(2,1)S(1)} %add_convert_fusion.6), channel_id=1, source_target_pairs={{0,1},{1,0},{2,3},{3,2},{4,5},{5,4},{6,7},{7,6},{8,9},{9,8},{10,11... | collective-permute-start | bytes 1572872 | tf_op jit(solution)/shard_map/ppermute | solution.py:708
  480.6 69.6 %reduce-scatter.9.cloned.1.call-start = ((), (), s32[]{:S(2)}) async-start(), calls=%async_computation.6 | async-start | bytes 1310720 | tf_op jit(solution)/shard_map/reduce_scatter | solution.py:948
  505.9 22.2 %collective-permute-start.76 = (bf16[512,512]{1,0:T(8,128)(2,1)}, bf16[512,512]{1,0:T(8,128)(2,1)S(1)}, u32[]{:S(2)}, u32[]{:S(2)}) collective-permute-start(bf16[512,512]{1,0:T(8,128)(2,1)} %get-tuple-element.221), channel_id=1, source_target_pairs={{0,1},{1,0},{2,3},{3,2},{4,5},{5,4},{6,7},{7,6},{8,9},{9,8},{10,11... | collective-permute-start | bytes 1572872 | tf_op jit(solution)/shard_map/ppermute | solution.py:708
  508.7 23.1 %collective-permute-start.97 = (bf16[3,704,128]{2,1,0:T(8,128)(2,1)S(1)}, bf16[3,704,128]{2,1,0:T(8,128)(2,1)S(1)}, u32[]{:S(2)}, u32[]{:S(2)}) collective-permute-start(bf16[3,704,128]{2,1,0:T(8,128)(2,1)S(1)} %pad_maximum_fusion.11), channel_id=1, source_target_pairs={{0,2},{2,0},{4,6},{6,4},{1,3},{3,1},{5,7},{7,5},{8,10},{10,8},{12,... | collective-permute-start | bytes 1622024 | tf_op jit(solution)/shard_map/ppermute | solution.py:705
  508.9 23.0 %collective-permute-start.98 = (bf16[3,704,128]{2,1,0:T(8,128)(2,1)S(1)}, bf16[3,704,128]{2,1,0:T(8,128)(2,1)S(1)}, u32[]{:S(2)}, u32[]{:S(2)}) collective-permute-start(bf16[3,704,128]{2,1,0:T(8,128)(2,1)S(1)} %pad_maximum_fusion.12), channel_id=1, source_target_pairs={{0,4},{2,6},{4,0},{6,2},{1,5},{3,7},{5,1},{7,3},{8,12},{10,14},{12... | collective-permute-start | bytes 1622024 | tf_op jit(solution)/shard_map/ppermute | solution.py:705
  510.1 24.7 %collective-permute-start.99 = (bf16[3,704,128]{2,1,0:T(8,128)(2,1)S(1)}, bf16[3,704,128]{2,1,0:T(8,128)(2,1)S(1)}, u32[]{:S(2)}, u32[]{:S(2)}) collective-permute-start(bf16[3,704,128]{2,1,0:T(8,128)(2,1)S(1)} %pad_maximum_fusion.13), channel_id=1, source_target_pairs={{0,6},{2,4},{4,2},{6,0},{1,7},{3,5},{5,3},{7,1},{8,14},{10,12},{12... | collective-permute-start | bytes 1622024 | tf_op jit(solution)/shard_map/ppermute | solution.py:705
  528.4 18.0 %collective-permute-start.77 = (bf16[512,512]{1,0:T(8,128)(2,1)S(1)}, bf16[512,512]{1,0:T(8,128)(2,1)S(1)}, u32[]{:S(2)}, u32[]{:S(2)}) collective-permute-start(bf16[512,512]{1,0:T(8,128)(2,1)S(1)} %add_convert_fusion.12), channel_id=1, source_target_pairs={{0,4},{2,6},{4,0},{6,2},{1,5},{3,7},{5,1},{7,3},{8,12},{10,14},{12... | collective-permute-start | bytes 1572872 | tf_op jit(solution)/shard_map/ppermute | solution.py:705
  (182 other events, 1199.8 us)
Sparse Core Ops, SparseCore 0:
  75.1 59.6 all-gather.4
  155.1 32.9 all-gather.6
  269.5 56.6 reduce-scatter.4
  328.4 102.0 reduce-scatter.6
  480.7 27.5 reduce-scatter.10
  510.6 26.0 reduce-scatter.8

commit v5 on v4

--- a/solution.py
+++ b/solution.py
@@ -15,7 +15,7 @@
 BF = jnp.bfloat16
 F32 = jnp.float32
 HEADS_PER_STEP = 4
-FL = {'f11': 0, 'f13': 1, 'f0': 1, 'f1': 1, 'f5': 2, 'f9': 1, 'f12': 2, 'f2': 1, 'f3': 1, 'f4': 0, 'f8': 1, 'f10': 3, 'f6': 1, 'f7': 1, 'f14': 1, 'f15': 0, 'f16': 0, 'f17': 0, 'b0': 1, 'b1': 0, 'b2': 1, 'b3': 0, 'b4': 0, 'b5': 2, 'b6': 0, 'b7': 1, 'b8': 1, 'b29': 0, 'b28': 0, 'b18': 2, 'b19': 1, 'b24': 2, 'b9': 3, 'b13': 5, 'b14': 1, 'b15': 0, 'b16': 0, 'b17': 2, 'b20': 0, 'b22': 0, 'b23': 0, 'b25': 1, 'b26': 1, 'b27': 0, 'b30': 0, 'b31': 0, 'b32': 0, 'b33': 0, 'b34': 0, 'b36': 0, 'b37': 1}
+FL = {'f11': 0, 'f13': 1, 'f0': 1, 'f1': 1, 'f5': 2, 'f9': 1, 'f12': 2, 'f2': 1, 'f3': 1, 'f4': 0, 'f8': 1, 'f10': 3, 'f6': 1, 'f7': 1, 'f14': 1, 'f15': 0, 'f16': 0, 'f17': 0, 'b0': 1, 'b1': 0, 'b2': 1, 'b3': 0, 'b4': 0, 'b5': 2, 'b6': 0, 'b7': 1, 'b8': 1, 'b29': 0, 'b28': 0, 'b18': 2, 'b19': 1, 'b24': 2, 'b9': 3, 'b13': 5, 'b14': 1, 'b15': 0, 'b16': 3, 'b17': 2, 'b20': 0, 'b22': 0, 'b23': 0, 'b25': 1, 'b26': 1, 'b27': 0, 'b30': 0, 'b31': 0, 'b32': 0, 'b33': 0, 'b34': 0, 'b36': 0, 'b37': 1}
 
 
 def dot_nn(a, b):

time: 569 us -> 548 us (0.963)
  waiting for transfers between devices: 174 us -> 152 us
  starting transfers between devices: 90.8 us -> 82.4 us
  other arithmetic: 75 us -> 80.9 us
    ppermute x18, waiting for transfers between devices: 66.8 us -> 51.2 us  [swap_col(): return lax.ppermute(a, 'col', [(0, 1), (1, 0)])]
    ppermute x18, starting transfers between devices: 41 us -> 31.9 us  [swap_col(): return lax.ppermute(a, 'col', [(0, 1), (1, 0)])]
    unnamed x255 -> x249, local copies, waits for them, and re-layouts: 21.1 us -> 25.4 us
  transfers between devices with their start and end apart: 106 -> 106, of which waited for: 40 -> 37; matrix products, arithmetic and copies ran while one was open for 22% -> 25% of each run, Pallas kernels for 23% -> 18%
where the time goes in v5:
time: 548 us; the launch traced here: 537 us
  waiting for transfers between devices  152 us (28%)
  Pallas kernels  130 us (24%)
  starting transfers between devices  82.4 us (15%)
  other arithmetic  80.9 us (15%)
  local copies, waits for them, and re-layouts  42.3 us (8%)
  matrix products  33.9 us (6%)
  between operations  16 us (3%)
    ppermute x79, waiting for transfers between devices, swap_row(): return lax.ppermute(a, 'row', [(i, i ^ bit) for i in range(R)])  99.6 us
    pallas_call x2, Pallas kernels, feed(): pl.pallas_call(functools.partial(feed_body, rows_n=R, parts=parts, near=n...  51.6 us
    ppermute x18, waiting for transfers between devices, swap_col(): return lax.ppermute(a, 'col', [(0, 1), (1, 0)])  51.2 us
    ppermute x79, starting transfers between devices, swap_row(): return lax.ppermute(a, 'row', [(i, i ^ bit) for i in range(R)])  45.2 us
    ppermute x18, starting transfers between devices, swap_col(): return lax.ppermute(a, 'col', [(0, 1), (1, 0)])  31.9 us
    convert_element_type x19, other arithmetic, add(): return total if wide else total.astype(BF)  26.1 us
    unnamed x249, local copies, waits for them, and re-layouts  25.4 us
    pallas_call x1, Pallas kernels, late_weight_grads(): pl.pallas_call(functools.partial(late_weight_body, rows_n=rows_n), grid=(...  19.5 us
  transfers between devices with their start and end apart: 106, of which 37 were waited for; matrix products, arithmetic and copies ran while one was open for 25% of the time, Pallas kernels for 18%

profile of v5, /device:TPU:0, one launch (start us, length us, event | category | flops | bytes accessed | tf_op | source)
XLA Modules:
  0.0 537.3 jit_solution(18194295754803462307)
XLA Ops:
  9.3 2.6 collective-permute-start.4
  16.9 2.6 fusion.3
  27.0 2.8 convert_element_type.509.refs_8_
  38.3 2.6 convolution_convert_fusion.2
  42.7 2.4 add_convert_fusion.5
  47.3 4.2 cut_weights.3
  58.1 7.6 %collective-permute-done.1 = bf16[256,1024]{1,0:T(8,128)(2,1)} collective-permute-done((bf16[256,1024]{1,0:T(8,128)(2,1)}, bf16[256,1024]{1,0:T(8,128)(2,1)}, u32[]{:S(2)}, u32[]{:S(2)}) %collective-permute-start.1) | collective-permute-done | bytes 524320 | tf_op jit(solution)/shard_map/ppermute | solution.py:705
  79.8 5.4 %attend.2 = (bf16[256,1024]{1,0:T(8,128)(2,1)}, bf16[256,1024]{1,0:T(8,128)(2,1)}, f32[8,1,256]{2,1,0:T(1,128)}) custom-call(s32[2]{0:T(128)} %pad_add_fusion.where, s32[2048]{0:T(1024)} %seq_ref.7, s32[2048]{0:T(1024)} %block_ref.7, f32[256,1024]{1,0:T(8,128)} %add_multiply_fusion.q_ref, f32[256,128]{1,0:T(8,128)} %get-tuple-element.325.cos_ref, ...), custom_call_target="tpu_custom_call" | custom-call | flops 1073741824 | bytes 3145728 | tf_op jit(solution)/shard_map/attend/pallas_call | solution.py:103
  86.5 22.1 %collective-permute-done.20 = bf16[256,1024]{1,0:T(8,128)(2,1)S(1)} collective-permute-done((bf16[256,1024]{1,0:T(8,128)(2,1)S(1)}, bf16[256,1024]{1,0:T(8,128)(2,1)S(1)}, u32[]{:S(2)}, u32[]{:S(2)}) %collective-permute-start.20) | collective-permute-done | bytes 524320 | tf_op jit(solution)/shard_map/ppermute | solution.py:705
  111.7 5.5 %attend.3 = (bf16[256,1024]{1,0:T(8,128)(2,1)}, bf16[256,1024]{1,0:T(8,128)(2,1)}, f32[8,1,256]{2,1,0:T(1,128)}) custom-call(s32[2]{0:T(128)} %pad_add_fusion.where, s32[2048]{0:T(1024)} %seq_ref.7, s32[2048]{0:T(1024)} %block_ref.7, f32[256,1024]{1,0:T(8,128)} %broadcast_multiply_fusion.q_ref, f32[256,128]{1,0:T(8,128)} %get-tuple-element.325.cos_ref, ...), custom_call_target="tpu_custom_call" | custom-call | flops 1073741824 | bytes 3145728 | tf_op jit(solution)/shard_map/attend/pallas_call | solution.py:103
  120.4 11.7 %collective-permute-done.24 = bf16[256,1024]{1,0:T(8,128)(2,1)S(1)} collective-permute-done((bf16[256,1024]{1,0:T(8,128)(2,1)}, bf16[256,1024]{1,0:T(8,128)(2,1)S(1)}, u32[]{:S(2)}, u32[]{:S(2)}) %collective-permute-start.24) | collective-permute-done | bytes 524320 | tf_op jit(solution)/shard_map/ppermute | solution.py:705
  134.2 5.8 %collective-permute-start.28 = (bf16[1024,512]{1,0:T(8,128)(2,1)}, bf16[1024,512]{1,0:T(8,128)(2,1)}, u32[]{:S(2)}, u32[]{:S(2)}) collective-permute-start(bf16[1024,512]{1,0:T(8,128)(2,1)} %collective-permute-done.23.refs_10_), channel_id=1, source_target_pairs={{0,1},{1,0},{2,3},{3,2},{4,5},{5,4},{6,7},{7,6},{8,9},{9,8},{10,11... | collective-permute-start | bytes 3145736 | tf_op jit(solution)/shard_map/ppermute | solution.py:708
  144.8 2.5 fusion.48
  147.3 2.5 convolution_add_fusion
  156.5 7.5 %collective-permute-done.28.refs_10_ = bf16[1024,512]{1,0:T(8,128)(2,1)} collective-permute-done((bf16[1024,512]{1,0:T(8,128)(2,1)}, bf16[1024,512]{1,0:T(8,128)(2,1)}, u32[]{:S(2)}, u32[]{:S(2)}) %collective-permute-start.28) | collective-permute-done | bytes 1048608 | tf_op jit(solution)/shard_map/ppermute | solution.py:708
  168.6 11.1 %collective-permute-done.44.refs_4_ = bf16[512,512]{1,0:T(8,128)(2,1)S(1)} collective-permute-done((bf16[512,512]{1,0:T(8,128)(2,1)S(1)}, bf16[512,512]{1,0:T(8,128)(2,1)S(1)}, u32[]{:S(2)}, u32[]{:S(2)}) %collective-permute-start.44) | collective-permute-done | bytes 524320 | tf_op jit(solution)/shard_map/ppermute | solution.py:708
  181.5 8.3 %collective-permute-done.35.refs_0_ = bf16[512,512]{1,0:T(8,128)(2,1)S(1)} collective-permute-done((bf16[512,512]{1,0:T(8,128)(2,1)}, bf16[512,512]{1,0:T(8,128)(2,1)S(1)}, u32[]{:S(2)}, u32[]{:S(2)}) %collective-permute-start.35) | collective-permute-done | bytes 524320 | tf_op jit(solution)/shard_map/ppermute | solution.py:708
  194.4 8.3 %collective-permute-done.46.refs_6_ = bf16[512,512]{1,0:T(8,128)(2,1)S(1)} collective-permute-done((bf16[512,512]{1,0:T(8,128)(2,1)}, bf16[512,512]{1,0:T(8,128)(2,1)S(1)}, u32[]{:S(2)}, u32[]{:S(2)}) %collective-permute-start.46) | collective-permute-done | bytes 524320 | tf_op jit(solution)/shard_map/ppermute | solution.py:708
  206.8 25.7 %feed.3 = (bf16[1024,704]{1,0:T(8,128)(2,1)}, bf16[1024,704]{1,0:T(8,128)(2,1)}, bf16[1024,704]{1,0:T(8,128)(2,1)}, bf16[1024,512]{1,0:T(8,128)(2,1)}, bf16[1024...) custom-call(bf16[512,512]{1,0:T(8,128)(2,1)} %copy-done.105, ...), custom_call_target="tpu_custom_call" | custom-call | flops 14763950080 | bytes 29622272 | tf_op jit(solution)/shard_map/feed/pallas_call | solution.py:373
  232.6 25.9 %feed.2 = (bf16[1024,704]{1,0:T(8,128)(2,1)}, bf16[1024,704]{1,0:T(8,128)(2,1)}, bf16[1024,704]{1,0:T(8,128)(2,1)}, bf16[1024,512]{1,0:T(8,128)(2,1)}, bf16[1024...) custom-call(bf16[512,512]{1,0:T(8,128)(2,1)} %get-tuple-element.301., ...), custom_call_target="tpu_custom_call" | custom-call | flops 14763950080 | bytes 29622272 | tf_op jit(solution)/shard_map/feed/pallas_call | solution.py:373
  260.0 9.4 %feed_weights.1 = bf16[4,4,704,128]{3,2,1,0:T(8,128)(2,1)} custom-call(bf16[1024,2048]{1,0:T(8,128)(2,1)} %get-tuple-element.168.x0, bf16[1024,2048]{1,0:T(8,128)(2,1)} %get-tuple-element.169.x1, bf16[1024,704]{1,0:T(8,128)(2,1)S(1)} %copy-done.12, bf16[1024,704]{1,0:T(8,128)(2,1)S(1)} %copy-done.11), custom_call_target="tpu_custom_call" | custom-call | flops 5905580032 | bytes 14155776 | tf_op jit(solution)/shard_map/feed_weights/pallas_call | solution.py:415
  273.4 2.3 add_convert_fusion.29
  283.9 19.5 %late_weights.1 = bf16[4,2,4,704,128]{4,3,2,1,0:T(8,128)(2,1)} custom-call(bf16[1024,2048]{1,0:T(8,128)(2,1)} %get-tuple-element.168.x0, bf16[1024,2048]{1,0:T(8,128)(2,1)} %get-tuple-element.169.x1, bf16[1024,704]{1,0:T(8,128)(2,1)} %get-tuple-element.176.u0, bf16[1024,704]{1,0:T(8,128)(2,1)} %get-tuple-element.177.u1, ...), custom_call_target="tpu_custom_call" | custom-call | flops 11811160064 | bytes 28311552 | tf_op jit(solution)/shard_map/late_weights/pallas_call | solution.py:489
  313.9 9.7 %collective-permute-done.56 = bf16[512,512]{1,0:T(8,128)(2,1)S(1)} collective-permute-done((bf16[512,512]{1,0:T(8,128)(2,1)S(1)}, bf16[512,512]{1,0:T(8,128)(2,1)S(1)}, u32[]{:S(2)}, u32[]{:S(2)}) %collective-permute-start.56) | collective-permute-done | bytes 524320 | tf_op jit(solution)/shard_map/ppermute | solution.py:705
  327.9 3.2 collective-permute-done.61
  333.4 2.9 convolution_convert_fusion.1
  337.4 2.6 convolution_convert_fusion
  345.9 2.3 convolution_convert_fusion.4
  350.6 8.6 %collective-permute-done.63 = bf16[256,1024]{1,0:T(8,128)(2,1)S(1)} collective-permute-done((bf16[256,1024]{1,0:T(8,128)(2,1)S(1)}, bf16[256,1024]{1,0:T(8,128)(2,1)S(1)}, u32[]{:S(2)}, u32[]{:S(2)}) %collective-permute-start.63) | collective-permute-done | bytes 524320 | tf_op jit(solution)/shard_map/ppermute | solution.py:705
  360.7 6.9 %attend_back.2 = (bf16[256,1024]{1,0:T(8,128)(2,1)}, f32[8,256,128]{2,1,0:T(8,128)}, f32[8,256,128]{2,1,0:T(8,128)}) custom-call(s32[2]{0:T(128)} %pad_add_fusion.where, s32[2048]{0:T(1024)} %seq_ref.7, s32[2048]{0:T(1024)} %block_ref.7, bf16[256,1024]{1,0:T(8,128)(2,1)} %get-tuple-element.157.rot_ref, bf16[256,1024]{1,0:T(8,128)(2,1)} %add_convert_fusion.19.grad_ref, ...), custom_call_target="tpu_custom_call" | custom-call | flops 2684354560 | bytes 5242880 | tf_op jit(solution)/shard_map/attend_back/pallas_call | solution.py:202
  369.2 13.8 %down_products.1 = (bf16[1024,512]{1,0:T(8,128)(2,1)}, bf16[1024,512]{1,0:T(8,128)(2,1)}, bf16[1024,512]{1,0:T(8,128)(2,1)}, bf16[1024,512]{1,0:T(8,128)(2,1)}, ...) custom-call(bf16[1024,704]{1,0:T(8,128)(2,1)} %get-tuple-element.198, ...), custom_call_target="tpu_custom_call" | custom-call | tf_op jit(solution)/shard_map/down_products/pallas_call | solution.py:535
  384.0 3.0 fusion.39
  387.0 8.4 %collective-permute-start.96 = (bf16[1024,512]{1,0:T(8,128)(2,1)}, bf16[1024,512]{1,0:T(8,128)(2,1)}, u32[]{:S(2)}, u32[]{:S(2)}) collective-permute-start(bf16[1024,512]{1,0:T(8,128)(2,1)} %convolution_convert_fusion.4), channel_id=1, source_target_pairs={{0,1},{1,0},{2,3},{3,2},{4,5},{5,4},{6,7},{7,6},{8,9},{9,8},{10,11... | collective-permute-start | bytes 3145736 | tf_op jit(solution)/shard_map/ppermute | solution.py:708
  408.4 7.5 %attend_back.3 = (bf16[256,1024]{1,0:T(8,128)(2,1)}, f32[8,256,128]{2,1,0:T(8,128)}, f32[8,256,128]{2,1,0:T(8,128)}) custom-call(s32[2]{0:T(128)} %pad_add_fusion.where, s32[2048]{0:T(1024)} %seq_ref.7, s32[2048]{0:T(1024)} %block_ref.7, bf16[256,1024]{1,0:T(8,128)(2,1)} %get-tuple-element.208.rot_ref, bf16[256,1024]{1,0:T(8,128)(2,1)} %add_convert_fusion.14.grad_ref, ...), custom_call_target="tpu_custom_call" | custom-call | flops 2684354560 | bytes 5242880 | tf_op jit(solution)/shard_map/attend_back/pallas_call | solution.py:202
  416.5 3.2 collective-permute-done.96
  419.6 10.2 %collective-permute-done.79 = bf16[512,512]{1,0:T(8,128)(2,1)} collective-permute-done((bf16[512,512]{1,0:T(8,128)(2,1)}, bf16[512,512]{1,0:T(8,128)(2,1)}, u32[]{:S(2)}, u32[]{:S(2)}) %collective-permute-start.79) | collective-permute-done | bytes 524320 | tf_op jit(solution)/shard_map/ppermute | solution.py:705
  434.3 3.8 fusion.49
  438.1 4.0 collective-permute-done.74
  443.1 2.6 add_convert_fusion
  465.5 2.6 fusion.50
  469.3 3.5 add_convert_fusion.1
  486.9 2.7 fusion.10
  492.8 2.5 collective-permute-done.91
  495.6 3.8 fusion.7
  499.7 3.3 collective-permute-done.76
  506.3 3.3 collective-permute-start.95
  512.3 4.1 finish_weights.1
  518.9 5.8 %collective-permute-done.77 = bf16[512,512]{1,0:T(8,128)(2,1)S(1)} collective-permute-done((bf16[512,512]{1,0:T(8,128)(2,1)S(1)}, bf16[512,512]{1,0:T(8,128)(2,1)S(1)}, u32[]{:S(2)}, u32[]{:S(2)}) %collective-permute-start.77) | collective-permute-done | bytes 524320 | tf_op jit(solution)/shard_map/ppermute | solution.py:705
  (568 shorter events, 198.9 us)
Async XLA Ops:
  7.2 199.6 %all-gather.5.cloned.1.call-start = ((), (), s32[]{:S(2)}) async-start(), calls=%async_computation.8 | async-start | bytes 3604480 | tf_op jit(solution)/shard_map/all_gather | solution.py:894
  9.3 28.4 %collective-permute-start.4 = (bf16[512,1024]{1,0:T(8,128)(2,1)}, bf16[512,1024]{1,0:T(8,128)(2,1)}, u32[]{:S(2)}, u32[]{:S(2)}) collective-permute-start(bf16[512,1024]{1,0:T(8,128)(2,1)} %param.20), channel_id=1, source_target_pairs={{0,1},{1,0},{2,3},{3,2},{4,5},{5,4},{6,7},{7,6},{8,9},{9,8},{10,11... | collective-permute-start | bytes 3145736 | tf_op jit(solution)/shard_map/ppermute | solution.py:708
  23.6 19.1 %collective-permute-start = (bf16[512,1024]{1,0:T(8,128)(2,1)}, bf16[512,1024]{1,0:T(8,128)(2,1)}, u32[]{:S(2)}, u32[]{:S(2)}) collective-permute-start(bf16[512,1024]{1,0:T(8,128)(2,1)} %slice.355), channel_id=1, source_target_pairs={{0,2},{2,0},{4,6},{6,4},{1,3},{3,1},{5,7},{7,5},{8,10},{10,8},{12,... | collective-permute-start | bytes 3145736 | tf_op jit(solution)/shard_map/ppermute | solution.py:705
  36.5 17.9 %collective-permute-start.8 = (bf16[2,704,128]{2,1,0:T(8,128)(2,1)S(1)}, bf16[2,704,128]{2,1,0:T(8,128)(2,1)S(1)}, u32[]{:S(2)}, u32[]{:S(2)}) collective-permute-start(bf16[2,704,128]{2,1,0:T(8,128)(2,1)S(1)} %get-tuple-element.130), channel_id=1, source_target_pairs={{0,4},{2,6},{4,0},{6,2},{1,5},{3,7},{5,1},{7,3},{8,12},{10,14},{12... | collective-permute-start | bytes 1081352 | tf_op jit(solution)/shard_map/ppermute | solution.py:705
  37.7 17.9 %collective-permute-start.9 = (bf16[2,704,128]{2,1,0:T(8,128)(2,1)S(1)}, bf16[2,704,128]{2,1,0:T(8,128)(2,1)S(1)}, u32[]{:S(2)}, u32[]{:S(2)}) collective-permute-start(bf16[2,704,128]{2,1,0:T(8,128)(2,1)S(1)} %get-tuple-element.131), channel_id=1, source_target_pairs={{0,6},{2,4},{4,2},{6,0},{1,7},{3,5},{5,3},{7,1},{8,14},{10,12},{12... | collective-permute-start | bytes 1081352 | tf_op jit(solution)/shard_map/ppermute | solution.py:705
  37.7 30.8 %collective-permute-start.5 = (bf16[1024,512]{1,0:T(8,128)(2,1)}, bf16[1024,512]{1,0:T(8,128)(2,1)}, u32[]{:S(2)}, u32[]{:S(2)}) collective-permute-start(bf16[1024,512]{1,0:T(8,128)(2,1)} %param.22), channel_id=1, source_target_pairs={{0,1},{1,0},{2,3},{3,2},{4,5},{5,4},{6,7},{7,6},{8,9},{9,8},{10,11... | collective-permute-start | bytes 3145736 | tf_op jit(solution)/shard_map/ppermute | solution.py:708
  42.0 29.3 %collective-permute-start.19 = (bf16[512,1024]{1,0:T(8,128)(2,1)}, bf16[512,1024]{1,0:T(8,128)(2,1)}, u32[]{:S(2)}, u32[]{:S(2)}) collective-permute-start(bf16[512,1024]{1,0:T(8,128)(2,1)} %slice.367), channel_id=1, source_target_pairs={{0,2},{2,0},{4,6},{6,4},{1,3},{3,1},{5,7},{7,5},{8,10},{10,8},{12,... | collective-permute-start | bytes 3145736 | tf_op jit(solution)/shard_map/ppermute | solution.py:705
  46.0 19.7 %collective-permute-start.1 = (bf16[256,1024]{1,0:T(8,128)(2,1)}, bf16[256,1024]{1,0:T(8,128)(2,1)}, u32[]{:S(2)}, u32[]{:S(2)}) collective-permute-start(bf16[256,1024]{1,0:T(8,128)(2,1)} %slice.357), channel_id=1, source_target_pairs={{0,4},{2,6},{4,0},{6,2},{1,5},{3,7},{5,1},{7,3},{8,12},{10,14},{12... | collective-permute-start | bytes 1572872 | tf_op jit(solution)/shard_map/ppermute | solution.py:705
  54.4 32.1 %collective-permute-start.21 = (bf16[2,704,512]{2,1,0:T(8,128)(2,1)}, bf16[2,704,512]{2,1,0:T(8,128)(2,1)}, u32[]{:S(2)}, u32[]{:S(2)}) collective-permute-start(bf16[2,704,512]{2,1,0:T(8,128)(2,1)} %get-tuple-element.136), channel_id=1, source_target_pairs={{0,2},{2,0},{4,6},{6,4},{1,3},{3,1},{5,7},{7,5},{8,10},{10,8},{12,... | collective-permute-start | bytes 4325384 | tf_op jit(solution)/shard_map/ppermute | solution.py:705
  70.7 39.9 %collective-permute-start.23 = (bf16[1024,512]{1,0:T(8,128)(2,1)}, bf16[1024,512]{1,0:T(8,128)(2,1)}, u32[]{:S(2)}, u32[]{:S(2)}) collective-permute-start(bf16[1024,512]{1,0:T(8,128)(2,1)} %convert_element_type.509.refs_8_), channel_id=1, source_target_pairs={{0,4},{2,6},{4,0},{6,2},{1,5},{3,7},{5,1},{7,3},{8,12},{10,14},{12... | collective-permute-start | bytes 3145736 | tf_op jit(solution)/shard_map/ppermute | solution.py:705
  71.3 39.3 %collective-permute-start.22 = (bf16[1024,512]{1,0:T(8,128)(2,1)}, bf16[1024,512]{1,0:T(8,128)(2,1)}, u32[]{:S(2)}, u32[]{:S(2)}) collective-permute-start(bf16[1024,512]{1,0:T(8,128)(2,1)} %convert_element_type.509.refs_8_), channel_id=1, source_target_pairs={{0,1},{1,0},{2,3},{3,2},{4,5},{5,4},{6,7},{7,6},{8,9},{9,8},{10,11... | collective-permute-start | bytes 3145736 | tf_op jit(solution)/shard_map/ppermute | solution.py:708
  73.5 35.1 %collective-permute-start.20 = (bf16[256,1024]{1,0:T(8,128)(2,1)S(1)}, bf16[256,1024]{1,0:T(8,128)(2,1)S(1)}, u32[]{:S(2)}, u32[]{:S(2)}) collective-permute-start(bf16[256,1024]{1,0:T(8,128)(2,1)S(1)} %slice.369), channel_id=1, source_target_pairs={{0,4},{2,6},{4,0},{6,2},{1,5},{3,7},{5,1},{7,3},{8,12},{10,14},{12... | collective-permute-start | bytes 1572872 | tf_op jit(solution)/shard_map/ppermute | solution.py:705
  75.1 131.7 %all-gather.7.cloned.1.call-start = ((), (), s32[]{:S(2)}) async-start(), calls=%async_computation.9 | async-start | bytes 1802240 | tf_op jit(solution)/shard_map/all_gather | solution.py:901
  85.2 34.1 %collective-permute-start.17 = (bf16[256,1024]{1,0:T(8,128)(2,1)}, bf16[256,1024]{1,0:T(8,128)(2,1)S(1)}, u32[]{:S(2)}, u32[]{:S(2)}) collective-permute-start(bf16[256,1024]{1,0:T(8,128)(2,1)} %get-tuple-element.133.att_ref), channel_id=1, source_target_pairs={{0,4},{2,6},{4,0},{6,2},{1,5},{3,7},{5,1},{7,3},{8,12},{10,14},{12... | collective-permute-start | bytes 1572872 | tf_op jit(solution)/shard_map/ppermute | solution.py:705
  120.4 19.7 %collective-permute-start.18 = (bf16[512,1024]{1,0:T(8,128)(2,1)}, bf16[512,1024]{1,0:T(8,128)(2,1)}, u32[]{:S(2)}, u32[]{:S(2)}) collective-permute-start(bf16[512,1024]{1,0:T(8,128)(2,1)} %pad_maximum_fusion.3), channel_id=1, source_target_pairs={{0,2},{2,0},{4,6},{6,4},{1,3},{3,1},{5,7},{7,5},{8,10},{10,8},{12,... | collective-permute-start | bytes 3145736 | tf_op jit(solution)/shard_map/ppermute | solution.py:705
  132.4 21.9 %collective-permute-start.39 = (bf16[176,512]{1,0:T(8,128)(2,1)S(1)}, bf16[176,512]{1,0:T(8,128)(2,1)S(1)}, u32[]{:S(2)}, u32[]{:S(2)}) collective-permute-start(bf16[176,512]{1,0:T(8,128)(2,1)S(1)} %get-tuple-element.151), channel_id=1, source_target_pairs={{0,4},{2,6},{4,0},{6,2},{1,5},{3,7},{5,1},{7,3},{8,12},{10,14},{12... | collective-permute-start | bytes 540680 | tf_op jit(solution)/shard_map/ppermute | solution.py:705
  133.9 20.4 %collective-permute-start.40 = (bf16[176,512]{1,0:T(8,128)(2,1)S(1)}, bf16[176,512]{1,0:T(8,128)(2,1)S(1)}, u32[]{:S(2)}, u32[]{:S(2)}) collective-permute-start(bf16[176,512]{1,0:T(8,128)(2,1)S(1)} %get-tuple-element.152), channel_id=1, source_target_pairs={{0,6},{2,4},{4,2},{6,0},{1,7},{3,5},{5,3},{7,1},{8,14},{10,12},{12... | collective-permute-start | bytes 540680 | tf_op jit(solution)/shard_map/ppermute | solution.py:705
  134.2 29.8 %collective-permute-start.28 = (bf16[1024,512]{1,0:T(8,128)(2,1)}, bf16[1024,512]{1,0:T(8,128)(2,1)}, u32[]{:S(2)}, u32[]{:S(2)}) collective-permute-start(bf16[1024,512]{1,0:T(8,128)(2,1)} %collective-permute-done.23.refs_10_), channel_id=1, source_target_pairs={{0,1},{1,0},{2,3},{3,2},{4,5},{5,4},{6,7},{7,6},{8,9},{9,8},{10,11... | collective-permute-start | bytes 3145736 | tf_op jit(solution)/shard_map/ppermute | solution.py:708
  155.0 205.7 %reduce-scatter.5.cloned.1.call-start = ((), (), s32[]{:S(2)}) async-start(), calls=%async_computation.4 | async-start | bytes 3604480 | tf_op jit(solution)/shard_map/reduce_scatter | solution.py:948
  166.6 24.6 %collective-permute-start.38 = (bf16[704,512]{1,0:T(8,128)(2,1)S(1)}, bf16[704,512]{1,0:T(8,128)(2,1)S(1)}, u32[]{:S(2)}, u32[]{:S(2)}) collective-permute-start(bf16[704,512]{1,0:T(8,128)(2,1)S(1)} %copy-done.10), channel_id=1, source_target_pairs={{0,2},{2,0},{4,6},{6,4},{1,3},{3,1},{5,7},{7,5},{8,10},{10,8},{12,... | collective-permute-start | bytes 2162696 | tf_op jit(solution)/shard_map/ppermute | solution.py:705
  168.3 21.4 %collective-permute-start.35 = (bf16[512,512]{1,0:T(8,128)(2,1)}, bf16[512,512]{1,0:T(8,128)(2,1)S(1)}, u32[]{:S(2)}, u32[]{:S(2)}) collective-permute-start(bf16[512,512]{1,0:T(8,128)(2,1)} %get-tuple-element.301.refs_0_), channel_id=1, source_target_pairs={{0,1},{1,0},{2,3},{3,2},{4,5},{5,4},{6,7},{7,6},{8,9},{9,8},{10,11... | collective-permute-start | bytes 1572872 | tf_op jit(solution)/shard_map/ppermute | solution.py:708
  168.6 24.4 %collective-permute-start.32 = (bf16[512,512]{1,0:T(8,128)(2,1)S(1)}, bf16[512,512]{1,0:T(8,128)(2,1)S(1)}, u32[]{:S(2)}, u32[]{:S(2)}) collective-permute-start(bf16[512,512]{1,0:T(8,128)(2,1)S(1)} %get-tuple-element.300.refs_4_), channel_id=1, source_target_pairs={{0,2},{2,0},{4,6},{6,4},{1,3},{3,1},{5,7},{7,5},{8,10},{10,8},{12,... | collective-permute-start | bytes 1572872 | tf_op jit(solution)/shard_map/ppermute | solution.py:705
  203.6 28.9 %collective-permute-start.29 = (bf16[512,512]{1,0:T(8,128)(2,1)}, bf16[512,512]{1,0:T(8,128)(2,1)}, u32[]{:S(2)}, u32[]{:S(2)}) collective-permute-start(bf16[512,512]{1,0:T(8,128)(2,1)} %get-tuple-element.301.refs_0_), channel_id=1, source_target_pairs={{0,2},{2,0},{4,6},{6,4},{1,3},{3,1},{5,7},{7,5},{8,10},{10,8},{12,... | collective-permute-start | bytes 1572872 | tf_op jit(solution)/shard_map/ppermute | solution.py:705
  204.7 27.9 %collective-permute-start.36 = (bf16[1024,512]{1,0:T(8,128)(2,1)}, bf16[1024,512]{1,0:T(8,128)(2,1)}, u32[]{:S(2)}, u32[]{:S(2)}) collective-permute-start(bf16[1024,512]{1,0:T(8,128)(2,1)} %convert_element_type.509.refs_8_), channel_id=1, source_target_pairs={{0,2},{2,0},{4,6},{6,4},{1,3},{3,1},{5,7},{7,5},{8,10},{10,8},{12,... | collective-permute-start | bytes 3145736 | tf_op jit(solution)/shard_map/ppermute | solution.py:705
  205.5 27.0 %collective-permute-start.37 = (bf16[1024,512]{1,0:T(8,128)(2,1)}, bf16[1024,512]{1,0:T(8,128)(2,1)}, u32[]{:S(2)}, u32[]{:S(2)}) collective-permute-start(bf16[1024,512]{1,0:T(8,128)(2,1)} %collective-permute-done.23.refs_10_), channel_id=1, source_target_pairs={{0,2},{2,0},{4,6},{6,4},{1,3},{3,1},{5,7},{7,5},{8,10},{10,8},{12,... | collective-permute-start | bytes 3145736 | tf_op jit(solution)/shard_map/ppermute | solution.py:705
  206.3 26.2 %collective-permute-start.34 = (bf16[512,512]{1,0:T(8,128)(2,1)}, bf16[512,512]{1,0:T(8,128)(2,1)}, u32[]{:S(2)}, u32[]{:S(2)}) collective-permute-start(bf16[512,512]{1,0:T(8,128)(2,1)} %collective-permute-done.33.refs_6_), channel_id=1, source_target_pairs={{0,2},{2,0},{4,6},{6,4},{1,3},{3,1},{5,7},{7,5},{8,10},{10,8},{12,... | collective-permute-start | bytes 1572872 | tf_op jit(solution)/shard_map/ppermute | solution.py:705
  206.5 26.1 %collective-permute-start.31 = (bf16[512,512]{1,0:T(8,128)(2,1)}, bf16[512,512]{1,0:T(8,128)(2,1)}, u32[]{:S(2)}, u32[]{:S(2)}) collective-permute-start(bf16[512,512]{1,0:T(8,128)(2,1)} %collective-permute-done.30.refs_2_), channel_id=1, source_target_pairs={{0,2},{2,0},{4,6},{6,4},{1,3},{3,1},{5,7},{7,5},{8,10},{10,8},{12,... | collective-permute-start | bytes 1572872 | tf_op jit(solution)/shard_map/ppermute | solution.py:705
  269.3 191.1 %reduce-scatter.7.cloned.1.call-start = ((), (), s32[]{:S(2)}) async-start(), calls=%async_computation.5 | async-start | bytes 7208960 | tf_op jit(solution)/shard_map/reduce_scatter | solution.py:948
  279.8 26.7 %collective-permute-start.57 = (bf16[512,512]{1,0:T(8,128)(2,1)}, bf16[512,512]{1,0:T(8,128)(2,1)}, u32[]{:S(2)}, u32[]{:S(2)}) collective-permute-start(bf16[512,512]{1,0:T(8,128)(2,1)} %get-tuple-element.187), channel_id=1, source_target_pairs={{0,4},{2,6},{4,0},{6,2},{1,5},{3,7},{5,1},{7,3},{8,12},{10,14},{12... | collective-permute-start | bytes 1572872 | tf_op jit(solution)/shard_map/ppermute | solution.py:705
  281.5 23.9 %collective-permute-start.58 = (bf16[512,512]{1,0:T(8,128)(2,1)}, bf16[512,512]{1,0:T(8,128)(2,1)}, u32[]{:S(2)}, u32[]{:S(2)}) collective-permute-start(bf16[512,512]{1,0:T(8,128)(2,1)} %get-tuple-element.190), channel_id=1, source_target_pairs={{0,4},{2,6},{4,0},{6,2},{1,5},{3,7},{5,1},{7,3},{8,12},{10,14},{12... | collective-permute-start | bytes 1572872 | tf_op jit(solution)/shard_map/ppermute | solution.py:705
  281.9 26.1 %collective-permute-start.54 = (bf16[512,512]{1,0:T(8,128)(2,1)}, bf16[512,512]{1,0:T(8,128)(2,1)}, u32[]{:S(2)}, u32[]{:S(2)}) collective-permute-start(bf16[512,512]{1,0:T(8,128)(2,1)} %get-tuple-element.167), channel_id=1, source_target_pairs={{0,1},{1,0},{2,3},{3,2},{4,5},{5,4},{6,7},{7,6},{8,9},{9,8},{10,11... | collective-permute-start | bytes 1572872 | tf_op jit(solution)/shard_map/ppermute | solution.py:708
  283.7 24.2 %collective-permute-start.55 = (bf16[512,512]{1,0:T(8,128)(2,1)}, bf16[512,512]{1,0:T(8,128)(2,1)}, u32[]{:S(2)}, u32[]{:S(2)}) collective-permute-start(bf16[512,512]{1,0:T(8,128)(2,1)} %get-tuple-element.182), channel_id=1, source_target_pairs={{0,1},{1,0},{2,3},{3,2},{4,5},{5,4},{6,7},{7,6},{8,9},{9,8},{10,11... | collective-permute-start | bytes 1572872 | tf_op jit(solution)/shard_map/ppermute | solution.py:708
  303.4 223.3 %reduce-scatter.11.cloned.1.call-start = ((), (), s32[]{:S(2)}) async-start(), calls=%async_computation.7 | async-start | bytes 1310720 | tf_op jit(solution)/shard_map/reduce_scatter | solution.py:948
  360.2 35.2 %collective-permute-start.69 = (bf16[256,1024]{1,0:T(8,128)(2,1)}, bf16[256,1024]{1,0:T(8,128)(2,1)}, u32[]{:S(2)}, u32[]{:S(2)}) collective-permute-start(bf16[256,1024]{1,0:T(8,128)(2,1)} %slice.389), channel_id=1, source_target_pairs={{0,4},{2,6},{4,0},{6,2},{1,5},{3,7},{5,1},{7,3},{8,12},{10,14},{12... | collective-permute-start | bytes 1572872 | tf_op jit(solution)/shard_map/ppermute | solution.py:705
  367.6 29.9 %collective-permute-start.70 = (bf16[256,1024]{1,0:T(8,128)(2,1)}, bf16[256,1024]{1,0:T(8,128)(2,1)S(1)}, u32[]{:S(2)}, u32[]{:S(2)}) collective-permute-start(bf16[256,1024]{1,0:T(8,128)(2,1)} %get-tuple-element.197), channel_id=1, source_target_pairs={{0,4},{2,6},{4,0},{6,2},{1,5},{3,7},{5,1},{7,3},{8,12},{10,14},{12... | collective-permute-start | bytes 1572872 | tf_op jit(solution)/shard_map/ppermute | solution.py:705
  383.9 15.9 %collective-permute-start.65 = (bf16[1024,512]{1,0:T(8,128)(2,1)}, bf16[1024,512]{1,0:T(8,128)(2,1)S(1)}, u32[]{:S(2)}, u32[]{:S(2)}) collective-permute-start(bf16[1024,512]{1,0:T(8,128)(2,1)} %get-tuple-element.203), channel_id=1, source_target_pairs={{0,2},{2,0},{4,6},{6,4},{1,3},{3,1},{5,7},{7,5},{8,10},{10,8},{12,... | collective-permute-start | bytes 3145736 | tf_op jit(solution)/shard_map/ppermute | solution.py:705
  387.0 32.6 %collective-permute-start.96 = (bf16[1024,512]{1,0:T(8,128)(2,1)}, bf16[1024,512]{1,0:T(8,128)(2,1)}, u32[]{:S(2)}, u32[]{:S(2)}) collective-permute-start(bf16[1024,512]{1,0:T(8,128)(2,1)} %convolution_convert_fusion.4), channel_id=1, source_target_pairs={{0,1},{1,0},{2,3},{3,2},{4,5},{5,4},{6,7},{7,6},{8,9},{9,8},{10,11... | collective-permute-start | bytes 3145736 | tf_op jit(solution)/shard_map/ppermute | solution.py:708
  403.6 16.0 %collective-permute-start.78 = (bf16[512,512]{1,0:T(8,128)(2,1)}, bf16[512,512]{1,0:T(8,128)(2,1)}, u32[]{:S(2)}, u32[]{:S(2)}) collective-permute-start(bf16[512,512]{1,0:T(8,128)(2,1)} %get-tuple-element.226), channel_id=1, source_target_pairs={{0,4},{2,6},{4,0},{6,2},{1,5},{3,7},{5,1},{7,3},{8,12},{10,14},{12... | collective-permute-start | bytes 1572872 | tf_op jit(solution)/shard_map/ppermute | solution.py:705
  404.1 25.8 %collective-permute-start.79 = (bf16[512,512]{1,0:T(8,128)(2,1)}, bf16[512,512]{1,0:T(8,128)(2,1)}, u32[]{:S(2)}, u32[]{:S(2)}) collective-permute-start(bf16[512,512]{1,0:T(8,128)(2,1)} %get-tuple-element.228), channel_id=1, source_target_pairs={{0,4},{2,6},{4,0},{6,2},{1,5},{3,7},{5,1},{7,3},{8,12},{10,14},{12... | collective-permute-start | bytes 1572872 | tf_op jit(solution)/shard_map/ppermute | solution.py:705
  408.0 34.1 %collective-permute-start.74 = (bf16[512,1024]{1,0:T(8,128)(2,1)}, bf16[512,1024]{1,0:T(8,128)(2,1)}, u32[]{:S(2)}, u32[]{:S(2)}) collective-permute-start(bf16[512,1024]{1,0:T(8,128)(2,1)} %convolution_convert_fusion.5), channel_id=1, source_target_pairs={{0,1},{1,0},{2,3},{3,2},{4,5},{5,4},{6,7},{7,6},{8,9},{9,8},{10,11... | collective-permute-start | bytes 3145736 | tf_op jit(solution)/shard_map/ppermute | solution.py:708
  415.9 33.8 %collective-permute-start.72 = (bf16[256,1024]{1,0:T(8,128)(2,1)}, bf16[256,1024]{1,0:T(8,128)(2,1)}, u32[]{:S(2)}, u32[]{:S(2)}) collective-permute-start(bf16[256,1024]{1,0:T(8,128)(2,1)} %get-tuple-element.215), channel_id=1, source_target_pairs={{0,4},{2,6},{4,0},{6,2},{1,5},{3,7},{5,1},{7,3},{8,12},{10,14},{12... | collective-permute-start | bytes 1572872 | tf_op jit(solution)/shard_map/ppermute | solution.py:705
  433.8 19.2 %collective-permute-start.80 = (bf16[512,512]{1,0:T(8,128)(2,1)}, bf16[512,512]{1,0:T(8,128)(2,1)}, u32[]{:S(2)}, u32[]{:S(2)}) collective-permute-start(bf16[512,512]{1,0:T(8,128)(2,1)} %add_convert_fusion.6), channel_id=1, source_target_pairs={{0,1},{1,0},{2,3},{3,2},{4,5},{5,4},{6,7},{7,6},{8,9},{9,8},{10,11... | collective-permute-start | bytes 1572872 | tf_op jit(solution)/shard_map/ppermute | solution.py:708
  460.5 68.0 %reduce-scatter.9.cloned.1.call-start = ((), (), s32[]{:S(2)}) async-start(), calls=%async_computation.6 | async-start | bytes 1310720 | tf_op jit(solution)/shard_map/reduce_scatter | solution.py:948
  475.6 34.0 %collective-permute-start.97 = (bf16[3,704,128]{2,1,0:T(8,128)(2,1)}, bf16[3,704,128]{2,1,0:T(8,128)(2,1)S(1)}, u32[]{:S(2)}, u32[]{:S(2)}) collective-permute-start(bf16[3,704,128]{2,1,0:T(8,128)(2,1)} %pad_maximum_fusion.11), channel_id=1, source_target_pairs={{0,2},{2,0},{4,6},{6,4},{1,3},{3,1},{5,7},{7,5},{8,10},{10,8},{12,... | collective-permute-start | bytes 1622024 | tf_op jit(solution)/shard_map/ppermute | solution.py:705
  476.4 34.9 %collective-permute-start.98 = (bf16[3,704,128]{2,1,0:T(8,128)(2,1)}, bf16[3,704,128]{2,1,0:T(8,128)(2,1)S(1)}, u32[]{:S(2)}, u32[]{:S(2)}) collective-permute-start(bf16[3,704,128]{2,1,0:T(8,128)(2,1)} %pad_maximum_fusion.12), channel_id=1, source_target_pairs={{0,4},{2,6},{4,0},{6,2},{1,5},{3,7},{5,1},{7,3},{8,12},{10,14},{12... | collective-permute-start | bytes 1622024 | tf_op jit(solution)/shard_map/ppermute | solution.py:705
  477.4 22.1 %collective-permute-start.75 = (bf16[512,512]{1,0:T(8,128)(2,1)}, bf16[512,512]{1,0:T(8,128)(2,1)}, u32[]{:S(2)}, u32[]{:S(2)}) collective-permute-start(bf16[512,512]{1,0:T(8,128)(2,1)} %get-tuple-element.220), channel_id=1, source_target_pairs={{0,1},{1,0},{2,3},{3,2},{4,5},{5,4},{6,7},{7,6},{8,9},{9,8},{10,11... | collective-permute-start | bytes 1572872 | tf_op jit(solution)/shard_map/ppermute | solution.py:708
  477.4 25.6 %collective-permute-start.76 = (bf16[512,512]{1,0:T(8,128)(2,1)}, bf16[512,512]{1,0:T(8,128)(2,1)}, u32[]{:S(2)}, u32[]{:S(2)}) collective-permute-start(bf16[512,512]{1,0:T(8,128)(2,1)} %get-tuple-element.222), channel_id=1, source_target_pairs={{0,1},{1,0},{2,3},{3,2},{4,5},{5,4},{6,7},{7,6},{8,9},{9,8},{10,11... | collective-permute-start | bytes 1572872 | tf_op jit(solution)/shard_map/ppermute | solution.py:708
  495.3 17.0 %collective-permute-start.99 = (bf16[3,704,128]{2,1,0:T(8,128)(2,1)}, bf16[3,704,128]{2,1,0:T(8,128)(2,1)S(1)}, u32[]{:S(2)}, u32[]{:S(2)}) collective-permute-start(bf16[3,704,128]{2,1,0:T(8,128)(2,1)} %pad_maximum_fusion.13), channel_id=1, source_target_pairs={{0,6},{2,4},{4,2},{6,0},{1,7},{3,5},{5,3},{7,1},{8,14},{10,12},{12... | collective-permute-start | bytes 1622024 | tf_op jit(solution)/shard_map/ppermute | solution.py:705
  (178 other events, 1260.7 us)
Sparse Core Ops, SparseCore 0:
  75.3 59.6 all-gather.4
  155.2 34.3 all-gather.6
  269.5 58.0 reduce-scatter.4
  329.7 102.0 reduce-scatter.6
  460.6 27.1 reduce-scatter.10
  490.1 28.1 reduce-scatter.8

commit v6 on v5

--- a/solution.py
+++ b/solution.py
@@ -15,7 +15,7 @@
 BF = jnp.bfloat16
 F32 = jnp.float32
 HEADS_PER_STEP = 4
-FL = {'f11': 0, 'f13': 1, 'f0': 1, 'f1': 1, 'f5': 2, 'f9': 1, 'f12': 2, 'f2': 1, 'f3': 1, 'f4': 0, 'f8': 1, 'f10': 3, 'f6': 1, 'f7': 1, 'f14': 1, 'f15': 0, 'f16': 0, 'f17': 0, 'b0': 1, 'b1': 0, 'b2': 1, 'b3': 0, 'b4': 0, 'b5': 2, 'b6': 0, 'b7': 1, 'b8': 1, 'b29': 0, 'b28': 0, 'b18': 2, 'b19': 1, 'b24': 2, 'b9': 3, 'b13': 5, 'b14': 1, 'b15': 0, 'b16': 3, 'b17': 2, 'b20': 0, 'b22': 0, 'b23': 0, 'b25': 1, 'b26': 1, 'b27': 0, 'b30': 0, 'b31': 0, 'b32': 0, 'b33': 0, 'b34': 0, 'b36': 0, 'b37': 1}
+FL = {'f11': 0, 'f13': 1, 'f0': 1, 'f1': 1, 'f5': 2, 'f9': 1, 'f12': 2, 'f2': 1, 'f3': 1, 'f4': 0, 'f8': 1, 'f10': 3, 'f6': 1, 'f7': 1, 'f14': 1, 'f15': 0, 'f16': 0, 'f17': 0, 'b0': 1, 'b1': 0, 'b2': 1, 'b3': 0, 'b4': 0, 'b5': 2, 'b6': 0, 'b7': 1, 'b8': 1, 'b29': 0, 'b28': 0, 'b18': 2, 'b19': 1, 'b24': 1, 'b9': 3, 'b13': 5, 'b14': 1, 'b15': 1, 'b16': 3, 'b17': 2, 'b20': 0, 'b22': 0, 'b23': 0, 'b25': 1, 'b26': 1, 'b27': 0, 'b30': 0, 'b31': 0, 'b32': 0, 'b33': 0, 'b34': 0, 'b36': 0, 'b37': 1}
 
 
 def dot_nn(a, b):

time: 548 us -> 534 us (0.974)
  waiting for transfers between devices: 152 us -> 139 us
  starting transfers between devices: 82.4 us -> 94 us
  other arithmetic: 80.9 us -> 73.3 us
    ppermute x18, starting transfers between devices: 31.9 us -> 43.5 us  [swap_col(): return lax.ppermute(a, 'col', [(0, 1), (1, 0)])]
    ppermute x79, waiting for transfers between devices: 99.6 us -> 91.9 us  [swap_row(): return lax.ppermute(a, 'row', [(i, i ^ bit) for i in range(R)])]
    ppermute x18, waiting for transfers between devices: 51.2 us -> 45.7 us  [swap_col(): return lax.ppermute(a, 'col', [(0, 1), (1, 0)])]
    unnamed x249 -> x247, local copies, waits for them, and re-layouts: 25.4 us -> 23.4 us
  transfers between devices with their start and end apart: 106 -> 106, of which waited for: 37 -> 38; matrix products, arithmetic and copies ran while one was open for 25% -> 23% of each run, Pallas kernels for 18% -> 18%
where the time goes in v6:
time: 534 us; the launch traced here: 523 us
  waiting for transfers between devices  139 us (26%)
  Pallas kernels  129 us (24%)
  starting transfers between devices  94 us (18%)
  other arithmetic  73.3 us (14%)
  local copies, waits for them, and re-layouts  39.5 us (7%)
  matrix products  32.3 us (6%)
  between operations  16.1 us (3%)
    ppermute x79, waiting for transfers between devices, swap_row(): return lax.ppermute(a, 'row', [(i, i ^ bit) for i in range(R)])  91.9 us
    pallas_call x2, Pallas kernels, feed(): pl.pallas_call(functools.partial(feed_body, rows_n=R, parts=parts, near=n...  51.6 us
    ppermute x18, waiting for transfers between devices, swap_col(): return lax.ppermute(a, 'col', [(0, 1), (1, 0)])  45.7 us
    ppermute x79, starting transfers between devices, swap_row(): return lax.ppermute(a, 'row', [(i, i ^ bit) for i in range(R)])  45.3 us
    ppermute x18, starting transfers between devices, swap_col(): return lax.ppermute(a, 'col', [(0, 1), (1, 0)])  43.5 us
    unnamed x247, local copies, waits for them, and re-layouts  23.4 us
    convert_element_type x19, other arithmetic, add(): return total if wide else total.astype(BF)  21.4 us
    pallas_call x1, Pallas kernels, late_weight_grads(): pl.pallas_call(functools.partial(late_weight_body, rows_n=rows_n), grid=(...  19.4 us
  transfers between devices with their start and end apart: 106, of which 38 were waited for; matrix products, arithmetic and copies ran while one was open for 23% of the time, Pallas kernels for 18%

profile of v6, /device:TPU:0, one launch (start us, length us, event | category | flops | bytes accessed | tf_op | source)
XLA Modules:
  0.0 523.2 jit_solution(9749251432738955076)
XLA Ops:
  9.3 2.6 collective-permute-start.4
  16.9 2.6 fusion.3
  27.0 2.8 convert_element_type.509.refs_8_
  38.3 2.6 convolution_convert_fusion.2
  42.7 2.4 add_convert_fusion.5
  47.3 4.2 cut_weights.3
  58.1 7.6 %collective-permute-done.1 = bf16[256,1024]{1,0:T(8,128)(2,1)} collective-permute-done((bf16[256,1024]{1,0:T(8,128)(2,1)}, bf16[256,1024]{1,0:T(8,128)(2,1)}, u32[]{:S(2)}, u32[]{:S(2)}) %collective-permute-start.1) | collective-permute-done | bytes 524320 | tf_op jit(solution)/shard_map/ppermute | solution.py:705
  79.8 5.4 %attend.2 = (bf16[256,1024]{1,0:T(8,128)(2,1)}, bf16[256,1024]{1,0:T(8,128)(2,1)}, f32[8,1,256]{2,1,0:T(1,128)}) custom-call(s32[2]{0:T(128)} %pad_add_fusion.where, s32[2048]{0:T(1024)} %seq_ref.7, s32[2048]{0:T(1024)} %block_ref.7, f32[256,1024]{1,0:T(8,128)} %add_multiply_fusion.q_ref, f32[256,128]{1,0:T(8,128)} %get-tuple-element.325.cos_ref, ...), custom_call_target="tpu_custom_call" | custom-call | flops 1073741824 | bytes 3145728 | tf_op jit(solution)/shard_map/attend/pallas_call | solution.py:103
  86.5 22.1 %collective-permute-done.20 = bf16[256,1024]{1,0:T(8,128)(2,1)S(1)} collective-permute-done((bf16[256,1024]{1,0:T(8,128)(2,1)S(1)}, bf16[256,1024]{1,0:T(8,128)(2,1)S(1)}, u32[]{:S(2)}, u32[]{:S(2)}) %collective-permute-start.20) | collective-permute-done | bytes 524320 | tf_op jit(solution)/shard_map/ppermute | solution.py:705
  111.7 5.5 %attend.3 = (bf16[256,1024]{1,0:T(8,128)(2,1)}, bf16[256,1024]{1,0:T(8,128)(2,1)}, f32[8,1,256]{2,1,0:T(1,128)}) custom-call(s32[2]{0:T(128)} %pad_add_fusion.where, s32[2048]{0:T(1024)} %seq_ref.7, s32[2048]{0:T(1024)} %block_ref.7, f32[256,1024]{1,0:T(8,128)} %broadcast_multiply_fusion.q_ref, f32[256,128]{1,0:T(8,128)} %get-tuple-element.325.cos_ref, ...), custom_call_target="tpu_custom_call" | custom-call | flops 1073741824 | bytes 3145728 | tf_op jit(solution)/shard_map/attend/pallas_call | solution.py:103
  120.4 11.7 %collective-permute-done.24 = bf16[256,1024]{1,0:T(8,128)(2,1)S(1)} collective-permute-done((bf16[256,1024]{1,0:T(8,128)(2,1)}, bf16[256,1024]{1,0:T(8,128)(2,1)S(1)}, u32[]{:S(2)}, u32[]{:S(2)}) %collective-permute-start.24) | collective-permute-done | bytes 524320 | tf_op jit(solution)/shard_map/ppermute | solution.py:705
  134.2 5.8 %collective-permute-start.28 = (bf16[1024,512]{1,0:T(8,128)(2,1)}, bf16[1024,512]{1,0:T(8,128)(2,1)}, u32[]{:S(2)}, u32[]{:S(2)}) collective-permute-start(bf16[1024,512]{1,0:T(8,128)(2,1)} %collective-permute-done.23.refs_10_), channel_id=1, source_target_pairs={{0,1},{1,0},{2,3},{3,2},{4,5},{5,4},{6,7},{7,6},{8,9},{9,8},{10,11... | collective-permute-start | bytes 3145736 | tf_op jit(solution)/shard_map/ppermute | solution.py:708
  144.8 2.5 fusion.48
  147.3 2.5 convolution_add_fusion
  156.4 7.5 %collective-permute-done.28.refs_10_ = bf16[1024,512]{1,0:T(8,128)(2,1)} collective-permute-done((bf16[1024,512]{1,0:T(8,128)(2,1)}, bf16[1024,512]{1,0:T(8,128)(2,1)}, u32[]{:S(2)}, u32[]{:S(2)}) %collective-permute-start.28) | collective-permute-done | bytes 1048608 | tf_op jit(solution)/shard_map/ppermute | solution.py:708
  168.6 11.1 %collective-permute-done.44.refs_4_ = bf16[512,512]{1,0:T(8,128)(2,1)S(1)} collective-permute-done((bf16[512,512]{1,0:T(8,128)(2,1)S(1)}, bf16[512,512]{1,0:T(8,128)(2,1)S(1)}, u32[]{:S(2)}, u32[]{:S(2)}) %collective-permute-start.44) | collective-permute-done | bytes 524320 | tf_op jit(solution)/shard_map/ppermute | solution.py:708
  181.4 8.3 %collective-permute-done.35.refs_0_ = bf16[512,512]{1,0:T(8,128)(2,1)S(1)} collective-permute-done((bf16[512,512]{1,0:T(8,128)(2,1)}, bf16[512,512]{1,0:T(8,128)(2,1)S(1)}, u32[]{:S(2)}, u32[]{:S(2)}) %collective-permute-start.35) | collective-permute-done | bytes 524320 | tf_op jit(solution)/shard_map/ppermute | solution.py:708
  194.4 8.4 %collective-permute-done.46.refs_6_ = bf16[512,512]{1,0:T(8,128)(2,1)S(1)} collective-permute-done((bf16[512,512]{1,0:T(8,128)(2,1)}, bf16[512,512]{1,0:T(8,128)(2,1)S(1)}, u32[]{:S(2)}, u32[]{:S(2)}) %collective-permute-start.46) | collective-permute-done | bytes 524320 | tf_op jit(solution)/shard_map/ppermute | solution.py:708
  206.8 25.6 %feed.3 = (bf16[1024,704]{1,0:T(8,128)(2,1)}, bf16[1024,704]{1,0:T(8,128)(2,1)}, bf16[1024,704]{1,0:T(8,128)(2,1)}, bf16[1024,512]{1,0:T(8,128)(2,1)}, bf16[1024...) custom-call(bf16[512,512]{1,0:T(8,128)(2,1)} %copy-done.104, ...), custom_call_target="tpu_custom_call" | custom-call | flops 14763950080 | bytes 29622272 | tf_op jit(solution)/shard_map/feed/pallas_call | solution.py:373
  232.5 25.9 %feed.2 = (bf16[1024,704]{1,0:T(8,128)(2,1)}, bf16[1024,704]{1,0:T(8,128)(2,1)}, bf16[1024,704]{1,0:T(8,128)(2,1)}, bf16[1024,512]{1,0:T(8,128)(2,1)}, bf16[1024...) custom-call(bf16[512,512]{1,0:T(8,128)(2,1)} %get-tuple-element.301., ...), custom_call_target="tpu_custom_call" | custom-call | flops 14763950080 | bytes 29622272 | tf_op jit(solution)/shard_map/feed/pallas_call | solution.py:373
  259.9 9.4 %feed_weights.1 = bf16[4,4,704,128]{3,2,1,0:T(8,128)(2,1)} custom-call(bf16[1024,2048]{1,0:T(8,128)(2,1)} %get-tuple-element.168.x0, bf16[1024,2048]{1,0:T(8,128)(2,1)} %get-tuple-element.169.x1, bf16[1024,704]{1,0:T(8,128)(2,1)S(1)} %copy-done.12, bf16[1024,704]{1,0:T(8,128)(2,1)S(1)} %copy-done.11), custom_call_target="tpu_custom_call" | custom-call | flops 5905580032 | bytes 14155776 | tf_op jit(solution)/shard_map/feed_weights/pallas_call | solution.py:415
  273.3 2.3 add_convert_fusion.29
  283.8 19.4 %late_weights.1 = bf16[4,2,4,704,128]{4,3,2,1,0:T(8,128)(2,1)} custom-call(bf16[1024,2048]{1,0:T(8,128)(2,1)} %get-tuple-element.168.x0, bf16[1024,2048]{1,0:T(8,128)(2,1)} %get-tuple-element.169.x1, bf16[1024,704]{1,0:T(8,128)(2,1)} %get-tuple-element.176.u0, bf16[1024,704]{1,0:T(8,128)(2,1)} %get-tuple-element.177.u1, ...), custom_call_target="tpu_custom_call" | custom-call | flops 11811160064 | bytes 28311552 | tf_op jit(solution)/shard_map/late_weights/pallas_call | solution.py:489
  313.7 9.6 %collective-permute-done.56 = bf16[512,512]{1,0:T(8,128)(2,1)S(1)} collective-permute-done((bf16[512,512]{1,0:T(8,128)(2,1)S(1)}, bf16[512,512]{1,0:T(8,128)(2,1)S(1)}, u32[]{:S(2)}, u32[]{:S(2)}) %collective-permute-start.56) | collective-permute-done | bytes 524320 | tf_op jit(solution)/shard_map/ppermute | solution.py:705
  327.6 3.2 collective-permute-done.61
  333.2 3.0 convolution_convert_fusion.1
  337.4 2.5 convolution_convert_fusion
  345.5 2.3 convolution_convert_fusion.4
  351.1 8.1 %collective-permute-done.63 = bf16[256,1024]{1,0:T(8,128)(2,1)S(1)} collective-permute-done((bf16[256,1024]{1,0:T(8,128)(2,1)S(1)}, bf16[256,1024]{1,0:T(8,128)(2,1)S(1)}, u32[]{:S(2)}, u32[]{:S(2)}) %collective-permute-start.63) | collective-permute-done | bytes 524320 | tf_op jit(solution)/shard_map/ppermute | solution.py:705
  360.5 6.8 %attend_back.2 = (bf16[256,1024]{1,0:T(8,128)(2,1)}, f32[8,256,128]{2,1,0:T(8,128)}, f32[8,256,128]{2,1,0:T(8,128)}) custom-call(s32[2]{0:T(128)} %pad_add_fusion.where, s32[2048]{0:T(1024)} %seq_ref.7, s32[2048]{0:T(1024)} %block_ref.7, bf16[256,1024]{1,0:T(8,128)(2,1)} %get-tuple-element.157.rot_ref, bf16[256,1024]{1,0:T(8,128)(2,1)} %add_convert_fusion.19.grad_ref, ...), custom_call_target="tpu_custom_call" | custom-call | flops 2684354560 | bytes 5242880 | tf_op jit(solution)/shard_map/attend_back/pallas_call | solution.py:202
  369.1 13.7 %down_products.1 = (bf16[1024,512]{1,0:T(8,128)(2,1)}, bf16[1024,512]{1,0:T(8,128)(2,1)}, bf16[1024,512]{1,0:T(8,128)(2,1)}, bf16[1024,512]{1,0:T(8,128)(2,1)}, ...) custom-call(bf16[1024,704]{1,0:T(8,128)(2,1)} %get-tuple-element.198, ...), custom_call_target="tpu_custom_call" | custom-call | tf_op jit(solution)/shard_map/down_products/pallas_call | solution.py:535
  394.9 2.3 convolution_convert_fusion.5
  397.2 8.2 %collective-permute-start.74 = (bf16[512,1024]{1,0:T(8,128)(2,1)}, bf16[512,1024]{1,0:T(8,128)(2,1)}, u32[]{:S(2)}, u32[]{:S(2)}) collective-permute-start(bf16[512,1024]{1,0:T(8,128)(2,1)} %convolution_convert_fusion.5), channel_id=1, source_target_pairs={{0,1},{1,0},{2,3},{3,2},{4,5},{5,4},{6,7},{7,6},{8,9},{9,8},{10,11... | collective-permute-start | bytes 3145736 | tf_op jit(solution)/shard_map/ppermute | solution.py:708
  405.4 2.6 add_convert_fusion
  408.0 7.5 %attend_back.3 = (bf16[256,1024]{1,0:T(8,128)(2,1)}, f32[8,256,128]{2,1,0:T(8,128)}, f32[8,256,128]{2,1,0:T(8,128)}) custom-call(s32[2]{0:T(128)} %pad_add_fusion.where, s32[2048]{0:T(1024)} %seq_ref.7, s32[2048]{0:T(1024)} %block_ref.7, bf16[256,1024]{1,0:T(8,128)(2,1)} %get-tuple-element.208.rot_ref, bf16[256,1024]{1,0:T(8,128)(2,1)} %add_convert_fusion.14.grad_ref, ...), custom_call_target="tpu_custom_call" | custom-call | flops 2684354560 | bytes 5242880 | tf_op jit(solution)/shard_map/attend_back/pallas_call | solution.py:202
  418.2 9.1 %collective-permute-start.80 = (bf16[512,512]{1,0:T(8,128)(2,1)S(1)}, bf16[512,512]{1,0:T(8,128)(2,1)S(1)}, u32[]{:S(2)}, u32[]{:S(2)}) collective-permute-start(bf16[512,512]{1,0:T(8,128)(2,1)S(1)} %add_convert_fusion.6), channel_id=1, source_target_pairs={{0,1},{1,0},{2,3},{3,2},{4,5},{5,4},{6,7},{7,6},{8,9},{9,8},{10,11... | collective-permute-start | bytes 1572872 | tf_op jit(solution)/shard_map/ppermute | solution.py:708
  427.4 2.4 collective-permute-done.74
  431.5 3.8 fusion.49
  437.3 2.5 collective-permute-done.80
  439.7 2.4 collective-permute-done.86
  451.3 2.6 fusion.50
  455.1 3.5 add_convert_fusion.1
  472.7 2.7 fusion.10
  478.6 2.5 collective-permute-done.91
  481.4 3.8 fusion.7
  492.9 2.6 collective-permute-start.95
  498.0 4.1 finish_weights.1
  504.2 6.4 %collective-permute-done.77 = bf16[512,512]{1,0:T(8,128)(2,1)S(1)} collective-permute-done((bf16[512,512]{1,0:T(8,128)(2,1)S(1)}, bf16[512,512]{1,0:T(8,128)(2,1)S(1)}, u32[]{:S(2)}, u32[]{:S(2)}) %collective-permute-start.77) | collective-permute-done | bytes 524320 | tf_op jit(solution)/shard_map/ppermute | solution.py:705
  (566 shorter events, 190.5 us)
Async XLA Ops:
  7.2 199.6 %all-gather.5.cloned.1.call-start = ((), (), s32[]{:S(2)}) async-start(), calls=%async_computation.8 | async-start | bytes 3604480 | tf_op jit(solution)/shard_map/all_gather | solution.py:894
  9.3 28.4 %collective-permute-start.4 = (bf16[512,1024]{1,0:T(8,128)(2,1)}, bf16[512,1024]{1,0:T(8,128)(2,1)}, u32[]{:S(2)}, u32[]{:S(2)}) collective-permute-start(bf16[512,1024]{1,0:T(8,128)(2,1)} %param.20), channel_id=1, source_target_pairs={{0,1},{1,0},{2,3},{3,2},{4,5},{5,4},{6,7},{7,6},{8,9},{9,8},{10,11... | collective-permute-start | bytes 3145736 | tf_op jit(solution)/shard_map/ppermute | solution.py:708
  23.6 19.1 %collective-permute-start = (bf16[512,1024]{1,0:T(8,128)(2,1)}, bf16[512,1024]{1,0:T(8,128)(2,1)}, u32[]{:S(2)}, u32[]{:S(2)}) collective-permute-start(bf16[512,1024]{1,0:T(8,128)(2,1)} %slice.355), channel_id=1, source_target_pairs={{0,2},{2,0},{4,6},{6,4},{1,3},{3,1},{5,7},{7,5},{8,10},{10,8},{12,... | collective-permute-start | bytes 3145736 | tf_op jit(solution)/shard_map/ppermute | solution.py:705
  36.5 17.9 %collective-permute-start.8 = (bf16[2,704,128]{2,1,0:T(8,128)(2,1)S(1)}, bf16[2,704,128]{2,1,0:T(8,128)(2,1)S(1)}, u32[]{:S(2)}, u32[]{:S(2)}) collective-permute-start(bf16[2,704,128]{2,1,0:T(8,128)(2,1)S(1)} %get-tuple-element.130), channel_id=1, source_target_pairs={{0,4},{2,6},{4,0},{6,2},{1,5},{3,7},{5,1},{7,3},{8,12},{10,14},{12... | collective-permute-start | bytes 1081352 | tf_op jit(solution)/shard_map/ppermute | solution.py:705
  37.7 17.9 %collective-permute-start.9 = (bf16[2,704,128]{2,1,0:T(8,128)(2,1)S(1)}, bf16[2,704,128]{2,1,0:T(8,128)(2,1)S(1)}, u32[]{:S(2)}, u32[]{:S(2)}) collective-permute-start(bf16[2,704,128]{2,1,0:T(8,128)(2,1)S(1)} %get-tuple-element.131), channel_id=1, source_target_pairs={{0,6},{2,4},{4,2},{6,0},{1,7},{3,5},{5,3},{7,1},{8,14},{10,12},{12... | collective-permute-start | bytes 1081352 | tf_op jit(solution)/shard_map/ppermute | solution.py:705
  37.7 30.8 %collective-permute-start.5 = (bf16[1024,512]{1,0:T(8,128)(2,1)}, bf16[1024,512]{1,0:T(8,128)(2,1)}, u32[]{:S(2)}, u32[]{:S(2)}) collective-permute-start(bf16[1024,512]{1,0:T(8,128)(2,1)} %param.22), channel_id=1, source_target_pairs={{0,1},{1,0},{2,3},{3,2},{4,5},{5,4},{6,7},{7,6},{8,9},{9,8},{10,11... | collective-permute-start | bytes 3145736 | tf_op jit(solution)/shard_map/ppermute | solution.py:708
  42.0 29.3 %collective-permute-start.19 = (bf16[512,1024]{1,0:T(8,128)(2,1)}, bf16[512,1024]{1,0:T(8,128)(2,1)}, u32[]{:S(2)}, u32[]{:S(2)}) collective-permute-start(bf16[512,1024]{1,0:T(8,128)(2,1)} %slice.367), channel_id=1, source_target_pairs={{0,2},{2,0},{4,6},{6,4},{1,3},{3,1},{5,7},{7,5},{8,10},{10,8},{12,... | collective-permute-start | bytes 3145736 | tf_op jit(solution)/shard_map/ppermute | solution.py:705
  46.0 19.7 %collective-permute-start.1 = (bf16[256,1024]{1,0:T(8,128)(2,1)}, bf16[256,1024]{1,0:T(8,128)(2,1)}, u32[]{:S(2)}, u32[]{:S(2)}) collective-permute-start(bf16[256,1024]{1,0:T(8,128)(2,1)} %slice.357), channel_id=1, source_target_pairs={{0,4},{2,6},{4,0},{6,2},{1,5},{3,7},{5,1},{7,3},{8,12},{10,14},{12... | collective-permute-start | bytes 1572872 | tf_op jit(solution)/shard_map/ppermute | solution.py:705
  54.4 32.1 %collective-permute-start.21 = (bf16[2,704,512]{2,1,0:T(8,128)(2,1)}, bf16[2,704,512]{2,1,0:T(8,128)(2,1)}, u32[]{:S(2)}, u32[]{:S(2)}) collective-permute-start(bf16[2,704,512]{2,1,0:T(8,128)(2,1)} %get-tuple-element.136), channel_id=1, source_target_pairs={{0,2},{2,0},{4,6},{6,4},{1,3},{3,1},{5,7},{7,5},{8,10},{10,8},{12,... | collective-permute-start | bytes 4325384 | tf_op jit(solution)/shard_map/ppermute | solution.py:705
  70.7 39.9 %collective-permute-start.23 = (bf16[1024,512]{1,0:T(8,128)(2,1)}, bf16[1024,512]{1,0:T(8,128)(2,1)}, u32[]{:S(2)}, u32[]{:S(2)}) collective-permute-start(bf16[1024,512]{1,0:T(8,128)(2,1)} %convert_element_type.509.refs_8_), channel_id=1, source_target_pairs={{0,4},{2,6},{4,0},{6,2},{1,5},{3,7},{5,1},{7,3},{8,12},{10,14},{12... | collective-permute-start | bytes 3145736 | tf_op jit(solution)/shard_map/ppermute | solution.py:705
  71.3 39.3 %collective-permute-start.22 = (bf16[1024,512]{1,0:T(8,128)(2,1)}, bf16[1024,512]{1,0:T(8,128)(2,1)}, u32[]{:S(2)}, u32[]{:S(2)}) collective-permute-start(bf16[1024,512]{1,0:T(8,128)(2,1)} %convert_element_type.509.refs_8_), channel_id=1, source_target_pairs={{0,1},{1,0},{2,3},{3,2},{4,5},{5,4},{6,7},{7,6},{8,9},{9,8},{10,11... | collective-permute-start | bytes 3145736 | tf_op jit(solution)/shard_map/ppermute | solution.py:708
  73.5 35.1 %collective-permute-start.20 = (bf16[256,1024]{1,0:T(8,128)(2,1)S(1)}, bf16[256,1024]{1,0:T(8,128)(2,1)S(1)}, u32[]{:S(2)}, u32[]{:S(2)}) collective-permute-start(bf16[256,1024]{1,0:T(8,128)(2,1)S(1)} %slice.369), channel_id=1, source_target_pairs={{0,4},{2,6},{4,0},{6,2},{1,5},{3,7},{5,1},{7,3},{8,12},{10,14},{12... | collective-permute-start | bytes 1572872 | tf_op jit(solution)/shard_map/ppermute | solution.py:705
  75.1 131.7 %all-gather.7.cloned.1.call-start = ((), (), s32[]{:S(2)}) async-start(), calls=%async_computation.9 | async-start | bytes 1802240 | tf_op jit(solution)/shard_map/all_gather | solution.py:901
  85.2 34.1 %collective-permute-start.17 = (bf16[256,1024]{1,0:T(8,128)(2,1)}, bf16[256,1024]{1,0:T(8,128)(2,1)S(1)}, u32[]{:S(2)}, u32[]{:S(2)}) collective-permute-start(bf16[256,1024]{1,0:T(8,128)(2,1)} %get-tuple-element.133.att_ref), channel_id=1, source_target_pairs={{0,4},{2,6},{4,0},{6,2},{1,5},{3,7},{5,1},{7,3},{8,12},{10,14},{12... | collective-permute-start | bytes 1572872 | tf_op jit(solution)/shard_map/ppermute | solution.py:705
  120.4 19.7 %collective-permute-start.18 = (bf16[512,1024]{1,0:T(8,128)(2,1)}, bf16[512,1024]{1,0:T(8,128)(2,1)}, u32[]{:S(2)}, u32[]{:S(2)}) collective-permute-start(bf16[512,1024]{1,0:T(8,128)(2,1)} %pad_maximum_fusion.3), channel_id=1, source_target_pairs={{0,2},{2,0},{4,6},{6,4},{1,3},{3,1},{5,7},{7,5},{8,10},{10,8},{12,... | collective-permute-start | bytes 3145736 | tf_op jit(solution)/shard_map/ppermute | solution.py:705
  132.4 21.9 %collective-permute-start.39 = (bf16[176,512]{1,0:T(8,128)(2,1)S(1)}, bf16[176,512]{1,0:T(8,128)(2,1)S(1)}, u32[]{:S(2)}, u32[]{:S(2)}) collective-permute-start(bf16[176,512]{1,0:T(8,128)(2,1)S(1)} %get-tuple-element.151), channel_id=1, source_target_pairs={{0,4},{2,6},{4,0},{6,2},{1,5},{3,7},{5,1},{7,3},{8,12},{10,14},{12... | collective-permute-start | bytes 540680 | tf_op jit(solution)/shard_map/ppermute | solution.py:705
  133.9 20.4 %collective-permute-start.40 = (bf16[176,512]{1,0:T(8,128)(2,1)S(1)}, bf16[176,512]{1,0:T(8,128)(2,1)S(1)}, u32[]{:S(2)}, u32[]{:S(2)}) collective-permute-start(bf16[176,512]{1,0:T(8,128)(2,1)S(1)} %get-tuple-element.152), channel_id=1, source_target_pairs={{0,6},{2,4},{4,2},{6,0},{1,7},{3,5},{5,3},{7,1},{8,14},{10,12},{12... | collective-permute-start | bytes 540680 | tf_op jit(solution)/shard_map/ppermute | solution.py:705
  134.2 29.8 %collective-permute-start.28 = (bf16[1024,512]{1,0:T(8,128)(2,1)}, bf16[1024,512]{1,0:T(8,128)(2,1)}, u32[]{:S(2)}, u32[]{:S(2)}) collective-permute-start(bf16[1024,512]{1,0:T(8,128)(2,1)} %collective-permute-done.23.refs_10_), channel_id=1, source_target_pairs={{0,1},{1,0},{2,3},{3,2},{4,5},{5,4},{6,7},{7,6},{8,9},{9,8},{10,11... | collective-permute-start | bytes 3145736 | tf_op jit(solution)/shard_map/ppermute | solution.py:708
  155.0 205.4 %reduce-scatter.5.cloned.1.call-start = ((), (), s32[]{:S(2)}) async-start(), calls=%async_computation.4 | async-start | bytes 3604480 | tf_op jit(solution)/shard_map/reduce_scatter | solution.py:948
  166.6 24.6 %collective-permute-start.38 = (bf16[704,512]{1,0:T(8,128)(2,1)S(1)}, bf16[704,512]{1,0:T(8,128)(2,1)S(1)}, u32[]{:S(2)}, u32[]{:S(2)}) collective-permute-start(bf16[704,512]{1,0:T(8,128)(2,1)S(1)} %copy-done.10), channel_id=1, source_target_pairs={{0,2},{2,0},{4,6},{6,4},{1,3},{3,1},{5,7},{7,5},{8,10},{10,8},{12,... | collective-permute-start | bytes 2162696 | tf_op jit(solution)/shard_map/ppermute | solution.py:705
  166.6 14.8 %collective-permute-start.33 = (bf16[512,512]{1,0:T(8,128)(2,1)S(1)}, bf16[512,512]{1,0:T(8,128)(2,1)}, u32[]{:S(2)}, u32[]{:S(2)}) collective-permute-start(bf16[512,512]{1,0:T(8,128)(2,1)S(1)} %get-tuple-element.300.refs_4_), channel_id=1, source_target_pairs={{0,4},{2,6},{4,0},{6,2},{1,5},{3,7},{5,1},{7,3},{8,12},{10,14},{12... | collective-permute-start | bytes 1572872 | tf_op jit(solution)/shard_map/ppermute | solution.py:705
  168.3 21.4 %collective-permute-start.35 = (bf16[512,512]{1,0:T(8,128)(2,1)}, bf16[512,512]{1,0:T(8,128)(2,1)S(1)}, u32[]{:S(2)}, u32[]{:S(2)}) collective-permute-start(bf16[512,512]{1,0:T(8,128)(2,1)} %get-tuple-element.301.refs_0_), channel_id=1, source_target_pairs={{0,1},{1,0},{2,3},{3,2},{4,5},{5,4},{6,7},{7,6},{8,9},{9,8},{10,11... | collective-permute-start | bytes 1572872 | tf_op jit(solution)/shard_map/ppermute | solution.py:708
  168.6 24.4 %collective-permute-start.32 = (bf16[512,512]{1,0:T(8,128)(2,1)S(1)}, bf16[512,512]{1,0:T(8,128)(2,1)S(1)}, u32[]{:S(2)}, u32[]{:S(2)}) collective-permute-start(bf16[512,512]{1,0:T(8,128)(2,1)S(1)} %get-tuple-element.300.refs_4_), channel_id=1, source_target_pairs={{0,2},{2,0},{4,6},{6,4},{1,3},{3,1},{5,7},{7,5},{8,10},{10,8},{12,... | collective-permute-start | bytes 1572872 | tf_op jit(solution)/shard_map/ppermute | solution.py:705
  203.6 28.9 %collective-permute-start.29 = (bf16[512,512]{1,0:T(8,128)(2,1)}, bf16[512,512]{1,0:T(8,128)(2,1)}, u32[]{:S(2)}, u32[]{:S(2)}) collective-permute-start(bf16[512,512]{1,0:T(8,128)(2,1)} %get-tuple-element.301.refs_0_), channel_id=1, source_target_pairs={{0,2},{2,0},{4,6},{6,4},{1,3},{3,1},{5,7},{7,5},{8,10},{10,8},{12,... | collective-permute-start | bytes 1572872 | tf_op jit(solution)/shard_map/ppermute | solution.py:705
  204.8 27.7 %collective-permute-start.36 = (bf16[1024,512]{1,0:T(8,128)(2,1)}, bf16[1024,512]{1,0:T(8,128)(2,1)}, u32[]{:S(2)}, u32[]{:S(2)}) collective-permute-start(bf16[1024,512]{1,0:T(8,128)(2,1)} %convert_element_type.509.refs_8_), channel_id=1, source_target_pairs={{0,2},{2,0},{4,6},{6,4},{1,3},{3,1},{5,7},{7,5},{8,10},{10,8},{12,... | collective-permute-start | bytes 3145736 | tf_op jit(solution)/shard_map/ppermute | solution.py:705
  205.5 27.0 %collective-permute-start.37 = (bf16[1024,512]{1,0:T(8,128)(2,1)}, bf16[1024,512]{1,0:T(8,128)(2,1)}, u32[]{:S(2)}, u32[]{:S(2)}) collective-permute-start(bf16[1024,512]{1,0:T(8,128)(2,1)} %collective-permute-done.23.refs_10_), channel_id=1, source_target_pairs={{0,2},{2,0},{4,6},{6,4},{1,3},{3,1},{5,7},{7,5},{8,10},{10,8},{12,... | collective-permute-start | bytes 3145736 | tf_op jit(solution)/shard_map/ppermute | solution.py:705
  206.3 26.2 %collective-permute-start.34 = (bf16[512,512]{1,0:T(8,128)(2,1)}, bf16[512,512]{1,0:T(8,128)(2,1)}, u32[]{:S(2)}, u32[]{:S(2)}) collective-permute-start(bf16[512,512]{1,0:T(8,128)(2,1)} %collective-permute-done.33.refs_6_), channel_id=1, source_target_pairs={{0,2},{2,0},{4,6},{6,4},{1,3},{3,1},{5,7},{7,5},{8,10},{10,8},{12,... | collective-permute-start | bytes 1572872 | tf_op jit(solution)/shard_map/ppermute | solution.py:705
  206.4 26.1 %collective-permute-start.31 = (bf16[512,512]{1,0:T(8,128)(2,1)}, bf16[512,512]{1,0:T(8,128)(2,1)}, u32[]{:S(2)}, u32[]{:S(2)}) collective-permute-start(bf16[512,512]{1,0:T(8,128)(2,1)} %collective-permute-done.30.refs_2_), channel_id=1, source_target_pairs={{0,2},{2,0},{4,6},{6,4},{1,3},{3,1},{5,7},{7,5},{8,10},{10,8},{12,... | collective-permute-start | bytes 1572872 | tf_op jit(solution)/shard_map/ppermute | solution.py:705
  269.3 177.2 %reduce-scatter.7.cloned.1.call-start = ((), (), s32[]{:S(2)}) async-start(), calls=%async_computation.5 | async-start | bytes 7208960 | tf_op jit(solution)/shard_map/reduce_scatter | solution.py:948
  279.8 26.7 %collective-permute-start.57 = (bf16[512,512]{1,0:T(8,128)(2,1)}, bf16[512,512]{1,0:T(8,128)(2,1)}, u32[]{:S(2)}, u32[]{:S(2)}) collective-permute-start(bf16[512,512]{1,0:T(8,128)(2,1)} %get-tuple-element.187), channel_id=1, source_target_pairs={{0,4},{2,6},{4,0},{6,2},{1,5},{3,7},{5,1},{7,3},{8,12},{10,14},{12... | collective-permute-start | bytes 1572872 | tf_op jit(solution)/shard_map/ppermute | solution.py:705
  281.4 23.8 %collective-permute-start.58 = (bf16[512,512]{1,0:T(8,128)(2,1)}, bf16[512,512]{1,0:T(8,128)(2,1)}, u32[]{:S(2)}, u32[]{:S(2)}) collective-permute-start(bf16[512,512]{1,0:T(8,128)(2,1)} %get-tuple-element.190), channel_id=1, source_target_pairs={{0,4},{2,6},{4,0},{6,2},{1,5},{3,7},{5,1},{7,3},{8,12},{10,14},{12... | collective-permute-start | bytes 1572872 | tf_op jit(solution)/shard_map/ppermute | solution.py:705
  281.8 26.0 %collective-permute-start.54 = (bf16[512,512]{1,0:T(8,128)(2,1)}, bf16[512,512]{1,0:T(8,128)(2,1)}, u32[]{:S(2)}, u32[]{:S(2)}) collective-permute-start(bf16[512,512]{1,0:T(8,128)(2,1)} %get-tuple-element.167), channel_id=1, source_target_pairs={{0,1},{1,0},{2,3},{3,2},{4,5},{5,4},{6,7},{7,6},{8,9},{9,8},{10,11... | collective-permute-start | bytes 1572872 | tf_op jit(solution)/shard_map/ppermute | solution.py:708
  283.5 24.3 %collective-permute-start.55 = (bf16[512,512]{1,0:T(8,128)(2,1)}, bf16[512,512]{1,0:T(8,128)(2,1)}, u32[]{:S(2)}, u32[]{:S(2)}) collective-permute-start(bf16[512,512]{1,0:T(8,128)(2,1)} %get-tuple-element.182), channel_id=1, source_target_pairs={{0,1},{1,0},{2,3},{3,2},{4,5},{5,4},{6,7},{7,6},{8,9},{9,8},{10,11... | collective-permute-start | bytes 1572872 | tf_op jit(solution)/shard_map/ppermute | solution.py:708
  303.2 209.3 %reduce-scatter.11.cloned.1.call-start = ((), (), s32[]{:S(2)}) async-start(), calls=%async_computation.7 | async-start | bytes 1310720 | tf_op jit(solution)/shard_map/reduce_scatter | solution.py:948
  347.8 38.9 %collective-permute-start.96 = (bf16[1024,512]{1,0:T(8,128)(2,1)}, bf16[1024,512]{1,0:T(8,128)(2,1)}, u32[]{:S(2)}, u32[]{:S(2)}) collective-permute-start(bf16[1024,512]{1,0:T(8,128)(2,1)} %convolution_convert_fusion.4), channel_id=1, source_target_pairs={{0,1},{1,0},{2,3},{3,2},{4,5},{5,4},{6,7},{7,6},{8,9},{9,8},{10,11... | collective-permute-start | bytes 3145736 | tf_op jit(solution)/shard_map/ppermute | solution.py:708
  360.2 25.1 %collective-permute-start.69 = (bf16[256,1024]{1,0:T(8,128)(2,1)S(1)}, bf16[256,1024]{1,0:T(8,128)(2,1)S(1)}, u32[]{:S(2)}, u32[]{:S(2)}) collective-permute-start(bf16[256,1024]{1,0:T(8,128)(2,1)S(1)} %slice.389), channel_id=1, source_target_pairs={{0,4},{2,6},{4,0},{6,2},{1,5},{3,7},{5,1},{7,3},{8,12},{10,14},{12... | collective-permute-start | bytes 1572872 | tf_op jit(solution)/shard_map/ppermute | solution.py:705
  367.3 19.6 %collective-permute-start.70 = (bf16[256,1024]{1,0:T(8,128)(2,1)}, bf16[256,1024]{1,0:T(8,128)(2,1)S(1)}, u32[]{:S(2)}, u32[]{:S(2)}) collective-permute-start(bf16[256,1024]{1,0:T(8,128)(2,1)} %get-tuple-element.197), channel_id=1, source_target_pairs={{0,4},{2,6},{4,0},{6,2},{1,5},{3,7},{5,1},{7,3},{8,12},{10,14},{12... | collective-permute-start | bytes 1572872 | tf_op jit(solution)/shard_map/ppermute | solution.py:705
  392.8 23.3 %collective-permute-start.78 = (bf16[512,512]{1,0:T(8,128)(2,1)S(1)}, bf16[512,512]{1,0:T(8,128)(2,1)S(1)}, u32[]{:S(2)}, u32[]{:S(2)}) collective-permute-start(bf16[512,512]{1,0:T(8,128)(2,1)S(1)} %get-tuple-element.226), channel_id=1, source_target_pairs={{0,4},{2,6},{4,0},{6,2},{1,5},{3,7},{5,1},{7,3},{8,12},{10,14},{12... | collective-permute-start | bytes 1572872 | tf_op jit(solution)/shard_map/ppermute | solution.py:705
  393.2 24.8 %collective-permute-start.79 = (bf16[512,512]{1,0:T(8,128)(2,1)}, bf16[512,512]{1,0:T(8,128)(2,1)S(1)}, u32[]{:S(2)}, u32[]{:S(2)}) collective-permute-start(bf16[512,512]{1,0:T(8,128)(2,1)} %get-tuple-element.228), channel_id=1, source_target_pairs={{0,4},{2,6},{4,0},{6,2},{1,5},{3,7},{5,1},{7,3},{8,12},{10,14},{12... | collective-permute-start | bytes 1572872 | tf_op jit(solution)/shard_map/ppermute | solution.py:705
  397.2 32.6 %collective-permute-start.74 = (bf16[512,1024]{1,0:T(8,128)(2,1)}, bf16[512,1024]{1,0:T(8,128)(2,1)}, u32[]{:S(2)}, u32[]{:S(2)}) collective-permute-start(bf16[512,1024]{1,0:T(8,128)(2,1)} %convolution_convert_fusion.5), channel_id=1, source_target_pairs={{0,1},{1,0},{2,3},{3,2},{4,5},{5,4},{6,7},{7,6},{8,9},{9,8},{10,11... | collective-permute-start | bytes 3145736 | tf_op jit(solution)/shard_map/ppermute | solution.py:708
  415.5 21.6 %collective-permute-start.72 = (bf16[256,1024]{1,0:T(8,128)(2,1)}, bf16[256,1024]{1,0:T(8,128)(2,1)S(1)}, u32[]{:S(2)}, u32[]{:S(2)}) collective-permute-start(bf16[256,1024]{1,0:T(8,128)(2,1)} %get-tuple-element.215), channel_id=1, source_target_pairs={{0,4},{2,6},{4,0},{6,2},{1,5},{3,7},{5,1},{7,3},{8,12},{10,14},{12... | collective-permute-start | bytes 1572872 | tf_op jit(solution)/shard_map/ppermute | solution.py:705
  418.2 21.5 %collective-permute-start.80 = (bf16[512,512]{1,0:T(8,128)(2,1)S(1)}, bf16[512,512]{1,0:T(8,128)(2,1)S(1)}, u32[]{:S(2)}, u32[]{:S(2)}) collective-permute-start(bf16[512,512]{1,0:T(8,128)(2,1)S(1)} %add_convert_fusion.6), channel_id=1, source_target_pairs={{0,1},{1,0},{2,3},{3,2},{4,5},{5,4},{6,7},{7,6},{8,9},{9,8},{10,11... | collective-permute-start | bytes 1572872 | tf_op jit(solution)/shard_map/ppermute | solution.py:708
  446.5 67.8 %reduce-scatter.9.cloned.1.call-start = ((), (), s32[]{:S(2)}) async-start(), calls=%async_computation.6 | async-start | bytes 1310720 | tf_op jit(solution)/shard_map/reduce_scatter | solution.py:948
  461.3 34.2 %collective-permute-start.97 = (bf16[3,704,128]{2,1,0:T(8,128)(2,1)}, bf16[3,704,128]{2,1,0:T(8,128)(2,1)S(1)}, u32[]{:S(2)}, u32[]{:S(2)}) collective-permute-start(bf16[3,704,128]{2,1,0:T(8,128)(2,1)} %pad_maximum_fusion.11), channel_id=1, source_target_pairs={{0,2},{2,0},{4,6},{6,4},{1,3},{3,1},{5,7},{7,5},{8,10},{10,8},{12,... | collective-permute-start | bytes 1622024 | tf_op jit(solution)/shard_map/ppermute | solution.py:705
  462.2 34.7 %collective-permute-start.98 = (bf16[3,704,128]{2,1,0:T(8,128)(2,1)}, bf16[3,704,128]{2,1,0:T(8,128)(2,1)S(1)}, u32[]{:S(2)}, u32[]{:S(2)}) collective-permute-start(bf16[3,704,128]{2,1,0:T(8,128)(2,1)} %pad_maximum_fusion.12), channel_id=1, source_target_pairs={{0,4},{2,6},{4,0},{6,2},{1,5},{3,7},{5,1},{7,3},{8,12},{10,14},{12... | collective-permute-start | bytes 1622024 | tf_op jit(solution)/shard_map/ppermute | solution.py:705
  463.2 22.1 %collective-permute-start.75 = (bf16[512,512]{1,0:T(8,128)(2,1)}, bf16[512,512]{1,0:T(8,128)(2,1)}, u32[]{:S(2)}, u32[]{:S(2)}) collective-permute-start(bf16[512,512]{1,0:T(8,128)(2,1)} %get-tuple-element.220), channel_id=1, source_target_pairs={{0,1},{1,0},{2,3},{3,2},{4,5},{5,4},{6,7},{7,6},{8,9},{9,8},{10,11... | collective-permute-start | bytes 1572872 | tf_op jit(solution)/shard_map/ppermute | solution.py:708
  465.2 23.9 %collective-permute-start.76 = (bf16[512,512]{1,0:T(8,128)(2,1)}, bf16[512,512]{1,0:T(8,128)(2,1)}, u32[]{:S(2)}, u32[]{:S(2)}) collective-permute-start(bf16[512,512]{1,0:T(8,128)(2,1)} %get-tuple-element.222), channel_id=1, source_target_pairs={{0,1},{1,0},{2,3},{3,2},{4,5},{5,4},{6,7},{7,6},{8,9},{9,8},{10,11... | collective-permute-start | bytes 1572872 | tf_op jit(solution)/shard_map/ppermute | solution.py:708
  481.1 16.9 %collective-permute-start.99 = (bf16[3,704,128]{2,1,0:T(8,128)(2,1)}, bf16[3,704,128]{2,1,0:T(8,128)(2,1)S(1)}, u32[]{:S(2)}, u32[]{:S(2)}) collective-permute-start(bf16[3,704,128]{2,1,0:T(8,128)(2,1)} %pad_maximum_fusion.13), channel_id=1, source_target_pairs={{0,6},{2,4},{4,2},{6,0},{1,7},{3,5},{5,3},{7,1},{8,14},{10,12},{12... | collective-permute-start | bytes 1622024 | tf_op jit(solution)/shard_map/ppermute | solution.py:705
  (177 other events, 1210.6 us)
Sparse Core Ops, SparseCore 0:
  75.3 59.6 all-gather.4
  155.2 34.3 all-gather.6
  269.4 57.1 reduce-scatter.4
  328.7 102.0 reduce-scatter.6
  446.6 26.4 reduce-scatter.10
  475.4 28.1 reduce-scatter.8
